TPU v7x, 32 devices: a whole 2x2x4 slice. The times are simulated.
32 devices in a mesh: shard: 4 (over z), ctx: 2 (over core), tp: 4 (over y, x).
Axes of the slice: x: 2, y: 2, z: 4, core: 2. Of those that a mesh axis runs over, the one named last changes fastest.
Arguments:
- tokens: bfloat16 [8, 2048, 768], P('shard', 'ctx'), may hold values from -6 to 6
- segment_ids: int32 [8, 2048], P('shard', 'ctx'), may hold values from 0 to 34, as said below
- offsets: int32 [8, 2048], P('shard', 'ctx'), may hold values from 0 to 799, as said below
- qkv_weight: bfloat16 [768, 3, 768], P(('shard', 'ctx'), None, 'tp'), may hold values from -0.3125 to 0.3125
- out_weight: bfloat16 [768, 768], P(('shard', 'ctx'), 'tp'), may hold values from -0.875 to 0.875
- ffn_weight: bfloat16 [768, 2, 3072], P(('shard', 'ctx'), None, 'tp'), may hold values from -0.21875 to 0.21875
- qkv_bias: float32 [3, 768], P(None, 'tp'), may hold values from -3 to 3
- ffn_bias: float32 [3072], P('tp'), may hold values from -3 to 3
- norm_gain: float32 [2, 768], replicated, may hold values from 0.5 to 1.5
- shift_params: float32 [4, 768], replicated, may hold values from -3 to 3
- out_grad: bfloat16 [8, 2048, 768], P('shard', 'ctx'), may hold values from -6 to 6
Outputs:
- outputs: bfloat16 [8, 2048, 768], P('shard', 'ctx')
- grad_tokens: bfloat16 [8, 2048, 768], P('shard', 'ctx')
- grad_qkv_weight: float32 [768, 3, 768], P(('shard', 'ctx'), None, 'tp')
- grad_out_weight: float32 [768, 768], P(('shard', 'ctx'), 'tp')
- grad_ffn_weight: float32 [768, 2, 3072], P(('shard', 'ctx'), None, 'tp')
- grad_qkv_bias: float32 [3, 768], P(None, 'tp')
- grad_ffn_bias: float32 [3072], P('tp')
- grad_norm_gain: float32 [2, 768], replicated
- grad_shift_params: float32 [4, 768], replicated
Inputs may be any that keep to these rules, and one draw needn't show every extreme that they name: `segment_ids`: segment numbers start at 0 in each sequence and rise by one where a new document begins. offsets are 0 at a document's first token and rise by one along it; a document has at most 800 tokens, and every document but a sequence's last has at least 60.
All inputs are finite; a program needn't handle non-finite values.
Results may differ from a plain program's by a relative error of at most 0.017.
The roundings to bfloat16 on the way count: a program that leaves them out, or rounds other values in their place, can miss the bound.
Values may be sent and summed in bfloat16 or wider, within the bound.
No kernel may reach another device: no remote copies, remote signals or barrier semaphores. Data moves between devices by JAX's collectives and lax.ppermute only.
A program may use at most 192 MiB of HBM per device.

v0:
```python
from functools import partial

import jax
import jax.numpy as jnp
from jax import lax
from jax.sharding import PartitionSpec as P

HEAD = 64


EPSILON = 1e-12


def rotate_pairs(values, offsets, direction):
    half_size = values.shape[-1] // 2
    frequency = 10000.0 ** (-2.0 * jnp.arange(half_size, dtype=jnp.float32) / values.shape[-1])
    angles = offsets.astype(jnp.float32)[:, None] * frequency[None, :]
    cosine = jnp.cos(angles)[:, None, :]
    sine_part = direction * jnp.sin(angles)[:, None, :]
    paired = values.reshape(values.shape[:-1] + (half_size, 2))
    even_part = paired[..., 0]
    odd_part = paired[..., 1]
    turned = jnp.stack(
        [even_part * cosine - odd_part * sine_part, even_part * sine_part + odd_part * cosine],
        axis=-1,
    )
    return turned.reshape(values.shape)


def norm_parts(rows_in):
    centre = rows_in - jnp.mean(rows_in, axis=-1, keepdims=True)
    inverse_root = lax.rsqrt(jnp.mean(centre * centre, axis=-1, keepdims=True) + EPSILON)
    return (centre * inverse_root, inverse_root)


def norm_back(grad_in, scaled, inverse_root, gain_row):
    grad_scaled = grad_in * gain_row
    term_mean = jnp.mean(grad_scaled, axis=-1, keepdims=True)
    term_along = jnp.mean(grad_scaled * scaled, axis=-1, keepdims=True)
    return inverse_root * (grad_scaled - term_mean - scaled * term_along)


def attention_weights(qkv_weight, out_weight):
    return (
        lax.all_gather(qkv_weight, ("shard", "ctx"), axis=0, tiled=True),
        lax.all_gather(out_weight, ("shard", "ctx"), axis=0, tiled=True),
    )


def feed_weights(ffn_weight):
    return lax.all_gather(ffn_weight, ("shard", "ctx"), axis=0, tiled=True)


def masked_scores(queries, keys_all, same_doc, score_scale):
    scores = (
        jnp.einsum("shd,thd->hst", queries, keys_all, preferred_element_type=jnp.float32)
        * score_scale
    )
    return jnp.where(same_doc, scores, -1e30)


def contract_last(left, right):
    return lax.dot_general(
        left, right, (((1,), (1,)), ((), ())), preferred_element_type=jnp.float32
    )


def contract_first(left, right):
    return lax.dot_general(
        left, right, (((0,), (0,)), ((), ())), preferred_element_type=jnp.float32
    )


def body(
    tokens,
    segment_ids,
    offsets,
    qkv_weight,
    out_weight,
    ffn_weight,
    qkv_bias,
    ffn_bias,
    norm_gain,
    shift_params,
    out_grad,
):
    model_width = tokens.shape[2]
    part_width = qkv_weight.shape[2]
    hidden_width = ffn_weight.shape[2]
    local_heads = part_width // HEAD
    score_scale = HEAD ** (-0.5)
    tp_count = lax.axis_size("tp")
    tp_rank = lax.axis_index("tp")

    def micro_step(totals, micro_batch):
        tokens_mb, segment_mb, offsets_mb, grad_mb = micro_batch
        half_len = tokens_mb.shape[0]
        share_len = half_len // tp_count
        share_start = tp_rank * share_len

        def share_rows(rows):
            return lax.dynamic_slice_in_dim(rows, share_start, share_len, 0)

        qkv_full, out_full = attention_weights(qkv_weight, out_weight)
        ffn_full = feed_weights(ffn_weight)
        projected = (
            jnp.einsum("sd,dke->kse", tokens_mb, qkv_full, preferred_element_type=jnp.float32)
            + qkv_bias[:, None, :]
        )
        per_head = projected.reshape(3, half_len, local_heads, HEAD)
        queries = rotate_pairs(per_head[0], offsets_mb, 1.0).astype(jnp.bfloat16)
        keys_own = rotate_pairs(per_head[1], offsets_mb, 1.0).astype(jnp.bfloat16)
        values_own = per_head[2].astype(jnp.bfloat16)
        pair_own = jnp.stack([keys_own, values_own]).reshape(2, half_len, part_width)
        segment_own = segment_mb.astype(jnp.bfloat16)
        pair_all, segment_all = (
            lax.all_gather(pair_own, "ctx", axis=1, tiled=True),
            lax.all_gather(segment_own, "ctx", axis=0, tiled=True),
        )
        seq_len = pair_all.shape[1]
        keys_all = pair_all[0].reshape(seq_len, local_heads, HEAD)
        values_all = pair_all[1].reshape(seq_len, local_heads, HEAD)
        same_doc = (segment_own[:, None] == segment_all[None, :])[None]
        scores = masked_scores(queries, keys_all, same_doc, score_scale)
        row_top = jnp.max(scores, axis=-1, keepdims=True)
        exponent = jnp.exp(scores - row_top)
        row_total = jnp.sum(exponent, axis=-1, keepdims=True)
        probs_b = (exponent / row_total).astype(jnp.bfloat16)
        log_total = row_top + jnp.log(row_total)
        context = jnp.einsum(
            "hst,thd->shd", probs_b, values_all, preferred_element_type=jnp.float32
        )
        context = context.reshape(half_len, part_width).astype(jnp.bfloat16)
        attended = lax.psum(contract_last(context, out_full), "tp")
        first_scaled, first_root = norm_parts(
            tokens_mb.astype(jnp.float32) + attended + shift_params[2]
        )
        normed = first_scaled * norm_gain[0] + shift_params[0]
        normed_b = normed.astype(jnp.bfloat16)
        hidden_in = (
            jnp.dot(normed_b, ffn_full[:, 0, :], preferred_element_type=jnp.float32) + ffn_bias
        )
        activated, gelu_pull = jax.vjp(partial(jax.nn.gelu, approximate=False), hidden_in)
        activated_b = activated.astype(jnp.bfloat16)
        returned = lax.psum(contract_last(activated_b, ffn_full[:, 1, :]), "tp")
        second_scaled, second_root = norm_parts(normed + returned + shift_params[3])
        layer_out = (second_scaled * norm_gain[1] + shift_params[1]).astype(jnp.bfloat16)
        qkv_back, out_back = attention_weights(qkv_weight, out_weight)
        ffn_back = feed_weights(ffn_weight)
        grad_top = grad_mb.astype(jnp.float32)
        grad_gain_two = jnp.sum(share_rows(grad_top) * share_rows(second_scaled), axis=0)
        grad_second = norm_back(grad_top, second_scaled, second_root, norm_gain[1])
        grad_second_b = grad_second.astype(jnp.bfloat16)
        grad_down = contract_first(grad_second_b, activated_b)
        grad_act = jnp.dot(grad_second_b, ffn_back[:, 1, :], preferred_element_type=jnp.float32)
        grad_hidden = gelu_pull(grad_act)[0].astype(jnp.bfloat16)
        grad_up = contract_first(normed_b, grad_hidden)
        grad_ffn_bias = jnp.sum(grad_hidden.astype(jnp.float32), axis=0)
        ffn_part = contract_last(grad_hidden, ffn_back[:, 0, :])
        grad_normed = grad_second + lax.psum(ffn_part, "tp")
        grad_first = norm_back(grad_normed, first_scaled, first_root, norm_gain[0])
        grad_first_b = grad_first.astype(jnp.bfloat16)
        normed_part = share_rows(grad_normed)
        first_part = share_rows(grad_first)
        grad_gain_one = jnp.sum(normed_part * share_rows(first_scaled), axis=0)
        grad_out_proj = contract_first(grad_first_b, context)
        grad_context = jnp.dot(grad_first_b, out_back, preferred_element_type=jnp.float32).astype(
            jnp.bfloat16
        )
        grad_context = grad_context.reshape(half_len, local_heads, HEAD)
        scores_again = masked_scores(queries, keys_all, same_doc, score_scale)
        probs = jnp.exp(scores_again - log_total)
        probs_again = probs.astype(jnp.bfloat16)
        grad_probs = jnp.einsum(
            "shd,thd->hst", grad_context, values_all, preferred_element_type=jnp.float32
        )
        row_dot = jnp.sum(probs * grad_probs, axis=-1, keepdims=True)
        grad_scores = (probs * (grad_probs - row_dot)).astype(jnp.bfloat16)
        grad_queries = (
            jnp.einsum("hst,thd->shd", grad_scores, keys_all, preferred_element_type=jnp.float32)
            * score_scale
        )
        grad_keys = (
            jnp.einsum("hst,shd->thd", grad_scores, queries, preferred_element_type=jnp.float32)
            * score_scale
        )
        grad_values = jnp.einsum(
            "hst,shd->thd", probs_again, grad_context, preferred_element_type=jnp.float32
        )
        grad_pair = lax.psum_scatter(
            jnp.stack([grad_keys, grad_values]).reshape(2, seq_len, part_width),
            "ctx",
            scatter_dimension=1,
            tiled=True,
        )
        grad_pair = grad_pair.reshape(2, half_len, local_heads, HEAD)
        grad_proj = jnp.stack(
            [
                rotate_pairs(grad_queries, offsets_mb, -1.0),
                rotate_pairs(grad_pair[0], offsets_mb, -1.0),
                grad_pair[1],
            ]
        )
        grad_proj = grad_proj.reshape(3, half_len, part_width).astype(jnp.bfloat16)
        grad_qkv_bias = jnp.sum(grad_proj.astype(jnp.float32), axis=1)
        grad_qkv = jnp.einsum(
            "sd,kse->dke", tokens_mb, grad_proj, preferred_element_type=jnp.float32
        )
        grad_branch = jnp.einsum(
            "kse,dke->sd", grad_proj, qkv_back, preferred_element_type=jnp.float32
        )
        grad_inputs = (grad_first + lax.psum(grad_branch, "tp")).astype(jnp.bfloat16)
        grad_shift = jnp.stack(
            [
                jnp.sum(normed_part, axis=0),
                jnp.sum(share_rows(grad_top), axis=0),
                jnp.sum(first_part, axis=0),
                jnp.sum(share_rows(grad_second), axis=0),
            ]
        )
        grad_gain = jnp.stack([grad_gain_one, grad_gain_two])
        grad_ffn = jnp.stack([grad_up, grad_down], axis=1)
        updated = (
            totals[0] + grad_qkv,
            totals[1] + grad_out_proj,
            totals[2] + grad_ffn,
            totals[3] + grad_qkv_bias,
            totals[4] + grad_ffn_bias,
            totals[5] + grad_gain,
            totals[6] + grad_shift,
        )
        return (updated, (layer_out, grad_inputs))

    zero_grads = (
        jnp.zeros((model_width, 3, part_width), jnp.float32),
        jnp.zeros((model_width, part_width), jnp.float32),
        jnp.zeros((model_width, 2, hidden_width), jnp.float32),
        jnp.zeros((3, part_width), jnp.float32),
        jnp.zeros((hidden_width,), jnp.float32),
        jnp.zeros((2, model_width), jnp.float32),
        jnp.zeros((4, model_width), jnp.float32),
    )
    totals, (outputs, grad_tokens) = lax.scan(
        micro_step, zero_grads, (tokens, segment_ids, offsets, out_grad)
    )
    grad_qkv_weight, grad_out_weight, grad_ffn_weight = (
        lax.psum_scatter(totals[0], ("shard", "ctx"), scatter_dimension=0, tiled=True),
        lax.psum_scatter(totals[1], ("shard", "ctx"), scatter_dimension=0, tiled=True),
        lax.psum_scatter(totals[2], ("shard", "ctx"), scatter_dimension=0, tiled=True),
    )
    placed_qkv = lax.dynamic_update_slice(
        jnp.zeros((3, part_width * tp_count), jnp.float32),
        totals[3],
        (jnp.int32(0), tp_rank * part_width),
    )
    placed_ffn = lax.dynamic_update_slice(
        jnp.zeros((hidden_width * tp_count,), jnp.float32), totals[4], (tp_rank * hidden_width,)
    )
    summed_qkv, summed_ffn, grad_norm_gain, grad_shift_params = lax.psum(
        (placed_qkv, placed_ffn, totals[5], totals[6]), ("shard", "ctx", "tp")
    )
    grad_qkv_bias = lax.dynamic_slice_in_dim(summed_qkv, tp_rank * part_width, part_width, 1)
    grad_ffn_bias = lax.dynamic_slice_in_dim(summed_ffn, tp_rank * hidden_width, hidden_width, 0)
    return (
        outputs,
        grad_tokens,
        grad_qkv_weight,
        grad_out_weight,
        grad_ffn_weight,
        grad_qkv_bias,
        grad_ffn_bias,
        grad_norm_gain,
        grad_shift_params,
    )


def solution(mesh):
    return jax.shard_map(
        body,
        mesh=mesh,
        in_specs=(
            P("shard", "ctx", None),
            P("shard", "ctx"),
            P("shard", "ctx"),
            P(("shard", "ctx"), None, "tp"),
            P(("shard", "ctx"), "tp"),
            P(("shard", "ctx"), None, "tp"),
            P(None, "tp"),
            P("tp"),
            P(),
            P(),
            P("shard", "ctx", None),
        ),
        out_specs=(
            P("shard", "ctx", None),
            P("shard", "ctx", None),
            P(("shard", "ctx"), None, "tp"),
            P(("shard", "ctx"), "tp"),
            P(("shard", "ctx"), None, "tp"),
            P(None, "tp"),
            P("tp"),
            P(),
            P(),
        ),
        check_vma=False,
    )
```

profile of v0, /device:TPU:1, one launch (start us, length us, event | category | flops | bytes accessed | tf_op | source)
XLA Modules:
  0.0 1403.5 jit_solution(18068525269604240569)
XLA Ops:
  10.9 1199.6 %while.29 = (s32[]{:T(128)}, f32[768,3,192]{0,2,1:T(8,128)}, f32[768,192]{0,1:T(8,128)}, f32[768,2,768]{2,0,1:T(8,128)}, f32[3,192]{1,0:T(4,128)}, /*index=5*/f3...) while((s32[]{:T(128)}, f32[768,3,192]{0,2,1:T(8,128)}, ...), condition=%wide.region_25.26_spmd.clone, body=%wide.region_0.25_spmd.clone.sunk | while | flops 15947476992 | bytes 964769600 | solution.py:243
  10.9 23.0 %all_gather.42 = bf16[768,3,192]{2,1,0:T(4,128)(2,1)} all-gather(bf16[96,3,192]{2,1,0:T(4,128)(2,1)S(1)} %get-tuple-element.828), channel_id=1, replica_groups=mesh['shard'=4,'ctx'=2,'tp'=4] {'shard','ctx'}, dimensions={0}, use_global_device_ids=true | all-gather | bytes 995328 | tf_op jit(solution)/shard_map/while/body/eval_jaxpr/all_gather | solution.py:45
  33.9 3.4 copy.39
  48.0 4.2 subtract_convert_fusion.6
  57.9 2.8 pad_maximum_fusion.15
  63.7 16.1 %all_gather.41 = bf16[768,192]{1,0:T(8,128)(2,1)} all-gather(bf16[96,192]{1,0:T(8,128)(2,1)} %get-tuple-element.832), channel_id=1, replica_groups=mesh['shard'=4,'ctx'=2,'tp'=4] {'shard','ctx'}, dimensions={0}, use_global_device_ids=true | all-gather | bytes 331776 | tf_op jit(solution)/shard_map/while/body/eval_jaxpr/all_gather | solution.py:46
  84.3 11.0 fusion.150
  95.3 10.4 fusion.151
  105.8 10.6 fusion.152
  122.1 84.0 %all-reduce.10.cloned.1.call-done = f32[1024,768]{1,0:T(8,128)} async-done(((f32[1024,768]{1,0:T(8,128)}), f32[1024,768]{1,0:T(8,128)}) %all-reduce.10.cloned.1.call-update) | async-done | bytes 3145744 | tf_op jit(solution)/shard_map/while/body/eval_jaxpr/psum | solution.py:134
  206.2 2.5 fusion.154
  211.2 11.2 multiply_convert_fusion.4
  223.6 3.2 fusion.155
  227.5 86.7 %all-reduce.12.cloned.1.call-done = f32[1024,768]{1,0:T(8,128)} async-done(((f32[1024,768]{1,0:T(8,128)}), f32[1024,768]{1,0:T(8,128)}) %all-reduce.12.cloned.1.call-update) | async-done | bytes 3145744 | tf_op jit(solution)/shard_map/while/body/eval_jaxpr/psum | solution.py:145
  326.5 2.9 convert_reduce_fusion.4
  330.6 3.1 fusion.159
  334.8 86.4 %all-reduce.14.cloned.1.call-done = f32[1024,768]{1,0:T(8,128)} async-done(((f32[1024,768]{1,0:T(8,128)}), f32[1024,768]{1,0:T(8,128)}) %all-reduce.14.cloned.1.call-update) | async-done | bytes 3145744 | tf_op jit(solution)/shard_map/while/body/eval_jaxpr/psum | solution.py:160
  421.2 3.6 multiply_reduce_fusion.13
  429.5 11.4 fusion.160
  440.9 16.4 %multiply_reduce_fusion.14 = (f32[3,1024]{1,0:T(4,128)}, f32[3,1024,2048]{2,1,0:T(8,128)}) fusion(f32[3,1024,2048]{2,1,0:T(8,128)} %get-tuple-element.731, f32[3,1024]{1,0:T(4,128)S(1)} %log_add_fusion.2, bf16[1024,3,64]{0,2,1:T(8,128)(2,1)} %bitcast.223, bf16[2048,3,64]{0,2,1:T(8,128)(2,1)} %bitcast.227), kind=kOutput, calls=%fused_computation.1.clone.1 | convolution fusion | flops 824177664 | bytes 51535872 | tf_op jit(solution)/shard_map/while/body/eval_jaxpr/shd,thd->hst/dot_general | solution.py:174
  457.3 16.8 %multiply_convert_fusion.5 = bf16[3,1024,2048]{2,1,0:T(8,128)(2,1)S(1)} fusion(f32[3,1024,2048]{2,1,0:T(8,128)} %get-tuple-element.750, f32[3,1024,2048]{2,1,0:T(8,128)} %get-tuple-element.731, f32[3,1024]{1,0:T(4,128)} %get-tuple-element.751, f32[3,1024]{1,0:T(4,128)S(1)} %log_add_fusion.2), kind=kLoop, calls=%fused_computation.clone.1 | loop fusion | flops 25165824 | bytes 62939136 | tf_op jit(solution)/shard_map/while/body/eval_jaxpr/convert_element_type | solution.py:178
  484.4 10.5 fusion.161
  494.9 2.5 reshape.312
  502.0 3.9 subtract_convert_fusion.7
  505.9 2.7 pad_maximum_fusion.17
  515.1 3.1 convolution_bitcast_fusion.8
  520.5 4.0 convolution_bitcast_fusion.6
  535.3 70.4 %all-reduce.16.cloned.1.call-done = f32[1024,768]{1,0:T(8,128)} async-done(((f32[1024,768]{1,0:T(8,128)}), f32[1024,768]{1,0:T(8,128)}) %all-reduce.16.cloned.1.call-update) | async-done | bytes 3145744 | tf_op jit(solution)/shard_map/while/body/eval_jaxpr/psum | solution.py:212
  605.7 3.4 fusion.164
  609.5 21.9 %all_gather.42 = bf16[768,3,192]{2,1,0:T(4,128)(2,1)} all-gather(bf16[96,3,192]{2,1,0:T(4,128)(2,1)S(1)} %get-tuple-element.828), channel_id=1, replica_groups=mesh['shard'=4,'ctx'=2,'tp'=4] {'shard','ctx'}, dimensions={0}, use_global_device_ids=true | all-gather | bytes 995328 | tf_op jit(solution)/shard_map/while/body/eval_jaxpr/all_gather | solution.py:45
  631.4 3.4 copy.39
  645.5 4.2 subtract_convert_fusion.6
  655.4 2.8 pad_maximum_fusion.15
  661.2 15.9 %all_gather.41 = bf16[768,192]{1,0:T(8,128)(2,1)} all-gather(bf16[96,192]{1,0:T(8,128)(2,1)} %get-tuple-element.832), channel_id=1, replica_groups=mesh['shard'=4,'ctx'=2,'tp'=4] {'shard','ctx'}, dimensions={0}, use_global_device_ids=true | all-gather | bytes 331776 | tf_op jit(solution)/shard_map/while/body/eval_jaxpr/all_gather | solution.py:46
  681.7 11.0 fusion.150
  692.6 10.4 fusion.151
  703.1 10.6 fusion.152
  719.3 83.2 %all-reduce.10.cloned.1.call-done = f32[1024,768]{1,0:T(8,128)} async-done(((f32[1024,768]{1,0:T(8,128)}), f32[1024,768]{1,0:T(8,128)}) %all-reduce.10.cloned.1.call-update) | async-done | bytes 3145744 | tf_op jit(solution)/shard_map/while/body/eval_jaxpr/psum | solution.py:134
  802.5 2.5 fusion.154
  807.6 11.2 multiply_convert_fusion.4
  820.0 3.2 fusion.155
  823.5 87.1 %all-reduce.12.cloned.1.call-done = f32[1024,768]{1,0:T(8,128)} async-done(((f32[1024,768]{1,0:T(8,128)}), f32[1024,768]{1,0:T(8,128)}) %all-reduce.12.cloned.1.call-update) | async-done | bytes 3145744 | tf_op jit(solution)/shard_map/while/body/eval_jaxpr/psum | solution.py:145
  922.9 2.9 convert_reduce_fusion.4
  927.0 3.1 fusion.159
  931.4 86.1 %all-reduce.14.cloned.1.call-done = f32[1024,768]{1,0:T(8,128)} async-done(((f32[1024,768]{1,0:T(8,128)}), f32[1024,768]{1,0:T(8,128)}) %all-reduce.14.cloned.1.call-update) | async-done | bytes 3145744 | tf_op jit(solution)/shard_map/while/body/eval_jaxpr/psum | solution.py:160
  1017.5 3.6 multiply_reduce_fusion.13
  1025.9 11.4 fusion.160
  1037.3 16.4 %multiply_reduce_fusion.14 = (f32[3,1024]{1,0:T(4,128)}, f32[3,1024,2048]{2,1,0:T(8,128)}) fusion(f32[3,1024,2048]{2,1,0:T(8,128)} %get-tuple-element.731, f32[3,1024]{1,0:T(4,128)S(1)} %log_add_fusion.2, bf16[1024,3,64]{0,2,1:T(8,128)(2,1)} %bitcast.223, bf16[2048,3,64]{0,2,1:T(8,128)(2,1)} %bitcast.227), kind=kOutput, calls=%fused_computation.1.clone.1 | convolution fusion | flops 824177664 | bytes 51535872 | tf_op jit(solution)/shard_map/while/body/eval_jaxpr/shd,thd->hst/dot_general | solution.py:174
  1053.7 16.8 %multiply_convert_fusion.5 = bf16[3,1024,2048]{2,1,0:T(8,128)(2,1)S(1)} fusion(f32[3,1024,2048]{2,1,0:T(8,128)} %get-tuple-element.750, f32[3,1024,2048]{2,1,0:T(8,128)} %get-tuple-element.731, f32[3,1024]{1,0:T(4,128)} %get-tuple-element.751, f32[3,1024]{1,0:T(4,128)S(1)} %log_add_fusion.2), kind=kLoop, calls=%fused_computation.clone.1 | loop fusion | flops 25165824 | bytes 62939136 | tf_op jit(solution)/shard_map/while/body/eval_jaxpr/convert_element_type | solution.py:178
  1080.8 10.5 fusion.161
  1091.2 2.5 reshape.312
  1098.4 3.8 subtract_convert_fusion.7
  1102.2 2.7 pad_maximum_fusion.17
  1111.4 3.1 convolution_bitcast_fusion.8
  1116.8 4.0 convolution_bitcast_fusion.6
  1130.0 3.3 select_add_fusion.6
  1133.2 68.7 %all-reduce.16.cloned.1.call-done = f32[1024,768]{1,0:T(8,128)} async-done(((f32[1024,768]{1,0:T(8,128)}), f32[1024,768]{1,0:T(8,128)}) %all-reduce.16.cloned.1.call-update) | async-done | bytes 3145744 | tf_op jit(solution)/shard_map/while/body/eval_jaxpr/psum | solution.py:212
  1202.0 3.4 fusion.164
  1210.5 8.1 copy.37
  1221.0 3.0 copy.35
  1224.6 42.2 %all-reduce.1 = (f32[3,768]{1,0:T(4,128)S(1)}, f32[3072]{0:T(1024)S(1)}, f32[2,768]{1,0:T(2,128)}, f32[4,768]{1,0:T(4,128)}) all-reduce(f32[3,768]{1,0:T(4,128)S(1)} %dynamic_update_slice.19, f32[3072]{0:T(1024)S(1)} %dynamic_update_slice.20, ...), channel_id=1, replica_groups=mesh['shard'=4,'ctx'=2,'tp'=4] {'shard','ctx','tp'}, use_global_device_ids=true, to_apply=%region_29.30 | all-reduce | flops 9984 | bytes 79872 | tf_op jit(solution)/shard_map/psum | solution.py:259
  1269.4 56.4 %all-reduce.8.cloned.1.call-done = f32[768,2,768]{2,1,0:T(2,128)} async-done(((f32[768,2,768]{2,1,0:T(2,128)}), f32[768,2,768]{2,1,0:T(2,128)}) %all-reduce.8.cloned.1.call-update) | async-done | bytes 4718608
  1327.8 29.3 %reduce-scatter.6.cloned.1.call-done = f32[96,192]{1,0:T(8,128)} async-done(((f32[768,192]{1,0:T(8,128)}), f32[96,192]{1,0:T(8,128)}) %reduce-scatter.6.cloned.1.call-update) | async-done | bytes 73744 | tf_op jit(solution)/shard_map/reduce_scatter | solution.py:248
  1357.1 38.5 %reduce-scatter.4.cloned.1.call-done = f32[96,3,192]{2,0,1:T(8,128)} async-done(((f32[768,3,192]{2,0,1:T(8,128)}), f32[96,3,192]{2,0,1:T(8,128)}) %reduce-scatter.4.cloned.1.call-update) | async-done | bytes 221200 | tf_op jit(solution)/shard_map/reduce_scatter | solution.py:247
  (487 shorter events, 181.7 us)
Async XLA Ops:
  10.9 28.7 %copy-start.33 = (bf16[96,3,192]{2,1,0:T(4,128)(2,1)}, bf16[96,3,192]{2,1,0:T(4,128)(2,1)S(1)}, u32[]{:S(2)}) copy-start(bf16[96,3,192]{2,1,0:T(4,128)(2,1)S(1)} %get-tuple-element.828) | copy-start | bytes 331780 | tf_op jit(solution)/shard_map/while
  10.9 26.4 %copy-start.9 = (bf16[2,1024,768]{2,1,0:T(8,128)(2,1)S(1)}, bf16[2,1024,768]{2,1,0:T(8,128)(2,1)}, u32[]{:S(2)}) copy-start(bf16[2,1024,768]{2,1,0:T(8,128)(2,1)} %get-tuple-element.827) | copy-start | bytes 9437188 | tf_op jit(solution)/shard_map/while
  10.9 71.4 %all-gather.7.cloned.1.call-start = ((), (), s32[]{:S(2)}) async-start(), calls=%async_computation.6 | async-start | bytes 2359296 | tf_op jit(solution)/shard_map/while/body/eval_jaxpr/all_gather | solution.py:117
  52.3 9.5 copy-start.62
  57.8 148.3 %all-reduce.10.cloned.1.call-start = ((), (), s32[]{:S(2)}) async-start(), calls=%async_computation.7 | async-start | bytes 6291456 | tf_op jit(solution)/shard_map/while/body/eval_jaxpr/psum | solution.py:134
  83.9 11.4 copy-start.16
  83.9 21.9 %copy-start.20 = (bf16[1,2048,192]{1,2,0:T(8,128)(2,1)}, bf16[1,2048,192]{1,2,0:T(8,128)(2,1)S(1)}, u32[]{:S(2)}) copy-start(bf16[1,2048,192]{1,2,0:T(8,128)(2,1)S(1)} %get-tuple-element.725) | copy-start | bytes 2359300 | tf_op jit(solution)/shard_map/while
  95.3 10.5 copy-start.38
  105.7 10.7 copy-start.39
  105.8 11.4 copy-start.18
  119.6 91.6 %all-gather.9.cloned.1.call-start = ((), (), s32[]{:S(2)}) async-start(), calls=%async_computation.8 | async-start | bytes 2654208 | tf_op jit(solution)/shard_map/while/body/eval_jaxpr/all_gather | solution.py:51
  120.2 194.0 %all-reduce.12.cloned.1.call-start = ((), (), s32[]{:S(2)}) async-start(), calls=%async_computation.9 | async-start | bytes 6291456 | tf_op jit(solution)/shard_map/while/body/eval_jaxpr/psum | solution.py:145
  120.6 193.6 %copy-start.35 = (f32[768]{0:T(1024)}, f32[768]{0:T(1024)S(1)}, u32[]{:S(2)}) copy-start(f32[768]{0:T(1024)S(1)} %get-tuple-element.733) | copy-start | bytes 9220 | tf_op jit(solution)/shard_map/while
  122.1 192.1 %copy-start.45 = (f32[768]{0:T(1024)}, f32[768]{0:T(1024)S(1)}, u32[]{:S(2)}) copy-start(f32[768]{0:T(1024)S(1)} %get-tuple-element.737) | copy-start | bytes 9220 | tf_op jit(solution)/shard_map/while
  211.2 12.4 copy-start.65
  226.8 87.4 %copy-start.48 = (f32[768]{0:T(1024)S(1)}, f32[768]{0:T(1024)}, u32[]{:S(2)}) copy-start(f32[768]{0:T(1024)} %get-tuple-element.736) | copy-start | bytes 9220 | tf_op jit(solution)/shard_map/while
  226.8 194.3 %all-reduce.14.cloned.1.call-start = ((), (), s32[]{:S(2)}) async-start(), calls=%async_computation.10 | async-start | bytes 6291456 | tf_op jit(solution)/shard_map/while/body/eval_jaxpr/psum | solution.py:160
  322.0 4.5 copy-start.72
  323.1 6.3 copy-start.6
  333.8 163.6 %reduce-scatter.8.cloned.1.call-start = ((), (), s32[]{:S(2)}) async-start(), calls=%async_computation.11 | async-start | bytes 4718592 | tf_op jit(solution)/shard_map/while/body/eval_jaxpr/reduce_scatter | solution.py:190
  474.1 4.7 copy-start
  474.1 4.7 copy-start.8
  480.9 124.8 %all-reduce.16.cloned.1.call-start = ((), (), s32[]{:S(2)}) async-start(), calls=%async_computation.12 | async-start | bytes 6291456 | tf_op jit(solution)/shard_map/while/body/eval_jaxpr/psum | solution.py:212
  494.9 7.1 copy-start.27
  494.9 7.1 copy-start.32
  518.9 5.5 copy-start.54
  520.4 4.0 copy-start.37
  520.4 4.0 copy-start.46
  520.4 5.5 slice-start
  527.3 4.4 copy-start.14
  533.6 72.0 %copy-start.3 = (f32[1024,768]{1,0:T(8,128)S(1)}, f32[1024,768]{1,0:T(8,128)}, u32[]{:S(2)}) copy-start(f32[1024,768]{1,0:T(8,128)} %copy-done.1) | copy-start | bytes 9437188 | tf_op jit(solution)/shard_map/while
  609.4 27.7 %copy-start.33 = (bf16[96,3,192]{2,1,0:T(4,128)(2,1)}, bf16[96,3,192]{2,1,0:T(4,128)(2,1)S(1)}, u32[]{:S(2)}) copy-start(bf16[96,3,192]{2,1,0:T(4,128)(2,1)S(1)} %get-tuple-element.828) | copy-start | bytes 331780 | tf_op jit(solution)/shard_map/while
  609.4 25.4 %copy-start.9 = (bf16[2,1024,768]{2,1,0:T(8,128)(2,1)S(1)}, bf16[2,1024,768]{2,1,0:T(8,128)(2,1)}, u32[]{:S(2)}) copy-start(bf16[2,1024,768]{2,1,0:T(8,128)(2,1)} %get-tuple-element.827) | copy-start | bytes 9437188 | tf_op jit(solution)/shard_map/while
  609.4 70.1 %all-gather.7.cloned.1.call-start = ((), (), s32[]{:S(2)}) async-start(), calls=%async_computation.6 | async-start | bytes 2359296 | tf_op jit(solution)/shard_map/while/body/eval_jaxpr/all_gather | solution.py:117
  649.8 9.5 copy-start.62
  655.3 147.2 %all-reduce.10.cloned.1.call-start = ((), (), s32[]{:S(2)}) async-start(), calls=%async_computation.7 | async-start | bytes 6291456 | tf_op jit(solution)/shard_map/while/body/eval_jaxpr/psum | solution.py:134
  681.2 11.4 copy-start.16
  681.2 21.9 %copy-start.20 = (bf16[1,2048,192]{1,2,0:T(8,128)(2,1)}, bf16[1,2048,192]{1,2,0:T(8,128)(2,1)S(1)}, u32[]{:S(2)}) copy-start(bf16[1,2048,192]{1,2,0:T(8,128)(2,1)S(1)} %get-tuple-element.725) | copy-start | bytes 2359300 | tf_op jit(solution)/shard_map/while
  692.6 10.5 copy-start.38
  703.1 10.7 copy-start.39
  703.1 11.4 copy-start.18
  716.9 90.7 %all-gather.9.cloned.1.call-start = ((), (), s32[]{:S(2)}) async-start(), calls=%async_computation.8 | async-start | bytes 2654208 | tf_op jit(solution)/shard_map/while/body/eval_jaxpr/all_gather | solution.py:51
  717.5 193.1 %all-reduce.12.cloned.1.call-start = ((), (), s32[]{:S(2)}) async-start(), calls=%async_computation.9 | async-start | bytes 6291456 | tf_op jit(solution)/shard_map/while/body/eval_jaxpr/psum | solution.py:145
  717.8 192.8 %copy-start.35 = (f32[768]{0:T(1024)}, f32[768]{0:T(1024)S(1)}, u32[]{:S(2)}) copy-start(f32[768]{0:T(1024)S(1)} %get-tuple-element.733) | copy-start | bytes 9220 | tf_op jit(solution)/shard_map/while
  719.3 191.3 %copy-start.45 = (f32[768]{0:T(1024)}, f32[768]{0:T(1024)S(1)}, u32[]{:S(2)}) copy-start(f32[768]{0:T(1024)S(1)} %get-tuple-element.737) | copy-start | bytes 9220 | tf_op jit(solution)/shard_map/while
  807.6 12.4 copy-start.65
  823.2 87.4 %copy-start.48 = (f32[768]{0:T(1024)S(1)}, f32[768]{0:T(1024)}, u32[]{:S(2)}) copy-start(f32[768]{0:T(1024)} %get-tuple-element.736) | copy-start | bytes 9220 | tf_op jit(solution)/shard_map/while
  823.2 194.3 %all-reduce.14.cloned.1.call-start = ((), (), s32[]{:S(2)}) async-start(), calls=%async_computation.10 | async-start | bytes 6291456 | tf_op jit(solution)/shard_map/while/body/eval_jaxpr/psum | solution.py:160
  918.4 4.5 copy-start.72
  919.5 6.4 copy-start.6
  930.2 163.6 %reduce-scatter.8.cloned.1.call-start = ((), (), s32[]{:S(2)}) async-start(), calls=%async_computation.11 | async-start | bytes 4718592 | tf_op jit(solution)/shard_map/while/body/eval_jaxpr/reduce_scatter | solution.py:190
  1070.5 4.7 copy-start
  1070.5 4.7 copy-start.8
  1077.2 124.7 %all-reduce.16.cloned.1.call-start = ((), (), s32[]{:S(2)}) async-start(), calls=%async_computation.12 | async-start | bytes 6291456 | tf_op jit(solution)/shard_map/while/body/eval_jaxpr/psum | solution.py:212
  1091.2 7.1 copy-start.27
  1091.2 7.1 copy-start.32
  1115.3 5.5 copy-start.54
  1116.8 5.5 slice-start
  1123.7 4.4 copy-start.14
  1130.0 72.0 %copy-start.3 = (f32[1024,768]{1,0:T(8,128)S(1)}, f32[1024,768]{1,0:T(8,128)}, u32[]{:S(2)}) copy-start(f32[1024,768]{1,0:T(8,128)} %copy-done.1) | copy-start | bytes 9437188 | tf_op jit(solution)/shard_map/while
  1210.5 115.4 %all-reduce.8.cloned.1.call-start = ((), (), s32[]{:S(2)}) async-start(), calls=%async_computation.5 | async-start | bytes 9437184
  1218.7 138.4 %reduce-scatter.6.cloned.1.call-start = ((), (), s32[]{:S(2)}) async-start(), calls=%async_computation.4 | async-start | bytes 884736 | tf_op jit(solution)/shard_map/reduce_scatter | solution.py:248
  1220.9 174.8 %reduce-scatter.4.cloned.1.call-start = ((), (), s32[]{:S(2)}) async-start(), calls=%async_computation.3 | async-start | bytes 2654208 | tf_op jit(solution)/shard_map/reduce_scatter | solution.py:247
  1221.0 46.5 %copy-start.68 = (u32[32]{0:T(128)S(1)}, u32[32]{0:T(128)}, u32[]{:S(2)}) copy-start(u32[32]{0:T(128)} %constant.281) | copy-start | bytes 388
  (99 other events, 238.5 us)
Sparse Core Ops, SparseCore 0:
  57.9 9.3 all-gather.6
  119.7 86.4 all-reduce.9
  226.9 87.2 all-reduce.11
  333.9 87.2 all-reduce.13
  481.0 11.2 reduce-scatter.7
  518.4 87.2 all-reduce.15
  655.4 8.3 all-gather.6
  717.0 85.4 all-reduce.9
  823.3 87.2 all-reduce.11
  930.3 87.1 all-reduce.13
  1077.4 11.2 reduce-scatter.7
  1114.7 87.2 all-reduce.15
Sparse Core Ops, SparseCore 1:
  122.2 30.9 all-gather.8
  719.6 30.0 all-gather.8
  1218.7 107.0 all-reduce.7
  1328.7 28.3 reduce-scatter.5
  1360.1 35.5 reduce-scatter.3
where the time goes:
time: 1410 us; the launch traced here: 1400 us
  waiting for transfers between devices  778 us (55%)
  matrix products  197 us (14%)
  other arithmetic  160 us (11%)
  blocking collectives  123 us (9%)
  local copies, waits for them, and re-layouts  119 us (8%)
  between operations  16.8 us (1%)
    psum x2, waiting for transfers between devices, micro_step(): returned = lax.psum(contract_last(activated_b, ffn_full[:, 1, :]), 'tp')  174 us
    psum x2, waiting for transfers between devices, micro_step(): grad_normed = grad_second + lax.psum(ffn_part, 'tp')  172 us
    psum x2, waiting for transfers between devices, micro_step(): attended = lax.psum(contract_last(context, out_full), 'tp')  167 us
    psum x2, waiting for transfers between devices, micro_step(): lax.psum(grad_branch, 'tp')  139 us
    unnamed x4, waiting for transfers between devices  56.5 us
    all_gather x2, blocking collectives, attention_weights(): lax.all_gather(qkv_weight, ('shard', 'ctx'), axis=0, tiled=True)  44.9 us
    while x280, local copies, waits for them, and re-layouts  43.6 us
    psum x1, blocking collectives, body(): lax.psum((placed_qkv, placed_ffn, totals[5], totals[6]), ('shard', 'ctx',...  42.2 us
  transfers between devices with their start and end apart: 17, of which 11 were waited for; matrix products, arithmetic and copies ran while one was open for 7% of the time, Pallas kernels for 0%

commit v1 on v0

v1 whole, which is shorter than its diff:
```python
from functools import partial

import jax
import jax.numpy as jnp
import numpy as np
from jax import lax
from jax.experimental import pallas as pl
from jax.experimental.pallas import tpu as pltpu
from jax.sharding import PartitionSpec as P

HEAD = 64
WIDE = 256
BLOCK = 256
CHUNK = 256
EPSILON = 1e-12
F32 = jnp.float32
BF = jnp.bfloat16
NEG = -1e30


def swap_pairs(x):
    lane=lax.broadcasted_iota(jnp.int32,x.shape,1)
    n=x.shape[1]
    return jnp.where(lane%2==0, pltpu.roll(x,n-1,1), pltpu.roll(x,1,1))

def nt(a,b): return lax.dot_general(a,b,(((1,),(1,)),((),())),preferred_element_type=F32)
def nn(a,b): return lax.dot_general(a,b,(((1,),(0,)),((),())),preferred_element_type=F32)

def stack_heads(x, heads):
    lane=lax.broadcasted_iota(jnp.int32,x.shape,1)//HEAD
    return jnp.concatenate([jnp.where(lane==h,x,jnp.zeros_like(x)) for h in range(heads)],axis=0)

def fwd_kernel(heads, bounds, tok, w, bias, cos, sin, segc, segr, q_o, k_o, v_o, ctx_o, lse_o, o32_o, s_sc, m_sc, l_sc, qc_sc, vm_sc):
    i=pl.program_id(0)
    length=tok.shape[0]
    rows=heads*BLOCK
    @pl.when(i==0)
    def _():
        def step(r,_):
            sl=pl.ds(pl.multiple_of(r*BLOCK,BLOCK),BLOCK)
            c=cos[sl,:]; s=sin[sl,:]
            c=jnp.concatenate([c,c],axis=1); s=jnp.concatenate([s,s],axis=1)
            x=tok[sl,:]
            p=nn(x,w[:,0:WIDE])+bias[0:1,:]
            q_o[sl,:]=((p*c+swap_pairs(p)*s).astype(BF).astype(F32)*(HEAD**-0.5)).astype(BF)
            p=nn(x,w[:,WIDE:2*WIDE])+bias[1:2,:]
            k_o[sl,:]=(p*c+swap_pairs(p)*s).astype(BF)
            p=(nn(x,w[:,2*WIDE:3*WIDE])+bias[2:3,:]).astype(BF)
            v_o[sl,:]=p
            lane=lax.broadcasted_iota(jnp.int32,p.shape,1)//HEAD
            for h in range(heads):
                vm_sc[h,sl,:]=jnp.where(lane==h,p,jnp.zeros_like(p))
            return 0
        lax.fori_loop(0,length//BLOCK,step,0)
    start=bounds[0,i]; count=bounds[1,i]
    q=q_o[pl.ds(pl.multiple_of(i*BLOCK,BLOCK),BLOCK),:]
    qc_sc[...]=stack_heads(q,heads)
    seg_q=segc[...]
    m_sc[...]=jnp.full(m_sc.shape,NEG,F32)
    l_sc[...]=jnp.zeros(l_sc.shape,F32)
    def at(j): return pl.ds(pl.multiple_of(start+j*CHUNK,128),CHUNK)
    def pass1(j,_):
        s=nt(qc_sc[...],k_o[at(j),:])
        keep=seg_q==segr[0:1,at(j)]
        for h in range(heads):
            sh=jnp.where(keep,s[h*BLOCK:(h+1)*BLOCK,:],NEG)
            s_sc[j,h*BLOCK:(h+1)*BLOCK,:]=sh
            m_sc[h*BLOCK:(h+1)*BLOCK,:]=jnp.maximum(m_sc[h*BLOCK:(h+1)*BLOCK,:],jnp.maximum(sh[:,:128],sh[:,128:]))
        return 0
    lax.fori_loop(0,count,pass1,0)
    m_sc[...]=jnp.broadcast_to(jnp.max(m_sc[...],axis=1,keepdims=True),m_sc.shape)
    def pass2(j,_):
        for h in range(heads):
            hs=slice(h*BLOCK,(h+1)*BLOCK)
            m=m_sc[hs,:]
            e=jnp.exp(s_sc[j,hs,:]-jnp.concatenate([m,m],axis=1))
            s_sc[j,hs,:]=e
            l_sc[hs,:]+=e[:,:128]+e[:,128:]
        return 0
    lax.fori_loop(0,count,pass2,0)
    total=jnp.sum(l_sc[...],axis=1,keepdims=True)
    lse=m_sc[:,0:1]+jnp.log(total)
    l_sc[...]=jnp.broadcast_to(1.0/total,l_sc.shape)
    lane=lax.broadcasted_iota(jnp.int32,(BLOCK,128),1)
    tile=jnp.zeros((BLOCK,128),F32)
    for h in range(heads):
        tile=jnp.where(lane==h,lse[h*BLOCK:(h+1)*BLOCK,:],tile)
    lse_o[...]=tile.T[0:8,:]
    o32_o[...]=jnp.zeros(o32_o.shape,F32)
    def pass3(j,_):
        ps=[];vs=[]
        for h in range(heads):
            hs=slice(h*BLOCK,(h+1)*BLOCK)
            inv=l_sc[hs,:]
            ps.append((s_sc[j,hs,:]*jnp.concatenate([inv,inv],axis=1)).astype(BF))
            vs.append(vm_sc[h,at(j),:])
        o32_o[...]+=nn(jnp.concatenate(ps,axis=1),jnp.concatenate(vs,axis=0))
        return 0
    lax.fori_loop(0,count,pass3,0)
    ctx_o[...]=o32_o[:,:heads*HEAD].astype(BF)

def attention_forward(bounds,tok,w,bias,cos,sin,segc,segr,heads):
    length,width=tok.shape
    nq=length//BLOCK; nch=length//CHUNK
    full=lambda shape: pl.BlockSpec(shape,lambda i:(0,)*len(shape),pipeline_mode=pl.Buffered(1))
    return pl.pallas_call(
        partial(fwd_kernel,heads),
        grid=(nq,),
        in_specs=[pl.BlockSpec(memory_space=pltpu.SMEM),full((length,width)),full(w.shape),full(bias.shape),full(cos.shape),full(sin.shape),
                  pl.BlockSpec((BLOCK,1),lambda i:(i,0)),full(segr.shape)],
        out_specs=[full((length,WIDE)),full((length,WIDE)),full((length,WIDE)),
                   pl.BlockSpec((BLOCK,heads*HEAD),lambda i:(i,0)),pl.BlockSpec((8,BLOCK),lambda i:(0,i))],
        out_shape=[jax.ShapeDtypeStruct((length,WIDE),BF)]*3+[jax.ShapeDtypeStruct((length,heads*HEAD),BF),jax.ShapeDtypeStruct((8,length),F32)],
        scratch_shapes=[pltpu.VMEM((BLOCK,WIDE),F32),pltpu.VMEM((nch,heads*BLOCK,CHUNK),F32),pltpu.VMEM((heads*BLOCK,128),F32),pltpu.VMEM((heads*BLOCK,128),F32),
                        pltpu.VMEM((heads*BLOCK,WIDE),BF),pltpu.VMEM((heads,length,WIDE),BF)],
        compiler_params=pltpu.CompilerParams(dimension_semantics=("arbitrary",),vmem_limit_bytes=56*1024*1024),
        name="attention_forward",
    )(bounds,tok,w,bias,cos,sin,segc,segr)

def bwd_kernel(heads, bounds, q, k, kt, v, do, lse, segc, segr, cos, sin, g_o, gb_o, dk_sc, dv_sc, qc_sc, dc_sc, dq_sc, p_sc, dp_sc, dl_sc):
    i=pl.program_id(0)
    length=k.shape[0]
    @pl.when(i==0)
    def _():
        dk_sc[...]=jnp.zeros(dk_sc.shape,F32)
        dv_sc[...]=jnp.zeros(dv_sc.shape,F32)
        gb_o[...]=jnp.zeros(gb_o.shape,F32)
    start=bounds[0,i]; count=bounds[1,i]
    qc_sc[...]=stack_heads(q[...],heads)
    d=do[...]
    dz=jnp.concatenate([d,jnp.zeros((BLOCK,WIDE-d.shape[1]),BF)],axis=1)
    dc_sc[...]=stack_heads(dz,heads)
    dq_sc[...]=jnp.zeros(dq_sc.shape,F32)
    seg_q=segr[0:1,pl.ds(pl.multiple_of(i*BLOCK,BLOCK),BLOCK)]
    dl_sc[...]=jnp.zeros(dl_sc.shape,F32)
    def at(j): return pl.ds(pl.multiple_of(start+j*CHUNK,128),CHUNK)
    def pass1(j,_):
        s=nt(k[at(j),:],qc_sc[...])
        dp=nt(v[at(j),:],dc_sc[...])
        keep=segc[at(j),:]==seg_q
        for h in range(heads):
            hs=slice(h*BLOCK,(h+1)*BLOCK)
            p=jnp.exp(jnp.where(keep,s[:,hs],NEG)-lse[h:h+1,:])
            p_sc[j,:,hs]=p
            dp_sc[j,:,hs]=dp[:,hs]
            dl_sc[:,hs]+=jnp.sum((p*dp[:,hs]).reshape(CHUNK//8,8,BLOCK),axis=0)
        return 0
    lax.fori_loop(0,count,pass1,0)
    delta=jnp.sum(dl_sc[...],axis=0,keepdims=True)
    def pass2(j,_):
        ps=[];dss=[]
        for h in range(heads):
            hs=slice(h*BLOCK,(h+1)*BLOCK)
            p=p_sc[j,:,hs]
            ds=(p*(dp_sc[j,:,hs]-delta[:,hs])).astype(BF)
            ps.append(p.astype(BF)); dss.append(ds)
            dq_sc[h*HEAD:(h+1)*HEAD,:]+=nn(kt[h*HEAD:(h+1)*HEAD,at(j)],ds)
        dv_sc[at(j),:]+=nn(jnp.concatenate(ps,axis=1),dc_sc[...])
        dk_sc[at(j),:]+=nn(jnp.concatenate(dss,axis=1),qc_sc[...])
        return 0
    lax.fori_loop(0,count,pass2,0)
    def turn(x,sl):
        c=cos[sl,:]; s=sin[sl,:]
        c=jnp.concatenate([c,c],axis=1); s=jnp.concatenate([s,s],axis=1)
        return (x*c-swap_pairs(x)*s).astype(BF)
    own=pl.ds(pl.multiple_of(i*BLOCK,BLOCK),BLOCK)
    dq=turn(dq_sc[...].T*(HEAD**-0.5),own)
    g_o[own,0:WIDE]=dq
    gb_o[0:1,0:WIDE]+=jnp.sum(dq.astype(F32),axis=0,keepdims=True)
    @pl.when(i==pl.num_programs(0)-1)
    def _():
        def fin(r,_):
            sl=pl.ds(pl.multiple_of(r*BLOCK,BLOCK),BLOCK)
            dk=turn(dk_sc[sl,:],sl)
            g_o[sl,WIDE:2*WIDE]=dk
            gb_o[0:1,WIDE:2*WIDE]+=jnp.sum(dk.astype(F32),axis=0,keepdims=True)
            dv=dv_sc[sl,:].astype(BF)
            g_o[sl,2*WIDE:]=dv
            gb_o[0:1,2*WIDE:]+=jnp.sum(dv.astype(F32),axis=0,keepdims=True)
            return 0
        lax.fori_loop(0,length//BLOCK,fin,0)

def attention_backward(bounds,q,k,kt,v,do,lse,segc,segr,cos,sin,heads):
    length=k.shape[0]; nq=length//BLOCK
    full=lambda shape: pl.BlockSpec(shape,lambda i:(0,)*len(shape),pipeline_mode=pl.Buffered(1))
    return pl.pallas_call(
        partial(bwd_kernel,heads),
        grid=(nq,),
        in_specs=[pl.BlockSpec(memory_space=pltpu.SMEM),pl.BlockSpec((BLOCK,WIDE),lambda i:(i,0)),full(k.shape),full(kt.shape),full(v.shape),
                  pl.BlockSpec((BLOCK,heads*HEAD),lambda i:(i,0)),pl.BlockSpec((8,BLOCK),lambda i:(0,i)),
                  full(segc.shape),full(segr.shape),full(cos.shape),full(sin.shape)],
        out_specs=[full((length,3*WIDE)),full((8,3*WIDE))],
        out_shape=[jax.ShapeDtypeStruct((length,3*WIDE),BF),jax.ShapeDtypeStruct((8,3*WIDE),F32)],
        scratch_shapes=[pltpu.VMEM((length,WIDE),F32),pltpu.VMEM((length,WIDE),F32),pltpu.VMEM((heads*BLOCK,WIDE),BF),pltpu.VMEM((heads*BLOCK,WIDE),BF),pltpu.VMEM((WIDE,BLOCK),F32)]+[pltpu.VMEM((length//CHUNK,CHUNK,heads*BLOCK),F32)]*2+[pltpu.VMEM((8,heads*BLOCK),F32)],
        compiler_params=pltpu.CompilerParams(dimension_semantics=("arbitrary",),vmem_limit_bytes=56*1024*1024),
        name="attention_backward",
    )(bounds,q,k,kt,v,do,lse,segc,segr,cos,sin)


def rotation_tables(offsets):
    lane = np.arange(128)
    frequency = (10000.0 ** (-2.0 * (lane % HEAD // 2) / HEAD)).astype(np.float32)
    angles = offsets.astype(F32)[:, None] * frequency[None, :]
    sign = np.where(lane % 2 == 0, -1.0, 1.0).astype(np.float32)
    return jnp.cos(angles), jnp.sin(angles) * sign


def key_bounds(segment):
    length = segment.shape[0]
    first, last = segment[::BLOCK], segment[BLOCK - 1 :: BLOCK]
    low = jnp.sum(segment[None, :] < first[:, None], axis=1)
    high = jnp.sum(segment[None, :] <= last[:, None], axis=1)
    low = low // 128 * 128
    count = (high - low + CHUNK - 1) // CHUNK
    return jnp.stack([jnp.minimum(low, length - CHUNK * count), count]).astype(jnp.int32)


def swap_ctx(x):
    return lax.ppermute(x, "ctx", [(0, 1), (1, 0)])


def swap_tp(x, k):
    return lax.ppermute(x, "tp", [(i, i ^ k) for i in range(4)])


def swap_shard(x, k):
    return lax.ppermute(x, "shard", [(i, i ^ k) for i in range(4)])


def order_four(parts, index):
    a, b, c, d = parts
    odd, high = index % 2 == 1, index // 2 == 1
    a, b = jnp.where(odd, b, a), jnp.where(odd, a, b)
    c, d = jnp.where(odd, d, c), jnp.where(odd, c, d)
    return jnp.stack([jnp.where(high, c, a), jnp.where(high, d, b), jnp.where(high, a, c), jnp.where(high, b, d)])


def gather_shard(x):
    if lax.axis_size("shard") != 4:
        return lax.all_gather(x, "shard", axis=0)
    return order_four([x] + [swap_shard(x, k) for k in (1, 2, 3)], lax.axis_index("shard"))


def scatter_shard(x):
    if lax.axis_size("shard") != 4:
        return lax.psum_scatter(x, "shard", scatter_dimension=0)
    z = lax.axis_index("shard")
    total = lax.dynamic_index_in_dim(x, z, 0, keepdims=False)
    for k in (1, 2, 3):
        piece = lax.dynamic_index_in_dim(x, z ^ k, 0, keepdims=False).astype(BF)
        total = total + swap_shard(piece, k).astype(F32)
    return total


def sum_shard(x):
    if lax.axis_size("shard") != 4:
        return lax.psum(x, "shard")
    x = x + swap_shard(x, 1)
    return x + swap_shard(x, 2)


def gather_tp(x):
    half = x.shape[0] // 2
    one, two = swap_tp(x, 1), swap_tp(x, 2)
    three = jnp.concatenate([swap_tp(one[:half], 2), swap_tp(two[half:], 1)])
    return [x, one, two, three]


def scatter_tp(parts):
    own, one, two, three = parts
    half = own.shape[0] // 2
    low, high = three[:half].astype(BF), three[half:].astype(BF)
    low, high = swap_tp(low, 2), swap_tp(high, 1)
    one = jnp.concatenate([one[:half] + low.astype(F32), one[half:]]).astype(BF)
    two = jnp.concatenate([two[:half], two[half:] + high.astype(F32)]).astype(BF)
    return own + swap_tp(one, 1).astype(F32) + swap_tp(two, 2).astype(F32)


def exchange_tp(parts):
    return [parts[0]] + [swap_tp(parts[k], k) for k in (1, 2, 3)]


def three_rows(x):
    high = lax.reduce_precision(x, 8, 7)
    middle = lax.reduce_precision(x - high, 8, 7)
    return jnp.stack([high, middle, x - high - middle]).astype(BF)


def norm_parts(rows_in):
    centre = rows_in - jnp.mean(rows_in, axis=-1, keepdims=True)
    inverse_root = lax.rsqrt(jnp.mean(centre * centre, axis=-1, keepdims=True) + EPSILON)
    return (centre * inverse_root, inverse_root)


def norm_back(grad_in, scaled, inverse_root, gain_row):
    grad_scaled = grad_in * gain_row
    term_mean = jnp.mean(grad_scaled, axis=-1, keepdims=True)
    term_along = jnp.mean(grad_scaled * scaled, axis=-1, keepdims=True)
    return inverse_root * (grad_scaled - term_mean - scaled * term_along)


def contract_last(left, right):
    return lax.dot_general(left, right, (((1,), (1,)), ((), ())), preferred_element_type=F32)


def contract_first(left, right):
    return lax.dot_general(left, right, (((0,), (0,)), ((), ())), preferred_element_type=F32)


def body(tokens, segment_ids, offsets, qkv_weight, out_weight, ffn_weight, qkv_bias, ffn_bias, norm_gain, shift_params, out_grad):
    t, c = lax.axis_index("tp"), lax.axis_index("ctx")
    shards = lax.axis_size("shard")
    half_len, width = tokens.shape[1:]
    rows, _, part = qkv_weight.shape
    hidden = ffn_weight.shape[2]
    heads = part // HEAD
    length = 2 * half_len
    share = length // 4
    hh = hidden // 2
    first_core = c == 0

    def take(x, index):
        return lax.dynamic_index_in_dim(x, index, 0, keepdims=False)

    def by_core(own, other):
        return jnp.where(first_core, jnp.stack([own, other]), jnp.stack([other, own]))

    def whole(x):
        return by_core(take(x, c), swap_ctx(take(x, 1 - c))).reshape((length,) + x.shape[2:])

    qkv_rows = gather_shard(qkv_weight.reshape(rows, 3 * part))
    tok = whole(tokens)
    marks = whole(jnp.stack([segment_ids, offsets], axis=-1))
    segment, places = marks[:, 0], marks[:, 1]
    grad_block = out_grad.reshape(2, 2, share, width)
    grad_own = take(take(grad_block, c), t % 2)
    grad_far = swap_ctx(take(take(grad_block, 1 - c), t % 2))
    grad_top = jnp.where(t // 2 == c, grad_own, grad_far).astype(F32)

    rest = jnp.concatenate([ffn_weight.reshape(rows, 2 * hidden), out_weight], axis=1)
    rest_rows = gather_shard(rest)

    def rows_of(x):
        return by_core(x, swap_ctx(x)).transpose(1, 0, 2, 3).reshape(width, x.shape[-1])

    qkv_own = rows_of(qkv_rows).reshape(width, 3, part)
    qkv_pad = jnp.pad(qkv_own, ((0, 0), (0, 0), (0, WIDE - part))).reshape(width, 3 * WIDE)
    bias_pad = jnp.pad(qkv_bias, ((0, 0), (0, WIDE - part)))

    rest_own = rows_of(rest_rows)
    ups, downs = rest_own[:, :hidden], rest_own[:, hidden : 2 * hidden]

    def half_of(x, index):
        return lax.dynamic_slice_in_dim(x, index * hh, hh, x.ndim - 1)

    def pack(core):
        feed = jnp.concatenate([half_of(ups, core), half_of(downs, core)], axis=1)
        out_part = lax.dynamic_index_in_dim(rest_own.reshape(shards, 2, rows, -1), core, 1, keepdims=False)
        out_part = out_part[:, :, 2 * hidden :].reshape(-1, hidden)
        bias = three_rows(half_of(ffn_bias, core)).reshape(-1)
        bias = jnp.pad(bias, (0, 16 * hidden - bias.shape[0])).reshape(16, hidden)
        return jnp.concatenate([feed, out_part, bias], axis=0)

    mine = jnp.stack(gather_tp(pack(c)))
    far = jnp.concatenate([pack(1 - c)[None], swap_ctx(mine[1:])])
    packs = [mine, far]
    n_out = shards * rows * part // hidden

    def join(cut):
        return jnp.concatenate([cut(p[k]) for p in packs for k in range(4)], axis=-1)

    up_all = join(lambda p: p[:width, :hh])
    down_all = join(lambda p: p[:width, hh:])

    def bias_of(p):
        three = p[width + n_out :].reshape(-1)[: 3 * hh].reshape(3, hh).astype(F32)
        return three[0] + three[1] + three[2]

    bias_all = join(bias_of)

    def out_of(k):
        own, other = (p[k][width : width + n_out].reshape(shards, rows, part) for p in packs)
        return by_core(own, other).transpose(1, 0, 2, 3).reshape(width, part)

    out_all = jnp.concatenate([out_of(k) for k in range(4)], axis=1)

    cosine, sine = rotation_tables(places)
    bounds = key_bounds(segment)
    seg_column = segment[:, None]
    seg_row = jnp.broadcast_to(segment[None, :], (8, length))
    q, k_rows, v_rows, context, log_total = attention_forward(
        bounds, tok, qkv_pad, bias_pad, cosine, sine, seg_column, seg_row, heads
    )

    blocks = context.reshape(4, share, part)
    context_all = jnp.concatenate(exchange_tp([take(blocks, t ^ k) for k in range(4)]), axis=1)
    tok_block = take(tok.reshape(4, share, width), t)
    attended = contract_last(context_all, out_all)
    first_scaled, first_root = norm_parts(tok_block.astype(F32) + attended + shift_params[2])
    normed = first_scaled * norm_gain[0] + shift_params[0]
    normed_b = normed.astype(BF)
    hidden_in = jnp.dot(normed_b, up_all, preferred_element_type=F32) + bias_all
    activated, gelu_pull = jax.vjp(partial(jax.nn.gelu, approximate=False), hidden_in)
    activated_b = activated.astype(BF)
    returned = contract_last(activated_b, down_all)
    second_scaled, second_root = norm_parts(normed + returned + shift_params[3])
    layer_out = (second_scaled * norm_gain[1] + shift_params[1]).astype(BF)

    def spread(block):
        full = order_four(gather_tp(block), t).reshape(2, half_len, width)
        own, other = take(full, c), swap_ctx(take(full, 1 - c))
        return by_core(own, other)

    outputs = spread(layer_out)

    grad_second = norm_back(grad_top, second_scaled, second_root, norm_gain[1])
    grad_second_b = grad_second.astype(BF)
    grad_act = jnp.dot(grad_second_b, down_all, preferred_element_type=F32)
    grad_hidden = gelu_pull(grad_act)[0].astype(BF)
    grad_normed = grad_second + contract_last(grad_hidden, up_all)
    grad_first = norm_back(grad_normed, first_scaled, first_root, norm_gain[0])
    grad_first_b = grad_first.astype(BF)
    grad_context = jnp.dot(grad_first_b, out_all, preferred_element_type=F32).astype(BF)
    grad_parts = exchange_tp([grad_context[:, k * part : (k + 1) * part] for k in range(4)])
    grad_heads = order_four(grad_parts, t).reshape(length, part)

    grad_proj, bias_sums = attention_backward(
        bounds, q, k_rows, k_rows.T, v_rows, grad_heads, log_total, seg_column, seg_row, cosine, sine, heads
    )

    branch = contract_last(grad_proj, qkv_pad).reshape(4, share, width)
    grad_branch = scatter_tp([take(branch, t ^ k) for k in range(4)])
    grad_tokens = spread((grad_first + grad_branch).astype(BF))

    grad_up = contract_first(normed_b, grad_hidden)
    grad_down = contract_first(grad_second_b, activated_b)
    grad_out = contract_first(grad_first_b, context_all)
    near, apart = slice(0, 4 * hh), slice(4 * hh, 8 * hh)
    got = swap_ctx(jnp.stack([grad_up[:, apart], grad_down[:, apart]]).astype(BF)).astype(F32)
    grad_up, grad_down = grad_up[:, near] + got[0], grad_down[:, near] + got[1]
    grad_out = grad_out.reshape(shards, 2, rows, width).transpose(1, 0, 2, 3)
    grad_out = take(grad_out, c) + swap_ctx(take(grad_out, 1 - c).astype(BF)).astype(F32)

    def bundle(k):
        at = slice(k * hh, (k + 1) * hh)
        feed = jnp.concatenate([grad_up[:, at], grad_down[:, at]], axis=1).reshape(shards, 2 * rows, hidden)
        out_part = grad_out[:, :, k * part : (k + 1) * part].reshape(shards, rows * part // hidden, hidden)
        return jnp.concatenate([feed, out_part], axis=1)

    summed = scatter_shard(scatter_tp([bundle(k) for k in range(4)]))
    grad_out_weight = summed[2 * rows :].reshape(rows, part)
    feed = summed[: 2 * rows].reshape(2, rows, hidden)
    feed = by_core(take(feed, c), swap_ctx(take(feed, 1 - c))).reshape(2, rows, 2, hh)
    grad_ffn_weight = feed.transpose(1, 2, 0, 3).reshape(rows, 2, hidden)

    grad_qkv = contract_first(tok, grad_proj).reshape(shards, 2, rows, 3, WIDE)[..., :part]
    grad_qkv = grad_qkv.transpose(1, 0, 2, 3, 4).reshape(2, shards, rows, 3 * part)
    grad_qkv = take(grad_qkv, c) + swap_ctx(take(grad_qkv, 1 - c).astype(BF)).astype(F32)
    grad_qkv_weight = scatter_shard(grad_qkv).reshape(rows, 3, part)

    sums = jnp.sum(grad_hidden.astype(F32), axis=0).reshape(2, 4, hh)
    sums = by_core(sums[0], sums[1])
    sums = order_four([sums[:, k] for k in range(4)], t).reshape(-1)
    small = jnp.concatenate(
        [sums]
        + [
            jnp.sum(x, axis=0)
            for x in (
                grad_normed * first_scaled,
                grad_top * second_scaled,
                grad_normed,
                grad_top,
                grad_first,
                grad_second,
            )
        ]
    ).reshape(-1, 128)
    for k in (1, 2):
        small = small + swap_tp(small, k)
    small = sum_shard(small + swap_ctx(small)).reshape(-1)
    grad_ffn_bias = lax.dynamic_slice_in_dim(small, t * hidden, hidden, 0)
    vectors = small[4 * hidden :].reshape(6, width)
    grad_qkv_bias = bias_sums[0].reshape(3, WIDE)[:, :part]
    grad_qkv_bias = sum_shard(grad_qkv_bias + swap_ctx(grad_qkv_bias))
    return (
        outputs,
        grad_tokens,
        grad_qkv_weight,
        grad_out_weight,
        grad_ffn_weight,
        grad_qkv_bias,
        grad_ffn_bias,
        vectors[:2],
        vectors[2:],
    )


def solution(mesh):
    return jax.shard_map(
        body,
        mesh=mesh,
        in_specs=(
            P("shard", "ctx", None),
            P("shard", "ctx"),
            P("shard", "ctx"),
            P(("shard", "ctx"), None, "tp"),
            P(("shard", "ctx"), "tp"),
            P(("shard", "ctx"), None, "tp"),
            P(None, "tp"),
            P("tp"),
            P(),
            P(),
            P("shard", "ctx", None),
        ),
        out_specs=(
            P("shard", "ctx", None),
            P("shard", "ctx", None),
            P(("shard", "ctx"), None, "tp"),
            P(("shard", "ctx"), "tp"),
            P(("shard", "ctx"), None, "tp"),
            P(None, "tp"),
            P("tp"),
            P(),
            P(),
        ),
        check_vma=False,
    )
```

time: 1410 us -> 588 us (0.42)
  waiting for transfers between devices: 778 us -> 165 us
  matrix products: 197 us -> 58.2 us
  blocking collectives: 123 us -> 0 us
  other arithmetic: 160 us -> 73.5 us
  starting transfers between devices: 2.84 us -> 74.2 us
  Pallas kernels: 0 us -> 64.5 us
  local copies, waits for them, and re-layouts: 119 us -> 140 us
  between operations: 16.8 us -> 2.45 us
    psum x8 -> x0, waiting for transfers between devices: 653 us -> none  [the longest x2 174 us: micro_step(): returned = lax.psum(contract_last(activated_b, ffn_full[:, 1, :]), 'tp')]
    ppermute x0 -> x58, waiting for transfers between devices: none -> 165 us  [the longest x28 112 us: swap_tp(): return lax.ppermute(x, 'tp', [(i, i ^ k) for i in range(4)])]
    dot_general x20 -> x3, matrix products: 160 us -> 25.7 us  [the longest x1 18 us: body(): hidden_in = jnp.dot(normed_b, up_all, preferred_element_type=F32) + bias_all]
    all_gather x6 -> x0, blocking collectives: 80.4 us -> none  [the longest x2 44.9 us: attention_weights(): lax.all_gather(qkv_weight, ('shard', 'ctx'), axis=0, tiled=True)]
    ppermute x0 -> x58, starting transfers between devices: none -> 74.2 us  [the longest x16 34.2 us: swap_shard(): return lax.ppermute(x, 'shard', [(i, i ^ k) for i in range(4)])]
    reduce_scatter x4 -> x0, waiting for transfers between devices: 67.9 us -> none  [the longest x1 38.5 us: body(): lax.psum_scatter(totals[0], ('shard', 'ctx'), scatter_dimension=0, tiled=...]
    pallas_call x0 -> x2, Pallas kernels: none -> 64.5 us  [the longest x1 32.4 us: attention_forward(): pl.pallas_call(partial(fwd_kernel, heads), grid=(nq,), in_specs=[pl.Block...]
    unnamed x4 -> x0, waiting for transfers between devices: 56.5 us -> none
  transfers between devices with their start and end apart: 17 -> 58, of which waited for: 11 -> 15; matrix products, arithmetic and copies ran while one was open for 7% -> 41% of each run, Pallas kernels for 0% -> 11%
where the time goes in v1:
time: 588 us; the launch traced here: 577 us
  waiting for transfers between devices  165 us (28%)
  local copies, waits for them, and re-layouts  140 us (24%)
  starting transfers between devices  74.2 us (13%)
  other arithmetic  73.5 us (12%)
  Pallas kernels  64.5 us (11%)
  matrix products  58.2 us (10%)
    ppermute x28, waiting for transfers between devices, swap_tp(): return lax.ppermute(x, 'tp', [(i, i ^ k) for i in range(4)])  112 us
    ppermute x16, waiting for transfers between devices, swap_shard(): return lax.ppermute(x, 'shard', [(i, i ^ k) for i in range(4)])  52.8 us
    unnamed x148, local copies, waits for them, and re-layouts  35.4 us
    ppermute x16, starting transfers between devices, swap_shard(): return lax.ppermute(x, 'shard', [(i, i ^ k) for i in range(4)])  34.2 us
    pallas_call x1, Pallas kernels, attention_forward(): pl.pallas_call(partial(fwd_kernel, heads), grid=(nq,), in_specs=[pl.Block...  32.4 us
    pallas_call x1, Pallas kernels, attention_backward(): pl.pallas_call(partial(bwd_kernel, heads), grid=(nq,), in_specs=[pl.Block...  32.1 us
    ppermute x28, starting transfers between devices, swap_tp(): return lax.ppermute(x, 'tp', [(i, i ^ k) for i in range(4)])  24 us
    dot_general x4, matrix products, contract_first(): lax.dot_general(left, right, (((0,), (0,)), ((), ())), preferred_element_...  19.4 us
  transfers between devices with their start and end apart: 58, of which 15 were waited for; matrix products, arithmetic and copies ran while one was open for 41% of the time, Pallas kernels for 11%

profile of v1, /device:TPU:1, one launch (start us, length us, event | category | flops | bytes accessed | tf_op | source)
XLA Modules:
  0.0 577.1 jit_solution(5139164542256542914)
XLA Ops:
  2.5 4.2 collective-permute-start.9
  6.9 7.6 %collective-permute-done.9 = bf16[96,1728]{1,0:T(8,128)(2,1)S(1)} collective-permute-done((bf16[96,1728]{1,0:T(8,128)(2,1)S(1)}, bf16[96,1728]{1,0:T(8,128)(2,1)S(1)}, u32[]{:S(2)}, u32[]{:S(2)}) %collective-permute-start.9) | collective-permute-done | bytes 331808 | tf_op jit(solution)/shard_map/ppermute | solution.py:227
  14.5 21.1 %collective-permute-done.10 = bf16[96,1728]{1,0:T(8,128)(2,1)S(1)} collective-permute-done((bf16[96,1728]{1,0:T(8,128)(2,1)S(1)}, bf16[96,1728]{1,0:T(8,128)(2,1)S(1)}, u32[]{:S(2)}, u32[]{:S(2)}) %collective-permute-start.10) | collective-permute-done | bytes 331808 | tf_op jit(solution)/shard_map/ppermute | solution.py:227
  38.6 2.3 collective-permute-start.2
  42.5 3.3 maximum_select_fusion.3
  55.0 2.1 dynamic-slice_bitcast_fusion.7
  65.1 18.0 %collective-permute-done.13 = bf16[880,768]{1,0:T(8,128)(2,1)S(1)} collective-permute-done((bf16[880,768]{1,0:T(8,128)(2,1)}, bf16[880,768]{1,0:T(8,128)(2,1)S(1)}, u32[]{:S(2)}, u32[]{:S(2)}) %collective-permute-start.13) | collective-permute-done | bytes 1351712 | tf_op jit(solution)/shard_map/ppermute | solution.py:223
  85.3 2.0 slice.618
  94.1 6.0 %collective-permute-done.15 = bf16[440,768]{1,0:T(8,128)(2,1)} collective-permute-done((bf16[440,768]{1,0:T(8,128)(2,1)}, bf16[440,768]{1,0:T(8,128)(2,1)}, u32[]{:S(2)}, u32[]{:S(2)}) %collective-permute-start.15) | collective-permute-done | bytes 675872 | tf_op jit(solution)/shard_map/ppermute | solution.py:223
  103.0 3.9 pad_maximum_fusion.1
  106.9 2.1 collective-permute-start.17
  109.0 5.6 fusion.37
  121.3 3.6 maximum_select_fusion
  125.6 32.4 %attention_forward.1 = (bf16[2048,256]{1,0:T(8,128)(2,1)}, bf16[2048,256]{1,0:T(8,128)(2,1)}, bf16[2048,256]{1,0:T(8,128)(2,1)}, bf16[2048,192]{1,0:T(8,128)(2,1)}, f32[8,2048]{1,0:T(8,128)}) custom-call(s32[2,8]{1,0:T(2,128)} %pad_add_fusion.bounds, bf16[2048,768]{1,0:T(8,128)(2,1)} %bitcast.290, bf16[768,768]{1,0:T(8,128)(2,1)} %copy.68.w, ...), custom_call_target="tpu_custom_call" | custom-call | tf_op jit(solution)/shard_map/attention_forward/pallas_call | solution.py:106
  158.0 2.4 dynamic-slice_bitcast_fusion.12
  163.0 2.3 copy.73
  165.3 2.9 copy.74
  181.3 2.5 slice_dynamic-update-slice_fusion.5
  183.8 2.4 slice_dynamic-update-slice_fusion.4
  190.0 2.5 slice_dynamic-update-slice_fusion.3
  201.6 2.1 reshape.570
  207.8 2.1 reshape.571
  219.7 2.5 fusion.110
  222.6 2.6 slice_bitcast_fusion.2
  228.8 18.0 %multiply_convert_fusion = (bf16[512,3072]{1,0:T(8,128)(2,1)S(1)}, f32[512,3072]{1,0:T(8,128)S(1)}, f32[512,3072]{1,0:T(8,128)}) fusion(f32[3072]{0:T(1024)S(1)} %constant_dynamic-update-slice_fusion.18, bf16[768,3072]{1,0:T(8,128)(2,1)S(1)} %get-tuple-element.135, f32[512,768]{1,0:T(8,128)S(1)} %get-tuple-element.192, f32[768]{0:T(1024)S(1)} %copy-done.45, ...), kind=kOutput, calls=%fused_computation.4 | convolution fusion | flops 2521694208 | bytes 22042624 | tf_op jit(solution)/shard_map/dot_general | solution.py:402
  246.9 2.8 fusion.111
  250.0 2.3 fusion.22
  253.0 5.1 fusion.57
  258.1 6.8 %convert_reduce_fusion = (f32[3072]{0:T(1024)S(1)}, bf16[512,3072]{1,0:T(8,128)(2,1)S(1)}) fusion(f32[512,3072]{1,0:T(8,128)S(1)} %get-tuple-element.74, bf16[768,3072]{1,0:T(8,128)(2,1)S(1)} %copy-done.36, f32[512,768]{1,0:T(8,128)S(1)} %get-tuple-element.67, f32[512,3072]{1,0:T(8,128)} %get-tuple-element.193, f32[3072]{0:T(1024)S(1)} %constant_dynamic-update-slice_fusion.18), kind=kOutput, calls=%fused_computation.2 | convolution fusion | flops 2443047936 | bytes 22044672 | tf_op jit(solution)/shard_map/dot_general | solution.py:418
  265.0 3.1 multiply_reduce_fusion
  268.0 5.7 fusion.90
  281.4 2.6 fusion.10
  284.0 15.9 %collective-permute-done.53 = f32[60,128]{1,0:T(8,128)S(1)} collective-permute-done((f32[60,128]{1,0:T(8,128)S(1)}, f32[60,128]{1,0:T(8,128)S(1)}, u32[]{:S(2)}, u32[]{:S(2)}) %collective-permute-start.53) | collective-permute-done | bytes 30752 | tf_op jit(solution)/shard_map/ppermute | solution.py:223
  300.4 2.6 fusion.9
  303.1 2.5 pad_maximum_fusion
  305.7 8.1 %collective-permute-start.56 = (f32[60,128]{1,0:T(8,128)S(1)}, f32[60,128]{1,0:T(8,128)S(1)}, u32[]{:S(2)}, u32[]{:S(2)}) collective-permute-start(f32[60,128]{1,0:T(8,128)S(1)} %add.472), channel_id=1, source_target_pairs={{0,8},{8,0},{16,24},{24,16},{1,9},{9,1},{17,25},{25,17},{2,10},{10... | collective-permute-start | bytes 92168 | tf_op jit(solution)/shard_map/ppermute | solution.py:227
  313.8 2.0 fusion.54
  315.8 3.7 collective-permute-start.57
  326.6 32.1 %attention_backward.1 = (bf16[2048,768]{1,0:T(8,128)(2,1)}, f32[8,768]{1,0:T(8,128)}) custom-call(s32[2,8]{1,0:T(2,128)} %pad_add_fusion.bounds, bf16[2048,256]{1,0:T(8,128)(2,1)} %get-tuple-element.17.q, bf16[2048,256]{1,0:T(8,128)(2,1)} %get-tuple-element.18.k, bf16[256,2048]{1,0:T(8,128)(2,1)} %bitcast.312, bf16[2048,256]{1,0:T(8,128)(2,1)} %get-tuple-element.19.v, ...), custom_call_target="tpu_custom_call" | custom-call | tf_op jit(solution)/shard_map/attention_backward/pallas_call | solution.py:186
  359.6 4.6 fusion.112
  364.2 2.6 copy-done.14
  369.9 4.7 copy.75
  374.6 4.9 collective-permute-start.51
  379.5 6.6 %fusion.16 = f32[2,4,96,3,192]{4,2,3,0,1:T(8,128)} fusion(bf16[4,2,96,2048,1]{3,2,4,1,0:T(8,128)(2,1)} %bitcast.314, bf16[3,256,2048,1,1]{2,1,0,4,3:T(8,128)(2,1)} %bitcast.317), kind=kOutput, calls=%fused_computation.53 | convolution fusion | flops 1811939328 | bytes 7274496 | tf_op jit(solution)/shard_map/dot_general | solution.py:307
  386.2 5.2 collective-permute-start.52
  391.4 2.2 fusion.48
  393.6 3.4 copy.76
  416.3 2.1 copy.78
  421.9 24.3 %collective-permute-done.19 = bf16[256,768]{1,0:T(8,128)(2,1)} collective-permute-done((bf16[256,768]{1,0:T(8,128)(2,1)}, bf16[256,768]{1,0:T(8,128)(2,1)}, u32[]{:S(2)}, u32[]{:S(2)}) %collective-permute-start.19) | collective-permute-done | bytes 393248 | tf_op jit(solution)/shard_map/ppermute | solution.py:223
  447.4 2.2 fusion.26
  451.6 4.4 collective-permute-done.21
  457.8 1.9 pad_maximum_fusion.2
  459.7 13.1 %collective-permute-done.31 = bf16[512,768]{1,0:T(8,128)(2,1)S(1)} collective-permute-done((bf16[512,768]{1,0:T(8,128)(2,1)S(1)}, bf16[512,768]{1,0:T(8,128)(2,1)S(1)}, u32[]{:S(2)}, u32[]{:S(2)}) %collective-permute-start.31) | collective-permute-done | bytes 786464 | tf_op jit(solution)/shard_map/ppermute | solution.py:223
  475.5 3.7 convert_element_type.243
  479.2 3.7 fusion.7
  488.0 10.5 %collective-permute-done.44 = bf16[2,216,768]{2,1,0:T(8,128)(2,1)S(1)} collective-permute-done((bf16[2,216,768]{2,1,0:T(8,128)(2,1)S(1)}, bf16[2,216,768]{2,1,0:T(8,128)(2,1)S(1)}, u32[]{:S(2)}, u32[]{:S(2)}) %collective-permute-start.44) | collective-permute-done | bytes 663584 | tf_op jit(solution)/shard_map/ppermute | solution.py:223
  503.0 3.7 collective-permute-start.22
  508.6 1.9 constant_dynamic-slice_fusion.1
  510.7 17.9 %collective-permute-done.45 = bf16[4,216,768]{2,1,0:T(8,128)(2,1)S(1)} collective-permute-done((bf16[4,216,768]{2,1,0:T(8,128)(2,1)S(1)}, bf16[4,216,768]{2,1,0:T(8,128)(2,1)S(1)}, u32[]{:S(2)}, u32[]{:S(2)}) %collective-permute-start.45) | collective-permute-done | bytes 1327136 | tf_op jit(solution)/shard_map/ppermute | solution.py:223
  530.2 3.4 collective-permute-start.48
  536.9 4.8 maximum_select_fusion.1
  542.4 22.2 %collective-permute-done.47 = bf16[216,768]{1,0:T(8,128)(2,1)} collective-permute-done((bf16[216,768]{1,0:T(8,128)(2,1)}, bf16[216,768]{1,0:T(8,128)(2,1)}, u32[]{:S(2)}, u32[]{:S(2)}) %collective-permute-start.47) | collective-permute-done | bytes 331808 | tf_op jit(solution)/shard_map/ppermute | solution.py:227
  566.0 3.0 collective-permute-start.49
  569.0 4.0 maximum_select_fusion.2
  (433 shorter events, 162.0 us)
Async XLA Ops:
  2.5 12.0 %collective-permute-start.9 = (bf16[96,1728]{1,0:T(8,128)(2,1)S(1)}, bf16[96,1728]{1,0:T(8,128)(2,1)S(1)}, u32[]{:S(2)}, u32[]{:S(2)}) collective-permute-start(bf16[96,1728]{1,0:T(8,128)(2,1)S(1)} %constant_dynamic-update-slice_fusion), channel_id=1, source_target_pairs={{0,24},{8,16},{16,8},{24,0},{1,25},{9,17},{17,9},{25,1},{2,26},{10... | collective-permute-start | bytes 995336 | tf_op jit(solution)/shard_map/ppermute | solution.py:227
  6.6 28.9 %collective-permute-start.10 = (bf16[96,1728]{1,0:T(8,128)(2,1)S(1)}, bf16[96,1728]{1,0:T(8,128)(2,1)S(1)}, u32[]{:S(2)}, u32[]{:S(2)}) collective-permute-start(bf16[96,1728]{1,0:T(8,128)(2,1)S(1)} %constant_dynamic-update-slice_fusion), channel_id=1, source_target_pairs={{0,16},{8,24},{16,0},{24,8},{1,17},{9,25},{17,1},{25,9},{2,18},{10... | collective-permute-start | bytes 995336 | tf_op jit(solution)/shard_map/ppermute | solution.py:227
  6.6 28.9 %collective-permute-start.11 = (bf16[96,1728]{1,0:T(8,128)(2,1)S(1)}, bf16[96,1728]{1,0:T(8,128)(2,1)S(1)}, u32[]{:S(2)}, u32[]{:S(2)}) collective-permute-start(bf16[96,1728]{1,0:T(8,128)(2,1)S(1)} %constant_dynamic-update-slice_fusion), channel_id=1, source_target_pairs={{0,8},{8,0},{16,24},{24,16},{1,9},{9,1},{17,25},{25,17},{2,10},{10... | collective-permute-start | bytes 995336 | tf_op jit(solution)/shard_map/ppermute | solution.py:227
  37.0 4.4 collective-permute-start.12
  38.6 50.6 %collective-permute-start.2 = (bf16[96,576]{0,1:T(8,128)(2,1)S(1)}, bf16[96,576]{0,1:T(8,128)(2,1)S(1)}, u32[]{:S(2)}, u32[]{:S(2)}) collective-permute-start(bf16[96,576]{0,1:T(8,128)(2,1)S(1)} %bitcast.326), channel_id=1, source_target_pairs={{0,24},{8,16},{16,8},{24,0},{1,25},{9,17},{17,9},{25,1},{2,26},{10... | collective-permute-start | bytes 331784 | tf_op jit(solution)/shard_map/ppermute | solution.py:227
  40.8 50.5 %collective-permute-start.3 = (bf16[96,576]{0,1:T(8,128)(2,1)S(1)}, bf16[96,576]{0,1:T(8,128)(2,1)}, u32[]{:S(2)}, u32[]{:S(2)}) collective-permute-start(bf16[96,576]{0,1:T(8,128)(2,1)S(1)} %bitcast.327), channel_id=1, source_target_pairs={{0,16},{8,24},{16,0},{24,8},{1,17},{9,25},{17,1},{25,9},{2,18},{10... | collective-permute-start | bytes 331784 | tf_op jit(solution)/shard_map/ppermute | solution.py:227
  40.9 20.6 %collective-permute-start.1 = (s32[1024,2]{0,1:T(2,128)S(1)}, s32[1024,2]{0,1:T(2,128)S(1)}, u32[]{:S(2)}, u32[]{:S(2)}) collective-permute-start(s32[1024,2]{0,1:T(2,128)S(1)} %bitcast.335), channel_id=1, source_target_pairs={{0,4},{4,0},{1,5},{5,1},{2,6},{6,2},{3,7},{7,3},{8,12},{12,8},{9,1... | collective-permute-start | bytes 24584 | tf_op jit(solution)/shard_map/ppermute | solution.py:219
  51.7 31.3 %collective-permute-start.13 = (bf16[880,768]{1,0:T(8,128)(2,1)}, bf16[880,768]{1,0:T(8,128)(2,1)S(1)}, u32[]{:S(2)}, u32[]{:S(2)}) collective-permute-start(bf16[880,768]{1,0:T(8,128)(2,1)} %pad_maximum_fusion.9), channel_id=1, source_target_pairs={{0,1},{1,0},{2,3},{3,2},{4,5},{5,4},{6,7},{7,6},{8,9},{9,8},{10,11... | collective-permute-start | bytes 4055048 | tf_op jit(solution)/shard_map/ppermute | solution.py:223
  53.0 32.3 %collective-permute-start.14 = (bf16[880,768]{1,0:T(8,128)(2,1)}, bf16[880,768]{1,0:T(8,128)(2,1)}, u32[]{:S(2)}, u32[]{:S(2)}) collective-permute-start(bf16[880,768]{1,0:T(8,128)(2,1)} %pad_maximum_fusion.9), channel_id=1, source_target_pairs={{0,2},{1,3},{2,0},{3,1},{4,6},{5,7},{6,4},{7,5},{8,10},{9,11},{10,... | collective-permute-start | bytes 4055048 | tf_op jit(solution)/shard_map/ppermute | solution.py:223
  61.5 29.9 %collective-permute-start.4 = (bf16[96,576]{0,1:T(8,128)(2,1)S(1)}, bf16[96,576]{0,1:T(8,128)(2,1)}, u32[]{:S(2)}, u32[]{:S(2)}) collective-permute-start(bf16[96,576]{0,1:T(8,128)(2,1)S(1)} %bitcast.328), channel_id=1, source_target_pairs={{0,8},{8,0},{16,24},{24,16},{1,9},{9,1},{17,25},{25,17},{2,10},{10... | collective-permute-start | bytes 331784 | tf_op jit(solution)/shard_map/ppermute | solution.py:227
  83.1 19.9 %copy-start.4 = (bf16[880,768]{1,0:T(8,128)(2,1)}, bf16[880,768]{1,0:T(8,128)(2,1)S(1)}, u32[]{:S(2)}) copy-start(bf16[880,768]{1,0:T(8,128)(2,1)S(1)} %collective-permute-done.13) | copy-start | bytes 4055044
  84.0 16.1 %collective-permute-start.15 = (bf16[440,768]{1,0:T(8,128)(2,1)}, bf16[440,768]{1,0:T(8,128)(2,1)}, u32[]{:S(2)}, u32[]{:S(2)}) collective-permute-start(bf16[440,768]{1,0:T(8,128)(2,1)} %slice.617), channel_id=1, source_target_pairs={{0,2},{1,3},{2,0},{3,1},{4,6},{5,7},{6,4},{7,5},{8,10},{9,11},{10,... | collective-permute-start | bytes 2027528 | tf_op jit(solution)/shard_map/ppermute | solution.py:223
  87.3 15.7 %collective-permute-start.16 = (bf16[440,768]{1,0:T(8,128)(2,1)}, bf16[440,768]{1,0:T(8,128)(2,1)S(1)}, u32[]{:S(2)}, u32[]{:S(2)}) collective-permute-start(bf16[440,768]{1,0:T(8,128)(2,1)} %slice.618), channel_id=1, source_target_pairs={{0,1},{1,0},{2,3},{3,2},{4,5},{5,4},{6,7},{7,6},{8,9},{9,8},{10,11... | collective-permute-start | bytes 2027528 | tf_op jit(solution)/shard_map/ppermute | solution.py:223
  89.1 32.2 %collective-permute-start = (bf16[1024,768]{1,0:T(8,128)(2,1)}, bf16[1024,768]{1,0:T(8,128)(2,1)}, u32[]{:S(2)}, u32[]{:S(2)}) collective-permute-start(bf16[1024,768]{1,0:T(8,128)(2,1)} %get-tuple-element.113), channel_id=1, source_target_pairs={{0,4},{4,0},{1,5},{5,1},{2,6},{6,2},{3,7},{7,3},{8,12},{12,8},{9,1... | collective-permute-start | bytes 4718600 | tf_op jit(solution)/shard_map/ppermute | solution.py:219
  91.3 158.7 %collective-permute-start.23 = (bf16[512,768]{1,0:T(8,128)(2,1)}, bf16[512,768]{1,0:T(8,128)(2,1)}, u32[]{:S(2)}, u32[]{:S(2)}) collective-permute-start(bf16[512,768]{1,0:T(8,128)(2,1)} %dynamic-slice_bitcast_fusion.7), channel_id=1, source_target_pairs={{0,4},{4,0},{1,5},{5,1},{2,6},{6,2},{3,7},{7,3},{8,12},{12,8},{9,1... | collective-permute-start | bytes 2359304 | tf_op jit(solution)/shard_map/ppermute | solution.py:219
  93.6 21.1 %collective-permute-start.5 = (bf16[4,96,576]{2,1,0:T(8,128)(2,1)}, bf16[4,96,576]{2,1,0:T(8,128)(2,1)S(1)}, u32[]{:S(2)}, u32[]{:S(2)}) collective-permute-start(bf16[4,96,576]{2,1,0:T(8,128)(2,1)} %copy.65), channel_id=1, source_target_pairs={{0,4},{4,0},{1,5},{5,1},{2,6},{6,2},{3,7},{7,3},{8,12},{12,8},{9,1... | collective-permute-start | bytes 1327112 | tf_op jit(solution)/shard_map/ppermute | solution.py:219
  106.9 87.5 %collective-permute-start.17 = (bf16[3,880,768]{2,1,0:T(8,128)(2,1)}, bf16[3,880,768]{2,1,0:T(8,128)(2,1)}, u32[]{:S(2)}, u32[]{:S(2)}) collective-permute-start(bf16[3,880,768]{2,1,0:T(8,128)(2,1)} %pad_maximum_fusion.1), channel_id=1, source_target_pairs={{0,4},{4,0},{1,5},{5,1},{2,6},{6,2},{3,7},{7,3},{8,12},{12,8},{9,1... | collective-permute-start | bytes 12165128 | tf_op jit(solution)/shard_map/ppermute | solution.py:219
  160.3 59.3 %collective-permute-start.8 = (bf16[512,192]{1,0:T(8,128)(2,1)}, bf16[512,192]{1,0:T(8,128)(2,1)}, u32[]{:S(2)}, u32[]{:S(2)}) collective-permute-start(bf16[512,192]{1,0:T(8,128)(2,1)} %get-tuple-element.155), channel_id=1, source_target_pairs={{0,3},{1,2},{2,1},{3,0},{4,7},{5,6},{6,5},{7,4},{8,11},{9,10},{10,... | collective-permute-start | bytes 589832 | tf_op jit(solution)/shard_map/ppermute | solution.py:223
  161.5 58.2 %collective-permute-start.7 = (bf16[512,192]{1,0:T(8,128)(2,1)}, bf16[512,192]{1,0:T(8,128)(2,1)}, u32[]{:S(2)}, u32[]{:S(2)}) collective-permute-start(bf16[512,192]{1,0:T(8,128)(2,1)} %get-tuple-element.156), channel_id=1, source_target_pairs={{0,2},{1,3},{2,0},{3,1},{4,6},{5,7},{6,4},{7,5},{8,10},{9,11},{10,... | collective-permute-start | bytes 589832 | tf_op jit(solution)/shard_map/ppermute | solution.py:223
  162.7 56.9 %collective-permute-start.6 = (bf16[512,192]{1,0:T(8,128)(2,1)}, bf16[512,192]{1,0:T(8,128)(2,1)}, u32[]{:S(2)}, u32[]{:S(2)}) collective-permute-start(bf16[512,192]{1,0:T(8,128)(2,1)} %get-tuple-element.157), channel_id=1, source_target_pairs={{0,1},{1,0},{2,3},{3,2},{4,5},{5,4},{6,7},{7,6},{8,9},{9,8},{10,11... | collective-permute-start | bytes 589832 | tf_op jit(solution)/shard_map/ppermute | solution.py:223
  273.8 133.2 %collective-permute-start.18 = (bf16[512,768]{1,0:T(8,128)(2,1)S(1)}, bf16[512,768]{1,0:T(8,128)(2,1)}, u32[]{:S(2)}, u32[]{:S(2)}) collective-permute-start(bf16[512,768]{1,0:T(8,128)(2,1)S(1)} %get-tuple-element.121), channel_id=1, source_target_pairs={{0,1},{1,0},{2,3},{3,2},{4,5},{5,4},{6,7},{7,6},{8,9},{9,8},{10,11... | collective-permute-start | bytes 2359304 | tf_op jit(solution)/shard_map/ppermute | solution.py:223
  278.2 45.9 %collective-permute-start.24 = (bf16[512,192]{1,0:T(8,128)(2,1)}, bf16[512,192]{1,0:T(8,128)(2,1)}, u32[]{:S(2)}, u32[]{:S(2)}) collective-permute-start(bf16[512,192]{1,0:T(8,128)(2,1)} %get-tuple-element.164), channel_id=1, source_target_pairs={{0,3},{1,2},{2,1},{3,0},{4,7},{5,6},{6,5},{7,4},{8,11},{9,10},{10,... | collective-permute-start | bytes 589832 | tf_op jit(solution)/shard_map/ppermute | solution.py:223
  278.2 45.9 %collective-permute-start.25 = (bf16[512,192]{1,0:T(8,128)(2,1)}, bf16[512,192]{1,0:T(8,128)(2,1)}, u32[]{:S(2)}, u32[]{:S(2)}) collective-permute-start(bf16[512,192]{1,0:T(8,128)(2,1)} %get-tuple-element.163), channel_id=1, source_target_pairs={{0,2},{1,3},{2,0},{3,1},{4,6},{5,7},{6,4},{7,5},{8,10},{9,11},{10,... | collective-permute-start | bytes 589832 | tf_op jit(solution)/shard_map/ppermute | solution.py:223
  279.7 44.5 %collective-permute-start.26 = (bf16[512,192]{1,0:T(8,128)(2,1)}, bf16[512,192]{1,0:T(8,128)(2,1)}, u32[]{:S(2)}, u32[]{:S(2)}) collective-permute-start(bf16[512,192]{1,0:T(8,128)(2,1)} %get-tuple-element.162), channel_id=1, source_target_pairs={{0,1},{1,0},{2,3},{3,2},{4,5},{5,4},{6,7},{7,6},{8,9},{9,8},{10,11... | collective-permute-start | bytes 589832 | tf_op jit(solution)/shard_map/ppermute | solution.py:223
  281.1 18.9 %collective-permute-start.53 = (f32[60,128]{1,0:T(8,128)S(1)}, f32[60,128]{1,0:T(8,128)S(1)}, u32[]{:S(2)}, u32[]{:S(2)}) collective-permute-start(f32[60,128]{1,0:T(8,128)S(1)} %bitcast.330), channel_id=1, source_target_pairs={{0,1},{1,0},{2,3},{3,2},{4,5},{5,4},{6,7},{7,6},{8,9},{9,8},{10,11... | collective-permute-start | bytes 92168 | tf_op jit(solution)/shard_map/ppermute | solution.py:223
  299.9 3.1 collective-permute-start.54
  303.1 2.6 collective-permute-start.55
  305.7 10.1 %collective-permute-start.56 = (f32[60,128]{1,0:T(8,128)S(1)}, f32[60,128]{1,0:T(8,128)S(1)}, u32[]{:S(2)}, u32[]{:S(2)}) collective-permute-start(f32[60,128]{1,0:T(8,128)S(1)} %add.472), channel_id=1, source_target_pairs={{0,8},{8,0},{16,24},{24,16},{1,9},{9,1},{17,25},{25,17},{2,10},{10... | collective-permute-start | bytes 92168 | tf_op jit(solution)/shard_map/ppermute | solution.py:227
  315.8 5.0 collective-permute-start.57
  320.8 154.6 %collective-permute-start.40 = (bf16[2,768,1536]{2,1,0:T(8,128)(2,1)}, bf16[2,768,1536]{2,1,0:T(8,128)(2,1)}, u32[]{:S(2)}, u32[]{:S(2)}) collective-permute-start(bf16[2,768,1536]{2,1,0:T(8,128)(2,1)} %pad_maximum_fusion), channel_id=1, source_target_pairs={{0,4},{4,0},{1,5},{5,1},{2,6},{6,2},{3,7},{7,3},{8,12},{12,8},{9,1... | collective-permute-start | bytes 14155784 | tf_op jit(solution)/shard_map/ppermute | solution.py:219
  326.6 33.0 %copy-start.9 = (bf16[768,3,256]{0,2,1:T(8,128)(2,1)S(1)}, bf16[768,3,256]{0,2,1:T(8,128)(2,1)}, u32[]{:S(2)}) copy-start(bf16[768,3,256]{0,2,1:T(8,128)(2,1)} %copy-done.8) | copy-start | bytes 3538948
  359.5 15.1 %collective-permute-start.50 = (f32[3,192]{1,0:T(4,128)S(1)}, f32[3,192]{1,0:T(4,128)S(1)}, u32[]{:S(2)}, u32[]{:S(2)}) collective-permute-start(f32[3,192]{1,0:T(4,128)S(1)} %bitcast.334), channel_id=1, source_target_pairs={{0,4},{4,0},{1,5},{5,1},{2,6},{6,2},{3,7},{7,3},{8,12},{12,8},{9,1... | collective-permute-start | bytes 6920 | tf_op jit(solution)/shard_map/ppermute | solution.py:219
  367.9 33.7 %collective-permute-start.27 = (bf16[256,768]{1,0:T(8,128)(2,1)}, bf16[256,768]{1,0:T(8,128)(2,1)}, u32[]{:S(2)}, u32[]{:S(2)}) collective-permute-start(bf16[256,768]{1,0:T(8,128)(2,1)} %get-tuple-element.160), channel_id=1, source_target_pairs={{0,2},{1,3},{2,0},{3,1},{4,6},{5,7},{6,4},{7,5},{8,10},{9,11},{10,... | collective-permute-start | bytes 1179656 | tf_op jit(solution)/shard_map/ppermute | solution.py:223
  368.7 33.5 %collective-permute-start.29 = (bf16[256,768]{1,0:T(8,128)(2,1)}, bf16[256,768]{1,0:T(8,128)(2,1)}, u32[]{:S(2)}, u32[]{:S(2)}) collective-permute-start(bf16[256,768]{1,0:T(8,128)(2,1)} %get-tuple-element.161), channel_id=1, source_target_pairs={{0,1},{1,0},{2,3},{3,2},{4,5},{5,4},{6,7},{7,6},{8,9},{9,8},{10,11... | collective-permute-start | bytes 1179656 | tf_op jit(solution)/shard_map/ppermute | solution.py:223
  374.6 11.5 %collective-permute-start.51 = (f32[3,192]{1,0:T(4,128)S(1)}, f32[3,192]{1,0:T(4,128)S(1)}, u32[]{:S(2)}, u32[]{:S(2)}) collective-permute-start(f32[3,192]{1,0:T(4,128)S(1)} %slice_add_fusion.14), channel_id=1, source_target_pairs={{0,8},{8,0},{16,24},{24,16},{1,9},{9,1},{17,25},{25,17},{2,10},{10... | collective-permute-start | bytes 6920 | tf_op jit(solution)/shard_map/ppermute | solution.py:227
  386.2 10.8 %collective-permute-start.52 = (f32[3,192]{1,0:T(4,128)S(1)}, f32[3,192]{1,0:T(4,128)S(1)}, u32[]{:S(2)}, u32[]{:S(2)}) collective-permute-start(f32[3,192]{1,0:T(4,128)S(1)} %add.468), channel_id=1, source_target_pairs={{0,16},{8,24},{16,0},{24,8},{1,17},{9,25},{17,1},{25,9},{2,18},{10... | collective-permute-start | bytes 6920 | tf_op jit(solution)/shard_map/ppermute | solution.py:227
  397.0 9.2 %collective-permute-start.41 = (bf16[4,96,768]{2,1,0:T(8,128)(2,1)}, bf16[4,96,768]{2,1,0:T(8,128)(2,1)}, u32[]{:S(2)}, u32[]{:S(2)}) collective-permute-start(bf16[4,96,768]{2,1,0:T(8,128)(2,1)} %fusion.46), channel_id=1, source_target_pairs={{0,4},{4,0},{1,5},{5,1},{2,6},{6,2},{3,7},{7,3},{8,12},{12,8},{9,1... | collective-permute-start | bytes 1769480 | tf_op jit(solution)/shard_map/ppermute | solution.py:219
  401.6 19.3 %collective-permute-start.20 = (bf16[512,768]{1,0:T(8,128)(2,1)S(1)}, bf16[512,768]{1,0:T(8,128)(2,1)}, u32[]{:S(2)}, u32[]{:S(2)}) collective-permute-start(bf16[512,768]{1,0:T(8,128)(2,1)S(1)} %get-tuple-element.121), channel_id=1, source_target_pairs={{0,2},{1,3},{2,0},{3,1},{4,6},{5,7},{6,4},{7,5},{8,10},{9,11},{10,... | collective-permute-start | bytes 2359304 | tf_op jit(solution)/shard_map/ppermute | solution.py:223
  402.2 8.0 %collective-permute-start.36 = (bf16[4,96,576]{2,1,0:T(8,128)(2,1)}, bf16[4,96,576]{2,1,0:T(8,128)(2,1)S(1)}, u32[]{:S(2)}, u32[]{:S(2)}) collective-permute-start(bf16[4,96,576]{2,1,0:T(8,128)(2,1)} %copy.77), channel_id=1, source_target_pairs={{0,4},{4,0},{1,5},{5,1},{2,6},{6,2},{3,7},{7,3},{8,12},{12,8},{9,1... | collective-permute-start | bytes 1327112 | tf_op jit(solution)/shard_map/ppermute | solution.py:219
  406.2 41.3 %collective-permute-start.30 = (bf16[512,768]{1,0:T(8,128)(2,1)}, bf16[512,768]{1,0:T(8,128)(2,1)}, u32[]{:S(2)}, u32[]{:S(2)}) collective-permute-start(bf16[512,768]{1,0:T(8,128)(2,1)} %pad_maximum_fusion.17), channel_id=1, source_target_pairs={{0,2},{1,3},{2,0},{3,1},{4,6},{5,7},{6,4},{7,5},{8,10},{9,11},{10,... | collective-permute-start | bytes 2359304 | tf_op jit(solution)/shard_map/ppermute | solution.py:223
  407.0 40.5 %collective-permute-start.28 = (bf16[512,768]{1,0:T(8,128)(2,1)}, bf16[512,768]{1,0:T(8,128)(2,1)}, u32[]{:S(2)}, u32[]{:S(2)}) collective-permute-start(bf16[512,768]{1,0:T(8,128)(2,1)} %pad_maximum_fusion.16), channel_id=1, source_target_pairs={{0,1},{1,0},{2,3},{3,2},{4,5},{5,4},{6,7},{7,6},{8,9},{9,8},{10,11... | collective-permute-start | bytes 2359304 | tf_op jit(solution)/shard_map/ppermute | solution.py:223
  410.2 35.9 %collective-permute-start.19 = (bf16[256,768]{1,0:T(8,128)(2,1)}, bf16[256,768]{1,0:T(8,128)(2,1)}, u32[]{:S(2)}, u32[]{:S(2)}) collective-permute-start(bf16[256,768]{1,0:T(8,128)(2,1)} %slice.672), channel_id=1, source_target_pairs={{0,2},{1,3},{2,0},{3,1},{4,6},{5,7},{6,4},{7,5},{8,10},{9,11},{10,... | collective-permute-start | bytes 1179656 | tf_op jit(solution)/shard_map/ppermute | solution.py:223
  419.9 27.5 %copy-start.18 = (f32[4,96,576]{1,2,0:T(8,128)}, f32[4,96,576]{1,2,0:T(8,128)S(1)}, u32[]{:S(2)}) copy-start(f32[4,96,576]{1,2,0:T(8,128)S(1)} %bitcast_add_fusion.2) | copy-start | bytes 2654212
  420.8 109.4 %collective-permute-start.39 = (bf16[96,576]{0,1:T(8,128)(2,1)}, bf16[96,576]{0,1:T(8,128)(2,1)}, u32[]{:S(2)}, u32[]{:S(2)}) collective-permute-start(bf16[96,576]{0,1:T(8,128)(2,1)} %get-tuple-element.152), channel_id=1, source_target_pairs={{0,24},{8,16},{16,8},{24,0},{1,25},{9,17},{17,9},{25,1},{2,26},{10... | collective-permute-start | bytes 331784 | tf_op jit(solution)/shard_map/ppermute | solution.py:227
  446.1 9.9 %collective-permute-start.21 = (bf16[256,768]{1,0:T(8,128)(2,1)S(1)}, bf16[256,768]{1,0:T(8,128)(2,1)S(1)}, u32[]{:S(2)}, u32[]{:S(2)}) collective-permute-start(bf16[256,768]{1,0:T(8,128)(2,1)S(1)} %slice.673), channel_id=1, source_target_pairs={{0,1},{1,0},{2,3},{3,2},{4,5},{5,4},{6,7},{7,6},{8,9},{9,8},{10,11... | collective-permute-start | bytes 1179656 | tf_op jit(solution)/shard_map/ppermute | solution.py:223
  449.7 23.2 %collective-permute-start.31 = (bf16[512,768]{1,0:T(8,128)(2,1)S(1)}, bf16[512,768]{1,0:T(8,128)(2,1)S(1)}, u32[]{:S(2)}, u32[]{:S(2)}) collective-permute-start(bf16[512,768]{1,0:T(8,128)(2,1)S(1)} %fusion.26), channel_id=1, source_target_pairs={{0,1},{1,0},{2,3},{3,2},{4,5},{5,4},{6,7},{7,6},{8,9},{9,8},{10,11... | collective-permute-start | bytes 2359304 | tf_op jit(solution)/shard_map/ppermute | solution.py:223
  450.9 23.4 %collective-permute-start.33 = (bf16[512,768]{1,0:T(8,128)(2,1)S(1)}, bf16[512,768]{1,0:T(8,128)(2,1)S(1)}, u32[]{:S(2)}, u32[]{:S(2)}) collective-permute-start(bf16[512,768]{1,0:T(8,128)(2,1)S(1)} %fusion.26), channel_id=1, source_target_pairs={{0,2},{1,3},{2,0},{3,1},{4,6},{5,7},{6,4},{7,5},{8,10},{9,11},{10,... | collective-permute-start | bytes 2359304 | tf_op jit(solution)/shard_map/ppermute | solution.py:223
  456.0 23.2 %slice-start = ((s8[9437184]{0:T(1024)(128)(4,1)}), s8[4194304]{0:T(1024)(128)(4,1)S(1)}, s32[]{:S(2)}) async-start(s8[9437184]{0:T(1024)(128)(4,1)} %bitcast.288), calls=%async_computation | async-start | bytes 8388608
  457.8 21.4 %slice-start.1 = ((s8[9437184]{0:T(1024)(128)(4,1)}), s8[4194304]{0:T(1024)(128)(4,1)S(1)}, s32[]{:S(2)}) async-start(s8[9437184]{0:T(1024)(128)(4,1)} %bitcast.288), calls=%async_computation.1 | async-start | bytes 8388608
  473.6 29.4 %collective-permute-start.32 = (bf16[256,768]{1,0:T(8,128)(2,1)}, bf16[256,768]{1,0:T(8,128)(2,1)S(1)}, u32[]{:S(2)}, u32[]{:S(2)}) collective-permute-start(bf16[256,768]{1,0:T(8,128)(2,1)} %slice.680), channel_id=1, source_target_pairs={{0,2},{1,3},{2,0},{3,1},{4,6},{5,7},{6,4},{7,5},{8,10},{9,11},{10,... | collective-permute-start | bytes 1179656 | tf_op jit(solution)/shard_map/ppermute | solution.py:223
  475.2 31.6 %collective-permute-start.34 = (bf16[256,768]{1,0:T(8,128)(2,1)}, bf16[256,768]{1,0:T(8,128)(2,1)}, u32[]{:S(2)}, u32[]{:S(2)}) collective-permute-start(bf16[256,768]{1,0:T(8,128)(2,1)} %slice.681), channel_id=1, source_target_pairs={{0,1},{1,0},{2,3},{3,2},{4,5},{5,4},{6,7},{7,6},{8,9},{9,8},{10,11... | collective-permute-start | bytes 1179656 | tf_op jit(solution)/shard_map/ppermute | solution.py:223
  484.2 14.3 %collective-permute-start.44 = (bf16[2,216,768]{2,1,0:T(8,128)(2,1)S(1)}, bf16[2,216,768]{2,1,0:T(8,128)(2,1)S(1)}, u32[]{:S(2)}, u32[]{:S(2)}) collective-permute-start(bf16[2,216,768]{2,1,0:T(8,128)(2,1)S(1)} %get-tuple-element.147), channel_id=1, source_target_pairs={{0,1},{1,0},{2,3},{3,2},{4,5},{5,4},{6,7},{7,6},{8,9},{9,8},{10,11... | collective-permute-start | bytes 1990664 | tf_op jit(solution)/shard_map/ppermute | solution.py:223
  485.7 14.0 %collective-permute-start.42 = (bf16[2,216,768]{2,1,0:T(8,128)(2,1)S(1)}, bf16[2,216,768]{2,1,0:T(8,128)(2,1)S(1)}, u32[]{:S(2)}, u32[]{:S(2)}) collective-permute-start(bf16[2,216,768]{2,1,0:T(8,128)(2,1)S(1)} %get-tuple-element.146), channel_id=1, source_target_pairs={{0,2},{1,3},{2,0},{3,1},{4,6},{5,7},{6,4},{7,5},{8,10},{9,11},{10,... | collective-permute-start | bytes 1990664 | tf_op jit(solution)/shard_map/ppermute | solution.py:223
  498.8 29.8 %collective-permute-start.45 = (bf16[4,216,768]{2,1,0:T(8,128)(2,1)S(1)}, bf16[4,216,768]{2,1,0:T(8,128)(2,1)S(1)}, u32[]{:S(2)}, u32[]{:S(2)}) collective-permute-start(bf16[4,216,768]{2,1,0:T(8,128)(2,1)S(1)} %pad_maximum_fusion.13), channel_id=1, source_target_pairs={{0,2},{1,3},{2,0},{3,1},{4,6},{5,7},{6,4},{7,5},{8,10},{9,11},{10,... | collective-permute-start | bytes 3981320 | tf_op jit(solution)/shard_map/ppermute | solution.py:223
  500.0 28.6 %collective-permute-start.43 = (bf16[4,216,768]{2,1,0:T(8,128)(2,1)S(1)}, bf16[4,216,768]{2,1,0:T(8,128)(2,1)S(1)}, u32[]{:S(2)}, u32[]{:S(2)}) collective-permute-start(bf16[4,216,768]{2,1,0:T(8,128)(2,1)S(1)} %pad_maximum_fusion.12), channel_id=1, source_target_pairs={{0,1},{1,0},{2,3},{3,2},{4,5},{5,4},{6,7},{7,6},{8,9},{9,8},{10,11... | collective-permute-start | bytes 3981320 | tf_op jit(solution)/shard_map/ppermute | solution.py:223
  503.0 33.9 %collective-permute-start.22 = (bf16[1024,768]{1,0:T(8,128)(2,1)}, bf16[1024,768]{1,0:T(8,128)(2,1)}, u32[]{:S(2)}, u32[]{:S(2)}) collective-permute-start(bf16[1024,768]{1,0:T(8,128)(2,1)} %get-tuple-element.107), channel_id=1, source_target_pairs={{0,4},{4,0},{1,5},{5,1},{2,6},{6,2},{3,7},{7,3},{8,12},{12,8},{9,1... | collective-permute-start | bytes 4718600 | tf_op jit(solution)/shard_map/ppermute | solution.py:219
  510.5 58.5 %collective-permute-start.35 = (bf16[1024,768]{1,0:T(8,128)(2,1)}, bf16[1024,768]{1,0:T(8,128)(2,1)}, u32[]{:S(2)}, u32[]{:S(2)}) collective-permute-start(bf16[1024,768]{1,0:T(8,128)(2,1)} %get-tuple-element.101), channel_id=1, source_target_pairs={{0,4},{4,0},{1,5},{5,1},{2,6},{6,2},{3,7},{7,3},{8,12},{12,8},{9,1... | collective-permute-start | bytes 4718600 | tf_op jit(solution)/shard_map/ppermute | solution.py:219
  528.6 5.9 %collective-permute-start.38 = (bf16[96,576]{0,1:T(8,128)(2,1)S(1)}, bf16[96,576]{0,1:T(8,128)(2,1)S(1)}, u32[]{:S(2)}, u32[]{:S(2)}) collective-permute-start(bf16[96,576]{0,1:T(8,128)(2,1)S(1)} %copy-done.34), channel_id=1, source_target_pairs={{0,16},{8,24},{16,0},{24,8},{1,17},{9,25},{17,1},{25,9},{2,18},{10... | collective-permute-start | bytes 331784 | tf_op jit(solution)/shard_map/ppermute | solution.py:227
  528.6 5.9 %collective-permute-start.37 = (bf16[96,576]{0,1:T(8,128)(2,1)S(1)}, bf16[96,576]{0,1:T(8,128)(2,1)S(1)}, u32[]{:S(2)}, u32[]{:S(2)}) collective-permute-start(bf16[96,576]{0,1:T(8,128)(2,1)S(1)} %copy-done.33), channel_id=1, source_target_pairs={{0,8},{8,0},{16,24},{24,16},{1,9},{9,1},{17,25},{25,17},{2,10},{10... | collective-permute-start | bytes 331784 | tf_op jit(solution)/shard_map/ppermute | solution.py:227
  530.2 12.2 %collective-permute-start.48 = (bf16[216,768]{1,0:T(8,128)(2,1)}, bf16[216,768]{1,0:T(8,128)(2,1)}, u32[]{:S(2)}, u32[]{:S(2)}) collective-permute-start(bf16[216,768]{1,0:T(8,128)(2,1)} %get-tuple-element.119), channel_id=1, source_target_pairs={{0,24},{8,16},{16,8},{24,0},{1,25},{9,17},{17,9},{25,1},{2,26},{10... | collective-permute-start | bytes 995336 | tf_op jit(solution)/shard_map/ppermute | solution.py:227
  534.5 30.1 %collective-permute-start.47 = (bf16[216,768]{1,0:T(8,128)(2,1)}, bf16[216,768]{1,0:T(8,128)(2,1)}, u32[]{:S(2)}, u32[]{:S(2)}) collective-permute-start(bf16[216,768]{1,0:T(8,128)(2,1)} %get-tuple-element.120), channel_id=1, source_target_pairs={{0,16},{8,24},{16,0},{24,8},{1,17},{9,25},{17,1},{25,9},{2,18},{10... | collective-permute-start | bytes 995336 | tf_op jit(solution)/shard_map/ppermute | solution.py:227
  534.5 30.1 %collective-permute-start.46 = (bf16[216,768]{1,0:T(8,128)(2,1)S(1)}, bf16[216,768]{1,0:T(8,128)(2,1)}, u32[]{:S(2)}, u32[]{:S(2)}) collective-permute-start(bf16[216,768]{1,0:T(8,128)(2,1)S(1)} %get-tuple-element.118), channel_id=1, source_target_pairs={{0,8},{8,0},{16,24},{24,16},{1,9},{9,1},{17,25},{25,17},{2,10},{10... | collective-permute-start | bytes 995336 | tf_op jit(solution)/shard_map/ppermute | solution.py:227
  541.7 27.3 %copy-start.7 = (bf16[1,1024,768]{2,1,0:T(8,128)(2,1)S(1)}, bf16[1,1024,768]{2,1,0:T(8,128)(2,1)}, u32[]{:S(2)}) copy-start(bf16[1,1024,768]{2,1,0:T(8,128)(2,1)} %get-tuple-element.100) | copy-start | bytes 4718596
  566.0 8.1 %collective-permute-start.49 = (f32[96,768]{1,0:T(8,128)S(1)}, f32[96,768]{1,0:T(8,128)S(1)}, u32[]{:S(2)}, u32[]{:S(2)}) collective-permute-start(f32[96,768]{1,0:T(8,128)S(1)} %get-tuple-element.166), channel_id=1, source_target_pairs={{0,4},{4,0},{1,5},{5,1},{2,6},{6,2},{3,7},{7,3},{8,12},{12,8},{9,1... | collective-permute-start | bytes 884744 | tf_op jit(solution)/shard_map/ppermute | solution.py:219
  (54 other events, 288.5 us)

commit v2 on v1

v2 whole, which is shorter than its diff:
```python
from functools import partial

import jax
import jax.numpy as jnp
import numpy as np
from jax import lax
from jax.experimental import pallas as pl
from jax.experimental.pallas import tpu as pltpu
from jax.sharding import PartitionSpec as P

HEAD = 64
WIDE = 256
BLOCK = 256
CHUNK = 256
EPSILON = 1e-12
F32 = jnp.float32
BF = jnp.bfloat16
NEG = -1e30


def swap_pairs(x):
    lane = lax.broadcasted_iota(jnp.int32, x.shape, 1)
    n = x.shape[1]
    return jnp.where(lane % 2 == 0, pltpu.roll(x, n - 1, 1), pltpu.roll(x, 1, 1))


def nt(a, b):
    return lax.dot_general(a, b, (((1,), (1,)), ((), ())), preferred_element_type=F32)


def nn(a, b):
    return lax.dot_general(a, b, (((1,), (0,)), ((), ())), preferred_element_type=F32)


def twice(x):
    return jnp.concatenate([x, x], axis=1)


def lanes_of_heads(x, heads):
    lane = lax.broadcasted_iota(jnp.int32, x.shape, 1) // HEAD
    return [jnp.where(lane == h, x, jnp.zeros_like(x)) for h in range(heads)]


def whole_block(shape, buffers=1):
    return pl.BlockSpec(shape, lambda *_: (0,) * len(shape), pipeline_mode=pl.Buffered(buffers))


def smem():
    return pl.BlockSpec(memory_space=pltpu.SMEM)


def params(mib):
    return pltpu.CompilerParams(dimension_semantics=("arbitrary",), vmem_limit_bytes=mib * 1024 * 1024)


def qkv_kernel(count, part, place, *refs):
    pieces = refs[:count]
    bias, own, other, cos, sin, q_o, k_o, v_o, kt_o, w_o = refs[count:]
    piece_rows = pieces[0].shape[0]
    pad = jnp.zeros((piece_rows, WIDE - part), BF)
    for n in range(count):
        sl = pl.ds(pl.multiple_of(place[n], 16), piece_rows)
        for m in range(3):
            w_o[sl, m * WIDE : (m + 1) * WIDE] = jnp.concatenate([pieces[n][:, m * part : (m + 1) * part], pad], axis=1)
    half_len = other.shape[0]

    def run(x, sl):
        c, s = twice(cos[sl, :]), twice(sin[sl, :])
        p = nn(x, w_o[:, 0:WIDE]) + bias[0:1, :]
        q_o[sl, :] = ((p * c + swap_pairs(p) * s).astype(BF).astype(F32) * (HEAD**-0.5)).astype(BF)
        p = nn(x, w_o[:, WIDE : 2 * WIDE]) + bias[1:2, :]
        k = (p * c + swap_pairs(p) * s).astype(BF)
        k_o[sl, :] = k
        kt_o[:, sl] = k.T
        v_o[sl, :] = (nn(x, w_o[:, 2 * WIDE : 3 * WIDE]) + bias[2:3, :]).astype(BF)

    def step(r, _):
        rows = pl.ds(pl.multiple_of(r * BLOCK, BLOCK), BLOCK)
        core = place[count]
        run(own[0, rows, :], pl.ds(pl.multiple_of(core * half_len + r * BLOCK, BLOCK), BLOCK))
        run(other[rows, :], pl.ds(pl.multiple_of((1 - core) * half_len + r * BLOCK, BLOCK), BLOCK))
        return 0

    lax.fori_loop(0, half_len // BLOCK, step, 0)


def project_qkv(place, pieces, bias, tokens, other, cos, sin, part):
    half_len, width = other.shape
    length, count = 2 * half_len, len(pieces)
    cost = pl.CostEstimate(flops=2 * length * width * 3 * WIDE, bytes_accessed=12 * 2**20, transcendentals=0)
    return pl.pallas_call(
        partial(qkv_kernel, count, part),
        grid_spec=pltpu.PrefetchScalarGridSpec(
            num_scalar_prefetch=1,
            grid=(1,),
            in_specs=[whole_block(p.shape) for p in pieces]
            + [whole_block(bias.shape), pl.BlockSpec((1, half_len, width), lambda i, s: (s[count], 0, 0))]
            + [whole_block(x.shape) for x in (other, cos, sin)],
            out_specs=[whole_block((length, WIDE))] * 3 + [whole_block((WIDE, length)), whole_block((width, 3 * WIDE))],
        ),
        out_shape=[jax.ShapeDtypeStruct((length, WIDE), BF)] * 3
        + [jax.ShapeDtypeStruct((WIDE, length), BF), jax.ShapeDtypeStruct((width, 3 * WIDE), BF)],
        compiler_params=params(32),
        cost_estimate=cost,
        name="project_qkv",
    )(place, *pieces, bias, tokens, other, cos, sin)


def forward_kernel(heads, place, q, k, v, segc, segr, ctx_o, lse_o, acc, s_sc, m_sc, l_sc, qc_sc):
    i = place[0] + pl.program_id(0)
    start, count = place[1 + 2 * i], place[2 + 2 * i]
    qc_sc[...] = jnp.concatenate(lanes_of_heads(q[...], heads), axis=0)
    seg_q = segc[...]
    m_sc[...] = jnp.full(m_sc.shape, NEG, F32)
    l_sc[...] = jnp.zeros(l_sc.shape, F32)

    def at(j):
        return pl.ds(pl.multiple_of(start + j * CHUNK, 128), CHUNK)

    def of(h):
        return slice(h * BLOCK, (h + 1) * BLOCK)

    def pass1(j, _):
        s = nt(qc_sc[...], k[at(j), :])
        keep = seg_q == segr[0:1, at(j)]
        for h in range(heads):
            sh = jnp.where(keep, s[of(h), :], NEG)
            s_sc[j, of(h), :] = sh
            m_sc[of(h), :] = jnp.maximum(m_sc[of(h), :], jnp.maximum(sh[:, :128], sh[:, 128:]))
        return 0

    lax.fori_loop(0, count, pass1, 0)
    m_sc[...] = jnp.broadcast_to(jnp.max(m_sc[...], axis=1, keepdims=True), m_sc.shape)

    def pass2(j, _):
        for h in range(heads):
            e = jnp.exp(s_sc[j, of(h), :] - twice(m_sc[of(h), :]))
            s_sc[j, of(h), :] = e
            l_sc[of(h), :] += e[:, :128] + e[:, 128:]
        return 0

    lax.fori_loop(0, count, pass2, 0)
    total = jnp.sum(l_sc[...], axis=1, keepdims=True)
    lse = m_sc[:, 0:1] + jnp.log(total)
    l_sc[...] = jnp.broadcast_to(1.0 / total, l_sc.shape)
    lane = lax.broadcasted_iota(jnp.int32, (BLOCK, 128), 1)
    tile = jnp.zeros((BLOCK, 128), F32)
    for h in range(heads):
        tile = jnp.where(lane == h, lse[of(h), :], tile)
    lse_o[...] = tile.T[0:8, :]
    acc[...] = jnp.zeros(acc.shape, F32)

    def pass3(j, _):
        ps = [(s_sc[j, of(h), :] * twice(l_sc[of(h), :])).astype(BF) for h in range(heads)]
        acc[...] += nn(jnp.concatenate(ps, axis=1), jnp.concatenate(lanes_of_heads(v[at(j), :], heads), axis=0))
        return 0

    lax.fori_loop(0, count, pass3, 0)
    ctx_o[...] = acc[:, : heads * HEAD].astype(BF)


def attention_forward(place, q, k, v, segc, segr, heads, share):
    length = q.shape[0]
    grid = share // BLOCK
    rows = lambda i, s: (s[0] + i, 0)
    flops = 4 * share * 1024 * heads * WIDE
    return pl.pallas_call(
        partial(forward_kernel, heads),
        grid_spec=pltpu.PrefetchScalarGridSpec(
            num_scalar_prefetch=1,
            grid=(grid,),
            in_specs=[
                pl.BlockSpec((BLOCK, WIDE), rows),
                whole_block(k.shape),
                whole_block(v.shape),
                pl.BlockSpec((BLOCK, 1), rows),
                whole_block(segr.shape),
            ],
            out_specs=[pl.BlockSpec((BLOCK, heads * HEAD), lambda i, s: (i, 0)), pl.BlockSpec((8, BLOCK), lambda i, s: (0, i))],
            scratch_shapes=[
                pltpu.VMEM((BLOCK, WIDE), F32),
                pltpu.VMEM((length // CHUNK, heads * BLOCK, CHUNK), F32),
                pltpu.VMEM((heads * BLOCK, 128), F32),
                pltpu.VMEM((heads * BLOCK, 128), F32),
                pltpu.VMEM((heads * BLOCK, WIDE), BF),
            ],
        ),
        out_shape=[jax.ShapeDtypeStruct((share, heads * HEAD), BF), jax.ShapeDtypeStruct((8, share), F32)],
        compiler_params=params(24),
        cost_estimate=pl.CostEstimate(flops=flops * 6, bytes_accessed=4 * 2**20, transcendentals=share * 1024 * heads),
        name="attention_forward",
    )(place, q, k, v, segc, segr)


def backward_kernel(heads, place, q, k, kt, v, do, lse, segc, segr, cos, sin, g_o, gb_o, dk_sc, dv_sc, qc_sc, dc_sc, dq_sc, p_sc, dp_sc, dl_sc):
    step_at = pl.program_id(0)
    i = step_at ^ place[0]
    length = k.shape[0]

    @pl.when(step_at == 0)
    def _():
        dk_sc[...] = jnp.zeros(dk_sc.shape, F32)
        dv_sc[...] = jnp.zeros(dv_sc.shape, F32)
        gb_o[...] = jnp.zeros(gb_o.shape, F32)

    start, count = place[1 + 2 * i], place[2 + 2 * i]
    qc_sc[...] = jnp.concatenate(lanes_of_heads(q[...], heads), axis=0)
    d = do[0]
    d = jnp.concatenate([d, jnp.zeros((BLOCK, WIDE - d.shape[1]), BF)], axis=1)
    dc_sc[...] = jnp.concatenate(lanes_of_heads(d, heads), axis=0)
    dq_sc[...] = jnp.zeros(dq_sc.shape, F32)
    own = pl.ds(pl.multiple_of(i * BLOCK, BLOCK), BLOCK)
    seg_q = segr[0:1, own]
    dl_sc[...] = jnp.zeros(dl_sc.shape, F32)

    def at(j):
        return pl.ds(pl.multiple_of(start + j * CHUNK, 128), CHUNK)

    def of(h):
        return slice(h * BLOCK, (h + 1) * BLOCK)

    def pass1(j, _):
        s = nt(k[at(j), :], qc_sc[...])
        dp = nt(v[at(j), :], dc_sc[...])
        keep = segc[at(j), :] == seg_q
        for h in range(heads):
            p = jnp.exp(jnp.where(keep, s[:, of(h)], NEG) - lse[h : h + 1, :])
            p_sc[j, :, of(h)] = p
            dp_sc[j, :, of(h)] = dp[:, of(h)]
            dl_sc[:, of(h)] += jnp.sum((p * dp[:, of(h)]).reshape(CHUNK // 8, 8, BLOCK), axis=0)
        return 0

    lax.fori_loop(0, count, pass1, 0)
    delta = jnp.sum(dl_sc[...], axis=0, keepdims=True)

    def pass2(j, _):
        ps, dss = [], []
        for h in range(heads):
            p = p_sc[j, :, of(h)]
            ds = (p * (dp_sc[j, :, of(h)] - delta[:, of(h)])).astype(BF)
            ps.append(p.astype(BF))
            dss.append(ds)
            dq_sc[h * HEAD : (h + 1) * HEAD, :] += nn(kt[h * HEAD : (h + 1) * HEAD, at(j)], ds)
        dv_sc[at(j), :] += nn(jnp.concatenate(ps, axis=1), dc_sc[...])
        dk_sc[at(j), :] += nn(jnp.concatenate(dss, axis=1), qc_sc[...])
        return 0

    lax.fori_loop(0, count, pass2, 0)

    def turn(x, sl):
        return (x * twice(cos[sl, :]) - swap_pairs(x) * twice(sin[sl, :])).astype(BF)

    def put(x, sl, m):
        g_o[sl, m * WIDE : (m + 1) * WIDE] = x
        gb_o[0:1, m * WIDE : (m + 1) * WIDE] += jnp.sum(x.astype(F32), axis=0, keepdims=True)

    put(turn(dq_sc[...].T * (HEAD**-0.5), own), own, 0)

    @pl.when(step_at == pl.num_programs(0) - 1)
    def _():
        def last(r, _):
            sl = pl.ds(pl.multiple_of(r * BLOCK, BLOCK), BLOCK)
            put(turn(dk_sc[sl, :], sl), sl, 1)
            put(dv_sc[sl, :].astype(BF), sl, 2)
            return 0

        lax.fori_loop(0, length // BLOCK, last, 0)


def attention_backward(place, q, k, kt, v, do, lse, segc, segr, cos, sin, heads):
    length = k.shape[0]
    steps, per = length // BLOCK, do.shape[1] // BLOCK
    flops = 10 * length * 1024 * heads * WIDE
    return pl.pallas_call(
        partial(backward_kernel, heads),
        grid_spec=pltpu.PrefetchScalarGridSpec(
            num_scalar_prefetch=1,
            grid=(steps,),
            in_specs=[
                pl.BlockSpec((BLOCK, WIDE), lambda i, s: (i ^ s[0], 0)),
                whole_block(k.shape),
                whole_block(kt.shape),
                whole_block(v.shape),
                pl.BlockSpec((1, BLOCK, heads * HEAD), lambda i, s: (i // per, i % per, 0)),
                pl.BlockSpec((8, BLOCK), lambda i, s: (0, i)),
                whole_block(segc.shape),
                whole_block(segr.shape),
                whole_block(cos.shape),
                whole_block(sin.shape),
            ],
            out_specs=[whole_block((length, 3 * WIDE)), whole_block((8, 3 * WIDE))],
            scratch_shapes=[pltpu.VMEM((length, WIDE), F32)] * 2
            + [pltpu.VMEM((heads * BLOCK, WIDE), BF)] * 2
            + [pltpu.VMEM((WIDE, BLOCK), F32)]
            + [pltpu.VMEM((length // CHUNK, CHUNK, heads * BLOCK), F32)] * 2
            + [pltpu.VMEM((8, heads * BLOCK), F32)],
        ),
        out_shape=[jax.ShapeDtypeStruct((length, 3 * WIDE), BF), jax.ShapeDtypeStruct((8, 3 * WIDE), F32)],
        compiler_params=params(44),
        cost_estimate=pl.CostEstimate(flops=flops * 4, bytes_accessed=16 * 2**20, transcendentals=length * 1024 * heads),
        name="attention_backward",
    )(place, q, k, kt, v, do, lse, segc, segr, cos, sin)


def fetches(place, pieces, w_feed, w_out, sems, per):
    out = []
    for n, (group, ref, lead) in enumerate(pieces):
        m = n % per
        src = ref if lead is None else ref.at[lead]
        rows = w_feed.shape[1] // per
        feed = w_feed.shape[2]
        sl = pl.ds(pl.multiple_of(place[m], 16), rows)
        a = pltpu.make_async_copy(src.at[0:rows, feed:], w_out.at[group, sl, :], sems.at[0, n])
        b = pltpu.make_async_copy(src.at[0:rows, 0:feed], w_feed.at[group, sl, :], sems.at[1, n])
        out.append((group, a, b))
    return out


def row_mean(x):
    return jnp.mean(x, axis=1, keepdims=True)


def gelu_parts(x):
    e = jnp.exp(x * x * -0.5)
    t = 1.0 / (1.0 + (0.3275911 * 0.7071067811865476) * jnp.abs(x))
    p = t * (0.254829592 + t * (-0.284496736 + t * (1.421413741 + t * (-1.453152027 + t * 1.061405429))))
    tail = 0.5 * p * e
    phi = jnp.where(x >= 0, 1.0 - tail, tail)
    return phi, phi + x * e * 0.3989422804014327


ROWS = 256


def feed_kernel(layout, per, place, *refs):
    arrays = refs[: layout[0]]
    (c0, c1, c2, c3, tokb, gtop, vec, bias, out_o, gs_o, gsb_o, fs_o, nb_o, act_o, gp_o, root_o, sum_o, w_feed, w_out, acc, normed, sems) = refs[layout[0] :]
    pieces = [(g, arrays[a], lead) for g, a, lead in layout[1]]
    copies = fetches(place, pieces, w_feed, w_out, sems, per)
    k = pl.program_id(0)
    share = tokb.shape[0]
    chunks = [pl.ds(r * ROWS, ROWS) for r in range(share // ROWS)]

    @pl.when(k == 0)
    def _():
        for _, a, _ in copies:
            a.start()
        for _, _, b in copies:
            b.start()
        for _, a, _ in copies:
            a.wait()
        for sl in chunks:
            x = tokb[sl, :].astype(F32) + vec[4:5, :]
            for n, ctx in enumerate((c0, c1, c2, c3)):
                x = x + nt(ctx[sl, :], w_out[n])
            x = x - row_mean(x)
            root = lax.rsqrt(row_mean(x * x) + EPSILON)
            x = x * root
            fs_o[sl, :] = x
            root_o[sl, :] = jnp.broadcast_to(root, (ROWS, 128))
            y = x * vec[0:1, :] + vec[2:3, :]
            normed[sl, :] = y
            nb_o[sl, :] = y.astype(BF)
            acc[sl, :] = y + vec[5:6, :]

    for group in range(4):

        @pl.when(k == group)
        def _():
            for g, _, b in copies:
                if g == group:
                    b.wait()

    hidden = act_o.shape[2]

    def rows_step(r, _):
        sl = pl.ds(pl.multiple_of(r * ROWS, ROWS), ROWS)
        h = nn(nb_o[sl, :], w_feed[k, :, 0:hidden]) + bias[pl.ds(k, 1), :]
        phi, slope = gelu_parts(h)
        a = (h * phi).astype(BF)
        act_o[0, sl, :] = a
        gp_o[0, sl, :] = slope
        acc[sl, :] += nt(a, w_feed[k, :, hidden:])
        return 0

    lax.fori_loop(0, share // ROWS, rows_step, 0)

    @pl.when(k == 3)
    def _():
        total = [jnp.zeros((1, tokb.shape[1]), F32)] * 3
        for sl in chunks:
            x = acc[sl, :]
            x = x - row_mean(x)
            root = lax.rsqrt(row_mean(x * x) + EPSILON)
            x = x * root
            out_o[sl, :] = (x * vec[1:2, :] + vec[3:4, :]).astype(BF)
            g = gtop[sl, :].astype(F32)
            gg = g * vec[1:2, :]
            gs = root * (gg - row_mean(gg) - x * row_mean(gg * x))
            gs_o[sl, :] = gs
            gsb_o[sl, :] = gs.astype(BF)
            for n, y in enumerate((g * x, g, gs)):
                total[n] = total[n] + jnp.sum(y, axis=0, keepdims=True)
        sum_o[...] = jnp.concatenate(total + [jnp.zeros((5, tokb.shape[1]), F32)], axis=0)


def layout_of(groups):
    arrays, pieces = [], []
    for k, group in enumerate(groups):
        for x in group:
            if x.ndim == 2:
                pieces.append((k, len(arrays), None))
            else:
                pieces += [(k, len(arrays), n) for n in range(x.shape[0])]
            arrays.append(x)
    return arrays, (len(arrays), pieces), len(pieces) // 4


def feed_forward(place, groups, contexts, tokb, gtop, vec, bias):
    arrays, layout, per = layout_of(groups)
    share, width = tokb.shape
    part, hidden = contexts[0].shape[1], bias.shape[1]
    block = lambda: pl.BlockSpec((1, share, hidden), lambda i, s: (i, 0, 0))
    sd = jax.ShapeDtypeStruct
    return pl.pallas_call(
        partial(feed_kernel, layout, per),
        grid_spec=pltpu.PrefetchScalarGridSpec(
            num_scalar_prefetch=1,
            grid=(4,),
            in_specs=[pl.BlockSpec(memory_space=pl.ANY)] * len(arrays)
            + [whole_block(x.shape) for x in (*contexts, tokb, gtop, vec, bias)],
            out_specs=[whole_block((share, width))] * 5
            + [block(), block(), whole_block((share, 128)), whole_block((8, width))],
            scratch_shapes=[
                pltpu.VMEM((4, width, 2 * hidden), BF),
                pltpu.VMEM((4, width, part), BF),
                pltpu.VMEM((share, width), F32),
                pltpu.VMEM((share, width), F32),
                pltpu.SemaphoreType.DMA((2, len(layout[1]))),
            ],
        ),
        out_shape=[
            sd((share, width), BF),
            sd((share, width), F32),
            sd((share, width), BF),
            sd((share, width), F32),
            sd((share, width), BF),
            sd((4, share, hidden), BF),
            sd((4, share, hidden), F32),
            sd((share, 128), F32),
            sd((8, width), F32),
        ],
        compiler_params=params(48),
        cost_estimate=pl.CostEstimate(flops=4 * share * width * 4 * hidden * 2, bytes_accessed=24 * 2**20, transcendentals=share * 4 * hidden),
        name="feed_forward",
    )(place, *arrays, *contexts, tokb, gtop, vec, bias)


def feed_back_kernel(layout, per, place, *refs):
    arrays = refs[: layout[0]]
    (gs, gsb, fs, gp, root, vec, gf_o, gfb_o, gc0, gc1, gc2, gc3, gh_o, ghs_o, sum_o, w_feed, w_out, acc, sems) = refs[layout[0] :]
    pieces = [(g, arrays[a], lead) for g, a, lead in layout[1]]
    copies = fetches(place, pieces, w_feed, w_out, sems, per)
    k = pl.program_id(0)
    share, width = gs.shape
    hidden = gh_o.shape[2]

    @pl.when(k == 0)
    def _():
        for _, _, b in copies:
            b.start()
        for _, a, _ in copies:
            a.start()

    for group in range(4):

        @pl.when(k == group)
        def _():
            for g, _, b in copies:
                if g == group:
                    b.wait()

    @pl.when(k == 0)
    def _():
        acc[...] = gs[...]

    def rows_step(r, total):
        sl = pl.ds(pl.multiple_of(r * ROWS, ROWS), ROWS)
        g = (nn(gsb[sl, :], w_feed[k, :, hidden:]) * gp[0, sl, :]).astype(BF)
        gh_o[0, sl, :] = g
        acc[sl, :] += nt(g, w_feed[k, :, 0:hidden])
        return total + jnp.sum(g.astype(F32), axis=0, keepdims=True)

    total = lax.fori_loop(0, share // ROWS, rows_step, jnp.zeros((1, hidden), F32))
    ghs_o[0] = jnp.broadcast_to(total, (8, hidden))

    @pl.when(k == 3)
    def _():
        for _, a, _ in copies:
            a.wait()
        sums = [jnp.zeros((1, width), F32)] * 3
        for r in range(share // ROWS):
            sl = pl.ds(r * ROWS, ROWS)
            gn = acc[sl, :]
            x = fs[sl, :]
            gg = gn * vec[0:1, :]
            gf = root[sl, 0:1] * (gg - row_mean(gg) - x * row_mean(gg * x))
            gf_o[sl, :] = gf
            b = gf.astype(BF)
            gfb_o[sl, :] = b
            for n, o in enumerate((gc0, gc1, gc2, gc3)):
                o[sl, :] = nn(b, w_out[n]).astype(BF)
            for n, y in enumerate((gn * x, gn, gf)):
                sums[n] = sums[n] + jnp.sum(y, axis=0, keepdims=True)
        sum_o[...] = jnp.concatenate(sums + [jnp.zeros((5, width), F32)], axis=0)


def feed_back(place, groups, gs, gsb, fs, gp, root, vec, part):
    arrays, layout, per = layout_of(groups)
    share, width = gs.shape
    hidden = gp.shape[2]
    block = lambda: pl.BlockSpec((1, share, hidden), lambda i, s: (i, 0, 0))
    sd = jax.ShapeDtypeStruct
    return pl.pallas_call(
        partial(feed_back_kernel, layout, per),
        grid_spec=pltpu.PrefetchScalarGridSpec(
            num_scalar_prefetch=1,
            grid=(4,),
            in_specs=[pl.BlockSpec(memory_space=pl.ANY)] * len(arrays)
            + [whole_block(gs.shape), whole_block(gsb.shape), whole_block(fs.shape), block(), whole_block(root.shape), whole_block(vec.shape)],
            out_specs=[whole_block((share, width))] * 2
            + [whole_block((share, part))] * 4
            + [block(), pl.BlockSpec((1, 8, hidden), lambda i, s: (i, 0, 0)), whole_block((8, width))],
            scratch_shapes=[
                pltpu.VMEM((4, width, 2 * hidden), BF),
                pltpu.VMEM((4, width, part), BF),
                pltpu.VMEM((share, width), F32),
                pltpu.SemaphoreType.DMA((2, len(layout[1]))),
            ],
        ),
        out_shape=[sd((share, width), F32), sd((share, width), BF)]
        + [sd((share, part), BF)] * 4
        + [sd((4, share, hidden), BF), sd((4, 8, hidden), F32), sd((8, width), F32)],
        compiler_params=params(48),
        cost_estimate=pl.CostEstimate(flops=4 * share * width * 4 * hidden * 2, bytes_accessed=24 * 2**20, transcendentals=0),
        name="feed_back",
    )(place, *arrays, gs, gsb, fs, gp, root, vec)


def split_rows(place, per, acc, source, near_o, far_o, lead, cols):
    if per == 1:
        near_o[(*lead, slice(None), cols)] = acc[:, source].astype(near_o.dtype)
        return
    rows = acc.shape[0] // per
    for n in range(per // 2):
        near, far = (pl.ds(pl.multiple_of(place[m], 16), rows) for m in (n, per // 2 + n))
        near_o[(*lead, n, slice(None), cols)] = acc[near, source].astype(near_o.dtype)
        far_o[(*lead, n, slice(None), cols)] = acc[far, source].astype(BF)


def weights_kernel(per, place, nb, gsb, gfb, c0, c1, c2, c3, gh, act, *refs):
    outs = refs[:-5]
    near_o, far_o = outs if per > 1 else (outs[0], None)
    nbt, gst, gft, acc, acc_out = refs[-5:]
    k = pl.program_id(0)

    @pl.when(k == 0)
    def _():
        nbt[...] = nb[...].T
        gst[...] = gsb[...].T
        gft[...] = gfb[...].T

    hidden = gh.shape[2]
    part = c0.shape[1]
    acc[...] = nn(nbt[...], gh[0])
    split_rows(place, per, acc, slice(None), near_o, far_o, (0,), slice(0, hidden))
    acc[...] = nn(gst[...], act[0])
    split_rows(place, per, acc, slice(None), near_o, far_o, (0,), slice(hidden, 2 * hidden))
    for n, ctx in enumerate((c0, c1, c2, c3)):

        @pl.when(k == n)
        def _(ctx=ctx):
            acc_out[...] = nn(gft[...], ctx[...])

    split_rows(place, per, acc_out, slice(None), near_o, far_o, (0,), slice(2 * hidden, 2 * hidden + part))


def weight_grads(place, per, nb, gsb, gfb, contexts, gh, act):
    share, width = nb.shape
    hidden, part = gh.shape[2], contexts[0].shape[1]
    block = lambda: pl.BlockSpec((1, share, hidden), lambda i, s: (i, 0, 0))
    cols = 2 * hidden + part
    if per > 1:
        shape = (4, per // 2, width // per, cols)
        outs = [jax.ShapeDtypeStruct(shape, BF)] * 2
        specs = [pl.BlockSpec((1,) + shape[1:], lambda i, s: (i, 0, 0, 0))] * 2
    else:
        outs = [jax.ShapeDtypeStruct((4, width, cols), BF)]
        specs = [pl.BlockSpec((1, width, cols), lambda i, s: (i, 0, 0))]
    return pl.pallas_call(
        partial(weights_kernel, per),
        grid_spec=pltpu.PrefetchScalarGridSpec(
            num_scalar_prefetch=1,
            grid=(4,),
            in_specs=[whole_block(x.shape) for x in (nb, gsb, gfb, *contexts)] + [block(), block()],
            out_specs=specs,
            scratch_shapes=[pltpu.VMEM((width, share), BF)] * 3 + [pltpu.VMEM((width, hidden), F32), pltpu.VMEM((width, part), F32)],
        ),
        out_shape=outs,
        compiler_params=params(40),
        cost_estimate=pl.CostEstimate(flops=4 * share * width * 4 * hidden, bytes_accessed=20 * 2**20, transcendentals=0),
        name="weight_grads",
    )(place, nb, gsb, gfb, *contexts, gh, act)


def qkv_weights_kernel(per, part, place, own, other, g, *refs):
    near_o, far_o = refs[:2] if per > 1 else (refs[0], None)
    acc = refs[-1]
    half_len = other.shape[0]
    core = place[per]
    rows = 512

    acc[...] = jnp.zeros(acc.shape, F32)

    def step(r, _):
        at = pl.ds(pl.multiple_of(r * rows, rows), rows)
        a = g[pl.ds(pl.multiple_of(core * half_len + r * rows, rows), rows), :]
        b = g[pl.ds(pl.multiple_of((1 - core) * half_len + r * rows, rows), rows), :]
        acc[...] += nn(own[0, at, :].T, a) + nn(other[at, :].T, b)
        return 0

    lax.fori_loop(0, half_len // rows, step, 0)
    for m in range(3):
        split_rows(place, per, acc, slice(m * WIDE, m * WIDE + part), near_o, far_o, (), slice(m * part, (m + 1) * part))


def qkv_weight_grads(place, per, tokens, other, g, part):
    half_len, width = other.shape
    if per > 1:
        shape = (per // 2, width // per, 3 * part)
        outs = [jax.ShapeDtypeStruct(shape, F32), jax.ShapeDtypeStruct(shape, BF)]
    else:
        outs = [jax.ShapeDtypeStruct((width, 3 * part), F32)]
    return pl.pallas_call(
        partial(qkv_weights_kernel, per, part),
        grid_spec=pltpu.PrefetchScalarGridSpec(
            num_scalar_prefetch=1,
            grid=(1,),
            in_specs=[pl.BlockSpec((1, half_len, width), lambda i, s: (s[per], 0, 0)), whole_block(other.shape), whole_block(g.shape)],
            out_specs=[whole_block(o.shape) for o in outs],
            scratch_shapes=[pltpu.VMEM((width, 3 * WIDE), F32)],
        ),
        out_shape=outs,
        compiler_params=params(32),
        cost_estimate=pl.CostEstimate(flops=4 * half_len * width * 3 * WIDE, bytes_accessed=8 * 2**20, transcendentals=0),
        name="qkv_weight_grads",
    )(place, tokens, other, g)


def rotation_tables(offsets):
    lane = np.arange(128)
    frequency = (10000.0 ** (-2.0 * (lane % HEAD // 2) / HEAD)).astype(np.float32)
    angles = offsets.astype(F32)[:, None] * frequency[None, :]
    sign = np.where(lane % 2 == 0, -1.0, 1.0).astype(np.float32)
    return jnp.cos(angles), jnp.sin(angles) * sign


def key_bounds(segment):
    length = segment.shape[0]
    first, last = segment[::BLOCK], segment[BLOCK - 1 :: BLOCK]
    low = jnp.sum(segment[None, :] < first[:, None], axis=1)
    high = jnp.sum(segment[None, :] <= last[:, None], axis=1)
    low = low // 128 * 128
    count = (high - low + CHUNK - 1) // CHUNK
    return jnp.stack([jnp.minimum(low, length - CHUNK * count), count], axis=1).reshape(-1).astype(jnp.int32)


def swap_ctx(x):
    return lax.ppermute(x, "ctx", [(0, 1), (1, 0)])


def swap_tp(x, k):
    return lax.ppermute(x, "tp", [(i, i ^ k) for i in range(4)])


def swap_shard(x, k):
    return lax.ppermute(x, "shard", [(i, i ^ k) for i in range(4)])


def order_four(parts, index):
    a, b, c, d = parts
    odd, high = index % 2 == 1, index // 2 == 1
    a, b = jnp.where(odd, b, a), jnp.where(odd, a, b)
    c, d = jnp.where(odd, d, c), jnp.where(odd, c, d)
    return jnp.stack([jnp.where(high, c, a), jnp.where(high, d, b), jnp.where(high, a, c), jnp.where(high, b, d)])


def sum_shard(x):
    if lax.axis_size("shard") != 4:
        return lax.psum(x, "shard")
    x = x + swap_shard(x, 1)
    return x + swap_shard(x, 2)


def gather_tp(x, half):
    one, two = swap_tp(x, 1), swap_tp(x, 2)
    three = jnp.concatenate([swap_tp(one[:half], 2), swap_tp(two[half:], 1)])
    return [x, one, two, three]


def scatter_tp(parts):
    own, one, two, three = parts
    half = own.shape[0] // 2
    low, high = three[:half].astype(BF), three[half:].astype(BF)
    low, high = swap_tp(low, 2), swap_tp(high, 1)
    one = jnp.concatenate([one[:half] + low.astype(F32), one[half:]]).astype(BF)
    two = jnp.concatenate([two[:half], two[half:] + high.astype(F32)]).astype(BF)
    return own + swap_tp(one, 1).astype(F32) + swap_tp(two, 2).astype(F32)


def three_rows(x):
    high = lax.reduce_precision(x, 8, 7)
    middle = lax.reduce_precision(x - high, 8, 7)
    return jnp.stack([high, middle, x - high - middle]).astype(BF)


def contract_last(left, right):
    return lax.dot_general(left, right, (((1,), (1,)), ((), ())), preferred_element_type=F32)


def body(tokens, segment_ids, offsets, qkv_weight, out_weight, ffn_weight, qkv_bias, ffn_bias, norm_gain, shift_params, out_grad):
    t, c, z = lax.axis_index("tp"), lax.axis_index("ctx"), lax.axis_index("shard")
    shards = lax.axis_size("shard")
    half_len, width = tokens.shape[1:]
    rows, _, part = qkv_weight.shape
    hidden = ffn_weight.shape[2]
    heads = part // HEAD
    length = 2 * half_len
    share = length // 4
    first_core = c == 0
    direct = shards == 4

    def take(x, index):
        return lax.dynamic_index_in_dim(x, index, 0, keepdims=False)

    def by_core(own, other):
        return jnp.where(first_core, jnp.stack([own, other]), jnp.stack([other, own]))

    feed = jnp.concatenate([ffn_weight.reshape(rows, 2 * hidden), out_weight], axis=1)
    bias_rows = jnp.pad(three_rows(ffn_bias), ((0, 13), (0, hidden + part)))
    qkv_rows = qkv_weight.reshape(rows, 3 * part)
    other_tokens = swap_ctx(take(tokens, 1 - c))
    if direct:
        place = jnp.stack([((z ^ j) * 2 + (c ^ f)) * rows for f in (0, 1) for j in range(4)] + [c]).astype(jnp.int32)
        near = [qkv_rows] + [swap_shard(qkv_rows, j) for j in (1, 2, 3)]
        qkv_pieces = near + [swap_ctx(x) for x in near]
        own = gather_tp(jnp.concatenate([feed, bias_rows]), rows // 2)
        far = jnp.concatenate([swap_shard(feed, j) for j in (1, 2, 3)])
        far = gather_tp(far, 3 * rows // 2)
        lifted = [x.reshape(3, rows, -1) for x in far]
        groups = [[own[k], lifted[k], swap_ctx(own[k]), swap_ctx(lifted[k])] for k in range(4)]
        bias_all = [x[rows : rows + 3, :hidden] for x in own]
    else:
        place = jnp.stack([jnp.zeros_like(c), c]).astype(jnp.int32)
        qkv_pieces = [lax.all_gather(qkv_rows, ("shard", "ctx"), axis=0, tiled=True)]
        full = lax.all_gather(feed, ("shard", "ctx"), axis=0, tiled=True)
        full = gather_tp(jnp.concatenate([full, bias_rows]), width // 2)
        groups = [[x] for x in full]
        bias_all = [x[width : width + 3, :hidden] for x in full]
    per = len(qkv_pieces)
    bias_all = jnp.stack([jnp.sum(x.astype(F32), axis=0) for x in bias_all])
    bias_pad = jnp.pad(qkv_bias, ((0, 0), (0, WIDE - part)))
    vec = jnp.concatenate([norm_gain, shift_params, jnp.zeros((2, width), F32)])

    marks = jnp.stack([segment_ids, offsets])
    marks = by_core(take(marks.swapaxes(0, 1), c), swap_ctx(take(marks.swapaxes(0, 1), 1 - c)))
    segment, places = marks[:, 0].reshape(length), marks[:, 1].reshape(length)
    halves = lambda x: x.reshape(2, 2, share, width)
    here = t // 2 == c
    tok_block = jnp.where(here, take(take(halves(tokens), c), t % 2), take(other_tokens.reshape(2, share, width), t % 2))
    grad_block = halves(out_grad)
    grad_far = swap_ctx(take(take(grad_block, 1 - c), t % 2))
    grad_top = jnp.where(here, take(take(grad_block, c), t % 2), grad_far)

    cosine, sine = rotation_tables(places)
    bounds = key_bounds(segment)
    seg_column = segment[:, None]
    seg_row = jnp.broadcast_to(segment[None, :], (8, length))
    q, k_rows, v_rows, k_turned, qkv_wide = project_qkv(place, qkv_pieces, bias_pad, tokens, other_tokens, cosine, sine, part)

    contexts, log_totals = [None] * 4, [None] * 4
    for j in (3, 1, 2, 0):
        spot = jnp.concatenate([((t ^ j) * (share // BLOCK))[None].astype(jnp.int32), bounds])
        context, log_totals[j] = attention_forward(spot, q, k_rows, v_rows, seg_column, seg_row, heads, share)
        contexts[j] = swap_tp(context, j) if j else context
    log_total = jnp.concatenate(log_totals, axis=1)

    layer_out, grad_second, grad_second_b, first_scaled, normed_b, activated, slope, root, sums_two = feed_forward(
        place, groups, contexts, tok_block, grad_top, vec, bias_all
    )

    def spread(block):
        a, b, d, e = gather_tp(block, share // 2)
        odd = t % 2 == 1
        mine = jnp.where(odd, jnp.stack([b, a]), jnp.stack([a, b]))
        rest = jnp.where(odd, jnp.stack([e, d]), jnp.stack([d, e]))
        keep, send = jnp.where(here, mine, rest), jnp.where(here, rest, mine)
        return by_core(keep, swap_ctx(send)).reshape(2, half_len, width)

    outputs = spread(layer_out)

    grad_first, grad_first_b, g0, g1, g2, g3, grad_hidden, hidden_sums, sums_one = feed_back(
        place, groups, grad_second, grad_second_b, first_scaled, slope, root, vec, part
    )
    grad_heads = jnp.stack([g0, swap_tp(g1, 1), swap_tp(g2, 2), swap_tp(g3, 3)])

    grads = weight_grads(place, per, normed_b, grad_second_b, grad_first_b, contexts, grad_hidden, activated)
    if direct:
        got = swap_ctx(grads[1])
        summed = scatter_tp([grads[0][k].astype(F32) + got[k].astype(F32) for k in range(4)])
        total = summed[0]
        for j in (1, 2, 3):
            total = total + swap_shard(summed[j].astype(BF), j).astype(F32)
    else:
        summed = scatter_tp([grads[0][k].astype(F32) for k in range(4)])
        total = lax.psum_scatter(summed, ("shard", "ctx"), scatter_dimension=0, tiled=True)
    grad_ffn_weight = total[:, : 2 * hidden].reshape(rows, 2, hidden)
    grad_out_weight = total[:, 2 * hidden :]

    spot = jnp.concatenate([(t * (share // BLOCK))[None].astype(jnp.int32), bounds])
    grad_proj, bias_sums = attention_backward(
        spot, q, k_rows, k_turned, v_rows, grad_heads, log_total, seg_column, seg_row, cosine, sine, heads
    )
    proj_blocks = grad_proj.reshape(4, share, 3 * WIDE)
    branch = [contract_last(take(proj_blocks, t ^ k), qkv_wide) for k in range(4)]
    grad_tokens = spread((grad_first + scatter_tp(branch)).astype(BF))

    grads = qkv_weight_grads(place, per, tokens, other_tokens, grad_proj, part)
    if direct:
        summed = grads[0] + swap_ctx(grads[1]).astype(F32)
        total = summed[0]
        for j in (1, 2, 3):
            total = total + swap_shard(summed[j].astype(BF), j).astype(F32)
    else:
        total = lax.psum_scatter(grads[0], ("shard", "ctx"), scatter_dimension=0, tiled=True)
    grad_qkv_weight = total.reshape(rows, 3, part)

    sums = order_four([hidden_sums[k, 0] for k in range(4)], t).reshape(4 * hidden)
    vectors = jnp.stack([sums_one[0], sums_two[0], sums_one[1], sums_two[1], sums_one[2], sums_two[2]])
    small = jnp.concatenate([sums, vectors.reshape(-1)]).reshape(-1, 128)
    for k in (1, 2):
        small = small + swap_tp(small, k)
    small = sum_shard(small + swap_ctx(small))
    cut = 4 * hidden // 128
    grad_ffn_bias = take(small[:cut].reshape(4, hidden), t)
    vectors = small[cut:].reshape(6, width)
    grad_qkv_bias = bias_sums[0].reshape(3, WIDE)[:, :part]
    grad_qkv_bias = sum_shard(grad_qkv_bias + swap_ctx(grad_qkv_bias))
    return (
        outputs,
        grad_tokens,
        grad_qkv_weight,
        grad_out_weight,
        grad_ffn_weight,
        grad_qkv_bias,
        grad_ffn_bias,
        vectors[:2],
        vectors[2:],
    )


def solution(mesh):
    return jax.shard_map(
        body,
        mesh=mesh,
        in_specs=(
            P("shard", "ctx", None),
            P("shard", "ctx"),
            P("shard", "ctx"),
            P(("shard", "ctx"), None, "tp"),
            P(("shard", "ctx"), "tp"),
            P(("shard", "ctx"), None, "tp"),
            P(None, "tp"),
            P("tp"),
            P(),
            P(),
            P("shard", "ctx", None),
        ),
        out_specs=(
            P("shard", "ctx", None),
            P("shard", "ctx", None),
            P(("shard", "ctx"), None, "tp"),
            P(("shard", "ctx"), "tp"),
            P(("shard", "ctx"), None, "tp"),
            P(None, "tp"),
            P("tp"),
            P(),
            P(),
        ),
        check_vma=False,
    )
```

time: 588 us -> 470 us (0.80)
  local copies, waits for them, and re-layouts: 140 us -> 52.1 us
  matrix products: 58.2 us -> 4.5 us
  Pallas kernels: 64.5 us -> 107 us
  other arithmetic: 73.5 us -> 39.4 us
  starting transfers between devices: 74.2 us -> 93.7 us
    dot_general x7 -> x0, matrix products: 45.1 us -> none  [the longest x4 19.4 us: contract_first(): lax.dot_general(left, right, (((0,), (0,)), ((), ())), preferred_element_...]
    pallas_call x2 -> x10, Pallas kernels: 64.5 us -> 107 us  [the longest x1 31.4 us: attention_backward(): pl.pallas_call(partial(backward_kernel, heads), grid_spec=pltpu.PrefetchS...]
    ppermute x14 -> x21, starting transfers between devices: 16.1 us -> 51.3 us  [swap_ctx(): return lax.ppermute(x, 'ctx', [(0, 1), (1, 0)])]
    ppermute x16, starting transfers between devices: 34.2 us -> 11.7 us  [swap_shard(): return lax.ppermute(x, 'shard', [(i, i ^ k) for i in range(4)])]
    reshape x14 -> x6, local copies, waits for them, and re-layouts: 15.2 us -> 1.48 us  [the longest x1 1.21 us: body(): grad_ffn_weight = total[:, :2 * hidden].reshape(rows, 2, hidden)]
    select_n x6 -> x3, other arithmetic: 15.8 us -> 3.84 us  [by_core(): jnp.where(first_core, jnp.stack([own, other]), jnp.stack([other, own]))]
    select_n x0 -> x5, other arithmetic: none -> 10.1 us  [the longest x3 6.64 us: spread(): keep, send = (jnp.where(here, mine, rest), jnp.where(here, rest, mine))]
    slice x32 -> x6, local copies, waits for them, and re-layouts: 10.8 us -> 0.82 us  [the longest x1 0.65 us: body(): grad_out_weight = total[:, 2 * hidden:]]
  transfers between devices with their start and end apart: 58 -> 69, of which waited for: 15 -> 23; matrix products, arithmetic and copies ran while one was open for 41% -> 14% of each run, Pallas kernels for 11% -> 15%
where the time goes in v2:
time: 470 us; the launch traced here: 464 us
  waiting for transfers between devices  166 us (35%)
  Pallas kernels  107 us (23%)
  starting transfers between devices  93.7 us (20%)
  local copies, waits for them, and re-layouts  52.1 us (11%)
  other arithmetic  39.4 us (8%)
    ppermute x32, waiting for transfers between devices, swap_tp(): return lax.ppermute(x, 'tp', [(i, i ^ k) for i in range(4)])  109 us
    ppermute x16, waiting for transfers between devices, swap_shard(): return lax.ppermute(x, 'shard', [(i, i ^ k) for i in range(4)])  57.1 us
    ppermute x21, starting transfers between devices, swap_ctx(): return lax.ppermute(x, 'ctx', [(0, 1), (1, 0)])  51.3 us
    unnamed x154, local copies, waits for them, and re-layouts  31.9 us
    pallas_call x1, Pallas kernels, attention_backward(): pl.pallas_call(partial(backward_kernel, heads), grid_spec=pltpu.PrefetchS...  31.4 us
    ppermute x32, starting transfers between devices, swap_tp(): return lax.ppermute(x, 'tp', [(i, i ^ k) for i in range(4)])  30.6 us
    pallas_call x1, Pallas kernels, feed_forward(): pl.pallas_call(partial(feed_kernel, layout, per), grid_spec=pltpu.Prefetc...  21 us
    pallas_call x4, Pallas kernels, attention_forward(): pl.pallas_call(partial(forward_kernel, heads), grid_spec=pltpu.PrefetchSc...  18.5 us
  transfers between devices with their start and end apart: 69, of which 23 were waited for; matrix products, arithmetic and copies ran while one was open for 14% of the time, Pallas kernels for 15%

profile of v2, /device:TPU:1, one launch (start us, length us, event | category | flops | bytes accessed | tf_op | source)
XLA Modules:
  0.0 464.3 jit_solution(10067718360717994109)
XLA Ops:
  3.8 4.2 collective-permute-start.2
  13.6 2.7 dynamic-slice_bitcast_fusion
  16.5 2.1 dynamic-slice_bitcast_fusion.1
  21.4 5.0 %fusion.9 = (f32[2048,128]{1,0:T(8,128)S(1)}, f32[2048,128]{1,0:T(8,128)}) fusion(f32[128]{0:T(128)S(1)} %copy-done.65, f32[128]{0:T(128)S(1)} %copy-done.64, f32[2048]{0:T(1024)S(1)} %bitcast.245), kind=kLoop, calls=%fused_computation.34 | loop fusion | flops 524288 | bytes 2106368 | tf_op jit(solution)/shard_map/mul | solution.py:665
  27.0 2.9 collective-permute-done
  32.4 4.8 %collective-permute-done.1 = bf16[96,1728]{1,0:T(8,128)(2,1)} collective-permute-done((bf16[96,1728]{1,0:T(8,128)(2,1)}, bf16[96,1728]{1,0:T(8,128)(2,1)}, u32[]{:S(2)}, u32[]{:S(2)}) %collective-permute-start.1) | collective-permute-done | bytes 331808 | tf_op jit(solution)/shard_map/ppermute | solution.py:687
  41.8 1.9 collective-permute-start.31
  45.8 20.1 %collective-permute-done.13 = bf16[48,1728]{1,0:T(8,128)(2,1)S(1)} collective-permute-done((bf16[48,1728]{1,0:T(8,128)(2,1)S(1)}, bf16[48,1728]{1,0:T(8,128)(2,1)S(1)}, u32[]{:S(2)}, u32[]{:S(2)}) %collective-permute-start.13) | collective-permute-done | bytes 165920 | tf_op jit(solution)/shard_map/ppermute | solution.py:683
  67.1 3.6 collective-permute-done.14
  70.8 1.8 collective-permute-start.22
  72.6 3.7 collective-permute-done.22.refs_3_
  76.4 6.5 %collective-permute-done.21.refs_2_ = bf16[96,576]{1,0:T(8,128)(2,1)S(1)} collective-permute-done((bf16[96,576]{1,0:T(8,128)(2,1)S(1)}, bf16[96,576]{1,0:T(8,128)(2,1)S(1)}, u32[]{:S(2)}, u32[]{:S(2)}) %collective-permute-start.21) | collective-permute-done | bytes 110624 | tf_op jit(solution)/shard_map/ppermute | solution.py:687
  82.9 4.8 %collective-permute-done.20.refs_1_ = bf16[96,576]{1,0:T(8,128)(2,1)S(1)} collective-permute-done((bf16[96,576]{1,0:T(8,128)(2,1)S(1)}, bf16[96,576]{1,0:T(8,128)(2,1)S(1)}, u32[]{:S(2)}, u32[]{:S(2)}) %collective-permute-start.20) | collective-permute-done | bytes 110624 | tf_op jit(solution)/shard_map/ppermute | solution.py:687
  87.6 5.9 %collective-permute-start.23 = (bf16[96,576]{1,0:T(8,128)(2,1)S(1)}, bf16[96,576]{1,0:T(8,128)(2,1)S(1)}, u32[]{:S(2)}, u32[]{:S(2)}) collective-permute-start(bf16[96,576]{1,0:T(8,128)(2,1)S(1)} %copy.31.refs_0_), channel_id=1, source_target_pairs={{0,4},{4,0},{1,5},{5,1},{2,6},{6,2},{3,7},{7,3},{8,12},{12,8},{9,1... | collective-permute-start | bytes 331784 | tf_op jit(solution)/shard_map/ppermute | solution.py:679
  94.1 2.5 bitcast_select_fusion.refs_21_
  99.0 5.1 %project_qkv.1 = (bf16[2048,256]{1,0:T(8,128)(2,1)S(1)}, bf16[2048,256]{1,0:T(8,128)(2,1)S(1)}, bf16[2048,256]{1,0:T(8,128)(2,1)S(1)}, bf16[256,2048]{1,0:T(8,128)(2,1)S(1)}, bf16[768,768]{1,0:T(8,128)(2,1)S(1)}) custom-call(s32[9]{0:T(128)S(1)} %stack.233.place, bf16[96,576]{1,0:T(8,128)(2,1)S(1)} %copy.31.refs_0_, ...), custom_call_target="tpu_custom_call" | custom-call | flops 2415919104 | bytes 12582912 | tf_op jit(solution)/shard_map/project_qkv/pallas_call | solution.py:91
  105.1 4.6 attention_forward.7
  109.8 4.6 attention_forward.6
  114.4 5.6 %collective-permute-start.17 = (bf16[112,1728]{1,0:T(8,128)(2,1)S(1)}, bf16[112,1728]{1,0:T(8,128)(2,1)S(1)}, u32[]{:S(2)}, u32[]{:S(2)}) collective-permute-start(bf16[112,1728]{1,0:T(8,128)(2,1)S(1)} %constant_dynamic-update-slice_fusion.5.refs_12_), channel_id=1, source_target_pairs={{0,4},{4,0},{1,5},{5,1},{2,6},{6,2},{3,7},{7,3},{8,12},{12,8},{9,1... | collective-permute-start | bytes 1161224 | tf_op jit(solution)/shard_map/ppermute | solution.py:679
  120.0 4.0 collective-permute-start.15
  124.0 4.6 attention_forward.5
  128.7 7.4 %collective-permute-done.15 = bf16[144,1728]{1,0:T(8,128)(2,1)S(1)} collective-permute-done((bf16[144,1728]{1,0:T(8,128)(2,1)S(1)}, bf16[144,1728]{1,0:T(8,128)(2,1)S(1)}, u32[]{:S(2)}, u32[]{:S(2)}) %collective-permute-start.15) | collective-permute-done | bytes 497696 | tf_op jit(solution)/shard_map/ppermute | solution.py:683
  140.0 4.2 collective-permute-done.30.refs_19_.c3
  144.2 2.7 collective-permute-start.18
  146.9 4.6 attention_forward.4
  154.7 21.0 %feed_forward.1 = (bf16[512,768]{1,0:T(8,128)(2,1)S(1)}, f32[512,768]{1,0:T(8,128)}, bf16[512,768]{1,0:T(8,128)(2,1)S(1)}, f32[512,768]{1,0:T(8,128)}, bf16[512,...) custom-call(s32[9]{0:T(128)S(1)} %stack.233.place, ...), custom_call_target="tpu_custom_call" | custom-call | flops 9663676416 | bytes 25165824 | tf_op jit(solution)/shard_map/feed_forward/pallas_call | solution.py:425
  177.3 16.0 %feed_back.1 = (f32[512,768]{1,0:T(8,128)}, bf16[512,768]{1,0:T(8,128)(2,1)S(1)}, bf16[512,192]{1,0:T(8,128)(2,1)S(1)}, bf16[512,192]{1,0:T(8,128)(2,1)S(1)}, bf...) custom-call(s32[9]{0:T(128)S(1)} %stack.233.place, ...), custom_call_target="tpu_custom_call" | custom-call | flops 9663676416 | bytes 25165824 | tf_op jit(solution)/shard_map/feed_back/pallas_call | solution.py:524
  198.2 2.5 collective-permute-done.64
  203.3 2.4 collective-permute-start.39
  205.7 6.8 %collective-permute-start.66 = (f32[60,128]{1,0:T(8,128)S(1)}, f32[60,128]{1,0:T(8,128)S(1)}, u32[]{:S(2)}, u32[]{:S(2)}) collective-permute-start(f32[60,128]{1,0:T(8,128)S(1)} %fusion.61), channel_id=1, source_target_pairs={{0,4},{4,0},{1,5},{5,1},{2,6},{6,2},{3,7},{7,3},{8,12},{12,8},{9,1... | collective-permute-start | bytes 92168 | tf_op jit(solution)/shard_map/ppermute | solution.py:679
  215.4 1.9 copy-done.37
  217.3 1.9 copy-done.38
  223.5 10.9 %weight_grads.1 = (bf16[4,4,96,1728]{3,2,1,0:T(8,128)(2,1)}, bf16[4,4,96,1728]{3,2,1,0:T(8,128)(2,1)}) custom-call(s32[9]{0:T(128)S(1)} %stack.233.place, bf16[512,768]{1,0:T(8,128)(2,1)S(1)} %copy-done.41, bf16[512,768]{1,0:T(8,128)(2,1)S(1)} %copy-done.40, bf16[512,768]{1,0:T(8,128)(2,1)S(1)} %copy-done.43, bf16[512,192]{1,0:T(8,128)(2,1)S(1)} %copy-done.45, ...), custom_call_target="tpu_custom_call" | custom-call | flops 4831838208 | bytes 20971520 | tf_op jit(solution)/shard_map/weight_grads/pallas_call | solution.py:600
  236.0 31.4 %attention_backward.1 = (bf16[2048,768]{1,0:T(8,128)(2,1)}, f32[8,768]{1,0:T(8,128)S(1)}) custom-call(s32[17]{0:T(128)S(1)} %get-tuple-element.149.place, bf16[2048,256]{1,0:T(8,128)(2,1)S(1)} %copy-done.30, bf16[2048,256]{1,0:T(8,128)(2,1)S(1)} %copy-done.32, bf16[256,2048]{1,0:T(8,128)(2,1)S(1)} %copy-done.36, bf16[2048,256]{1,0:T(8,128)(2,1)S(1)} %copy-done.34, ...), custom_call_target="tpu_custom_call" | custom-call | flops 64424509440 | bytes 16777216 | tf_op jit(solution)/shard_map/attention_backward/pallas_call | solution.py:274
  267.4 15.6 %collective-permute-start.61 = (f32[3,192]{1,0:T(4,128)S(1)}, f32[3,192]{1,0:T(4,128)S(1)}, u32[]{:S(2)}, u32[]{:S(2)}) collective-permute-start(f32[3,192]{1,0:T(4,128)S(1)} %bitcast.246), channel_id=1, source_target_pairs={{0,4},{4,0},{1,5},{5,1},{2,6},{6,2},{3,7},{7,3},{8,12},{12,8},{9,1... | collective-permute-start | bytes 6920 | tf_op jit(solution)/shard_map/ppermute | solution.py:679
  283.0 1.9 copy-done.1
  286.3 1.9 copy-done.26
  288.2 3.8 qkv_weight_grads.1
  295.1 8.1 %collective-permute-done.42 = bf16[256,768]{1,0:T(8,128)(2,1)S(1)} collective-permute-done((bf16[256,768]{1,0:T(8,128)(2,1)S(1)}, bf16[256,768]{1,0:T(8,128)(2,1)S(1)}, u32[]{:S(2)}, u32[]{:S(2)}) %collective-permute-start.42) | collective-permute-done | bytes 393248 | tf_op jit(solution)/shard_map/ppermute | solution.py:683
  304.2 8.2 %collective-permute-done.40 = bf16[256,768]{1,0:T(8,128)(2,1)S(1)} collective-permute-done((bf16[256,768]{1,0:T(8,128)(2,1)S(1)}, bf16[256,768]{1,0:T(8,128)(2,1)S(1)}, u32[]{:S(2)}, u32[]{:S(2)}) %collective-permute-start.40) | collective-permute-done | bytes 393248 | tf_op jit(solution)/shard_map/ppermute | solution.py:683
  317.7 2.7 collective-permute-done.62
  320.4 3.9 collective-permute-done.68
  324.3 3.4 collective-permute-done.63
  329.6 2.1 fusion.18
  332.9 1.9 add_convert_fusion.1
  334.8 9.7 %collective-permute-done.34 = bf16[512,768]{1,0:T(8,128)(2,1)S(1)} collective-permute-done((bf16[512,768]{1,0:T(8,128)(2,1)S(1)}, bf16[512,768]{1,0:T(8,128)(2,1)S(1)}, u32[]{:S(2)}, u32[]{:S(2)}) %collective-permute-start.34) | collective-permute-done | bytes 786464 | tf_op jit(solution)/shard_map/ppermute | solution.py:683
  347.1 1.8 slice.293
  350.0 1.9 collective-permute-start.33
  354.4 1.8 fusion.32
  358.1 10.9 %collective-permute-done.33 = bf16[256,768]{1,0:T(8,128)(2,1)} collective-permute-done((bf16[256,768]{1,0:T(8,128)(2,1)}, bf16[256,768]{1,0:T(8,128)(2,1)}, u32[]{:S(2)}, u32[]{:S(2)}) %collective-permute-start.33) | collective-permute-done | bytes 393248 | tf_op jit(solution)/shard_map/ppermute | solution.py:683
  372.9 1.9 collective-permute-start.45
  374.8 4.3 convert_add_fusion.1
  380.6 16.0 %collective-permute-done.56 = bf16[2,96,1728]{2,1,0:T(8,128)(2,1)S(1)} collective-permute-done((bf16[2,96,1728]{2,1,0:T(8,128)(2,1)S(1)}, bf16[2,96,1728]{2,1,0:T(8,128)(2,1)S(1)}, u32[]{:S(2)}, u32[]{:S(2)}) %collective-permute-start.56) | collective-permute-done | bytes 663584 | tf_op jit(solution)/shard_map/ppermute | solution.py:683
  398.6 1.8 fusion.2
  400.3 6.8 %collective-permute-start.36 = (bf16[2,512,768]{2,1,0:T(8,128)(2,1)S(1)}, bf16[2,512,768]{2,1,0:T(8,128)(2,1)S(1)}, u32[]{:S(2)}, u32[]{:S(2)}) collective-permute-start(bf16[2,512,768]{2,1,0:T(8,128)(2,1)S(1)} %fusion.2), channel_id=1, source_target_pairs={{0,4},{4,0},{1,5},{5,1},{2,6},{6,2},{3,7},{7,3},{8,12},{12,8},{9,1... | collective-permute-start | bytes 4718600 | tf_op jit(solution)/shard_map/ppermute | solution.py:679
  407.3 1.7 fusion.4
  409.1 3.2 fusion.1
  412.2 16.2 %collective-permute-done.57 = bf16[4,96,1728]{2,1,0:T(8,128)(2,1)S(1)} collective-permute-done((bf16[4,96,1728]{2,1,0:T(8,128)(2,1)S(1)}, bf16[4,96,1728]{2,1,0:T(8,128)(2,1)S(1)}, u32[]{:S(2)}, u32[]{:S(2)}) %collective-permute-start.57) | collective-permute-done | bytes 1327136 | tf_op jit(solution)/shard_map/ppermute | solution.py:683
  428.5 2.5 fusion.50
  431.2 2.6 collective-permute-start.59
  433.7 1.9 maximum_select_fusion
  435.6 1.9 maximum_select_fusion.1
  437.5 6.1 %collective-permute-done.58 = bf16[96,1728]{1,0:T(8,128)(2,1)S(1)} collective-permute-done((bf16[96,1728]{1,0:T(8,128)(2,1)S(1)}, bf16[96,1728]{1,0:T(8,128)(2,1)S(1)}, u32[]{:S(2)}, u32[]{:S(2)}) %collective-permute-start.58) | collective-permute-done | bytes 331808 | tf_op jit(solution)/shard_map/ppermute | solution.py:687
  443.6 18.4 %collective-permute-done.59 = bf16[96,1728]{1,0:T(8,128)(2,1)S(1)} collective-permute-done((bf16[96,1728]{1,0:T(8,128)(2,1)S(1)}, bf16[96,1728]{1,0:T(8,128)(2,1)S(1)}, u32[]{:S(2)}, u32[]{:S(2)}) %collective-permute-start.59) | collective-permute-done | bytes 331808 | tf_op jit(solution)/shard_map/ppermute | solution.py:687
  (351 shorter events, 83.3 us)
Async XLA Ops:
  3.8 34.4 %collective-permute-start.2 = (bf16[96,1728]{1,0:T(8,128)(2,1)}, bf16[96,1728]{1,0:T(8,128)(2,1)}, u32[]{:S(2)}, u32[]{:S(2)}) collective-permute-start(bf16[96,1728]{1,0:T(8,128)(2,1)} %constant_dynamic-update-slice_fusion), channel_id=1, source_target_pairs={{0,24},{8,16},{16,8},{24,0},{1,25},{9,17},{17,9},{25,1},{2,26},{10... | collective-permute-start | bytes 995336 | tf_op jit(solution)/shard_map/ppermute | solution.py:687
  7.9 29.2 %collective-permute-start.1 = (bf16[96,1728]{1,0:T(8,128)(2,1)}, bf16[96,1728]{1,0:T(8,128)(2,1)}, u32[]{:S(2)}, u32[]{:S(2)}) collective-permute-start(bf16[96,1728]{1,0:T(8,128)(2,1)} %constant_dynamic-update-slice_fusion), channel_id=1, source_target_pairs={{0,16},{8,24},{16,0},{24,8},{1,17},{9,25},{17,1},{25,9},{2,18},{10... | collective-permute-start | bytes 995336 | tf_op jit(solution)/shard_map/ppermute | solution.py:687
  7.9 21.9 %collective-permute-start = (bf16[96,1728]{1,0:T(8,128)(2,1)}, bf16[96,1728]{1,0:T(8,128)(2,1)}, u32[]{:S(2)}, u32[]{:S(2)}) collective-permute-start(bf16[96,1728]{1,0:T(8,128)(2,1)} %constant_dynamic-update-slice_fusion), channel_id=1, source_target_pairs={{0,8},{8,0},{16,24},{24,16},{1,9},{9,1},{17,25},{25,17},{2,10},{10... | collective-permute-start | bytes 995336 | tf_op jit(solution)/shard_map/ppermute | solution.py:687
  9.0 10.5 %collective-permute-start.19 = (s32[2,1024]{1,0:T(2,128)S(1)}, s32[2,1024]{1,0:T(2,128)S(1)}, u32[]{:S(2)}, u32[]{:S(2)}) collective-permute-start(s32[2,1024]{1,0:T(2,128)S(1)} %bitcast.247), channel_id=1, source_target_pairs={{0,4},{4,0},{1,5},{5,1},{2,6},{6,2},{3,7},{7,3},{8,12},{12,8},{9,1... | collective-permute-start | bytes 24584 | tf_op jit(solution)/shard_map/ppermute | solution.py:679
  12.1 32.6 %collective-permute-start.9 = (bf16[112,1728]{1,0:T(8,128)(2,1)S(1)}, bf16[112,1728]{1,0:T(8,128)(2,1)S(1)}, u32[]{:S(2)}, u32[]{:S(2)}) collective-permute-start(bf16[112,1728]{1,0:T(8,128)(2,1)S(1)} %fusion.29.refs_0_), channel_id=1, source_target_pairs={{0,2},{1,3},{2,0},{3,1},{4,6},{5,7},{6,4},{7,5},{8,10},{9,11},{10,... | collective-permute-start | bytes 1161224 | tf_op jit(solution)/shard_map/ppermute | solution.py:683
  19.6 22.2 %collective-permute-start.5 = (bf16[112,1728]{1,0:T(8,128)(2,1)S(1)}, bf16[112,1728]{1,0:T(8,128)(2,1)}, u32[]{:S(2)}, u32[]{:S(2)}) collective-permute-start(bf16[112,1728]{1,0:T(8,128)(2,1)S(1)} %fusion.29.refs_0_), channel_id=1, source_target_pairs={{0,1},{1,0},{2,3},{3,2},{4,5},{5,4},{6,7},{7,6},{8,9},{9,8},{10,11... | collective-permute-start | bytes 1161224 | tf_op jit(solution)/shard_map/ppermute | solution.py:683
  29.9 67.9 %collective-permute-start.27 = (bf16[1024,768]{1,0:T(8,128)(2,1)}, bf16[1024,768]{1,0:T(8,128)(2,1)S(1)}, u32[]{:S(2)}, u32[]{:S(2)}) collective-permute-start(bf16[1024,768]{1,0:T(8,128)(2,1)} %dynamic-slice_bitcast_fusion), channel_id=1, source_target_pairs={{0,4},{4,0},{1,5},{5,1},{2,6},{6,2},{3,7},{7,3},{8,12},{12,8},{9,1... | collective-permute-start | bytes 4718600 | tf_op jit(solution)/shard_map/ppermute | solution.py:679
  39.2 54.3 %collective-permute-start.10 = (bf16[288,1728]{1,0:T(8,128)(2,1)S(1)}, bf16[288,1728]{1,0:T(8,128)(2,1)S(1)}, u32[]{:S(2)}, u32[]{:S(2)}) collective-permute-start(bf16[288,1728]{1,0:T(8,128)(2,1)S(1)} %constant_dynamic-update-slice_fusion.2), channel_id=1, source_target_pairs={{0,2},{1,3},{2,0},{3,1},{4,6},{5,7},{6,4},{7,5},{8,10},{9,11},{10,... | collective-permute-start | bytes 2985992 | tf_op jit(solution)/shard_map/ppermute | solution.py:683
  40.5 53.5 %collective-permute-start.6 = (bf16[288,1728]{1,0:T(8,128)(2,1)S(1)}, bf16[288,1728]{1,0:T(8,128)(2,1)S(1)}, u32[]{:S(2)}, u32[]{:S(2)}) collective-permute-start(bf16[288,1728]{1,0:T(8,128)(2,1)S(1)} %constant_dynamic-update-slice_fusion.2), channel_id=1, source_target_pairs={{0,1},{1,0},{2,3},{3,2},{4,5},{5,4},{6,7},{7,6},{8,9},{9,8},{10,11... | collective-permute-start | bytes 2985992 | tf_op jit(solution)/shard_map/ppermute | solution.py:683
  41.8 51.7 %collective-permute-start.31 = (bf16[512,768]{1,0:T(8,128)(2,1)S(1)}, bf16[512,768]{1,0:T(8,128)(2,1)S(1)}, u32[]{:S(2)}, u32[]{:S(2)}) collective-permute-start(bf16[512,768]{1,0:T(8,128)(2,1)S(1)} %copy-done.48), channel_id=1, source_target_pairs={{0,4},{4,0},{1,5},{5,1},{2,6},{6,2},{3,7},{7,3},{8,12},{12,8},{9,1... | collective-permute-start | bytes 2359304 | tf_op jit(solution)/shard_map/ppermute | solution.py:679
  44.7 21.2 %collective-permute-start.13 = (bf16[48,1728]{1,0:T(8,128)(2,1)S(1)}, bf16[48,1728]{1,0:T(8,128)(2,1)S(1)}, u32[]{:S(2)}, u32[]{:S(2)}) collective-permute-start(bf16[48,1728]{1,0:T(8,128)(2,1)S(1)} %slice.284), channel_id=1, source_target_pairs={{0,2},{1,3},{2,0},{3,1},{4,6},{5,7},{6,4},{7,5},{8,10},{9,11},{10,... | collective-permute-start | bytes 497672 | tf_op jit(solution)/shard_map/ppermute | solution.py:683
  65.9 4.9 %collective-permute-start.14 = (bf16[64,1728]{1,0:T(8,128)(2,1)S(1)}, bf16[64,1728]{1,0:T(8,128)(2,1)S(1)}, u32[]{:S(2)}, u32[]{:S(2)}) collective-permute-start(bf16[64,1728]{1,0:T(8,128)(2,1)S(1)} %slice.285), channel_id=1, source_target_pairs={{0,1},{1,0},{2,3},{3,2},{4,5},{5,4},{6,7},{7,6},{8,9},{9,8},{10,11... | collective-permute-start | bytes 663560 | tf_op jit(solution)/shard_map/ppermute | solution.py:683
  70.8 5.6 %collective-permute-start.22 = (bf16[96,576]{1,0:T(8,128)(2,1)S(1)}, bf16[96,576]{1,0:T(8,128)(2,1)S(1)}, u32[]{:S(2)}, u32[]{:S(2)}) collective-permute-start(bf16[96,576]{1,0:T(8,128)(2,1)S(1)} %copy.31.refs_0_), channel_id=1, source_target_pairs={{0,24},{8,16},{16,8},{24,0},{1,25},{9,17},{17,9},{25,1},{2,26},{10... | collective-permute-start | bytes 331784 | tf_op jit(solution)/shard_map/ppermute | solution.py:687
  76.3 6.5 %collective-permute-start.21 = (bf16[96,576]{1,0:T(8,128)(2,1)S(1)}, bf16[96,576]{1,0:T(8,128)(2,1)S(1)}, u32[]{:S(2)}, u32[]{:S(2)}) collective-permute-start(bf16[96,576]{1,0:T(8,128)(2,1)S(1)} %copy.31.refs_0_), channel_id=1, source_target_pairs={{0,16},{8,24},{16,0},{24,8},{1,17},{9,25},{17,1},{25,9},{2,18},{10... | collective-permute-start | bytes 331784 | tf_op jit(solution)/shard_map/ppermute | solution.py:687
  82.8 4.8 %collective-permute-start.20 = (bf16[96,576]{1,0:T(8,128)(2,1)S(1)}, bf16[96,576]{1,0:T(8,128)(2,1)S(1)}, u32[]{:S(2)}, u32[]{:S(2)}) collective-permute-start(bf16[96,576]{1,0:T(8,128)(2,1)S(1)} %copy.31.refs_0_), channel_id=1, source_target_pairs={{0,8},{8,0},{16,24},{24,16},{1,9},{9,1},{17,25},{25,17},{2,10},{10... | collective-permute-start | bytes 331784 | tf_op jit(solution)/shard_map/ppermute | solution.py:687
  87.6 9.1 %collective-permute-start.23 = (bf16[96,576]{1,0:T(8,128)(2,1)S(1)}, bf16[96,576]{1,0:T(8,128)(2,1)S(1)}, u32[]{:S(2)}, u32[]{:S(2)}) collective-permute-start(bf16[96,576]{1,0:T(8,128)(2,1)S(1)} %copy.31.refs_0_), channel_id=1, source_target_pairs={{0,4},{4,0},{1,5},{5,1},{2,6},{6,2},{3,7},{7,3},{8,12},{12,8},{9,1... | collective-permute-start | bytes 331784 | tf_op jit(solution)/shard_map/ppermute | solution.py:679
  96.7 17.7 %collective-permute-start.3 = (bf16[112,1728]{1,0:T(8,128)(2,1)S(1)}, bf16[112,1728]{1,0:T(8,128)(2,1)S(1)}, u32[]{:S(2)}, u32[]{:S(2)}) collective-permute-start(bf16[112,1728]{1,0:T(8,128)(2,1)S(1)} %fusion.29.refs_0_), channel_id=1, source_target_pairs={{0,4},{4,0},{1,5},{5,1},{2,6},{6,2},{3,7},{7,3},{8,12},{12,8},{9,1... | collective-permute-start | bytes 1161224 | tf_op jit(solution)/shard_map/ppermute | solution.py:679
  97.1 41.7 %collective-permute-start.4 = (bf16[3,96,1728]{2,1,0:T(8,128)(2,1)S(1)}, bf16[3,96,1728]{2,1,0:T(8,128)(2,1)S(1)}, u32[]{:S(2)}, u32[]{:S(2)}) collective-permute-start(bf16[3,96,1728]{2,1,0:T(8,128)(2,1)S(1)} %bitcast.237), channel_id=1, source_target_pairs={{0,4},{4,0},{1,5},{5,1},{2,6},{6,2},{3,7},{7,3},{8,12},{12,8},{9,1... | collective-permute-start | bytes 2985992 | tf_op jit(solution)/shard_map/ppermute | solution.py:679
  97.3 40.1 %collective-permute-start.11 = (bf16[112,1728]{1,0:T(8,128)(2,1)S(1)}, bf16[112,1728]{1,0:T(8,128)(2,1)S(1)}, u32[]{:S(2)}, u32[]{:S(2)}) collective-permute-start(bf16[112,1728]{1,0:T(8,128)(2,1)S(1)} %collective-permute-done.9.refs_8_), channel_id=1, source_target_pairs={{0,4},{4,0},{1,5},{5,1},{2,6},{6,2},{3,7},{7,3},{8,12},{12,8},{9,1... | collective-permute-start | bytes 1161224 | tf_op jit(solution)/shard_map/ppermute | solution.py:679
  97.6 41.0 %collective-permute-start.7 = (bf16[112,1728]{1,0:T(8,128)(2,1)}, bf16[112,1728]{1,0:T(8,128)(2,1)S(1)}, u32[]{:S(2)}, u32[]{:S(2)}) collective-permute-start(bf16[112,1728]{1,0:T(8,128)(2,1)} %collective-permute-done.5.refs_4_), channel_id=1, source_target_pairs={{0,4},{4,0},{1,5},{5,1},{2,6},{6,2},{3,7},{7,3},{8,12},{12,8},{9,1... | collective-permute-start | bytes 1161224 | tf_op jit(solution)/shard_map/ppermute | solution.py:679
  97.8 22.2 %collective-permute-start.16 = (bf16[144,1728]{1,0:T(8,128)(2,1)S(1)}, bf16[144,1728]{1,0:T(8,128)(2,1)S(1)}, u32[]{:S(2)}, u32[]{:S(2)}) collective-permute-start(bf16[144,1728]{1,0:T(8,128)(2,1)S(1)} %slice.287), channel_id=1, source_target_pairs={{0,1},{1,0},{2,3},{3,2},{4,5},{5,4},{6,7},{7,6},{8,9},{9,8},{10,11... | collective-permute-start | bytes 1493000 | tf_op jit(solution)/shard_map/ppermute | solution.py:683
  114.4 24.3 %collective-permute-start.17 = (bf16[112,1728]{1,0:T(8,128)(2,1)S(1)}, bf16[112,1728]{1,0:T(8,128)(2,1)S(1)}, u32[]{:S(2)}, u32[]{:S(2)}) collective-permute-start(bf16[112,1728]{1,0:T(8,128)(2,1)S(1)} %constant_dynamic-update-slice_fusion.5.refs_12_), channel_id=1, source_target_pairs={{0,4},{4,0},{1,5},{5,1},{2,6},{6,2},{3,7},{7,3},{8,12},{12,8},{9,1... | collective-permute-start | bytes 1161224 | tf_op jit(solution)/shard_map/ppermute | solution.py:679
  120.0 16.1 %collective-permute-start.15 = (bf16[144,1728]{1,0:T(8,128)(2,1)S(1)}, bf16[144,1728]{1,0:T(8,128)(2,1)S(1)}, u32[]{:S(2)}, u32[]{:S(2)}) collective-permute-start(bf16[144,1728]{1,0:T(8,128)(2,1)S(1)} %slice.286), channel_id=1, source_target_pairs={{0,2},{1,3},{2,0},{3,1},{4,6},{5,7},{6,4},{7,5},{8,10},{9,11},{10,... | collective-permute-start | bytes 1493000 | tf_op jit(solution)/shard_map/ppermute | solution.py:683
  136.1 8.1 %collective-permute-start.30 = (bf16[512,192]{1,0:T(8,128)(2,1)S(1)}, bf16[512,192]{1,0:T(8,128)(2,1)S(1)}, u32[]{:S(2)}, u32[]{:S(2)}) collective-permute-start(bf16[512,192]{1,0:T(8,128)(2,1)S(1)} %get-tuple-element.52), channel_id=1, source_target_pairs={{0,3},{1,2},{2,1},{3,0},{4,7},{5,6},{6,5},{7,4},{8,11},{9,10},{10,... | collective-permute-start | bytes 589832 | tf_op jit(solution)/shard_map/ppermute | solution.py:683
  137.4 15.1 %collective-permute-start.12 = (bf16[3,96,1728]{2,1,0:T(8,128)(2,1)S(1)}, bf16[3,96,1728]{2,1,0:T(8,128)(2,1)S(1)}, u32[]{:S(2)}, u32[]{:S(2)}) collective-permute-start(bf16[3,96,1728]{2,1,0:T(8,128)(2,1)S(1)} %bitcast.231), channel_id=1, source_target_pairs={{0,4},{4,0},{1,5},{5,1},{2,6},{6,2},{3,7},{7,3},{8,12},{12,8},{9,1... | collective-permute-start | bytes 2985992 | tf_op jit(solution)/shard_map/ppermute | solution.py:679
  138.7 14.0 %collective-permute-start.8 = (bf16[3,96,1728]{2,1,0:T(8,128)(2,1)S(1)}, bf16[3,96,1728]{2,1,0:T(8,128)(2,1)S(1)}, u32[]{:S(2)}, u32[]{:S(2)}) collective-permute-start(bf16[3,96,1728]{2,1,0:T(8,128)(2,1)S(1)} %bitcast.234), channel_id=1, source_target_pairs={{0,4},{4,0},{1,5},{5,1},{2,6},{6,2},{3,7},{7,3},{8,12},{12,8},{9,1... | collective-permute-start | bytes 2985992 | tf_op jit(solution)/shard_map/ppermute | solution.py:679
  138.8 13.8 %collective-permute-start.29 = (bf16[512,192]{1,0:T(8,128)(2,1)S(1)}, bf16[512,192]{1,0:T(8,128)(2,1)S(1)}, u32[]{:S(2)}, u32[]{:S(2)}) collective-permute-start(bf16[512,192]{1,0:T(8,128)(2,1)S(1)} %get-tuple-element.51), channel_id=1, source_target_pairs={{0,2},{1,3},{2,0},{3,1},{4,6},{5,7},{6,4},{7,5},{8,10},{9,11},{10,... | collective-permute-start | bytes 589832 | tf_op jit(solution)/shard_map/ppermute | solution.py:683
  138.8 13.8 %collective-permute-start.28 = (bf16[512,192]{1,0:T(8,128)(2,1)S(1)}, bf16[512,192]{1,0:T(8,128)(2,1)S(1)}, u32[]{:S(2)}, u32[]{:S(2)}) collective-permute-start(bf16[512,192]{1,0:T(8,128)(2,1)S(1)} %get-tuple-element.50), channel_id=1, source_target_pairs={{0,1},{1,0},{2,3},{3,2},{4,5},{5,4},{6,7},{7,6},{8,9},{9,8},{10,11... | collective-permute-start | bytes 589832 | tf_op jit(solution)/shard_map/ppermute | solution.py:683
  144.2 8.4 %collective-permute-start.18 = (bf16[3,96,1728]{2,1,0:T(8,128)(2,1)S(1)}, bf16[3,96,1728]{2,1,0:T(8,128)(2,1)S(1)}, u32[]{:S(2)}, u32[]{:S(2)}) collective-permute-start(bf16[3,96,1728]{2,1,0:T(8,128)(2,1)S(1)} %bitcast.221), channel_id=1, source_target_pairs={{0,4},{4,0},{1,5},{5,1},{2,6},{6,2},{3,7},{7,3},{8,12},{12,8},{9,1... | collective-permute-start | bytes 2985992 | tf_op jit(solution)/shard_map/ppermute | solution.py:679
  200.8 4.9 %collective-permute-start.65 = (f32[60,128]{1,0:T(8,128)S(1)}, f32[60,128]{1,0:T(8,128)S(1)}, u32[]{:S(2)}, u32[]{:S(2)}) collective-permute-start(f32[60,128]{1,0:T(8,128)S(1)} %fusion.49), channel_id=1, source_target_pairs={{0,2},{1,3},{2,0},{3,1},{4,6},{5,7},{6,4},{7,5},{8,10},{9,11},{10,... | collective-permute-start | bytes 92168 | tf_op jit(solution)/shard_map/ppermute | solution.py:683
  203.0 31.6 %collective-permute-start.37 = (bf16[512,192]{1,0:T(8,128)(2,1)}, bf16[512,192]{1,0:T(8,128)(2,1)S(1)}, u32[]{:S(2)}, u32[]{:S(2)}) collective-permute-start(bf16[512,192]{1,0:T(8,128)(2,1)} %copy-done.25), channel_id=1, source_target_pairs={{0,1},{1,0},{2,3},{3,2},{4,5},{5,4},{6,7},{7,6},{8,9},{9,8},{10,11... | collective-permute-start | bytes 589832 | tf_op jit(solution)/shard_map/ppermute | solution.py:683
  203.3 31.3 %collective-permute-start.38 = (bf16[512,192]{1,0:T(8,128)(2,1)}, bf16[512,192]{1,0:T(8,128)(2,1)S(1)}, u32[]{:S(2)}, u32[]{:S(2)}) collective-permute-start(bf16[512,192]{1,0:T(8,128)(2,1)} %copy-done.24), channel_id=1, source_target_pairs={{0,2},{1,3},{2,0},{3,1},{4,6},{5,7},{6,4},{7,5},{8,10},{9,11},{10,... | collective-permute-start | bytes 589832 | tf_op jit(solution)/shard_map/ppermute | solution.py:683
  203.3 31.3 %collective-permute-start.39 = (bf16[512,192]{1,0:T(8,128)(2,1)}, bf16[512,192]{1,0:T(8,128)(2,1)S(1)}, u32[]{:S(2)}, u32[]{:S(2)}) collective-permute-start(bf16[512,192]{1,0:T(8,128)(2,1)} %copy-done.23), channel_id=1, source_target_pairs={{0,3},{1,2},{2,1},{3,0},{4,7},{5,6},{6,5},{7,4},{8,11},{9,10},{10,... | collective-permute-start | bytes 589832 | tf_op jit(solution)/shard_map/ppermute | solution.py:683
  205.7 28.8 %collective-permute-start.66 = (f32[60,128]{1,0:T(8,128)S(1)}, f32[60,128]{1,0:T(8,128)S(1)}, u32[]{:S(2)}, u32[]{:S(2)}) collective-permute-start(f32[60,128]{1,0:T(8,128)S(1)} %fusion.61), channel_id=1, source_target_pairs={{0,4},{4,0},{1,5},{5,1},{2,6},{6,2},{3,7},{7,3},{8,12},{12,8},{9,1... | collective-permute-start | bytes 92168 | tf_op jit(solution)/shard_map/ppermute | solution.py:679
  234.4 140.4 %collective-permute-start.53 = (bf16[4,4,96,1728]{3,2,1,0:T(8,128)(2,1)}, bf16[4,4,96,1728]{3,2,1,0:T(8,128)(2,1)}, u32[]{:S(2)}, u32[]{:S(2)}) collective-permute-start(bf16[4,4,96,1728]{3,2,1,0:T(8,128)(2,1)} %get-tuple-element.78), channel_id=1, source_target_pairs={{0,4},{4,0},{1,5},{5,1},{2,6},{6,2},{3,7},{7,3},{8,12},{12,8},{9,1... | collective-permute-start | bytes 15925256 | tf_op jit(solution)/shard_map/ppermute | solution.py:679
  234.5 81.7 %collective-permute-start.67 = (f32[60,128]{1,0:T(8,128)S(1)}, f32[60,128]{1,0:T(8,128)S(1)}, u32[]{:S(2)}, u32[]{:S(2)}) collective-permute-start(f32[60,128]{1,0:T(8,128)S(1)} %add.260), channel_id=1, source_target_pairs={{0,8},{8,0},{16,24},{24,16},{1,9},{9,1},{17,25},{25,17},{2,10},{10... | collective-permute-start | bytes 92168 | tf_op jit(solution)/shard_map/ppermute | solution.py:687
  267.4 48.8 %collective-permute-start.61 = (f32[3,192]{1,0:T(4,128)S(1)}, f32[3,192]{1,0:T(4,128)S(1)}, u32[]{:S(2)}, u32[]{:S(2)}) collective-permute-start(f32[3,192]{1,0:T(4,128)S(1)} %bitcast.246), channel_id=1, source_target_pairs={{0,4},{4,0},{1,5},{5,1},{2,6},{6,2},{3,7},{7,3},{8,12},{12,8},{9,1... | collective-permute-start | bytes 6920 | tf_op jit(solution)/shard_map/ppermute | solution.py:679
  292.0 21.8 %collective-permute-start.49 = (bf16[4,96,576]{2,1,0:T(8,128)(2,1)S(1)}, bf16[4,96,576]{2,1,0:T(8,128)(2,1)S(1)}, u32[]{:S(2)}, u32[]{:S(2)}) collective-permute-start(bf16[4,96,576]{2,1,0:T(8,128)(2,1)S(1)} %get-tuple-element.72), channel_id=1, source_target_pairs={{0,4},{4,0},{1,5},{5,1},{2,6},{6,2},{3,7},{7,3},{8,12},{12,8},{9,1... | collective-permute-start | bytes 1327112 | tf_op jit(solution)/shard_map/ppermute | solution.py:679
  292.9 10.3 %collective-permute-start.42 = (bf16[256,768]{1,0:T(8,128)(2,1)S(1)}, bf16[256,768]{1,0:T(8,128)(2,1)S(1)}, u32[]{:S(2)}, u32[]{:S(2)}) collective-permute-start(bf16[256,768]{1,0:T(8,128)(2,1)S(1)} %get-tuple-element.118), channel_id=1, source_target_pairs={{0,1},{1,0},{2,3},{3,2},{4,5},{5,4},{6,7},{7,6},{8,9},{9,8},{10,11... | collective-permute-start | bytes 1179656 | tf_op jit(solution)/shard_map/ppermute | solution.py:683
  303.2 9.3 %collective-permute-start.40 = (bf16[256,768]{1,0:T(8,128)(2,1)S(1)}, bf16[256,768]{1,0:T(8,128)(2,1)S(1)}, u32[]{:S(2)}, u32[]{:S(2)}) collective-permute-start(bf16[256,768]{1,0:T(8,128)(2,1)S(1)} %get-tuple-element.117), channel_id=1, source_target_pairs={{0,2},{1,3},{2,0},{3,1},{4,6},{5,7},{6,4},{7,5},{8,10},{9,11},{10,... | collective-permute-start | bytes 1179656 | tf_op jit(solution)/shard_map/ppermute | solution.py:683
  312.4 19.3 %collective-permute-start.43 = (bf16[512,768]{1,0:T(8,128)(2,1)}, bf16[512,768]{1,0:T(8,128)(2,1)}, u32[]{:S(2)}, u32[]{:S(2)}) collective-permute-start(bf16[512,768]{1,0:T(8,128)(2,1)} %pad_maximum_fusion.5), channel_id=1, source_target_pairs={{0,2},{1,3},{2,0},{3,1},{4,6},{5,7},{6,4},{7,5},{8,10},{9,11},{10,... | collective-permute-start | bytes 2359304 | tf_op jit(solution)/shard_map/ppermute | solution.py:683
  313.8 18.0 %collective-permute-start.41 = (bf16[512,768]{1,0:T(8,128)(2,1)}, bf16[512,768]{1,0:T(8,128)(2,1)}, u32[]{:S(2)}, u32[]{:S(2)}) collective-permute-start(bf16[512,768]{1,0:T(8,128)(2,1)} %pad_maximum_fusion.4), channel_id=1, source_target_pairs={{0,1},{1,0},{2,3},{3,2},{4,5},{5,4},{6,7},{7,6},{8,9},{9,8},{10,11... | collective-permute-start | bytes 2359304 | tf_op jit(solution)/shard_map/ppermute | solution.py:683
  316.2 12.3 %collective-permute-start.50 = (bf16[96,576]{1,0:T(8,128)(2,1)S(1)}, bf16[96,576]{1,0:T(8,128)(2,1)S(1)}, u32[]{:S(2)}, u32[]{:S(2)}) collective-permute-start(bf16[96,576]{1,0:T(8,128)(2,1)S(1)} %get-tuple-element.119), channel_id=1, source_target_pairs={{0,8},{8,0},{16,24},{24,16},{1,9},{9,1},{17,25},{25,17},{2,10},{10... | collective-permute-start | bytes 331784 | tf_op jit(solution)/shard_map/ppermute | solution.py:687
  316.2 4.2 collective-permute-start.62
  320.4 3.9 collective-permute-start.68
  327.6 16.9 %collective-permute-start.34 = (bf16[512,768]{1,0:T(8,128)(2,1)S(1)}, bf16[512,768]{1,0:T(8,128)(2,1)S(1)}, u32[]{:S(2)}, u32[]{:S(2)}) collective-permute-start(bf16[512,768]{1,0:T(8,128)(2,1)S(1)} %get-tuple-element.53), channel_id=1, source_target_pairs={{0,2},{1,3},{2,0},{3,1},{4,6},{5,7},{6,4},{7,5},{8,10},{9,11},{10,... | collective-permute-start | bytes 2359304 | tf_op jit(solution)/shard_map/ppermute | solution.py:683
  328.6 17.5 %collective-permute-start.32 = (bf16[512,768]{1,0:T(8,128)(2,1)S(1)}, bf16[512,768]{1,0:T(8,128)(2,1)}, u32[]{:S(2)}, u32[]{:S(2)}) collective-permute-start(bf16[512,768]{1,0:T(8,128)(2,1)S(1)} %get-tuple-element.53), channel_id=1, source_target_pairs={{0,1},{1,0},{2,3},{3,2},{4,5},{5,4},{6,7},{7,6},{8,9},{9,8},{10,11... | collective-permute-start | bytes 2359304 | tf_op jit(solution)/shard_map/ppermute | solution.py:683
  331.7 17.1 %collective-permute-start.52 = (bf16[96,576]{1,0:T(8,128)(2,1)S(1)}, bf16[96,576]{1,0:T(8,128)(2,1)S(1)}, u32[]{:S(2)}, u32[]{:S(2)}) collective-permute-start(bf16[96,576]{1,0:T(8,128)(2,1)S(1)} %copy-done.52), channel_id=1, source_target_pairs={{0,24},{8,16},{16,8},{24,0},{1,25},{9,17},{17,9},{25,1},{2,26},{10... | collective-permute-start | bytes 331784 | tf_op jit(solution)/shard_map/ppermute | solution.py:687
  331.8 18.2 %collective-permute-start.51 = (bf16[96,576]{1,0:T(8,128)(2,1)S(1)}, bf16[96,576]{1,0:T(8,128)(2,1)S(1)}, u32[]{:S(2)}, u32[]{:S(2)}) collective-permute-start(bf16[96,576]{1,0:T(8,128)(2,1)S(1)} %get-tuple-element.121), channel_id=1, source_target_pairs={{0,16},{8,24},{16,0},{24,8},{1,17},{9,25},{17,1},{25,9},{2,18},{10... | collective-permute-start | bytes 331784 | tf_op jit(solution)/shard_map/ppermute | solution.py:687
  344.5 27.0 %collective-permute-start.46 = (bf16[512,768]{1,0:T(8,128)(2,1)S(1)}, bf16[512,768]{1,0:T(8,128)(2,1)S(1)}, u32[]{:S(2)}, u32[]{:S(2)}) collective-permute-start(bf16[512,768]{1,0:T(8,128)(2,1)S(1)} %add_convert_fusion.1), channel_id=1, source_target_pairs={{0,2},{1,3},{2,0},{3,1},{4,6},{5,7},{6,4},{7,5},{8,10},{9,11},{10,... | collective-permute-start | bytes 2359304 | tf_op jit(solution)/shard_map/ppermute | solution.py:683
  346.0 25.8 %collective-permute-start.44 = (bf16[512,768]{1,0:T(8,128)(2,1)S(1)}, bf16[512,768]{1,0:T(8,128)(2,1)}, u32[]{:S(2)}, u32[]{:S(2)}) collective-permute-start(bf16[512,768]{1,0:T(8,128)(2,1)S(1)} %add_convert_fusion.1), channel_id=1, source_target_pairs={{0,1},{1,0},{2,3},{3,2},{4,5},{5,4},{6,7},{7,6},{8,9},{9,8},{10,11... | collective-permute-start | bytes 2359304 | tf_op jit(solution)/shard_map/ppermute | solution.py:683
  348.9 21.6 %collective-permute-start.35 = (bf16[256,768]{1,0:T(8,128)(2,1)}, bf16[256,768]{1,0:T(8,128)(2,1)}, u32[]{:S(2)}, u32[]{:S(2)}) collective-permute-start(bf16[256,768]{1,0:T(8,128)(2,1)} %slice.294), channel_id=1, source_target_pairs={{0,1},{1,0},{2,3},{3,2},{4,5},{5,4},{6,7},{7,6},{8,9},{9,8},{10,11... | collective-permute-start | bytes 1179656 | tf_op jit(solution)/shard_map/ppermute | solution.py:683
  350.0 19.0 %collective-permute-start.33 = (bf16[256,768]{1,0:T(8,128)(2,1)}, bf16[256,768]{1,0:T(8,128)(2,1)}, u32[]{:S(2)}, u32[]{:S(2)}) collective-permute-start(bf16[256,768]{1,0:T(8,128)(2,1)} %slice.293), channel_id=1, source_target_pairs={{0,2},{1,3},{2,0},{3,1},{4,6},{5,7},{6,4},{7,5},{8,10},{9,11},{10,... | collective-permute-start | bytes 1179656 | tf_op jit(solution)/shard_map/ppermute | solution.py:683
  371.5 35.7 %collective-permute-start.47 = (bf16[256,768]{1,0:T(8,128)(2,1)S(1)}, bf16[256,768]{1,0:T(8,128)(2,1)S(1)}, u32[]{:S(2)}, u32[]{:S(2)}) collective-permute-start(bf16[256,768]{1,0:T(8,128)(2,1)S(1)} %slice.302), channel_id=1, source_target_pairs={{0,1},{1,0},{2,3},{3,2},{4,5},{5,4},{6,7},{7,6},{8,9},{9,8},{10,11... | collective-permute-start | bytes 1179656 | tf_op jit(solution)/shard_map/ppermute | solution.py:683
  372.9 34.3 %collective-permute-start.45 = (bf16[256,768]{1,0:T(8,128)(2,1)S(1)}, bf16[256,768]{1,0:T(8,128)(2,1)S(1)}, u32[]{:S(2)}, u32[]{:S(2)}) collective-permute-start(bf16[256,768]{1,0:T(8,128)(2,1)S(1)} %slice.301), channel_id=1, source_target_pairs={{0,2},{1,3},{2,0},{3,1},{4,6},{5,7},{6,4},{7,5},{8,10},{9,11},{10,... | collective-permute-start | bytes 1179656 | tf_op jit(solution)/shard_map/ppermute | solution.py:683
  379.1 17.5 %collective-permute-start.56 = (bf16[2,96,1728]{2,1,0:T(8,128)(2,1)S(1)}, bf16[2,96,1728]{2,1,0:T(8,128)(2,1)S(1)}, u32[]{:S(2)}, u32[]{:S(2)}) collective-permute-start(bf16[2,96,1728]{2,1,0:T(8,128)(2,1)S(1)} %get-tuple-element.116), channel_id=1, source_target_pairs={{0,1},{1,0},{2,3},{3,2},{4,5},{5,4},{6,7},{7,6},{8,9},{9,8},{10,11... | collective-permute-start | bytes 1990664 | tf_op jit(solution)/shard_map/ppermute | solution.py:683
  380.5 16.6 %collective-permute-start.54 = (bf16[2,96,1728]{2,1,0:T(8,128)(2,1)S(1)}, bf16[2,96,1728]{2,1,0:T(8,128)(2,1)S(1)}, u32[]{:S(2)}, u32[]{:S(2)}) collective-permute-start(bf16[2,96,1728]{2,1,0:T(8,128)(2,1)S(1)} %get-tuple-element.115), channel_id=1, source_target_pairs={{0,2},{1,3},{2,0},{3,1},{4,6},{5,7},{6,4},{7,5},{8,10},{9,11},{10,... | collective-permute-start | bytes 1990664 | tf_op jit(solution)/shard_map/ppermute | solution.py:683
  396.9 31.5 %collective-permute-start.57 = (bf16[4,96,1728]{2,1,0:T(8,128)(2,1)S(1)}, bf16[4,96,1728]{2,1,0:T(8,128)(2,1)S(1)}, u32[]{:S(2)}, u32[]{:S(2)}) collective-permute-start(bf16[4,96,1728]{2,1,0:T(8,128)(2,1)S(1)} %pad_maximum_fusion.1), channel_id=1, source_target_pairs={{0,2},{1,3},{2,0},{3,1},{4,6},{5,7},{6,4},{7,5},{8,10},{9,11},{10,... | collective-permute-start | bytes 3981320 | tf_op jit(solution)/shard_map/ppermute | solution.py:683
  397.3 31.1 %collective-permute-start.55 = (bf16[4,96,1728]{2,1,0:T(8,128)(2,1)S(1)}, bf16[4,96,1728]{2,1,0:T(8,128)(2,1)S(1)}, u32[]{:S(2)}, u32[]{:S(2)}) collective-permute-start(bf16[4,96,1728]{2,1,0:T(8,128)(2,1)S(1)} %pad_maximum_fusion), channel_id=1, source_target_pairs={{0,1},{1,0},{2,3},{3,2},{4,5},{5,4},{6,7},{7,6},{8,9},{9,8},{10,11... | collective-permute-start | bytes 3981320 | tf_op jit(solution)/shard_map/ppermute | solution.py:683
  400.3 33.4 %collective-permute-start.36 = (bf16[2,512,768]{2,1,0:T(8,128)(2,1)S(1)}, bf16[2,512,768]{2,1,0:T(8,128)(2,1)S(1)}, u32[]{:S(2)}, u32[]{:S(2)}) collective-permute-start(bf16[2,512,768]{2,1,0:T(8,128)(2,1)S(1)} %fusion.2), channel_id=1, source_target_pairs={{0,4},{4,0},{1,5},{5,1},{2,6},{6,2},{3,7},{7,3},{8,12},{12,8},{9,1... | collective-permute-start | bytes 4718600 | tf_op jit(solution)/shard_map/ppermute | solution.py:679
  409.0 26.6 %collective-permute-start.48 = (bf16[2,512,768]{2,1,0:T(8,128)(2,1)S(1)}, bf16[2,512,768]{2,1,0:T(8,128)(2,1)S(1)}, u32[]{:S(2)}, u32[]{:S(2)}) collective-permute-start(bf16[2,512,768]{2,1,0:T(8,128)(2,1)S(1)} %fusion.4), channel_id=1, source_target_pairs={{0,4},{4,0},{1,5},{5,1},{2,6},{6,2},{3,7},{7,3},{8,12},{12,8},{9,1... | collective-permute-start | bytes 4718600 | tf_op jit(solution)/shard_map/ppermute | solution.py:679
  431.0 12.6 %collective-permute-start.58 = (bf16[96,1728]{1,0:T(8,128)(2,1)S(1)}, bf16[96,1728]{1,0:T(8,128)(2,1)S(1)}, u32[]{:S(2)}, u32[]{:S(2)}) collective-permute-start(bf16[96,1728]{1,0:T(8,128)(2,1)S(1)} %get-tuple-element.112), channel_id=1, source_target_pairs={{0,8},{8,0},{16,24},{24,16},{1,9},{9,1},{17,25},{25,17},{2,10},{10... | collective-permute-start | bytes 995336 | tf_op jit(solution)/shard_map/ppermute | solution.py:687
  431.1 12.6 %collective-permute-start.60 = (bf16[96,1728]{1,0:T(8,128)(2,1)S(1)}, bf16[96,1728]{1,0:T(8,128)(2,1)S(1)}, u32[]{:S(2)}, u32[]{:S(2)}) collective-permute-start(bf16[96,1728]{1,0:T(8,128)(2,1)S(1)} %get-tuple-element.113), channel_id=1, source_target_pairs={{0,24},{8,16},{16,8},{24,0},{1,25},{9,17},{17,9},{25,1},{2,26},{10... | collective-permute-start | bytes 995336 | tf_op jit(solution)/shard_map/ppermute | solution.py:687
  431.2 30.9 %collective-permute-start.59 = (bf16[96,1728]{1,0:T(8,128)(2,1)S(1)}, bf16[96,1728]{1,0:T(8,128)(2,1)S(1)}, u32[]{:S(2)}, u32[]{:S(2)}) collective-permute-start(bf16[96,1728]{1,0:T(8,128)(2,1)S(1)} %get-tuple-element.114), channel_id=1, source_target_pairs={{0,16},{8,24},{16,0},{24,8},{1,17},{9,25},{17,1},{25,9},{2,18},{10... | collective-permute-start | bytes 995336 | tf_op jit(solution)/shard_map/ppermute | solution.py:687
  (75 other events, 954.4 us)

commit v3 on v2

--- a/solution.py
+++ b/solution.py
@@ -16,6 +16,7 @@
 F32 = jnp.float32
 BF = jnp.bfloat16
 NEG = -1e30
+COST = pl.CostEstimate(flops=0, bytes_accessed=0, transcendentals=0)
 
 
 def swap_pairs(x):
@@ -53,12 +54,14 @@
     return pltpu.CompilerParams(dimension_semantics=("arbitrary",), vmem_limit_bytes=mib * 1024 * 1024)
 
 
-def qkv_kernel(count, part, place, *refs):
-    pieces = refs[:count]
+def qkv_kernel(count, per, part, place, *refs):
+    pieces = []
+    for x in refs[:count]:
+        pieces += [x] if len(x.shape) == 2 else [x.at[n] for n in range(x.shape[0])]
     bias, own, other, cos, sin, q_o, k_o, v_o, kt_o, w_o = refs[count:]
     piece_rows = pieces[0].shape[0]
     pad = jnp.zeros((piece_rows, WIDE - part), BF)
-    for n in range(count):
+    for n in range(per):
         sl = pl.ds(pl.multiple_of(place[n], 16), piece_rows)
         for m in range(3):
             w_o[sl, m * WIDE : (m + 1) * WIDE] = jnp.concatenate([pieces[n][:, m * part : (m + 1) * part], pad], axis=1)
@@ -76,7 +79,7 @@
 
     def step(r, _):
         rows = pl.ds(pl.multiple_of(r * BLOCK, BLOCK), BLOCK)
-        core = place[count]
+        core = place[per]
         run(own[0, rows, :], pl.ds(pl.multiple_of(core * half_len + r * BLOCK, BLOCK), BLOCK))
         run(other[rows, :], pl.ds(pl.multiple_of((1 - core) * half_len + r * BLOCK, BLOCK), BLOCK))
         return 0
@@ -84,24 +87,23 @@
     lax.fori_loop(0, half_len // BLOCK, step, 0)
 
 
-def project_qkv(place, pieces, bias, tokens, other, cos, sin, part):
+def project_qkv(place, pieces, per, bias, tokens, other, cos, sin, part):
     half_len, width = other.shape
     length, count = 2 * half_len, len(pieces)
-    cost = pl.CostEstimate(flops=2 * length * width * 3 * WIDE, bytes_accessed=12 * 2**20, transcendentals=0)
     return pl.pallas_call(
-        partial(qkv_kernel, count, part),
+        partial(qkv_kernel, count, per, part),
         grid_spec=pltpu.PrefetchScalarGridSpec(
             num_scalar_prefetch=1,
             grid=(1,),
             in_specs=[whole_block(p.shape) for p in pieces]
-            + [whole_block(bias.shape), pl.BlockSpec((1, half_len, width), lambda i, s: (s[count], 0, 0))]
+            + [whole_block(bias.shape), pl.BlockSpec((1, half_len, width), lambda i, s: (s[per], 0, 0))]
             + [whole_block(x.shape) for x in (other, cos, sin)],
             out_specs=[whole_block((length, WIDE))] * 3 + [whole_block((WIDE, length)), whole_block((width, 3 * WIDE))],
         ),
         out_shape=[jax.ShapeDtypeStruct((length, WIDE), BF)] * 3
         + [jax.ShapeDtypeStruct((WIDE, length), BF), jax.ShapeDtypeStruct((width, 3 * WIDE), BF)],
         compiler_params=params(32),
-        cost_estimate=cost,
+        cost_estimate=COST,
         name="project_qkv",
     )(place, *pieces, bias, tokens, other, cos, sin)
 
@@ -163,7 +165,6 @@
     length = q.shape[0]
     grid = share // BLOCK
     rows = lambda i, s: (s[0] + i, 0)
-    flops = 4 * share * 1024 * heads * WIDE
     return pl.pallas_call(
         partial(forward_kernel, heads),
         grid_spec=pltpu.PrefetchScalarGridSpec(
@@ -186,8 +187,8 @@
             ],
         ),
         out_shape=[jax.ShapeDtypeStruct((share, heads * HEAD), BF), jax.ShapeDtypeStruct((8, share), F32)],
-        compiler_params=params(24),
-        cost_estimate=pl.CostEstimate(flops=flops * 6, bytes_accessed=4 * 2**20, transcendentals=share * 1024 * heads),
+        compiler_params=params(16),
+        cost_estimate=COST,
         name="attention_forward",
     )(place, q, k, v, segc, segr)
 
@@ -270,7 +271,6 @@
 def attention_backward(place, q, k, kt, v, do, lse, segc, segr, cos, sin, heads):
     length = k.shape[0]
     steps, per = length // BLOCK, do.shape[1] // BLOCK
-    flops = 10 * length * 1024 * heads * WIDE
     return pl.pallas_call(
         partial(backward_kernel, heads),
         grid_spec=pltpu.PrefetchScalarGridSpec(
@@ -296,24 +296,16 @@
             + [pltpu.VMEM((8, heads * BLOCK), F32)],
         ),
         out_shape=[jax.ShapeDtypeStruct((length, 3 * WIDE), BF), jax.ShapeDtypeStruct((8, 3 * WIDE), F32)],
-        compiler_params=params(44),
-        cost_estimate=pl.CostEstimate(flops=flops * 4, bytes_accessed=16 * 2**20, transcendentals=length * 1024 * heads),
+        compiler_params=params(32),
+        cost_estimate=COST,
         name="attention_backward",
     )(place, q, k, kt, v, do, lse, segc, segr, cos, sin)
 
 
-def fetches(place, pieces, w_feed, w_out, sems, per):
-    out = []
-    for n, (group, ref, lead) in enumerate(pieces):
-        m = n % per
-        src = ref if lead is None else ref.at[lead]
-        rows = w_feed.shape[1] // per
-        feed = w_feed.shape[2]
-        sl = pl.ds(pl.multiple_of(place[m], 16), rows)
-        a = pltpu.make_async_copy(src.at[0:rows, feed:], w_out.at[group, sl, :], sems.at[0, n])
-        b = pltpu.make_async_copy(src.at[0:rows, 0:feed], w_feed.at[group, sl, :], sems.at[1, n])
-        out.append((group, a, b))
-    return out
+def out_copies(place, gathered, w_out, sems):
+    here = place[place.shape[0] - 1]
+    feed = gathered.shape[2] - w_out.shape[2]
+    return [pltpu.make_async_copy(gathered.at[here ^ k, :, feed:], w_out.at[k], sems.at[k]) for k in range(4)]
 
 
 def row_mean(x):
@@ -332,27 +324,24 @@
 ROWS = 256
 
 
-def feed_kernel(layout, per, place, *refs):
-    arrays = refs[: layout[0]]
-    (c0, c1, c2, c3, tokb, gtop, vec, bias, out_o, gs_o, gsb_o, fs_o, nb_o, act_o, gp_o, root_o, sum_o, w_feed, w_out, acc, normed, sems) = refs[layout[0] :]
-    pieces = [(g, arrays[a], lead) for g, a, lead in layout[1]]
-    copies = fetches(place, pieces, w_feed, w_out, sems, per)
+def feed_kernel(place, gathered, w, c0, c1, c2, c3, tokb, gtop, vec, bias, *refs):
+    (out_o, gs_o, gsb_o, fs_o, nbt_o, gst_o, act_o, gp_o, root_o, sum_o, nb_o, w_out, acc, normed, sems) = refs
+    copies = out_copies(place, gathered, w_out, sems)
     k = pl.program_id(0)
     share = tokb.shape[0]
+    part = c0.shape[1]
     chunks = [pl.ds(r * ROWS, ROWS) for r in range(share // ROWS)]
 
     @pl.when(k == 0)
     def _():
-        for _, a, _ in copies:
-            a.start()
-        for _, _, b in copies:
-            b.start()
-        for _, a, _ in copies:
-            a.wait()
+        for copy in copies:
+            copy.start()
+        for copy in copies:
+            copy.wait()
         for sl in chunks:
             x = tokb[sl, :].astype(F32) + vec[4:5, :]
             for n, ctx in enumerate((c0, c1, c2, c3)):
-                x = x + nt(ctx[sl, :], w_out[n])
+                x = x + nt(ctx[sl, :], w_out[n, :, 0:part])
             x = x - row_mean(x)
             root = lax.rsqrt(row_mean(x * x) + EPSILON)
             x = x * root
@@ -361,26 +350,19 @@
             y = x * vec[0:1, :] + vec[2:3, :]
             normed[sl, :] = y
             nb_o[sl, :] = y.astype(BF)
+            nbt_o[:, sl] = y.astype(BF).T
             acc[sl, :] = y + vec[5:6, :]
-
-    for group in range(4):
-
-        @pl.when(k == group)
-        def _():
-            for g, _, b in copies:
-                if g == group:
-                    b.wait()
 
     hidden = act_o.shape[2]
 
     def rows_step(r, _):
         sl = pl.ds(pl.multiple_of(r * ROWS, ROWS), ROWS)
-        h = nn(nb_o[sl, :], w_feed[k, :, 0:hidden]) + bias[pl.ds(k, 1), :]
+        h = nn(nb_o[sl, :], w[0, :, 0:hidden]) + bias[pl.ds(k, 1), :]
         phi, slope = gelu_parts(h)
         a = (h * phi).astype(BF)
         act_o[0, sl, :] = a
         gp_o[0, sl, :] = slope
-        acc[sl, :] += nt(a, w_feed[k, :, hidden:])
+        acc[sl, :] += nt(a, w[0, :, hidden:])
         return 0
 
     lax.fori_loop(0, share // ROWS, rows_step, 0)
@@ -399,44 +381,37 @@
             gs = root * (gg - row_mean(gg) - x * row_mean(gg * x))
             gs_o[sl, :] = gs
             gsb_o[sl, :] = gs.astype(BF)
+            gst_o[:, sl] = gs.astype(BF).T
             for n, y in enumerate((g * x, g, gs)):
                 total[n] = total[n] + jnp.sum(y, axis=0, keepdims=True)
         sum_o[...] = jnp.concatenate(total + [jnp.zeros((5, tokb.shape[1]), F32)], axis=0)
 
 
-def layout_of(groups):
-    arrays, pieces = [], []
-    for k, group in enumerate(groups):
-        for x in group:
-            if x.ndim == 2:
-                pieces.append((k, len(arrays), None))
-            else:
-                pieces += [(k, len(arrays), n) for n in range(x.shape[0])]
-            arrays.append(x)
-    return arrays, (len(arrays), pieces), len(pieces) // 4
-
-
-def feed_forward(place, groups, contexts, tokb, gtop, vec, bias):
-    arrays, layout, per = layout_of(groups)
+def feed_specs(place, gathered, hidden):
+    width, last = gathered.shape[1], place.shape[0] - 1
+    return [pl.BlockSpec(memory_space=pl.ANY), pl.BlockSpec((1, width, 2 * hidden), lambda i, s: (s[last] ^ i, 0, 0))]
+
+
+def feed_forward(place, gathered, contexts, tokb, gtop, vec, bias):
     share, width = tokb.shape
-    part, hidden = contexts[0].shape[1], bias.shape[1]
+    hidden = bias.shape[1]
     block = lambda: pl.BlockSpec((1, share, hidden), lambda i, s: (i, 0, 0))
     sd = jax.ShapeDtypeStruct
     return pl.pallas_call(
-        partial(feed_kernel, layout, per),
+        feed_kernel,
         grid_spec=pltpu.PrefetchScalarGridSpec(
             num_scalar_prefetch=1,
             grid=(4,),
-            in_specs=[pl.BlockSpec(memory_space=pl.ANY)] * len(arrays)
-            + [whole_block(x.shape) for x in (*contexts, tokb, gtop, vec, bias)],
-            out_specs=[whole_block((share, width))] * 5
+            in_specs=feed_specs(place, gathered, hidden) + [whole_block(x.shape) for x in (*contexts, tokb, gtop, vec, bias)],
+            out_specs=[whole_block((share, width))] * 4
+            + [whole_block((width, share))] * 2
             + [block(), block(), whole_block((share, 128)), whole_block((8, width))],
             scratch_shapes=[
-                pltpu.VMEM((4, width, 2 * hidden), BF),
-                pltpu.VMEM((4, width, part), BF),
+                pltpu.VMEM((share, width), BF),
+                pltpu.VMEM((4, width, gathered.shape[2] - 2 * hidden), BF),
                 pltpu.VMEM((share, width), F32),
                 pltpu.VMEM((share, width), F32),
-                pltpu.SemaphoreType.DMA((2, len(layout[1]))),
+                pltpu.SemaphoreType.DMA((4,)),
             ],
         ),
         out_shape=[
@@ -444,51 +419,37 @@
             sd((share, width), F32),
             sd((share, width), BF),
             sd((share, width), F32),
-            sd((share, width), BF),
+            sd((width, share), BF),
+            sd((width, share), BF),
             sd((4, share, hidden), BF),
             sd((4, share, hidden), F32),
             sd((share, 128), F32),
             sd((8, width), F32),
         ],
-        compiler_params=params(48),
-        cost_estimate=pl.CostEstimate(flops=4 * share * width * 4 * hidden * 2, bytes_accessed=24 * 2**20, transcendentals=share * 4 * hidden),
+        compiler_params=params(32),
+        cost_estimate=COST,
         name="feed_forward",
-    )(place, *arrays, *contexts, tokb, gtop, vec, bias)
-
-
-def feed_back_kernel(layout, per, place, *refs):
-    arrays = refs[: layout[0]]
-    (gs, gsb, fs, gp, root, vec, gf_o, gfb_o, gc0, gc1, gc2, gc3, gh_o, ghs_o, sum_o, w_feed, w_out, acc, sems) = refs[layout[0] :]
-    pieces = [(g, arrays[a], lead) for g, a, lead in layout[1]]
-    copies = fetches(place, pieces, w_feed, w_out, sems, per)
+    )(place, gathered, gathered, *contexts, tokb, gtop, vec, bias)
+
+
+def feed_back_kernel(place, gathered, w, gs, gsb, fs, gp, root, vec, *refs):
+    (gf_o, gft_o, gc0, gc1, gc2, gc3, gh_o, ghs_o, sum_o, w_out, acc, sems) = refs
+    copies = out_copies(place, gathered, w_out, sems)
     k = pl.program_id(0)
     share, width = gs.shape
-    hidden = gh_o.shape[2]
+    hidden, part = gh_o.shape[2], gc0.shape[1]
 
     @pl.when(k == 0)
     def _():
-        for _, _, b in copies:
-            b.start()
-        for _, a, _ in copies:
-            a.start()
-
-    for group in range(4):
-
-        @pl.when(k == group)
-        def _():
-            for g, _, b in copies:
-                if g == group:
-                    b.wait()
-
-    @pl.when(k == 0)
-    def _():
+        for copy in copies:
+            copy.start()
         acc[...] = gs[...]
 
     def rows_step(r, total):
         sl = pl.ds(pl.multiple_of(r * ROWS, ROWS), ROWS)
-        g = (nn(gsb[sl, :], w_feed[k, :, hidden:]) * gp[0, sl, :]).astype(BF)
+        g = (nn(gsb[sl, :], w[0, :, hidden:]) * gp[0, sl, :]).astype(BF)
         gh_o[0, sl, :] = g
-        acc[sl, :] += nt(g, w_feed[k, :, 0:hidden])
+        acc[sl, :] += nt(g, w[0, :, 0:hidden])
         return total + jnp.sum(g.astype(F32), axis=0, keepdims=True)
 
     total = lax.fori_loop(0, share // ROWS, rows_step, jnp.zeros((1, hidden), F32))
@@ -496,8 +457,8 @@
 
     @pl.when(k == 3)
     def _():
-        for _, a, _ in copies:
-            a.wait()
+        for copy in copies:
+            copy.wait()
         sums = [jnp.zeros((1, width), F32)] * 3
         for r in range(share // ROWS):
             sl = pl.ds(r * ROWS, ROWS)
@@ -507,44 +468,42 @@
             gf = root[sl, 0:1] * (gg - row_mean(gg) - x * row_mean(gg * x))
             gf_o[sl, :] = gf
             b = gf.astype(BF)
-            gfb_o[sl, :] = b
+            gft_o[:, sl] = b.T
             for n, o in enumerate((gc0, gc1, gc2, gc3)):
-                o[sl, :] = nn(b, w_out[n]).astype(BF)
+                o[sl, :] = nn(b, w_out[n, :, 0:part]).astype(BF)
             for n, y in enumerate((gn * x, gn, gf)):
                 sums[n] = sums[n] + jnp.sum(y, axis=0, keepdims=True)
         sum_o[...] = jnp.concatenate(sums + [jnp.zeros((5, width), F32)], axis=0)
 
 
-def feed_back(place, groups, gs, gsb, fs, gp, root, vec, part):
-    arrays, layout, per = layout_of(groups)
+def feed_back(place, gathered, gs, gsb, fs, gp, root, vec, part):
     share, width = gs.shape
     hidden = gp.shape[2]
     block = lambda: pl.BlockSpec((1, share, hidden), lambda i, s: (i, 0, 0))
     sd = jax.ShapeDtypeStruct
     return pl.pallas_call(
-        partial(feed_back_kernel, layout, per),
+        feed_back_kernel,
         grid_spec=pltpu.PrefetchScalarGridSpec(
             num_scalar_prefetch=1,
             grid=(4,),
-            in_specs=[pl.BlockSpec(memory_space=pl.ANY)] * len(arrays)
+            in_specs=feed_specs(place, gathered, hidden)
             + [whole_block(gs.shape), whole_block(gsb.shape), whole_block(fs.shape), block(), whole_block(root.shape), whole_block(vec.shape)],
-            out_specs=[whole_block((share, width))] * 2
+            out_specs=[whole_block((share, width)), whole_block((width, share))]
             + [whole_block((share, part))] * 4
             + [block(), pl.BlockSpec((1, 8, hidden), lambda i, s: (i, 0, 0)), whole_block((8, width))],
             scratch_shapes=[
-                pltpu.VMEM((4, width, 2 * hidden), BF),
-                pltpu.VMEM((4, width, part), BF),
+                pltpu.VMEM((4, width, gathered.shape[2] - 2 * hidden), BF),
                 pltpu.VMEM((share, width), F32),
-                pltpu.SemaphoreType.DMA((2, len(layout[1]))),
+                pltpu.SemaphoreType.DMA((4,)),
             ],
         ),
-        out_shape=[sd((share, width), F32), sd((share, width), BF)]
+        out_shape=[sd((share, width), F32), sd((width, share), BF)]
         + [sd((share, part), BF)] * 4
         + [sd((4, share, hidden), BF), sd((4, 8, hidden), F32), sd((8, width), F32)],
-        compiler_params=params(48),
-        cost_estimate=pl.CostEstimate(flops=4 * share * width * 4 * hidden * 2, bytes_accessed=24 * 2**20, transcendentals=0),
+        compiler_params=params(28),
+        cost_estimate=COST,
         name="feed_back",
-    )(place, *arrays, gs, gsb, fs, gp, root, vec)
+    )(place, gathered, gathered, gs, gsb, fs, gp, root, vec)
 
 
 def split_rows(place, per, acc, source, near_o, far_o, lead, cols):
@@ -558,59 +517,56 @@
         far_o[(*lead, n, slice(None), cols)] = acc[far, source].astype(BF)
 
 
-def weights_kernel(per, place, nb, gsb, gfb, c0, c1, c2, c3, gh, act, *refs):
-    outs = refs[:-5]
-    near_o, far_o = outs if per > 1 else (outs[0], None)
-    nbt, gst, gft, acc, acc_out = refs[-5:]
-    k = pl.program_id(0)
-
-    @pl.when(k == 0)
-    def _():
-        nbt[...] = nb[...].T
-        gst[...] = gsb[...].T
-        gft[...] = gfb[...].T
-
-    hidden = gh.shape[2]
-    part = c0.shape[1]
-    acc[...] = nn(nbt[...], gh[0])
-    split_rows(place, per, acc, slice(None), near_o, far_o, (0,), slice(0, hidden))
-    acc[...] = nn(gst[...], act[0])
-    split_rows(place, per, acc, slice(None), near_o, far_o, (0,), slice(hidden, 2 * hidden))
-    for n, ctx in enumerate((c0, c1, c2, c3)):
-
-        @pl.when(k == n)
-        def _(ctx=ctx):
-            acc_out[...] = nn(gft[...], ctx[...])
-
-    split_rows(place, per, acc_out, slice(None), near_o, far_o, (0,), slice(2 * hidden, 2 * hidden + part))
-
-
-def weight_grads(place, per, nb, gsb, gfb, contexts, gh, act):
-    share, width = nb.shape
-    hidden, part = gh.shape[2], contexts[0].shape[1]
-    block = lambda: pl.BlockSpec((1, share, hidden), lambda i, s: (i, 0, 0))
-    cols = 2 * hidden + part
+def weights_kernel(per, place, nbt, gst, gh, act, *refs):
+    hh = gh.shape[2]
+    if per > 1:
+        near_o, far_o, acc = refs
+        for n, (left, right) in enumerate(((nbt, gh), (gst, act))):
+            acc[...] = nn(left[...], right[0])
+            split_rows(place, per, acc, slice(None), near_o, far_o, (0,), slice(n * hh, (n + 1) * hh))
+        return
+    *more, out = refs
+    out[0, :, 0:hh] = nn(nbt[...], gh[0]).astype(BF)
+    out[0, :, hh : 2 * hh] = nn(gst[...], act[0]).astype(BF)
+    if more:
+        gft, ctx = more
+        out[0, :, 2 * hh :] = nn(gft[...], ctx[0]).astype(BF)
+
+
+def weight_grads(place, per, side, nbt, gst, gh, act, *more):
+    width, share = nbt.shape
+    hh = gh.shape[2] // 2
+    here = len(place.shape) and place.shape[0] - 1
+    block = pl.BlockSpec((1, share, hh), lambda i, s: (i, 0, side))
+    cols = 2 * hh
+    ins = [whole_block(nbt.shape), whole_block(gst.shape), block, block]
+    if more:
+        part = more[1].shape[2]
+        cols += part
+        ins += [whole_block(more[0].shape), pl.BlockSpec((1, share, part), lambda i, s: (i, 0, 0))]
     if per > 1:
         shape = (4, per // 2, width // per, cols)
         outs = [jax.ShapeDtypeStruct(shape, BF)] * 2
         specs = [pl.BlockSpec((1,) + shape[1:], lambda i, s: (i, 0, 0, 0))] * 2
+        scratch = [pltpu.VMEM((width, hh), F32)]
     else:
         outs = [jax.ShapeDtypeStruct((4, width, cols), BF)]
-        specs = [pl.BlockSpec((1, width, cols), lambda i, s: (i, 0, 0))]
+        specs = [pl.BlockSpec((1, width, cols), lambda i, s: (i ^ s[here], 0, 0))]
+        scratch = []
     return pl.pallas_call(
         partial(weights_kernel, per),
         grid_spec=pltpu.PrefetchScalarGridSpec(
             num_scalar_prefetch=1,
             grid=(4,),
-            in_specs=[whole_block(x.shape) for x in (nb, gsb, gfb, *contexts)] + [block(), block()],
+            in_specs=ins,
             out_specs=specs,
-            scratch_shapes=[pltpu.VMEM((width, share), BF)] * 3 + [pltpu.VMEM((width, hidden), F32), pltpu.VMEM((width, part), F32)],
+            scratch_shapes=scratch,
         ),
         out_shape=outs,
-        compiler_params=params(40),
-        cost_estimate=pl.CostEstimate(flops=4 * share * width * 4 * hidden, bytes_accessed=20 * 2**20, transcendentals=0),
+        compiler_params=params(20),
+        cost_estimate=COST,
         name="weight_grads",
-    )(place, nb, gsb, gfb, *contexts, gh, act)
+    )(place, nbt, gst, gh, act, *more)
 
 
 def qkv_weights_kernel(per, part, place, own, other, g, *refs):
@@ -652,7 +608,7 @@
         ),
         out_shape=outs,
         compiler_params=params(32),
-        cost_estimate=pl.CostEstimate(flops=4 * half_len * width * 3 * WIDE, bytes_accessed=8 * 2**20, transcendentals=0),
+        cost_estimate=COST,
         name="qkv_weight_grads",
     )(place, tokens, other, g)
 
@@ -693,6 +649,10 @@
     a, b = jnp.where(odd, b, a), jnp.where(odd, a, b)
     c, d = jnp.where(odd, d, c), jnp.where(odd, c, d)
     return jnp.stack([jnp.where(high, c, a), jnp.where(high, d, b), jnp.where(high, a, c), jnp.where(high, b, d)])
+
+
+def after(x, *others):
+    return lax.optimization_barrier((x, others))[0]
 
 
 def sum_shard(x):
@@ -746,29 +706,23 @@
     def by_core(own, other):
         return jnp.where(first_core, jnp.stack([own, other]), jnp.stack([other, own]))
 
-    feed = jnp.concatenate([ffn_weight.reshape(rows, 2 * hidden), out_weight], axis=1)
-    bias_rows = jnp.pad(three_rows(ffn_bias), ((0, 13), (0, hidden + part)))
+    hh = hidden // 2
+    row = z * 2 + c
+    bias_terms = lax.dynamic_slice_in_dim(three_rows(ffn_bias), row * rows, rows, 1).T
+    extra = jnp.pad(bias_terms, ((0, 0), (0, 256 - part - 3)))
+    gathered = jnp.concatenate([ffn_weight.reshape(rows, 2 * hidden), out_weight, extra], axis=1)
+    gathered = lax.all_gather(gathered, ("tp", "shard", "ctx"), axis=0, tiled=True).reshape(4, width, 2 * hidden + 256)
     qkv_rows = qkv_weight.reshape(rows, 3 * part)
     other_tokens = swap_ctx(take(tokens, 1 - c))
     if direct:
-        place = jnp.stack([((z ^ j) * 2 + (c ^ f)) * rows for f in (0, 1) for j in range(4)] + [c]).astype(jnp.int32)
+        places = [((z ^ j) * 2 + (c ^ f)) * rows for f in (0, 1) for j in range(4)]
         near = [qkv_rows] + [swap_shard(qkv_rows, j) for j in (1, 2, 3)]
-        qkv_pieces = near + [swap_ctx(x) for x in near]
-        own = gather_tp(jnp.concatenate([feed, bias_rows]), rows // 2)
-        far = jnp.concatenate([swap_shard(feed, j) for j in (1, 2, 3)])
-        far = gather_tp(far, 3 * rows // 2)
-        lifted = [x.reshape(3, rows, -1) for x in far]
-        groups = [[own[k], lifted[k], swap_ctx(own[k]), swap_ctx(lifted[k])] for k in range(4)]
-        bias_all = [x[rows : rows + 3, :hidden] for x in own]
+        qkv_pieces = [*near, swap_ctx(jnp.stack(near))]
     else:
-        place = jnp.stack([jnp.zeros_like(c), c]).astype(jnp.int32)
+        places = [jnp.zeros_like(c)]
         qkv_pieces = [lax.all_gather(qkv_rows, ("shard", "ctx"), axis=0, tiled=True)]
-        full = lax.all_gather(feed, ("shard", "ctx"), axis=0, tiled=True)
-        full = gather_tp(jnp.concatenate([full, bias_rows]), width // 2)
-        groups = [[x] for x in full]
-        bias_all = [x[width : width + 3, :hidden] for x in full]
-    per = len(qkv_pieces)
-    bias_all = jnp.stack([jnp.sum(x.astype(F32), axis=0) for x in bias_all])
+    per = len(places)
+    place = jnp.stack(places + [c, t]).astype(jnp.int32)
     bias_pad = jnp.pad(qkv_bias, ((0, 0), (0, WIDE - part)))
     vec = jnp.concatenate([norm_gain, shift_params, jnp.zeros((2, width), F32)])
 
@@ -786,56 +740,96 @@
     bounds = key_bounds(segment)
     seg_column = segment[:, None]
     seg_row = jnp.broadcast_to(segment[None, :], (8, length))
-    q, k_rows, v_rows, k_turned, qkv_wide = project_qkv(place, qkv_pieces, bias_pad, tokens, other_tokens, cosine, sine, part)
+    q, k_rows, v_rows, k_turned, qkv_wide = project_qkv(place, qkv_pieces, per, bias_pad, tokens, other_tokens, cosine, sine, part)
 
     contexts, log_totals = [None] * 4, [None] * 4
-    for j in (3, 1, 2, 0):
+
+    def forward(j, q):
         spot = jnp.concatenate([((t ^ j) * (share // BLOCK))[None].astype(jnp.int32), bounds])
         context, log_totals[j] = attention_forward(spot, q, k_rows, v_rows, seg_column, seg_row, heads, share)
         contexts[j] = swap_tp(context, j) if j else context
+
+    forward(3, q)
+    q_next, log_totals[3] = lax.optimization_barrier((q, log_totals[3]))
+    forward(1, q_next)
+    q_next, log_totals[1], contexts[3] = lax.optimization_barrier((q, log_totals[1], contexts[3]))
+    forward(2, q_next)
+    q_next, log_totals[2], contexts[1] = lax.optimization_barrier((q, log_totals[2], contexts[1]))
+    forward(0, q_next)
     log_total = jnp.concatenate(log_totals, axis=1)
-
-    layer_out, grad_second, grad_second_b, first_scaled, normed_b, activated, slope, root, sums_two = feed_forward(
-        place, groups, contexts, tok_block, grad_top, vec, bias_all
+    terms = gathered[:, :, 2 * hidden + part : 2 * hidden + part + 3].astype(F32)
+    bias_all = order_four(list(jnp.sum(terms, axis=2)), t)
+
+    (
+        layer_out,
+        grad_second,
+        grad_second_b,
+        first_scaled,
+        normed_t,
+        second_t,
+        activated,
+        slope,
+        root,
+        sums_two,
+    ) = feed_forward(place, gathered, contexts, tok_block, grad_top, vec, bias_all)
+
+    def finish_spread(full):
+        keep, send = take(full, c), take(full, 1 - c)
+        return by_core(keep, swap_ctx(send))
+
+    out_blocks = [layer_out, swap_tp(layer_out, 1), swap_tp(layer_out, 2)]
+
+    grad_first, first_t, g0, g1, g2, g3, grad_hidden, hidden_sums, sums_one = feed_back(
+        place, gathered, grad_second, grad_second_b, first_scaled, slope, root, vec, part
     )
-
-    def spread(block):
-        a, b, d, e = gather_tp(block, share // 2)
-        odd = t % 2 == 1
-        mine = jnp.where(odd, jnp.stack([b, a]), jnp.stack([a, b]))
-        rest = jnp.where(odd, jnp.stack([e, d]), jnp.stack([d, e]))
-        keep, send = jnp.where(here, mine, rest), jnp.where(here, rest, mine)
-        return by_core(keep, swap_ctx(send)).reshape(2, half_len, width)
-
-    outputs = spread(layer_out)
-
-    grad_first, grad_first_b, g0, g1, g2, g3, grad_hidden, hidden_sums, sums_one = feed_back(
-        place, groups, grad_second, grad_second_b, first_scaled, slope, root, vec, part
+    heads_grads = [g0, swap_tp(g1, 1), swap_tp(g2, 2), swap_tp(g3, 3)]
+
+    contexts = jnp.stack(contexts)
+    normed_t, out_blocks = lax.optimization_barrier((normed_t, out_blocks))
+    made = weight_grads(place, per, 1, normed_t, second_t, grad_hidden, activated)
+    normed_t, made, heads_grads[1] = lax.optimization_barrier((normed_t, made, heads_grads[1]))
+    whole = weight_grads(place, 1, 0, normed_t, second_t, grad_hidden, activated, first_t, contexts)[0]
+    whole = lax.psum_scatter(whole.reshape(-1, 2 * hh + part), ("tp", "shard", "ctx"), scatter_dimension=0, tiled=True)
+    whole = whole.astype(F32)
+    grad_heads = jnp.stack(heads_grads)
+
+    spot = jnp.concatenate([(t * (share // BLOCK))[None].astype(jnp.int32), bounds])
+    if direct:
+        got = swap_ctx(made[1])
+        packs = [made[0][k].astype(F32) + got[k].astype(F32) for k in range(4)]
+        low, high = packs[3][:2].astype(BF), packs[3][2:].astype(BF)
+        grad_heads, low, high = lax.optimization_barrier((grad_heads, low, high))
+        low, high = swap_tp(low, 2), swap_tp(high, 1)
+    corner = [swap_tp(out_blocks[1][: share // 2], 2), swap_tp(out_blocks[2][share // 2 :], 1)]
+    grad_proj, bias_sums = attention_backward(
+        spot, q, k_rows, k_turned, v_rows, grad_heads, log_total, seg_column, seg_row, cosine, sine, heads
     )
-    grad_heads = jnp.stack([g0, swap_tp(g1, 1), swap_tp(g2, 2), swap_tp(g3, 3)])
-
-    grads = weight_grads(place, per, normed_b, grad_second_b, grad_first_b, contexts, grad_hidden, activated)
+    proj_blocks = grad_proj.reshape(4, share, 3 * WIDE)
+    corner, proj_blocks = lax.optimization_barrier((corner, proj_blocks))
+    out_blocks = [*out_blocks, jnp.concatenate(corner)]
+    branch = {3: contract_last(take(proj_blocks, t ^ 3), qkv_wide)}
     if direct:
-        got = swap_ctx(grads[1])
-        summed = scatter_tp([grads[0][k].astype(F32) + got[k].astype(F32) for k in range(4)])
+        branch[3], low, high = lax.optimization_barrier((branch[3], low, high))
+        one = jnp.concatenate([packs[1][:2] + low.astype(F32), packs[1][2:]]).astype(BF)
+        two = jnp.concatenate([packs[2][:2], packs[2][2:] + high.astype(F32)]).astype(BF)
+        summed = packs[0] + swap_tp(one, 1).astype(F32) + swap_tp(two, 2).astype(F32)
         total = summed[0]
         for j in (1, 2, 3):
             total = total + swap_shard(summed[j].astype(BF), j).astype(F32)
     else:
-        summed = scatter_tp([grads[0][k].astype(F32) for k in range(4)])
-        total = lax.psum_scatter(summed, ("shard", "ctx"), scatter_dimension=0, tiled=True)
-    grad_ffn_weight = total[:, : 2 * hidden].reshape(rows, 2, hidden)
-    grad_out_weight = total[:, 2 * hidden :]
-
-    spot = jnp.concatenate([(t * (share // BLOCK))[None].astype(jnp.int32), bounds])
-    grad_proj, bias_sums = attention_backward(
-        spot, q, k_rows, k_turned, v_rows, grad_heads, log_total, seg_column, seg_row, cosine, sine, heads
-    )
-    proj_blocks = grad_proj.reshape(4, share, 3 * WIDE)
-    branch = [contract_last(take(proj_blocks, t ^ k), qkv_wide) for k in range(4)]
-    grad_tokens = spread((grad_first + scatter_tp(branch)).astype(BF))
-
-    grads = qkv_weight_grads(place, per, tokens, other_tokens, grad_proj, part)
+        total = lax.psum_scatter(made[0].reshape(-1, 2 * hh), ("tp", "shard", "ctx"), scatter_dimension=0, tiled=True).astype(F32)
+    grad_up = jnp.concatenate([whole[:, :hh], total[:, :hh]], axis=1)
+    grad_down = jnp.concatenate([whole[:, hh : 2 * hh], total[:, hh:]], axis=1)
+    grad_ffn_weight = jnp.stack([grad_up, grad_down], axis=1)
+    grad_out_weight = whole[:, 2 * hh :]
+
+    for k in (1, 2, 0):
+        branch[k] = contract_last(take(proj_blocks, t ^ k), qkv_wide)
+    grad_branch = scatter_tp([branch[k] for k in range(4)])
+    grad_blocks = gather_tp((grad_first + grad_branch).astype(BF), share // 2)
+    grad_full = order_four(grad_blocks, t).reshape(2, half_len, width)
+
+    grads = qkv_weight_grads(after(place, branch[0]), per, tokens, other_tokens, grad_proj, part)
     if direct:
         summed = grads[0] + swap_ctx(grads[1]).astype(F32)
         total = summed[0]
@@ -847,15 +841,18 @@
 
     sums = order_four([hidden_sums[k, 0] for k in range(4)], t).reshape(4 * hidden)
     vectors = jnp.stack([sums_one[0], sums_two[0], sums_one[1], sums_two[1], sums_one[2], sums_two[2]])
-    small = jnp.concatenate([sums, vectors.reshape(-1)]).reshape(-1, 128)
+    mine = bias_sums[0].reshape(3, WIDE)
+    others = jnp.where(jnp.arange(4)[:, None, None] == t, mine[None], 0.0)
+    small = jnp.concatenate([sums, vectors.reshape(-1), others.reshape(-1)]).reshape(-1, 128)
     for k in (1, 2):
         small = small + swap_tp(small, k)
     small = sum_shard(small + swap_ctx(small))
-    cut = 4 * hidden // 128
+    cut, end = 4 * hidden // 128, (4 * hidden + 6 * width) // 128
     grad_ffn_bias = take(small[:cut].reshape(4, hidden), t)
-    vectors = small[cut:].reshape(6, width)
-    grad_qkv_bias = bias_sums[0].reshape(3, WIDE)[:, :part]
-    grad_qkv_bias = sum_shard(grad_qkv_bias + swap_ctx(grad_qkv_bias))
+    vectors = small[cut:end].reshape(6, width)
+    grad_qkv_bias = take(small[end:].reshape(4, 3, WIDE), t)[:, :part]
+    outputs = finish_spread(order_four(out_blocks, t).reshape(2, half_len, width))
+    grad_tokens = finish_spread(grad_full)
     return (
         outputs,
         grad_tokens,

time: 470 us -> 385 us (0.82); the launches traced: 464 us -> 384 us
  waiting for transfers between devices: 166 us -> 83.8 us
  starting transfers between devices: 93.7 us -> 59.7 us
  local copies, waits for them, and re-layouts: 52.1 us -> 65.8 us
  between operations: 1.97 us -> 15.2 us
    ppermute x32 -> x24, waiting for transfers between devices: 109 us -> 39 us  [swap_tp(): return lax.ppermute(x, 'tp', [(i, i ^ k) for i in range(4)])]
    ppermute x16 -> x11, waiting for transfers between devices: 57.1 us -> 12 us  [swap_shard(): return lax.ppermute(x, 'shard', [(i, i ^ k) for i in range(4)])]
    ppermute x21 -> x9, starting transfers between devices: 51.3 us -> 11.6 us  [swap_ctx(): return lax.ppermute(x, 'ctx', [(0, 1), (1, 0)])]
    all_gather x0 -> x1, waiting for transfers between devices: none -> 32.7 us  [body(): lax.all_gather(gathered, ('tp', 'shard', 'ctx'), axis=0, tiled=True)]
    ppermute x16 -> x11, starting transfers between devices: 11.7 us -> 29 us  [swap_shard(): return lax.ppermute(x, 'shard', [(i, i ^ k) for i in range(4)])]
    ppermute x32 -> x24, starting transfers between devices: 30.6 us -> 19 us  [swap_tp(): return lax.ppermute(x, 'tp', [(i, i ^ k) for i in range(4)])]
    pallas_call x4, Pallas kernels: 18.5 us -> 27.5 us  [attention_forward(): pl.pallas_call(partial(forward_kernel, heads), grid_spec=pltpu.PrefetchSc...]
    slice x3 -> x8, local copies, waits for them, and re-layouts: 0.71 us -> 8.18 us  [the longest x1 1.85 us: body(): out_blocks[1][:share // 2]]
  transfers between devices with their start and end apart: 69 -> 46, of which waited for: 23 -> 10; matrix products, arithmetic and copies ran while one was open for 14% -> 21% of each run, Pallas kernels for 15% -> 24%
where the time goes in v3:
time: 385 us; the launch traced here: 384 us
  Pallas kernels  109 us (28%)
  waiting for transfers between devices  83.8 us (22%)
  local copies, waits for them, and re-layouts  65.8 us (17%)
  starting transfers between devices  59.7 us (16%)
  other arithmetic  43.4 us (11%)
  between operations  15.2 us (4%)
  matrix products  7.4 us (2%)
    ppermute x24, waiting for transfers between devices, swap_tp(): return lax.ppermute(x, 'tp', [(i, i ^ k) for i in range(4)])  39 us
    unnamed x158, local copies, waits for them, and re-layouts  35.5 us
    all_gather x1, waiting for transfers between devices, body(): lax.all_gather(gathered, ('tp', 'shard', 'ctx'), axis=0, tiled=True)  32.7 us
    pallas_call x1, Pallas kernels, attention_backward(): pl.pallas_call(partial(backward_kernel, heads), grid_spec=pltpu.PrefetchS...  30 us
    ppermute x11, starting transfers between devices, swap_shard(): return lax.ppermute(x, 'shard', [(i, i ^ k) for i in range(4)])  29 us
    pallas_call x4, Pallas kernels, attention_forward(): pl.pallas_call(partial(forward_kernel, heads), grid_spec=pltpu.PrefetchSc...  27.5 us
    ppermute x24, starting transfers between devices, swap_tp(): return lax.ppermute(x, 'tp', [(i, i ^ k) for i in range(4)])  19 us
    pallas_call x1, Pallas kernels, feed_forward(): pl.pallas_call(feed_kernel, grid_spec=pltpu.PrefetchScalarGridSpec(num_sc...  17.9 us
  transfers between devices with their start and end apart: 46, of which 10 were waited for; matrix products, arithmetic and copies ran while one was open for 21% of the time, Pallas kernels for 24%

profile of v3, /device:TPU:1, one launch (start us, length us, event | category | flops | bytes accessed | tf_op | source)
XLA Modules:
  0.0 384.0 jit_solution(10612568341292403111)
XLA Ops:
  9.2 1.6 concatenate.53
  11.3 4.2 %collective-permute-start.3 = (bf16[96,576]{1,0:T(8,128)(2,1)S(1)}, bf16[96,576]{1,0:T(8,128)(2,1)S(1)}, u32[]{:S(2)}, u32[]{:S(2)}) collective-permute-start(bf16[96,576]{1,0:T(8,128)(2,1)S(1)} %copy.35.refs_0_), channel_id=1, source_target_pairs={{0,24},{8,16},{16,8},{24,0},{1,25},{9,17},{17,9},{25,1},{2,26},{10... | collective-permute-start | bytes 331784 | tf_op jit(solution)/shard_map/ppermute | solution.py:643
  15.9 1.3 collective-permute-start
  17.2 2.7 dynamic-slice_bitcast_fusion.2
  20.1 2.1 dynamic-slice_bitcast_fusion.3
  24.1 1.3 collective-permute-done.2.refs_2_
  25.6 1.5 collective-permute-start.4
  27.1 3.7 fusion.1
  32.0 1.9 copy-done.3
  33.9 1.4 copy-done.10
  36.2 5.1 %project_qkv.1 = (bf16[2048,256]{1,0:T(8,128)(2,1)S(1)}, bf16[2048,256]{1,0:T(8,128)(2,1)S(1)}, bf16[2048,256]{1,0:T(8,128)(2,1)S(1)}, bf16[256,2048]{1,0:T(8,128)(2,1)S(1)}, bf16[768,768]{1,0:T(8,128)(2,1)S(1)}) custom-call(s32[10]{0:T(128)S(1)} %stack.207.place, bf16[96,576]{1,0:T(8,128)(2,1)S(1)} %copy.35.refs_0_, bf16[96,576]{1,0:T(8,128)(2,1)S(1)} %copy-done.39, ...), custom_call_target="tpu_custom_call" | custom-call | tf_op jit(solution)/shard_map/project_qkv/pallas_call | solution.py:93
  43.3 6.7 %attention_forward.4 = (bf16[512,192]{1,0:T(8,128)(2,1)S(1)}, f32[8,512]{1,0:T(8,128)S(1)}) custom-call(s32[17]{0:T(128)S(1)} %get-tuple-element.219.place, bf16[2048,256]{1,0:T(8,128)(2,1)S(1)} %get-tuple-element.83.q, bf16[2048,256]{1,0:T(8,128)(2,1)S(1)} %get-tuple-element.74.k, bf16[2048,256]{1,0:T(8,128)(2,1)S(1)} %get-tuple-element.75.v, ...), custom_call_target="tpu_custom_call" | custom-call | tf_op jit(solution)/shard_map/attention_forward/pallas_call | solution.py:168
  51.4 7.4 %attention_forward.5 = (bf16[512,192]{1,0:T(8,128)(2,1)S(1)}, f32[8,512]{1,0:T(8,128)S(1)}) custom-call(s32[17]{0:T(128)S(1)} %get-tuple-element.221.place, bf16[2048,256]{1,0:T(8,128)(2,1)S(1)} %get-tuple-element.83.q, bf16[2048,256]{1,0:T(8,128)(2,1)S(1)} %get-tuple-element.74.k, bf16[2048,256]{1,0:T(8,128)(2,1)S(1)} %get-tuple-element.75.v, ...), custom_call_target="tpu_custom_call" | custom-call | tf_op jit(solution)/shard_map/attention_forward/pallas_call | solution.py:168
  59.2 2.3 bitcast_select_fusion.gtop
  62.5 8.0 %attention_forward.6 = (bf16[512,192]{1,0:T(8,128)(2,1)}, f32[8,512]{1,0:T(8,128)S(1)}) custom-call(s32[17]{0:T(128)S(1)} %get-tuple-element.220.place, bf16[2048,256]{1,0:T(8,128)(2,1)S(1)} %get-tuple-element.83.q, bf16[2048,256]{1,0:T(8,128)(2,1)S(1)} %get-tuple-element.74.k, bf16[2048,256]{1,0:T(8,128)(2,1)S(1)} %get-tuple-element.75.v, ...), custom_call_target="tpu_custom_call" | custom-call | tf_op jit(solution)/shard_map/attention_forward/pallas_call | solution.py:168
  71.8 5.3 %attention_forward.7 = (bf16[512,192]{1,0:T(8,128)(2,1)S(1)}, f32[8,512]{1,0:T(8,128)S(1)}) custom-call(s32[17]{0:T(128)S(1)} %get-tuple-element.222.place, bf16[2048,256]{1,0:T(8,128)(2,1)S(1)} %get-tuple-element.83.q, bf16[2048,256]{1,0:T(8,128)(2,1)S(1)} %get-tuple-element.74.k, bf16[2048,256]{1,0:T(8,128)(2,1)S(1)} %get-tuple-element.75.v, ...), custom_call_target="tpu_custom_call" | custom-call | tf_op jit(solution)/shard_map/attention_forward/pallas_call | solution.py:168
  78.4 32.7 %all-gather.2.cloned.1.call-done = bf16[3072,1792]{1,0:T(8,128)(2,1)} async-done(((bf16[96,1792]{1,0:T(8,128)(2,1)}), bf16[3072,1792]{1,0:T(8,128)(2,1)}) %all-gather.2.cloned.1.call-update) | async-done | bytes 11010064 | tf_op jit(solution)/shard_map/all_gather | solution.py:714
  111.1 1.7 convert_reduce_fusion
  117.1 17.9 %feed_forward.1 = (bf16[512,768]{1,0:T(8,128)(2,1)S(1)}, f32[512,768]{1,0:T(8,128)S(1)}, bf16[512,768]{1,0:T(8,128)(2,1)S(1)}, f32[512,768]{1,0:T(8,128)S(1)}, b...) custom-call(s32[10]{0:T(128)S(1)} %stack.207.place, ...), custom_call_target="tpu_custom_call" | custom-call | tf_op jit(solution)/shard_map/feed_forward/pallas_call | solution.py:400
  136.6 12.4 %feed_back.1 = (f32[512,768]{1,0:T(8,128)S(1)}, bf16[768,512]{1,0:T(8,128)(2,1)S(1)}, bf16[512,192]{1,0:T(8,128)(2,1)S(1)}, bf16[512,192]{1,0:T(8,128)(2,1)S(1)}...) custom-call(s32[10]{0:T(128)S(1)} %stack.207.place, ...), custom_call_target="tpu_custom_call" | custom-call | tf_op jit(solution)/shard_map/feed_back/pallas_call | solution.py:484
  149.8 4.2 %collective-permute-done.11 = bf16[512,768]{1,0:T(8,128)(2,1)S(1)} collective-permute-done((bf16[512,768]{1,0:T(8,128)(2,1)S(1)}, bf16[512,768]{1,0:T(8,128)(2,1)S(1)}, u32[]{:S(2)}, u32[]{:S(2)}) %collective-permute-start.11) | collective-permute-done | bytes 786464 | tf_op jit(solution)/shard_map/ppermute | solution.py:639
  154.0 6.0 %weight_grads.2 = (bf16[4,4,96,768]{3,2,1,0:T(8,128)(2,1)S(1)}, bf16[4,4,96,768]{3,2,1,0:T(8,128)(2,1)}) custom-call(s32[10]{0:T(128)S(1)} %stack.207.place, bf16[768,512]{1,0:T(8,128)(2,1)S(1)} %get-tuple-element.129.nbt, bf16[768,512]{1,0:T(8,128)(2,1)S(1)} %get-tuple-element.100.gst, bf16[4,512,768]{2,1,0:T(8,128)(2,1)S(1)} %get-tuple-element.101.gh, ...), custom_call_target="tpu_custom_call" | custom-call | tf_op jit(solution)/shard_map/weight_grads/pallas_call | solution.py:556
  160.1 1.5 copy-done.25
  162.3 2.3 collective-permute-start.17
  165.4 2.3 pad_maximum_fusion.3.refs_1_
  173.8 1.9 slice.216
  175.7 1.8 slice.217
  179.0 1.9 copy-done.6
  180.8 1.9 copy-done.8
  186.1 5.7 %weight_grads.3 = bf16[4,768,960]{2,1,0:T(8,128)(2,1)S(1)} custom-call(s32[10]{0:T(128)S(1)} %stack.207.place, bf16[768,512]{1,0:T(8,128)(2,1)S(1)} %copy-done.20, bf16[768,512]{1,0:T(8,128)(2,1)S(1)} %copy-done.22, bf16[4,512,768]{2,1,0:T(8,128)(2,1)S(1)} %copy-done.8, bf16[4,512,768]{2,1,0:T(8,128)(2,1)S(1)} %copy-done.6, bf16[768,512]{1,0:T(8,128)(2,1)S(1)} %copy-done.35, ...), custom_call_target="tpu_custom_call" | custom-call | tf_op jit(solution)/shard_map/weight_grads/pallas_call | solution.py:556
  191.8 2.6 copy-done.2
  195.4 1.3 pad_maximum_fusion.2.do
  196.7 4.0 %convert_add_fusion.1 = (f32[1,4,96,768]{3,2,1,0:T(8,128)}, f32[1,4,96,768]{3,2,1,0:T(8,128)}, bf16[1,4,96,768]{3,2,1,0:T(8,128)(2,1)S(1)}) fusion(bf16[4,4,96,768]{3,2,1,0:T(8,128)(2,1)} %collective-permute-done.17, bf16[4,4,96,768]{3,2,1,0:T(8,128)(2,1)} %copy-done.25), kind=kLoop, calls=%fused_computation.14 | loop fusion | flops 2949120 | bytes 6488064 | tf_op jit(solution)/shard_map/add | solution.py:799
  202.2 30.0 %attention_backward.1 = (bf16[2048,768]{1,0:T(8,128)(2,1)S(1)}, f32[8,768]{1,0:T(8,128)S(1)}) custom-call(s32[17]{0:T(128)S(1)} %get-tuple-element.222.place, bf16[2048,256]{1,0:T(8,128)(2,1)S(1)} %get-tuple-element.83.q, bf16[2048,256]{1,0:T(8,128)(2,1)S(1)} %get-tuple-element.74.k, bf16[256,2048]{1,0:T(8,128)(2,1)S(1)} %copy-done.33, ...), custom_call_target="tpu_custom_call" | custom-call | tf_op jit(solution)/shard_map/attention_backward/pallas_call | solution.py:274
  232.3 1.7 copy-done.23
  234.1 1.3 collective-permute-start.39
  235.9 3.6 fusion.10
  239.5 2.2 fusion.4
  246.0 1.3 collective-permute-start.40
  247.5 14.1 %collective-permute-done.23 = bf16[256,768]{1,0:T(8,128)(2,1)S(1)} collective-permute-done((bf16[256,768]{1,0:T(8,128)(2,1)S(1)}, bf16[256,768]{1,0:T(8,128)(2,1)S(1)}, u32[]{:S(2)}, u32[]{:S(2)}) %collective-permute-start.23) | collective-permute-done | bytes 393248 | tf_op jit(solution)/shard_map/ppermute | solution.py:639
  263.8 1.4 collective-permute-done.21
  267.4 2.5 collective-permute-start.41
  269.9 1.8 fusion.21
  272.4 1.8 constant_dynamic-update-slice_fusion.1
  274.2 4.0 %qkv_weight_grads.1 = (f32[4,96,576]{2,1,0:T(8,128)S(1)}, bf16[4,96,576]{2,1,0:T(8,128)(2,1)S(1)}) custom-call(s32[10]{0:T(128)S(1)} %stack.207.place, bf16[2,1024,768]{2,1,0:T(8,128)(2,1)S(1)} %copy-done.4, bf16[1024,768]{1,0:T(8,128)(2,1)S(1)} %copy-done.11, bf16[2048,768]{1,0:T(8,128)(2,1)S(1)} %copy-done.24), custom_call_target="tpu_custom_call" | custom-call | tf_op jit(solution)/shard_map/qkv_weight_grads/pallas_call | solution.py:600
  278.6 2.0 collective-permute-start.43
  280.6 1.8 constant_dynamic-update-slice_fusion
  282.8 3.1 add_convert_fusion
  286.5 1.9 collective-permute-start.25
  294.1 7.6 %collective-permute-done.27 = bf16[512,768]{1,0:T(8,128)(2,1)} collective-permute-done((bf16[512,768]{1,0:T(8,128)(2,1)}, bf16[512,768]{1,0:T(8,128)(2,1)}, u32[]{:S(2)}, u32[]{:S(2)}) %collective-permute-start.27) | collective-permute-done | bytes 786464 | tf_op jit(solution)/shard_map/ppermute | solution.py:639
  306.6 6.2 %collective-permute-start.31 = (bf16[96,576]{1,0:T(8,128)(2,1)S(1)}, bf16[96,576]{1,0:T(8,128)(2,1)S(1)}, u32[]{:S(2)}, u32[]{:S(2)}) collective-permute-start(bf16[96,576]{1,0:T(8,128)(2,1)S(1)} %get-tuple-element.183), channel_id=1, source_target_pairs={{0,8},{8,0},{16,24},{24,16},{1,9},{9,1},{17,25},{25,17},{2,10},{10... | collective-permute-start | bytes 331784 | tf_op jit(solution)/shard_map/ppermute | solution.py:643
  312.8 11.3 %collective-permute-done.26 = bf16[256,768]{1,0:T(8,128)(2,1)S(1)} collective-permute-done((bf16[256,768]{1,0:T(8,128)(2,1)S(1)}, bf16[256,768]{1,0:T(8,128)(2,1)S(1)}, u32[]{:S(2)}, u32[]{:S(2)}) %collective-permute-start.26) | collective-permute-done | bytes 393248 | tf_op jit(solution)/shard_map/ppermute | solution.py:639
  324.1 6.9 %collective-permute-start.33 = (bf16[96,576]{1,0:T(8,128)(2,1)S(1)}, bf16[96,576]{1,0:T(8,128)(2,1)S(1)}, u32[]{:S(2)}, u32[]{:S(2)}) collective-permute-start(bf16[96,576]{1,0:T(8,128)(2,1)S(1)} %get-tuple-element.184), channel_id=1, source_target_pairs={{0,24},{8,16},{16,8},{24,0},{1,25},{9,17},{17,9},{25,1},{2,26},{10... | collective-permute-start | bytes 331784 | tf_op jit(solution)/shard_map/ppermute | solution.py:643
  331.1 2.2 select_bitcast_fusion.3
  333.7 1.4 constant_dynamic-slice_fusion.2
  335.1 2.8 collective-permute-start.29
  338.3 1.4 constant_dynamic-slice_fusion.3
  339.6 5.8 %collective-permute-start.32 = (bf16[96,576]{1,0:T(8,128)(2,1)S(1)}, bf16[96,576]{1,0:T(8,128)(2,1)S(1)}, u32[]{:S(2)}, u32[]{:S(2)}) collective-permute-start(bf16[96,576]{1,0:T(8,128)(2,1)S(1)} %get-tuple-element.185), channel_id=1, source_target_pairs={{0,16},{8,24},{16,0},{24,8},{1,17},{9,25},{17,1},{25,9},{2,18},{10... | collective-permute-start | bytes 331784 | tf_op jit(solution)/shard_map/ppermute | solution.py:643
  345.7 2.6 fusion.49
  349.3 2.3 collective-permute-start.38
  354.7 4.5 %collective-permute-done.38 = bf16[96,768]{1,0:T(8,128)(2,1)} collective-permute-done((bf16[96,768]{1,0:T(8,128)(2,1)}, bf16[96,768]{1,0:T(8,128)(2,1)}, u32[]{:S(2)}, u32[]{:S(2)}) %collective-permute-start.38) | collective-permute-done | bytes 147488 | tf_op jit(solution)/shard_map/ppermute | solution.py:643
  359.2 6.1 %collective-permute-done.37 = bf16[96,768]{1,0:T(8,128)(2,1)} collective-permute-done((bf16[96,768]{1,0:T(8,128)(2,1)}, bf16[96,768]{1,0:T(8,128)(2,1)}, u32[]{:S(2)}, u32[]{:S(2)}) %collective-permute-start.37) | collective-permute-done | bytes 147488 | tf_op jit(solution)/shard_map/ppermute | solution.py:643
  366.6 3.8 maximum_select_fusion.1
  370.4 3.7 maximum_select_fusion
  (309 shorter events, 67.2 us)
Async XLA Ops:
  7.2 103.9 %all-gather.2.cloned.1.call-start = ((), (), s32[]{:S(2)}) async-start(), calls=%async_computation.1 | async-start | bytes 11354112 | tf_op jit(solution)/shard_map/all_gather | solution.py:714
  10.9 363.2 %reduce-scatter.2.cloned.1.call-start = ((), (), s32[]{:S(2)}) async-start(), calls=%async_computation.2 | async-start | bytes 6488064 | tf_op jit(solution)/shard_map/reduce_scatter | solution.py:792
  11.3 12.9 %collective-permute-start.3 = (bf16[96,576]{1,0:T(8,128)(2,1)S(1)}, bf16[96,576]{1,0:T(8,128)(2,1)S(1)}, u32[]{:S(2)}, u32[]{:S(2)}) collective-permute-start(bf16[96,576]{1,0:T(8,128)(2,1)S(1)} %copy.35.refs_0_), channel_id=1, source_target_pairs={{0,24},{8,16},{16,8},{24,0},{1,25},{9,17},{17,9},{25,1},{2,26},{10... | collective-permute-start | bytes 331784 | tf_op jit(solution)/shard_map/ppermute | solution.py:643
  15.5 10.0 %collective-permute-start.2 = (bf16[96,576]{1,0:T(8,128)(2,1)S(1)}, bf16[96,576]{1,0:T(8,128)(2,1)S(1)}, u32[]{:S(2)}, u32[]{:S(2)}) collective-permute-start(bf16[96,576]{1,0:T(8,128)(2,1)S(1)} %copy.35.refs_0_), channel_id=1, source_target_pairs={{0,16},{8,24},{16,0},{24,8},{1,17},{9,25},{17,1},{25,9},{2,18},{10... | collective-permute-start | bytes 331784 | tf_op jit(solution)/shard_map/ppermute | solution.py:643
  15.5 10.0 %collective-permute-start.1 = (bf16[96,576]{1,0:T(8,128)(2,1)S(1)}, bf16[96,576]{1,0:T(8,128)(2,1)S(1)}, u32[]{:S(2)}, u32[]{:S(2)}) collective-permute-start(bf16[96,576]{1,0:T(8,128)(2,1)S(1)} %copy.35.refs_0_), channel_id=1, source_target_pairs={{0,8},{8,0},{16,24},{24,16},{1,9},{9,1},{17,25},{25,17},{2,10},{10... | collective-permute-start | bytes 331784 | tf_op jit(solution)/shard_map/ppermute | solution.py:643
  15.9 6.5 %collective-permute-start = (s32[2,1024]{1,0:T(2,128)S(1)}, s32[2,1024]{1,0:T(2,128)S(1)}, u32[]{:S(2)}, u32[]{:S(2)}) collective-permute-start(s32[2,1024]{1,0:T(2,128)S(1)} %bitcast.250), channel_id=1, source_target_pairs={{0,4},{4,0},{1,5},{5,1},{2,6},{6,2},{3,7},{7,3},{8,12},{12,8},{9,1... | collective-permute-start | bytes 24584 | tf_op jit(solution)/shard_map/ppermute | solution.py:635
  19.9 11.0 %collective-permute-start.5 = (bf16[1024,768]{1,0:T(8,128)(2,1)}, bf16[1024,768]{1,0:T(8,128)(2,1)S(1)}, u32[]{:S(2)}, u32[]{:S(2)}) collective-permute-start(bf16[1024,768]{1,0:T(8,128)(2,1)} %dynamic-slice_bitcast_fusion.2), channel_id=1, source_target_pairs={{0,4},{4,0},{1,5},{5,1},{2,6},{6,2},{3,7},{7,3},{8,12},{12,8},{9,1... | collective-permute-start | bytes 4718600 | tf_op jit(solution)/shard_map/ppermute | solution.py:635
  22.4 36.8 %collective-permute-start.9 = (bf16[512,768]{1,0:T(8,128)(2,1)}, bf16[512,768]{1,0:T(8,128)(2,1)}, u32[]{:S(2)}, u32[]{:S(2)}) collective-permute-start(bf16[512,768]{1,0:T(8,128)(2,1)} %dynamic-slice_bitcast_fusion.3), channel_id=1, source_target_pairs={{0,4},{4,0},{1,5},{5,1},{2,6},{6,2},{3,7},{7,3},{8,12},{12,8},{9,1... | collective-permute-start | bytes 2359304 | tf_op jit(solution)/shard_map/ppermute | solution.py:635
  25.6 5.3 %collective-permute-start.4 = (bf16[4,96,576]{2,1,0:T(8,128)(2,1)S(1)}, bf16[4,96,576]{2,1,0:T(8,128)(2,1)S(1)}, u32[]{:S(2)}, u32[]{:S(2)}) collective-permute-start(bf16[4,96,576]{2,1,0:T(8,128)(2,1)S(1)} %pad_maximum_fusion.9), channel_id=1, source_target_pairs={{0,4},{4,0},{1,5},{5,1},{2,6},{6,2},{3,7},{7,3},{8,12},{12,8},{9,1... | collective-permute-start | bytes 1327112 | tf_op jit(solution)/shard_map/ppermute | solution.py:635
  43.3 28.5 %copy-start = (bf16[2048,256]{1,0:T(8,128)(2,1)}, bf16[2048,256]{1,0:T(8,128)(2,1)S(1)}, u32[]{:S(2)}) copy-start(bf16[2048,256]{1,0:T(8,128)(2,1)S(1)} %get-tuple-element.75.v) | copy-start | bytes 3145732
  50.6 11.8 %collective-permute-start.6 = (bf16[512,192]{1,0:T(8,128)(2,1)S(1)}, bf16[512,192]{1,0:T(8,128)(2,1)S(1)}, u32[]{:S(2)}, u32[]{:S(2)}) collective-permute-start(bf16[512,192]{1,0:T(8,128)(2,1)S(1)} %get-tuple-element.79), channel_id=1, source_target_pairs={{0,3},{1,2},{2,1},{3,0},{4,7},{5,6},{6,5},{7,4},{8,11},{9,10},{10,... | collective-permute-start | bytes 589832 | tf_op jit(solution)/shard_map/ppermute | solution.py:639
  58.9 12.2 %collective-permute-start.7 = (bf16[512,192]{1,0:T(8,128)(2,1)S(1)}, bf16[512,192]{1,0:T(8,128)(2,1)S(1)}, u32[]{:S(2)}, u32[]{:S(2)}) collective-permute-start(bf16[512,192]{1,0:T(8,128)(2,1)S(1)} %get-tuple-element.82), channel_id=1, source_target_pairs={{0,1},{1,0},{2,3},{3,2},{4,5},{5,4},{6,7},{7,6},{8,9},{9,8},{10,11... | collective-permute-start | bytes 589832 | tf_op jit(solution)/shard_map/ppermute | solution.py:639
  71.8 41.1 %collective-permute-start.8 = (bf16[512,192]{1,0:T(8,128)(2,1)}, bf16[512,192]{1,0:T(8,128)(2,1)}, u32[]{:S(2)}, u32[]{:S(2)}) collective-permute-start(bf16[512,192]{1,0:T(8,128)(2,1)} %get-tuple-element.86), channel_id=1, source_target_pairs={{0,2},{1,3},{2,0},{3,1},{4,6},{5,7},{6,4},{7,5},{8,10},{9,11},{10,... | collective-permute-start | bytes 589832 | tf_op jit(solution)/shard_map/ppermute | solution.py:639
  135.0 14.0 %copy-start.36 = (bf16[512,768]{1,0:T(8,128)(2,1)}, bf16[512,768]{1,0:T(8,128)(2,1)S(1)}, u32[]{:S(2)}) copy-start(bf16[512,768]{1,0:T(8,128)(2,1)S(1)} %get-tuple-element.119) | copy-start | bytes 2359300
  135.0 14.0 %copy-start.46 = (f32[8,768]{1,0:T(8,128)}, f32[8,768]{1,0:T(8,128)S(1)}, u32[]{:S(2)}) copy-start(f32[8,768]{1,0:T(8,128)S(1)} %get-tuple-element.135) | copy-start | bytes 73732
  135.0 19.0 %copy-start.5 = (bf16[4,512,768]{2,1,0:T(8,128)(2,1)}, bf16[4,512,768]{2,1,0:T(8,128)(2,1)S(1)}, u32[]{:S(2)}) copy-start(bf16[4,512,768]{2,1,0:T(8,128)(2,1)S(1)} %get-tuple-element.102.act) | copy-start | bytes 9437188
  135.0 19.0 %copy-start.19 = (bf16[768,512]{1,0:T(8,128)(2,1)}, bf16[768,512]{1,0:T(8,128)(2,1)S(1)}, u32[]{:S(2)}) copy-start(bf16[768,512]{1,0:T(8,128)(2,1)S(1)} %get-tuple-element.129.nbt) | copy-start | bytes 2359300
  135.0 19.0 %copy-start.21 = (bf16[768,512]{1,0:T(8,128)(2,1)}, bf16[768,512]{1,0:T(8,128)(2,1)S(1)}, u32[]{:S(2)}) copy-start(bf16[768,512]{1,0:T(8,128)(2,1)S(1)} %get-tuple-element.100.gst) | copy-start | bytes 2359300
  135.0 19.0 %collective-permute-start.11 = (bf16[512,768]{1,0:T(8,128)(2,1)S(1)}, bf16[512,768]{1,0:T(8,128)(2,1)S(1)}, u32[]{:S(2)}, u32[]{:S(2)}) collective-permute-start(bf16[512,768]{1,0:T(8,128)(2,1)S(1)} %get-tuple-element.119), channel_id=1, source_target_pairs={{0,2},{1,3},{2,0},{3,1},{4,6},{5,7},{6,4},{7,5},{8,10},{9,11},{10,... | collective-permute-start | bytes 2359304 | tf_op jit(solution)/shard_map/ppermute | solution.py:639
  135.4 18.6 %collective-permute-start.10 = (bf16[512,768]{1,0:T(8,128)(2,1)S(1)}, bf16[512,768]{1,0:T(8,128)(2,1)S(1)}, u32[]{:S(2)}, u32[]{:S(2)}) collective-permute-start(bf16[512,768]{1,0:T(8,128)(2,1)S(1)} %get-tuple-element.119), channel_id=1, source_target_pairs={{0,1},{1,0},{2,3},{3,2},{4,5},{5,4},{6,7},{7,6},{8,9},{9,8},{10,11... | collective-permute-start | bytes 2359304 | tf_op jit(solution)/shard_map/ppermute | solution.py:639
  149.0 11.1 %copy-start.7 = (bf16[4,512,768]{2,1,0:T(8,128)(2,1)}, bf16[4,512,768]{2,1,0:T(8,128)(2,1)S(1)}, u32[]{:S(2)}) copy-start(bf16[4,512,768]{2,1,0:T(8,128)(2,1)S(1)} %get-tuple-element.101.gh) | copy-start | bytes 9437188
  149.0 11.0 %copy-start.26 = (f32[512,768]{1,0:T(8,128)}, f32[512,768]{1,0:T(8,128)S(1)}, u32[]{:S(2)}) copy-start(f32[512,768]{1,0:T(8,128)S(1)} %get-tuple-element.120) | copy-start | bytes 4718596
  149.0 11.0 %copy-start.34 = (bf16[768,512]{1,0:T(8,128)(2,1)}, bf16[768,512]{1,0:T(8,128)(2,1)S(1)}, u32[]{:S(2)}) copy-start(bf16[768,512]{1,0:T(8,128)(2,1)S(1)} %get-tuple-element.130.refs_0_) | copy-start | bytes 2359300
  149.0 11.0 %copy-start.40 = (bf16[512,192]{1,0:T(8,128)(2,1)}, bf16[512,192]{1,0:T(8,128)(2,1)S(1)}, u32[]{:S(2)}) copy-start(bf16[512,192]{1,0:T(8,128)(2,1)S(1)} %get-tuple-element.98) | copy-start | bytes 589828
  149.0 11.0 %copy-start.47 = (f32[8,768]{1,0:T(8,128)}, f32[8,768]{1,0:T(8,128)S(1)}, u32[]{:S(2)}) copy-start(f32[8,768]{1,0:T(8,128)S(1)} %get-tuple-element.134) | copy-start | bytes 73732
  149.0 11.0 %copy-start.48 = (f32[4,8,768]{2,1,0:T(8,128)}, f32[4,8,768]{2,1,0:T(8,128)S(1)}, u32[]{:S(2)}) copy-start(f32[4,8,768]{2,1,0:T(8,128)S(1)} %get-tuple-element.133) | copy-start | bytes 294916
  149.0 12.5 %collective-permute-start.14 = (bf16[512,192]{1,0:T(8,128)(2,1)S(1)}, bf16[512,192]{1,0:T(8,128)(2,1)S(1)}, u32[]{:S(2)}, u32[]{:S(2)}) collective-permute-start(bf16[512,192]{1,0:T(8,128)(2,1)S(1)} %get-tuple-element.105), channel_id=1, source_target_pairs={{0,1},{1,0},{2,3},{3,2},{4,5},{5,4},{6,7},{7,6},{8,9},{9,8},{10,11... | collective-permute-start | bytes 589832 | tf_op jit(solution)/shard_map/ppermute | solution.py:639
  162.3 34.4 %collective-permute-start.17 = (bf16[4,4,96,768]{3,2,1,0:T(8,128)(2,1)}, bf16[4,4,96,768]{3,2,1,0:T(8,128)(2,1)}, u32[]{:S(2)}, u32[]{:S(2)}) collective-permute-start(bf16[4,4,96,768]{3,2,1,0:T(8,128)(2,1)} %get-tuple-element.110), channel_id=1, source_target_pairs={{0,4},{4,0},{1,5},{5,1},{2,6},{6,2},{3,7},{7,3},{8,12},{12,8},{9,1... | collective-permute-start | bytes 7077896 | tf_op jit(solution)/shard_map/ppermute | solution.py:635
  167.7 26.7 %collective-permute-start.15 = (bf16[512,192]{1,0:T(8,128)(2,1)}, bf16[512,192]{1,0:T(8,128)(2,1)}, u32[]{:S(2)}, u32[]{:S(2)}) collective-permute-start(bf16[512,192]{1,0:T(8,128)(2,1)} %get-tuple-element.107), channel_id=1, source_target_pairs={{0,2},{1,3},{2,0},{3,1},{4,6},{5,7},{6,4},{7,5},{8,10},{9,11},{10,... | collective-permute-start | bytes 589832 | tf_op jit(solution)/shard_map/ppermute | solution.py:639
  168.9 25.6 %collective-permute-start.16 = (bf16[512,192]{1,0:T(8,128)(2,1)}, bf16[512,192]{1,0:T(8,128)(2,1)}, u32[]{:S(2)}, u32[]{:S(2)}) collective-permute-start(bf16[512,192]{1,0:T(8,128)(2,1)} %get-tuple-element.108), channel_id=1, source_target_pairs={{0,3},{1,2},{2,1},{3,0},{4,7},{5,6},{6,5},{7,4},{8,11},{9,10},{10,... | collective-permute-start | bytes 589832 | tf_op jit(solution)/shard_map/ppermute | solution.py:639
  177.5 56.5 %collective-permute-start.13 = (bf16[256,768]{1,0:T(8,128)(2,1)}, bf16[256,768]{1,0:T(8,128)(2,1)}, u32[]{:S(2)}, u32[]{:S(2)}) collective-permute-start(bf16[256,768]{1,0:T(8,128)(2,1)} %slice.217), channel_id=1, source_target_pairs={{0,1},{1,0},{2,3},{3,2},{4,5},{5,4},{6,7},{7,6},{8,9},{9,8},{10,11... | collective-permute-start | bytes 1179656 | tf_op jit(solution)/shard_map/ppermute | solution.py:639
  177.8 56.2 %collective-permute-start.12 = (bf16[256,768]{1,0:T(8,128)(2,1)}, bf16[256,768]{1,0:T(8,128)(2,1)}, u32[]{:S(2)}, u32[]{:S(2)}) collective-permute-start(bf16[256,768]{1,0:T(8,128)(2,1)} %slice.216), channel_id=1, source_target_pairs={{0,2},{1,3},{2,0},{3,1},{4,6},{5,7},{6,4},{7,5},{8,10},{9,11},{10,... | collective-permute-start | bytes 1179656 | tf_op jit(solution)/shard_map/ppermute | solution.py:639
  202.2 31.9 %copy-start.58 = (f32[4608]{0:T(1024)S(1)}, f32[4608]{0:T(1024)}, u32[]{:S(2)}) copy-start(f32[4608]{0:T(1024)} %reshape.395) | copy-start | bytes 55300
  202.2 31.9 %copy-start.62 = (f32[3072]{0:T(1024)S(1)}, f32[3072]{0:T(1024)}, u32[]{:S(2)}) copy-start(f32[3072]{0:T(1024)} %reshape.394) | copy-start | bytes 36868
  234.1 11.8 %collective-permute-start.39 = (f32[84,128]{1,0:T(8,128)S(1)}, f32[84,128]{1,0:T(8,128)S(1)}, u32[]{:S(2)}, u32[]{:S(2)}) collective-permute-start(f32[84,128]{1,0:T(8,128)S(1)} %maximum_bitcast_fusion.2), channel_id=1, source_target_pairs={{0,1},{1,0},{2,3},{3,2},{4,5},{5,4},{6,7},{7,6},{8,9},{9,8},{10,11... | collective-permute-start | bytes 129032 | tf_op jit(solution)/shard_map/ppermute | solution.py:639
  235.4 8.0 %collective-permute-start.19 = (bf16[2,96,768]{2,1,0:T(8,128)(2,1)}, bf16[2,96,768]{2,1,0:T(8,128)(2,1)S(1)}, u32[]{:S(2)}, u32[]{:S(2)}) collective-permute-start(bf16[2,96,768]{2,1,0:T(8,128)(2,1)} %get-tuple-element.123), channel_id=1, source_target_pairs={{0,2},{1,3},{2,0},{3,1},{4,6},{5,7},{6,4},{7,5},{8,10},{9,11},{10,... | collective-permute-start | bytes 884744 | tf_op jit(solution)/shard_map/ppermute | solution.py:639
  235.6 7.7 %collective-permute-start.20 = (bf16[2,96,768]{2,1,0:T(8,128)(2,1)}, bf16[2,96,768]{2,1,0:T(8,128)(2,1)S(1)}, u32[]{:S(2)}, u32[]{:S(2)}) collective-permute-start(bf16[2,96,768]{2,1,0:T(8,128)(2,1)} %get-tuple-element.124), channel_id=1, source_target_pairs={{0,1},{1,0},{2,3},{3,2},{4,5},{5,4},{6,7},{7,6},{8,9},{9,8},{10,11... | collective-permute-start | bytes 884744 | tf_op jit(solution)/shard_map/ppermute | solution.py:639
  243.5 18.1 %collective-permute-start.23 = (bf16[256,768]{1,0:T(8,128)(2,1)S(1)}, bf16[256,768]{1,0:T(8,128)(2,1)S(1)}, u32[]{:S(2)}, u32[]{:S(2)}) collective-permute-start(bf16[256,768]{1,0:T(8,128)(2,1)S(1)} %get-tuple-element.177), channel_id=1, source_target_pairs={{0,1},{1,0},{2,3},{3,2},{4,5},{5,4},{6,7},{7,6},{8,9},{9,8},{10,11... | collective-permute-start | bytes 1179656 | tf_op jit(solution)/shard_map/ppermute | solution.py:639
  246.0 21.4 %collective-permute-start.40 = (f32[84,128]{1,0:T(8,128)S(1)}, f32[84,128]{1,0:T(8,128)S(1)}, u32[]{:S(2)}, u32[]{:S(2)}) collective-permute-start(f32[84,128]{1,0:T(8,128)S(1)} %fusion.48), channel_id=1, source_target_pairs={{0,2},{1,3},{2,0},{3,1},{4,6},{5,7},{6,4},{7,5},{8,10},{9,11},{10,... | collective-permute-start | bytes 129032 | tf_op jit(solution)/shard_map/ppermute | solution.py:639
  247.3 17.9 %collective-permute-start.21 = (bf16[256,768]{1,0:T(8,128)(2,1)S(1)}, bf16[256,768]{1,0:T(8,128)(2,1)S(1)}, u32[]{:S(2)}, u32[]{:S(2)}) collective-permute-start(bf16[256,768]{1,0:T(8,128)(2,1)S(1)} %get-tuple-element.176), channel_id=1, source_target_pairs={{0,2},{1,3},{2,0},{3,1},{4,6},{5,7},{6,4},{7,5},{8,10},{9,11},{10,... | collective-permute-start | bytes 1179656 | tf_op jit(solution)/shard_map/ppermute | solution.py:639
  262.6 19.8 %collective-permute-start.24 = (bf16[512,768]{1,0:T(8,128)(2,1)}, bf16[512,768]{1,0:T(8,128)(2,1)}, u32[]{:S(2)}, u32[]{:S(2)}) collective-permute-start(bf16[512,768]{1,0:T(8,128)(2,1)} %pad_maximum_fusion.5), channel_id=1, source_target_pairs={{0,2},{1,3},{2,0},{3,1},{4,6},{5,7},{6,4},{7,5},{8,10},{9,11},{10,... | collective-permute-start | bytes 2359304 | tf_op jit(solution)/shard_map/ppermute | solution.py:639
  265.2 9.0 %copy-start.11 = (bf16[1024,768]{1,0:T(8,128)(2,1)S(1)}, bf16[1024,768]{1,0:T(8,128)(2,1)}, u32[]{:S(2)}) copy-start(bf16[1024,768]{1,0:T(8,128)(2,1)} %copy-done.9) | copy-start | bytes 4718596
  266.3 16.5 %collective-permute-start.22 = (bf16[512,768]{1,0:T(8,128)(2,1)}, bf16[512,768]{1,0:T(8,128)(2,1)}, u32[]{:S(2)}, u32[]{:S(2)}) collective-permute-start(bf16[512,768]{1,0:T(8,128)(2,1)} %pad_maximum_fusion.4), channel_id=1, source_target_pairs={{0,1},{1,0},{2,3},{3,2},{4,5},{5,4},{6,7},{7,6},{8,9},{9,8},{10,11... | collective-permute-start | bytes 2359304 | tf_op jit(solution)/shard_map/ppermute | solution.py:639
  267.4 4.3 %collective-permute-start.41 = (f32[84,128]{1,0:T(8,128)S(1)}, f32[84,128]{1,0:T(8,128)S(1)}, u32[]{:S(2)}, u32[]{:S(2)}) collective-permute-start(f32[84,128]{1,0:T(8,128)S(1)} %fusion.62), channel_id=1, source_target_pairs={{0,4},{4,0},{1,5},{5,1},{2,6},{6,2},{3,7},{7,3},{8,12},{12,8},{9,1... | collective-permute-start | bytes 129032 | tf_op jit(solution)/shard_map/ppermute | solution.py:635
  271.7 6.8 %collective-permute-start.42 = (f32[84,128]{1,0:T(8,128)S(1)}, f32[84,128]{1,0:T(8,128)S(1)}, u32[]{:S(2)}, u32[]{:S(2)}) collective-permute-start(f32[84,128]{1,0:T(8,128)S(1)} %add.262), channel_id=1, source_target_pairs={{0,8},{8,0},{16,24},{24,16},{1,9},{9,1},{17,25},{25,17},{2,10},{10... | collective-permute-start | bytes 129032 | tf_op jit(solution)/shard_map/ppermute | solution.py:643
  278.2 27.1 %collective-permute-start.30 = (bf16[4,96,576]{2,1,0:T(8,128)(2,1)S(1)}, bf16[4,96,576]{2,1,0:T(8,128)(2,1)}, u32[]{:S(2)}, u32[]{:S(2)}) collective-permute-start(bf16[4,96,576]{2,1,0:T(8,128)(2,1)S(1)} %get-tuple-element.128), channel_id=1, source_target_pairs={{0,4},{4,0},{1,5},{5,1},{2,6},{6,2},{3,7},{7,3},{8,12},{12,8},{9,1... | collective-permute-start | bytes 1327112 | tf_op jit(solution)/shard_map/ppermute | solution.py:635
  278.6 3.9 %collective-permute-start.43 = (f32[84,128]{1,0:T(8,128)S(1)}, f32[84,128]{1,0:T(8,128)S(1)}, u32[]{:S(2)}, u32[]{:S(2)}) collective-permute-start(f32[84,128]{1,0:T(8,128)S(1)} %add.263), channel_id=1, source_target_pairs={{0,16},{8,24},{16,0},{24,8},{1,17},{9,25},{17,1},{25,9},{2,18},{10... | collective-permute-start | bytes 129032 | tf_op jit(solution)/shard_map/ppermute | solution.py:643
  285.8 15.9 %collective-permute-start.27 = (bf16[512,768]{1,0:T(8,128)(2,1)}, bf16[512,768]{1,0:T(8,128)(2,1)}, u32[]{:S(2)}, u32[]{:S(2)}) collective-permute-start(bf16[512,768]{1,0:T(8,128)(2,1)} %add_convert_fusion), channel_id=1, source_target_pairs={{0,2},{1,3},{2,0},{3,1},{4,6},{5,7},{6,4},{7,5},{8,10},{9,11},{10,... | collective-permute-start | bytes 2359304 | tf_op jit(solution)/shard_map/ppermute | solution.py:639
  286.5 17.5 %collective-permute-start.25 = (bf16[512,768]{1,0:T(8,128)(2,1)}, bf16[512,768]{1,0:T(8,128)(2,1)}, u32[]{:S(2)}, u32[]{:S(2)}) collective-permute-start(bf16[512,768]{1,0:T(8,128)(2,1)} %add_convert_fusion), channel_id=1, source_target_pairs={{0,1},{1,0},{2,3},{3,2},{4,5},{5,4},{6,7},{7,6},{8,9},{9,8},{10,11... | collective-permute-start | bytes 2359304 | tf_op jit(solution)/shard_map/ppermute | solution.py:639
  292.1 47.5 %collective-permute-start.34 = (bf16[4,96,768]{2,1,0:T(8,128)(2,1)S(1)}, bf16[4,96,768]{2,1,0:T(8,128)(2,1)S(1)}, u32[]{:S(2)}, u32[]{:S(2)}) collective-permute-start(bf16[4,96,768]{2,1,0:T(8,128)(2,1)S(1)} %pad_maximum_fusion.6), channel_id=1, source_target_pairs={{0,1},{1,0},{2,3},{3,2},{4,5},{5,4},{6,7},{7,6},{8,9},{9,8},{10,11... | collective-permute-start | bytes 1769480 | tf_op jit(solution)/shard_map/ppermute | solution.py:639
  293.3 52.1 %collective-permute-start.35 = (bf16[4,96,768]{2,1,0:T(8,128)(2,1)S(1)}, bf16[4,96,768]{2,1,0:T(8,128)(2,1)S(1)}, u32[]{:S(2)}, u32[]{:S(2)}) collective-permute-start(bf16[4,96,768]{2,1,0:T(8,128)(2,1)S(1)} %pad_maximum_fusion.7), channel_id=1, source_target_pairs={{0,2},{1,3},{2,0},{3,1},{4,6},{5,7},{6,4},{7,5},{8,10},{9,11},{10,... | collective-permute-start | bytes 1769480 | tf_op jit(solution)/shard_map/ppermute | solution.py:639
  302.8 28.2 %collective-permute-start.28 = (bf16[256,768]{1,0:T(8,128)(2,1)S(1)}, bf16[256,768]{1,0:T(8,128)(2,1)S(1)}, u32[]{:S(2)}, u32[]{:S(2)}) collective-permute-start(bf16[256,768]{1,0:T(8,128)(2,1)S(1)} %slice.288), channel_id=1, source_target_pairs={{0,1},{1,0},{2,3},{3,2},{4,5},{5,4},{6,7},{7,6},{8,9},{9,8},{10,11... | collective-permute-start | bytes 1179656 | tf_op jit(solution)/shard_map/ppermute | solution.py:639
  305.0 19.2 %collective-permute-start.26 = (bf16[256,768]{1,0:T(8,128)(2,1)S(1)}, bf16[256,768]{1,0:T(8,128)(2,1)S(1)}, u32[]{:S(2)}, u32[]{:S(2)}) collective-permute-start(bf16[256,768]{1,0:T(8,128)(2,1)S(1)} %slice.287), channel_id=1, source_target_pairs={{0,2},{1,3},{2,0},{3,1},{4,6},{5,7},{6,4},{7,5},{8,10},{9,11},{10,... | collective-permute-start | bytes 1179656 | tf_op jit(solution)/shard_map/ppermute | solution.py:639
  305.3 25.8 %copy-start.55 = (bf16[512,768]{1,0:T(8,128)(2,1)S(1)}, bf16[512,768]{1,0:T(8,128)(2,1)}, u32[]{:S(2)}) copy-start(bf16[512,768]{1,0:T(8,128)(2,1)} %copy-done.54) | copy-start | bytes 2359300
  306.5 24.5 %copy-start.37 = (bf16[512,768]{1,0:T(8,128)(2,1)S(1)}, bf16[512,768]{1,0:T(8,128)(2,1)}, u32[]{:S(2)}) copy-start(bf16[512,768]{1,0:T(8,128)(2,1)} %copy-done.36) | copy-start | bytes 2359300
  306.5 24.5 %copy-start.53 = (bf16[512,768]{1,0:T(8,128)(2,1)S(1)}, bf16[512,768]{1,0:T(8,128)(2,1)}, u32[]{:S(2)}) copy-start(bf16[512,768]{1,0:T(8,128)(2,1)} %copy-done.52) | copy-start | bytes 2359300
  306.6 42.4 %collective-permute-start.31 = (bf16[96,576]{1,0:T(8,128)(2,1)S(1)}, bf16[96,576]{1,0:T(8,128)(2,1)S(1)}, u32[]{:S(2)}, u32[]{:S(2)}) collective-permute-start(bf16[96,576]{1,0:T(8,128)(2,1)S(1)} %get-tuple-element.183), channel_id=1, source_target_pairs={{0,8},{8,0},{16,24},{24,16},{1,9},{9,1},{17,25},{25,17},{2,10},{10... | collective-permute-start | bytes 331784 | tf_op jit(solution)/shard_map/ppermute | solution.py:643
  324.1 25.2 %collective-permute-start.33 = (bf16[96,576]{1,0:T(8,128)(2,1)S(1)}, bf16[96,576]{1,0:T(8,128)(2,1)S(1)}, u32[]{:S(2)}, u32[]{:S(2)}) collective-permute-start(bf16[96,576]{1,0:T(8,128)(2,1)S(1)} %get-tuple-element.184), channel_id=1, source_target_pairs={{0,24},{8,16},{16,8},{24,0},{1,25},{9,17},{17,9},{25,1},{2,26},{10... | collective-permute-start | bytes 331784 | tf_op jit(solution)/shard_map/ppermute | solution.py:643
  335.1 31.5 %collective-permute-start.29 = (bf16[1024,768]{1,0:T(8,128)(2,1)}, bf16[1024,768]{1,0:T(8,128)(2,1)}, u32[]{:S(2)}, u32[]{:S(2)}) collective-permute-start(bf16[1024,768]{1,0:T(8,128)(2,1)} %get-tuple-element.165), channel_id=1, source_target_pairs={{0,4},{4,0},{1,5},{5,1},{2,6},{6,2},{3,7},{7,3},{8,12},{12,8},{9,1... | collective-permute-start | bytes 4718600 | tf_op jit(solution)/shard_map/ppermute | solution.py:635
  339.6 12.0 %collective-permute-start.32 = (bf16[96,576]{1,0:T(8,128)(2,1)S(1)}, bf16[96,576]{1,0:T(8,128)(2,1)S(1)}, u32[]{:S(2)}, u32[]{:S(2)}) collective-permute-start(bf16[96,576]{1,0:T(8,128)(2,1)S(1)} %get-tuple-element.185), channel_id=1, source_target_pairs={{0,16},{8,24},{16,0},{24,8},{1,17},{9,25},{17,1},{25,9},{2,18},{10... | collective-permute-start | bytes 331784 | tf_op jit(solution)/shard_map/ppermute | solution.py:643
  345.4 25.0 %collective-permute-start.18 = (bf16[1024,768]{1,0:T(8,128)(2,1)}, bf16[1024,768]{1,0:T(8,128)(2,1)}, u32[]{:S(2)}, u32[]{:S(2)}) collective-permute-start(bf16[1024,768]{1,0:T(8,128)(2,1)} %get-tuple-element.171), channel_id=1, source_target_pairs={{0,4},{4,0},{1,5},{5,1},{2,6},{6,2},{3,7},{7,3},{8,12},{12,8},{9,1... | collective-permute-start | bytes 4718600 | tf_op jit(solution)/shard_map/ppermute | solution.py:635
  349.0 5.6 %collective-permute-start.36 = (bf16[96,768]{1,0:T(8,128)(2,1)}, bf16[96,768]{1,0:T(8,128)(2,1)}, u32[]{:S(2)}, u32[]{:S(2)}) collective-permute-start(bf16[96,768]{1,0:T(8,128)(2,1)} %get-tuple-element.178), channel_id=1, source_target_pairs={{0,8},{8,0},{16,24},{24,16},{1,9},{9,1},{17,25},{25,17},{2,10},{10... | collective-permute-start | bytes 442376 | tf_op jit(solution)/shard_map/ppermute | solution.py:643
  349.3 9.9 %collective-permute-start.38 = (bf16[96,768]{1,0:T(8,128)(2,1)}, bf16[96,768]{1,0:T(8,128)(2,1)}, u32[]{:S(2)}, u32[]{:S(2)}) collective-permute-start(bf16[96,768]{1,0:T(8,128)(2,1)} %get-tuple-element.179), channel_id=1, source_target_pairs={{0,24},{8,16},{16,8},{24,0},{1,25},{9,17},{17,9},{25,1},{2,26},{10... | collective-permute-start | bytes 442376 | tf_op jit(solution)/shard_map/ppermute | solution.py:643
  351.7 13.7 %collective-permute-start.37 = (bf16[96,768]{1,0:T(8,128)(2,1)}, bf16[96,768]{1,0:T(8,128)(2,1)}, u32[]{:S(2)}, u32[]{:S(2)}) collective-permute-start(bf16[96,768]{1,0:T(8,128)(2,1)} %get-tuple-element.180), channel_id=1, source_target_pairs={{0,16},{8,24},{16,0},{24,8},{1,17},{9,25},{17,1},{25,9},{2,18},{10... | collective-permute-start | bytes 442376 | tf_op jit(solution)/shard_map/ppermute | solution.py:643
  (55 other events, 181.1 us)
Sparse Core Ops, SparseCore 0:
  11.6 99.4 all-gather.1
  194.6 123.4 reduce-scatter.1

commit v4 on v3

--- a/solution.py
+++ b/solution.py
@@ -365,7 +365,7 @@
         acc[sl, :] += nt(a, w[0, :, hidden:])
         return 0
 
-    lax.fori_loop(0, share // ROWS, rows_step, 0)
+    lax.fori_loop(0, share // ROWS, rows_step, 0, unroll=True)
 
     @pl.when(k == 3)
     def _():
@@ -396,7 +396,7 @@
     share, width = tokb.shape
     hidden = bias.shape[1]
     block = lambda: pl.BlockSpec((1, share, hidden), lambda i, s: (i, 0, 0))
-    sd = jax.ShapeDtypeStruct
+    sd, far = jax.ShapeDtypeStruct, pltpu.HBM
     return pl.pallas_call(
         feed_kernel,
         grid_spec=pltpu.PrefetchScalarGridSpec(
@@ -419,10 +419,10 @@
             sd((share, width), F32),
             sd((share, width), BF),
             sd((share, width), F32),
-            sd((width, share), BF),
-            sd((width, share), BF),
-            sd((4, share, hidden), BF),
-            sd((4, share, hidden), F32),
+            far((width, share), BF),
+            far((width, share), BF),
+            far((4, share, hidden), BF),
+            far((4, share, hidden), F32),
             sd((share, 128), F32),
             sd((8, width), F32),
         ],
@@ -452,7 +452,7 @@
         acc[sl, :] += nt(g, w[0, :, 0:hidden])
         return total + jnp.sum(g.astype(F32), axis=0, keepdims=True)
 
-    total = lax.fori_loop(0, share // ROWS, rows_step, jnp.zeros((1, hidden), F32))
+    total = lax.fori_loop(0, share // ROWS, rows_step, jnp.zeros((1, hidden), F32), unroll=True)
     ghs_o[0] = jnp.broadcast_to(total, (8, hidden))
 
     @pl.when(k == 3)
@@ -480,7 +480,7 @@
     share, width = gs.shape
     hidden = gp.shape[2]
     block = lambda: pl.BlockSpec((1, share, hidden), lambda i, s: (i, 0, 0))
-    sd = jax.ShapeDtypeStruct
+    sd, far = jax.ShapeDtypeStruct, pltpu.HBM
     return pl.pallas_call(
         feed_back_kernel,
         grid_spec=pltpu.PrefetchScalarGridSpec(
@@ -497,9 +497,9 @@
                 pltpu.SemaphoreType.DMA((4,)),
             ],
         ),
-        out_shape=[sd((share, width), F32), sd((width, share), BF)]
+        out_shape=[far((share, width), F32), far((width, share), BF)]
         + [sd((share, part), BF)] * 4
-        + [sd((4, share, hidden), BF), sd((4, 8, hidden), F32), sd((8, width), F32)],
+        + [far((4, share, hidden), BF), sd((4, 8, hidden), F32), sd((8, width), F32)],
         compiler_params=params(28),
         cost_estimate=COST,
         name="feed_back",
@@ -517,56 +517,52 @@
         far_o[(*lead, n, slice(None), cols)] = acc[far, source].astype(BF)
 
 
-def weights_kernel(per, place, nbt, gst, gh, act, *refs):
-    hh = gh.shape[2]
+def weights_kernel(per, place, nbt, gst, gft, ctx, gh, act, *refs):
+    hh = gh.shape[2] // 2
     if per > 1:
-        near_o, far_o, acc = refs
-        for n, (left, right) in enumerate(((nbt, gh), (gst, act))):
-            acc[...] = nn(left[...], right[0])
+        near_o, far_o, out, acc = refs
+    else:
+        other, out = refs
+    for n, (left, right) in enumerate(((nbt, gh), (gst, act))):
+        made = nn(left[...], right[0])
+        out[0, :, n * hh : (n + 1) * hh] = made[:, 0:hh].astype(BF)
+        if per > 1:
+            acc[...] = made[:, hh:]
             split_rows(place, per, acc, slice(None), near_o, far_o, (0,), slice(n * hh, (n + 1) * hh))
-        return
-    *more, out = refs
-    out[0, :, 0:hh] = nn(nbt[...], gh[0]).astype(BF)
-    out[0, :, hh : 2 * hh] = nn(gst[...], act[0]).astype(BF)
-    if more:
-        gft, ctx = more
-        out[0, :, 2 * hh :] = nn(gft[...], ctx[0]).astype(BF)
-
-
-def weight_grads(place, per, side, nbt, gst, gh, act, *more):
+        else:
+            other[0, :, n * hh : (n + 1) * hh] = made[:, hh:].astype(BF)
+    out[0, :, 2 * hh :] = nn(gft[...], ctx[0]).astype(BF)
+
+
+def weight_grads(place, per, nbt, gst, gft, contexts, gh, act):
     width, share = nbt.shape
-    hh = gh.shape[2] // 2
-    here = len(place.shape) and place.shape[0] - 1
-    block = pl.BlockSpec((1, share, hh), lambda i, s: (i, 0, side))
-    cols = 2 * hh
-    ins = [whole_block(nbt.shape), whole_block(gst.shape), block, block]
-    if more:
-        part = more[1].shape[2]
-        cols += part
-        ins += [whole_block(more[0].shape), pl.BlockSpec((1, share, part), lambda i, s: (i, 0, 0))]
+    hidden, part = gh.shape[2], contexts.shape[2]
+    last = place.shape[0] - 1
+    block = lambda cols: pl.BlockSpec((1, share, cols), lambda i, s: (i, 0, 0))
+    ordered = lambda cols: pl.BlockSpec((1, width, cols), lambda i, s: (i ^ s[last], 0, 0))
     if per > 1:
-        shape = (4, per // 2, width // per, cols)
+        shape = (4, per // 2, width // per, hidden)
         outs = [jax.ShapeDtypeStruct(shape, BF)] * 2
         specs = [pl.BlockSpec((1,) + shape[1:], lambda i, s: (i, 0, 0, 0))] * 2
-        scratch = [pltpu.VMEM((width, hh), F32)]
+        scratch = [pltpu.VMEM((width, hidden // 2), F32)]
     else:
-        outs = [jax.ShapeDtypeStruct((4, width, cols), BF)]
-        specs = [pl.BlockSpec((1, width, cols), lambda i, s: (i ^ s[here], 0, 0))]
+        outs = [jax.ShapeDtypeStruct((4, width, hidden), BF)]
+        specs = [ordered(hidden)]
         scratch = []
     return pl.pallas_call(
         partial(weights_kernel, per),
         grid_spec=pltpu.PrefetchScalarGridSpec(
             num_scalar_prefetch=1,
             grid=(4,),
-            in_specs=ins,
-            out_specs=specs,
+            in_specs=[whole_block(x.shape) for x in (nbt, gst, gft)] + [block(part), block(hidden), block(hidden)],
+            out_specs=specs + [ordered(hidden + part)],
             scratch_shapes=scratch,
         ),
-        out_shape=outs,
-        compiler_params=params(20),
+        out_shape=outs + [jax.ShapeDtypeStruct((4, width, hidden + part), BF)],
+        compiler_params=params(58),
         cost_estimate=COST,
         name="weight_grads",
-    )(place, nbt, gst, gh, act, *more)
+    )(place, nbt, gst, gft, contexts, gh, act)
 
 
 def qkv_weights_kernel(per, part, place, own, other, g, *refs):
@@ -611,6 +607,211 @@
         cost_estimate=COST,
         name="qkv_weight_grads",
     )(place, tokens, other, g)
+
+
+def branch_kernel(place, *refs):
+    count = (len(refs) - 1) // 2
+    w = refs[count]
+    for g, o in zip(refs[:count], refs[count + 1 :]):
+        rows = 256
+        for r in range(g.shape[0] // rows):
+            sl = slice(r * rows, (r + 1) * rows)
+            o[sl, :] = nt(g[sl, :], w[...]).astype(o.dtype)
+
+
+def branch(place, blocks, kinds, g, w):
+    share, last = g.shape[0] // 4, place.shape[0] - 1
+    return pl.pallas_call(
+        branch_kernel,
+        grid_spec=pltpu.PrefetchScalarGridSpec(
+            num_scalar_prefetch=1,
+            grid=(1,),
+            in_specs=[pl.BlockSpec((share, g.shape[1]), lambda i, s, k=k: (s[last] ^ k, 0)) for k in blocks] + [whole_block(w.shape)],
+            out_specs=[whole_block((share, w.shape[0]))] * len(blocks),
+        ),
+        out_shape=[jax.ShapeDtypeStruct((share, w.shape[0]), kind) for kind in kinds],
+        compiler_params=params(24),
+        cost_estimate=COST,
+        name="branch",
+    )(place, *[g] * len(blocks), w)
+
+
+def split_kernel(place, *refs):
+    keep, send, last = refs[5], refs[6], place.shape[0] - 1
+    share = refs[0].shape[0]
+    core, here = place[last - 1], place[last]
+
+    def put(out, sl, k):
+        if k < 3:
+            out[sl, :] = refs[k][...]
+        else:
+            half = share // 2
+            out[pl.ds(pl.multiple_of(sl.start, half), half), :] = refs[3][...]
+            out[pl.ds(pl.multiple_of(sl.start + half, half), half), :] = refs[4][...]
+
+    for k in range(4):
+        owner = here ^ k
+        sl = pl.ds(pl.multiple_of(owner % 2 * share, share), share)
+        mine = owner // 2 == core
+
+        @pl.when(mine)
+        def _(k=k, sl=sl):
+            put(keep, sl, k)
+
+        @pl.when(jnp.logical_not(mine))
+        def _(k=k, sl=sl):
+            put(send, sl, k)
+
+
+def split_halves(place, blocks):
+    share, width = blocks[0].shape
+    shape = (2 * share, width)
+    return pl.pallas_call(
+        split_kernel,
+        grid_spec=pltpu.PrefetchScalarGridSpec(
+            num_scalar_prefetch=1,
+            grid=(1,),
+            in_specs=[whole_block(x.shape) for x in blocks],
+            out_specs=[whole_block(shape)] * 2,
+        ),
+        out_shape=[jax.ShapeDtypeStruct(shape, blocks[0].dtype)] * 2,
+        compiler_params=params(12),
+        cost_estimate=COST,
+        name="split_halves",
+    )(place, *blocks)
+
+
+def join_kernel(place, keep, other, out):
+    @pl.when(pl.program_id(0) == place[place.shape[0] - 2])
+    def _():
+        out[0] = keep[...]
+
+    @pl.when(pl.program_id(0) != place[place.shape[0] - 2])
+    def _():
+        out[0] = other[...]
+
+
+def join_halves(place, keep, other):
+    return pl.pallas_call(
+        join_kernel,
+        grid_spec=pltpu.PrefetchScalarGridSpec(
+            num_scalar_prefetch=1,
+            grid=(2,),
+            in_specs=[whole_block(keep.shape), whole_block(other.shape)],
+            out_specs=pl.BlockSpec((1,) + keep.shape, lambda i, s: (i, 0, 0)),
+        ),
+        out_shape=jax.ShapeDtypeStruct((2,) + keep.shape, keep.dtype),
+        compiler_params=params(16),
+        cost_estimate=COST,
+        name="join_halves",
+    )(place, keep, other)
+
+
+def collect_kernel(place, hidden_sums, one, two, bias, out):
+    here = place[place.shape[0] - 1]
+    out[...] = jnp.zeros(out.shape, F32)
+    for k in range(4):
+        out[pl.ds(here ^ k, 1), :] = hidden_sums[k, 0:1, :]
+    for n, (x, row) in enumerate(((one, 0), (two, 0), (one, 1), (two, 1), (one, 2), (two, 2))):
+        out[4 + n : 5 + n, :] = x[row : row + 1, :]
+    out[pl.ds(10 + here, 1), :] = bias[0:1, :]
+
+
+def collect(place, hidden_sums, one, two, bias):
+    return pl.pallas_call(
+        collect_kernel,
+        grid_spec=pltpu.PrefetchScalarGridSpec(
+            num_scalar_prefetch=1,
+            grid=(1,),
+            in_specs=[whole_block(x.shape) for x in (hidden_sums, one, two, bias)],
+            out_specs=whole_block((16, one.shape[1])),
+        ),
+        out_shape=jax.ShapeDtypeStruct((16, one.shape[1]), F32),
+        compiler_params=params(8),
+        cost_estimate=COST,
+        name="collect",
+    )(place, hidden_sums, one, two, bias)
+
+
+def settle_kernel(count, *refs):
+    ins, outs = refs[:count], refs[count:]
+    for j, out in enumerate(outs):
+        total = ins[0][j].astype(F32)
+        for x in ins[1:]:
+            total = total + x[j].astype(F32)
+        out[...] = total.astype(out.dtype)
+
+
+def settle(*stacks):
+    shape = stacks[0].shape
+    vmem = pl.BlockSpec(memory_space=pltpu.VMEM)
+    return pl.pallas_call(
+        partial(settle_kernel, len(stacks)),
+        in_specs=[vmem] * len(stacks),
+        out_specs=[vmem] * shape[0],
+        out_shape=[jax.ShapeDtypeStruct(shape[1:], F32 if j == 0 else BF) for j in range(shape[0])],
+        compiler_params=pltpu.CompilerParams(vmem_limit_bytes=16 * 1024 * 1024),
+        cost_estimate=COST,
+        name="settle",
+    )(*stacks)
+
+
+def finish_kernel(*refs):
+    out = refs[-1]
+    total = refs[0][...]
+    for x in refs[1:-1]:
+        total = total + x[...].astype(F32)
+    out[...] = total
+
+
+def finish(*parts):
+    vmem = pl.BlockSpec(memory_space=pltpu.VMEM)
+    return pl.pallas_call(
+        finish_kernel,
+        in_specs=[vmem] * len(parts),
+        out_specs=vmem,
+        out_shape=jax.ShapeDtypeStruct(parts[0].shape, F32),
+        compiler_params=pltpu.CompilerParams(vmem_limit_bytes=8 * 1024 * 1024),
+        cost_estimate=COST,
+        name="finish",
+    )(*parts)
+
+
+def block_kernel(own, first, one, two, out):
+    out[...] = (own[...] + first[...] + one[...].astype(F32) + two[...].astype(F32)).astype(BF)
+
+
+def add_block(own, first, one, two):
+    vmem = pl.BlockSpec(memory_space=pltpu.VMEM)
+    return pl.pallas_call(
+        block_kernel,
+        in_specs=[vmem] * 4,
+        out_specs=vmem,
+        out_shape=jax.ShapeDtypeStruct(own.shape, BF),
+        compiler_params=pltpu.CompilerParams(vmem_limit_bytes=12 * 1024 * 1024),
+        cost_estimate=COST,
+        name="add_block",
+    )(own, first, one, two)
+
+
+def relay_kernel(one, two, low, high, one_o, two_o):
+    half = low.shape[0]
+    one_o[0:half, :] = (one[0:half, :] + low[...].astype(F32)).astype(BF)
+    one_o[half:, :] = one[half:, :].astype(BF)
+    two_o[0:half, :] = two[0:half, :].astype(BF)
+    two_o[half:, :] = (two[half:, :] + high[...].astype(F32)).astype(BF)
+
+
+def relay(one, two, low, high):
+    return pl.pallas_call(
+        relay_kernel,
+        in_specs=[pl.BlockSpec(memory_space=pltpu.VMEM)] * 4,
+        out_specs=[pl.BlockSpec(memory_space=pltpu.VMEM)] * 2,
+        out_shape=[jax.ShapeDtypeStruct(one.shape, BF)] * 2,
+        compiler_params=pltpu.CompilerParams(vmem_limit_bytes=16 * 1024 * 1024),
+        cost_estimate=COST,
+        name="relay",
+    )(one, two, low, high)
 
 
 def rotation_tables(offsets):
@@ -773,10 +974,7 @@
         sums_two,
     ) = feed_forward(place, gathered, contexts, tok_block, grad_top, vec, bias_all)
 
-    def finish_spread(full):
-        keep, send = take(full, c), take(full, 1 - c)
-        return by_core(keep, swap_ctx(send))
-
+    barrier = lax.optimization_barrier
     out_blocks = [layer_out, swap_tp(layer_out, 1), swap_tp(layer_out, 2)]
 
     grad_first, first_t, g0, g1, g2, g3, grad_hidden, hidden_sums, sums_one = feed_back(
@@ -785,74 +983,77 @@
     heads_grads = [g0, swap_tp(g1, 1), swap_tp(g2, 2), swap_tp(g3, 3)]
 
     contexts = jnp.stack(contexts)
-    normed_t, out_blocks = lax.optimization_barrier((normed_t, out_blocks))
-    made = weight_grads(place, per, 1, normed_t, second_t, grad_hidden, activated)
-    normed_t, made, heads_grads[1] = lax.optimization_barrier((normed_t, made, heads_grads[1]))
-    whole = weight_grads(place, 1, 0, normed_t, second_t, grad_hidden, activated, first_t, contexts)[0]
+    *made, whole = weight_grads(place, per, normed_t, second_t, first_t, contexts, grad_hidden, activated)
+    made, whole, heads_grads, out_blocks = barrier((made, whole, heads_grads, out_blocks))
     whole = lax.psum_scatter(whole.reshape(-1, 2 * hh + part), ("tp", "shard", "ctx"), scatter_dimension=0, tiled=True)
-    whole = whole.astype(F32)
+    corner = [swap_tp(out_blocks[1][: share // 2], 2), swap_tp(out_blocks[2][share // 2 :], 1)]
     grad_heads = jnp.stack(heads_grads)
-
-    spot = jnp.concatenate([(t * (share // BLOCK))[None].astype(jnp.int32), bounds])
     if direct:
         got = swap_ctx(made[1])
+        grad_heads, got = barrier((grad_heads, got))
         packs = [made[0][k].astype(F32) + got[k].astype(F32) for k in range(4)]
-        low, high = packs[3][:2].astype(BF), packs[3][2:].astype(BF)
-        grad_heads, low, high = lax.optimization_barrier((grad_heads, low, high))
-        low, high = swap_tp(low, 2), swap_tp(high, 1)
-    corner = [swap_tp(out_blocks[1][: share // 2], 2), swap_tp(out_blocks[2][share // 2 :], 1)]
+        sent = [packs[k].astype(BF) for k in (1, 2, 3)]
+        grad_heads, sent = barrier((grad_heads, sent))
+        sent = [swap_tp(sent[k - 1], k) for k in (1, 2, 3)]
+
+    spot = jnp.concatenate([(t * (share // BLOCK))[None].astype(jnp.int32), bounds])
     grad_proj, bias_sums = attention_backward(
         spot, q, k_rows, k_turned, v_rows, grad_heads, log_total, seg_column, seg_row, cosine, sine, heads
     )
-    proj_blocks = grad_proj.reshape(4, share, 3 * WIDE)
-    corner, proj_blocks = lax.optimization_barrier((corner, proj_blocks))
-    out_blocks = [*out_blocks, jnp.concatenate(corner)]
-    branch = {3: contract_last(take(proj_blocks, t ^ 3), qkv_wide)}
+    grad_proj, bias_sums, corner, hidden_sums, sums_one, sums_two = barrier((grad_proj, bias_sums, corner, hidden_sums, sums_one, sums_two))
     if direct:
-        branch[3], low, high = lax.optimization_barrier((branch[3], low, high))
-        one = jnp.concatenate([packs[1][:2] + low.astype(F32), packs[1][2:]]).astype(BF)
-        two = jnp.concatenate([packs[2][:2], packs[2][2:] + high.astype(F32)]).astype(BF)
-        summed = packs[0] + swap_tp(one, 1).astype(F32) + swap_tp(two, 2).astype(F32)
-        total = summed[0]
-        for j in (1, 2, 3):
-            total = total + swap_shard(summed[j].astype(BF), j).astype(F32)
+        grad_proj, sent, packs[0] = barrier((grad_proj, sent, packs[0]))
+
+    three = branch(place, (3,), (BF,), grad_proj, qkv_wide)[0]
+    three, grad_proj, corner, bias_sums = barrier((three, grad_proj, corner, bias_sums))
+    low, high = swap_tp(three[: share // 2], 2), swap_tp(three[share // 2 :], 1)
+    one, two, own = branch(place, (1, 2, 0), (F32, F32, F32), grad_proj, qkv_wide)
+    keep, send = split_halves(place, [*out_blocks, *corner])
+    small = collect(place, hidden_sums, sums_one, sums_two, bias_sums)
+    low, high, one, two, own, keep, send, grad_proj, small = barrier((low, high, one, two, own, keep, send, grad_proj, small))
+
+    one, two = relay(one, two, low, high)
+    one, two, send, keep, grad_proj, small = barrier((one, two, send, keep, grad_proj, small))
+    one, two = swap_tp(one, 1), swap_tp(two, 2)
+    grads = qkv_weight_grads(place, per, tokens, other_tokens, grad_proj, part)
+    outputs = join_halves(place, keep, swap_ctx(send))
+    small = sum_shard(small + swap_ctx(small))
+    if direct:
+        summed, *pieces = settle(packs[0], *sent)
+        qkv_sum, *qkv_pieces = settle(grads[0], swap_ctx(grads[1]))
+        one, two, own, small, outputs, summed, pieces, qkv_sum, qkv_pieces = barrier(
+            (one, two, own, small, outputs, summed, pieces, qkv_sum, qkv_pieces)
+        )
     else:
+        one, two, own, small, outputs = barrier((one, two, own, small, outputs))
+
+    block = add_block(own, grad_first, one, two)
+    ready = [block, swap_tp(block, 1), swap_tp(block, 2)]
+    small = small + swap_tp(small, 1)
+    if direct:
+        total = finish(summed, *[swap_shard(pieces[j - 1], j) for j in (1, 2, 3)])
+        ready, total, small, qkv_pieces = barrier((ready, total, small, qkv_pieces))
+    corner = [swap_tp(ready[1][: share // 2], 2), swap_tp(ready[2][share // 2 :], 1)]
+    if direct:
+        qkv_total = finish(qkv_sum, *[swap_shard(qkv_pieces[j - 1], j) for j in (1, 2, 3)])
+    else:
+        qkv_total = lax.psum_scatter(grads[0], ("shard", "ctx"), scatter_dimension=0, tiled=True)
         total = lax.psum_scatter(made[0].reshape(-1, 2 * hh), ("tp", "shard", "ctx"), scatter_dimension=0, tiled=True).astype(F32)
+    small = small + swap_tp(small, 2)
+    qkv_total = qkv_total.reshape(rows, 3, part)
+    corner, qkv_total, total, small = barrier((corner, qkv_total, total, small))
+    keep, send = split_halves(place, [*ready, *corner])
+    grad_tokens = join_halves(place, keep, swap_ctx(send))
+
+    grad_qkv_weight = qkv_total
+    whole = whole.astype(F32)
     grad_up = jnp.concatenate([whole[:, :hh], total[:, :hh]], axis=1)
     grad_down = jnp.concatenate([whole[:, hh : 2 * hh], total[:, hh:]], axis=1)
     grad_ffn_weight = jnp.stack([grad_up, grad_down], axis=1)
     grad_out_weight = whole[:, 2 * hh :]
-
-    for k in (1, 2, 0):
-        branch[k] = contract_last(take(proj_blocks, t ^ k), qkv_wide)
-    grad_branch = scatter_tp([branch[k] for k in range(4)])
-    grad_blocks = gather_tp((grad_first + grad_branch).astype(BF), share // 2)
-    grad_full = order_four(grad_blocks, t).reshape(2, half_len, width)
-
-    grads = qkv_weight_grads(after(place, branch[0]), per, tokens, other_tokens, grad_proj, part)
-    if direct:
-        summed = grads[0] + swap_ctx(grads[1]).astype(F32)
-        total = summed[0]
-        for j in (1, 2, 3):
-            total = total + swap_shard(summed[j].astype(BF), j).astype(F32)
-    else:
-        total = lax.psum_scatter(grads[0], ("shard", "ctx"), scatter_dimension=0, tiled=True)
-    grad_qkv_weight = total.reshape(rows, 3, part)
-
-    sums = order_four([hidden_sums[k, 0] for k in range(4)], t).reshape(4 * hidden)
-    vectors = jnp.stack([sums_one[0], sums_two[0], sums_one[1], sums_two[1], sums_one[2], sums_two[2]])
-    mine = bias_sums[0].reshape(3, WIDE)
-    others = jnp.where(jnp.arange(4)[:, None, None] == t, mine[None], 0.0)
-    small = jnp.concatenate([sums, vectors.reshape(-1), others.reshape(-1)]).reshape(-1, 128)
-    for k in (1, 2):
-        small = small + swap_tp(small, k)
-    small = sum_shard(small + swap_ctx(small))
-    cut, end = 4 * hidden // 128, (4 * hidden + 6 * width) // 128
-    grad_ffn_bias = take(small[:cut].reshape(4, hidden), t)
-    vectors = small[cut:end].reshape(6, width)
-    grad_qkv_bias = take(small[end:].reshape(4, 3, WIDE), t)[:, :part]
-    outputs = finish_spread(order_four(out_blocks, t).reshape(2, half_len, width))
-    grad_tokens = finish_spread(grad_full)
+    grad_ffn_bias = take(small, t)
+    vectors = small[4:10]
+    grad_qkv_bias = take(small[10:14], t).reshape(3, WIDE)[:, :part]
     return (
         outputs,
         grad_tokens,

time: 385 us -> 339 us (0.88)
  other arithmetic: 43.4 us -> 17 us
  local copies, waits for them, and re-layouts: 65.8 us -> 48.4 us
  Pallas kernels: 109 us -> 121 us
  waiting for transfers between devices: 83.8 us -> 72 us
  matrix products: 7.4 us -> 0 us
    ppermute x24 -> x23, waiting for transfers between devices: 39 us -> 20.1 us  [swap_tp(): return lax.ppermute(x, 'tp', [(i, i ^ k) for i in range(4)])]
    pallas_call x0 -> x13, Pallas kernels: none -> 15.8 us  [the longest x2 5.36 us: split_halves(): pl.pallas_call(split_kernel, grid_spec=pltpu.PrefetchScalarGridSpec(num_s...]
    ppermute x9, starting transfers between devices: 11.6 us -> 20 us  [swap_ctx(): return lax.ppermute(x, 'ctx', [(0, 1), (1, 0)])]
    select_n x3 -> x1, other arithmetic: 7.59 us -> 0.03 us  [by_core(): jnp.where(first_core, jnp.stack([own, other]), jnp.stack([other, own]))]
    dot_general x4 -> x0, matrix products: 7.4 us -> none  [contract_last(): lax.dot_general(left, right, (((1,), (1,)), ((), ())), preferred_element_...]
    another operation x7 -> x1, other arithmetic: 6.95 us -> 0.71 us
    slice x10 -> x3, local copies, waits for them, and re-layouts: 6.82 us -> 1.6 us  [the longest x1 0.77 us: body(): ready[1][:share // 2]]
    ppermute x11, starting transfers between devices: 29 us -> 24.1 us  [swap_shard(): return lax.ppermute(x, 'shard', [(i, i ^ k) for i in range(4)])]
  transfers between devices with their start and end apart: 46 -> 45, of which waited for: 10 -> 16; matrix products, arithmetic and copies ran while one was open for 21% -> 9% of each run, Pallas kernels for 24% -> 31%
where the time goes in v4:
time: 339 us; the launch traced here: 335 us
  Pallas kernels  121 us (36%)
  waiting for transfers between devices  72 us (21%)
  starting transfers between devices  62.5 us (18%)
  local copies, waits for them, and re-layouts  48.4 us (14%)
  other arithmetic  17 us (5%)
  between operations  14.9 us (4%)
    all_gather x1, waiting for transfers between devices, body(): lax.all_gather(gathered, ('tp', 'shard', 'ctx'), axis=0, tiled=True)  34.8 us
    unnamed x130, local copies, waits for them, and re-layouts  32.6 us
    pallas_call x1, Pallas kernels, attention_backward(): pl.pallas_call(partial(backward_kernel, heads), grid_spec=pltpu.PrefetchS...  28.3 us
    pallas_call x4, Pallas kernels, attention_forward(): pl.pallas_call(partial(forward_kernel, heads), grid_spec=pltpu.PrefetchSc...  26.1 us
    ppermute x11, starting transfers between devices, swap_shard(): return lax.ppermute(x, 'shard', [(i, i ^ k) for i in range(4)])  24.1 us
    ppermute x23, waiting for transfers between devices, swap_tp(): return lax.ppermute(x, 'tp', [(i, i ^ k) for i in range(4)])  20.1 us
    ppermute x9, starting transfers between devices, swap_ctx(): return lax.ppermute(x, 'ctx', [(0, 1), (1, 0)])  20 us
    ppermute x23, starting transfers between devices, swap_tp(): return lax.ppermute(x, 'tp', [(i, i ^ k) for i in range(4)])  18.3 us
  transfers between devices with their start and end apart: 45, of which 16 were waited for; matrix products, arithmetic and copies ran while one was open for 9% of the time, Pallas kernels for 31%

profile of v4, /device:TPU:1, one launch (start us, length us, event | category | flops | bytes accessed | tf_op | source)
XLA Modules:
  0.0 335.4 jit_solution(16433186454358881231)
XLA Ops:
  9.2 1.6 concatenate.29
  11.3 4.2 %collective-permute-start.3 = (bf16[96,576]{1,0:T(8,128)(2,1)S(1)}, bf16[96,576]{1,0:T(8,128)(2,1)S(1)}, u32[]{:S(2)}, u32[]{:S(2)}) collective-permute-start(bf16[96,576]{1,0:T(8,128)(2,1)S(1)} %copy.34.refs_0_), channel_id=1, source_target_pairs={{0,24},{8,16},{16,8},{24,0},{1,25},{9,17},{17,9},{25,1},{2,26},{10... | collective-permute-start | bytes 331784 | tf_op jit(solution)/shard_map/ppermute | solution.py:844
  15.9 1.3 collective-permute-start
  17.2 2.7 dynamic-slice_bitcast_fusion
  20.1 2.1 dynamic-slice_bitcast_fusion.1
  24.1 1.3 collective-permute-done.2.refs_2_
  25.6 1.5 collective-permute-start.4
  27.1 3.7 %fusion = (f32[2048,128]{1,0:T(8,128)S(1)}, f32[2048,128]{1,0:T(8,128)S(1)}) fusion(f32[128]{0:T(128)S(1)} %copy-done.59, f32[128]{0:T(128)S(1)} %copy-done.58, f32[2048]{0:T(1024)S(1)} %bitcast.139), kind=kLoop, calls=%fused_computation.8 | loop fusion | flops 524288 | bytes 2106368 | tf_op jit(solution)/shard_map/mul | solution.py:822
  30.9 1.1 copy-done.6
  32.0 1.9 copy-done.4
  33.9 1.4 copy-done.7
  36.2 5.1 %project_qkv.1 = (bf16[2048,256]{1,0:T(8,128)(2,1)S(1)}, bf16[2048,256]{1,0:T(8,128)(2,1)S(1)}, bf16[2048,256]{1,0:T(8,128)(2,1)S(1)}, bf16[256,2048]{1,0:T(8,128)(2,1)S(1)}, bf16[768,768]{1,0:T(8,128)(2,1)S(1)}) custom-call(s32[10]{0:T(128)S(1)} %stack.143.place, bf16[96,576]{1,0:T(8,128)(2,1)S(1)} %copy.34.refs_0_, bf16[96,576]{1,0:T(8,128)(2,1)S(1)} %copy-done.32, ...), custom_call_target="tpu_custom_call" | custom-call | tf_op jit(solution)/shard_map/project_qkv/pallas_call | solution.py:93
  43.3 6.0 %attention_forward.4 = (bf16[512,192]{1,0:T(8,128)(2,1)S(1)}, f32[8,512]{1,0:T(8,128)S(1)}) custom-call(s32[17]{0:T(128)S(1)} %get-tuple-element.333.place, bf16[2048,256]{1,0:T(8,128)(2,1)S(1)} %get-tuple-element.158.q, bf16[2048,256]{1,0:T(8,128)(2,1)S(1)} %get-tuple-element.148.k, bf16[2048,256]{1,0:T(8,128)(2,1)S(1)} %get-tuple-element.150.v, ...), custom_call_target="tpu_custom_call" | custom-call | tf_op jit(solution)/shard_map/attention_forward/pallas_call | solution.py:168
  49.4 1.5 collective-permute-start.6
  50.9 6.7 %attention_forward.5 = (bf16[512,192]{1,0:T(8,128)(2,1)S(1)}, f32[8,512]{1,0:T(8,128)S(1)}) custom-call(s32[17]{0:T(128)S(1)} %get-tuple-element.335.place, bf16[2048,256]{1,0:T(8,128)(2,1)S(1)} %get-tuple-element.158.q, bf16[2048,256]{1,0:T(8,128)(2,1)S(1)} %get-tuple-element.148.k, bf16[2048,256]{1,0:T(8,128)(2,1)S(1)} %get-tuple-element.150.v, ...), custom_call_target="tpu_custom_call" | custom-call | tf_op jit(solution)/shard_map/attention_forward/pallas_call | solution.py:168
  58.0 2.3 bitcast_select_fusion.gtop
  61.3 8.0 %attention_forward.6 = (bf16[512,192]{1,0:T(8,128)(2,1)}, f32[8,512]{1,0:T(8,128)S(1)}) custom-call(s32[17]{0:T(128)S(1)} %get-tuple-element.334.place, bf16[2048,256]{1,0:T(8,128)(2,1)S(1)} %get-tuple-element.158.q, bf16[2048,256]{1,0:T(8,128)(2,1)S(1)} %get-tuple-element.148.k, bf16[2048,256]{1,0:T(8,128)(2,1)S(1)} %get-tuple-element.150.v, ...), custom_call_target="tpu_custom_call" | custom-call | tf_op jit(solution)/shard_map/attention_forward/pallas_call | solution.py:168
  70.6 5.3 %attention_forward.7 = (bf16[512,192]{1,0:T(8,128)(2,1)S(1)}, f32[8,512]{1,0:T(8,128)S(1)}) custom-call(s32[17]{0:T(128)S(1)} %get-tuple-element.336.place, bf16[2048,256]{1,0:T(8,128)(2,1)S(1)} %get-tuple-element.158.q, bf16[2048,256]{1,0:T(8,128)(2,1)S(1)} %get-tuple-element.148.k, bf16[2048,256]{1,0:T(8,128)(2,1)S(1)} %get-tuple-element.150.v, ...), custom_call_target="tpu_custom_call" | custom-call | tf_op jit(solution)/shard_map/attention_forward/pallas_call | solution.py:168
  76.7 34.8 %all-gather.2.cloned.1.call-done = bf16[3072,1792]{1,0:T(8,128)(2,1)} async-done(((bf16[96,1792]{1,0:T(8,128)(2,1)}), bf16[3072,1792]{1,0:T(8,128)(2,1)}) %all-gather.2.cloned.1.call-update) | async-done | bytes 11010064 | tf_op jit(solution)/shard_map/all_gather | solution.py:915
  111.5 1.7 convert_reduce_fusion
  113.3 4.1 %copy-done = bf16[3072,1792]{1,0:T(8,128)(2,1)S(1)} copy-done((bf16[3072,1792]{1,0:T(8,128)(2,1)S(1)}, bf16[3072,1792]{1,0:T(8,128)(2,1)}, u32[]{:S(2)}) %copy-start) | copy-done | bytes 11010072
  118.5 1.1 copy-done.17
  121.6 17.7 %feed_forward.1 = (bf16[512,768]{1,0:T(8,128)(2,1)}, f32[512,768]{1,0:T(8,128)S(1)}, bf16[512,768]{1,0:T(8,128)(2,1)S(1)}, f32[512,768]{1,0:T(8,128)S(1)}, bf16[...) custom-call(s32[10]{0:T(128)S(1)} %stack.143.place, ...), custom_call_target="tpu_custom_call" | custom-call | tf_op jit(solution)/shard_map/feed_forward/pallas_call | solution.py:400
  141.9 2.8 copy-done.13
  144.6 1.1 copy-done.30
  146.7 11.4 %feed_back.1 = (f32[512,768]{1,0:T(8,128)}, bf16[768,512]{1,0:T(8,128)(2,1)}, bf16[512,192]{1,0:T(8,128)(2,1)S(1)}, bf16[512,192]{1,0:T(8,128)(2,1)}, bf16[512,1...) custom-call(s32[10]{0:T(128)S(1)} %stack.143.place, ...), custom_call_target="tpu_custom_call" | custom-call | tf_op jit(solution)/shard_map/feed_back/pallas_call | solution.py:484
  158.7 1.5 collective-permute-start.11
  160.9 2.2 pad_maximum_fusion.ctx
  163.1 12.1 %weight_grads.1 = (bf16[4,4,96,768]{3,2,1,0:T(8,128)(2,1)}, bf16[4,4,96,768]{3,2,1,0:T(8,128)(2,1)}, bf16[4,768,960]{2,1,0:T(8,128)(2,1)}) custom-call(s32[10]{0:T(128)} %copy-done.39, bf16[768,512]{1,0:T(8,128)(2,1)} %get-tuple-element.163.nbt, bf16[768,512]{1,0:T(8,128)(2,1)} %get-tuple-element.164.gst, bf16[768,512]{1,0:T(8,128)(2,1)} %get-tuple-element.170.gft, ...), custom_call_target="tpu_custom_call" | custom-call | tf_op jit(solution)/shard_map/weight_grads/pallas_call | solution.py:552
  175.3 1.7 collective-permute-start.15
  178.0 1.3 pad_maximum_fusion.1.do
  179.3 2.2 collective-permute-done.15
  181.5 3.2 add_bitcast_fusion
  185.2 1.5 collective-permute-start.19
  190.1 1.5 collective-permute-start.16
  191.6 28.3 %attention_backward.1 = (bf16[2048,768]{1,0:T(8,128)(2,1)S(1)}, f32[8,768]{1,0:T(8,128)S(1)}) custom-call(s32[17]{0:T(128)S(1)} %get-tuple-element.336.place, bf16[2048,256]{1,0:T(8,128)(2,1)S(1)} %get-tuple-element.158.q, bf16[2048,256]{1,0:T(8,128)(2,1)S(1)} %get-tuple-element.148.k, bf16[256,2048]{1,0:T(8,128)(2,1)S(1)} %copy-done.28, ...), custom_call_target="tpu_custom_call" | custom-call | tf_op jit(solution)/shard_map/attention_backward/pallas_call | solution.py:274
  220.7 1.4 branch.2
  223.9 2.6 branch.3
  226.5 2.4 split_halves.2
  229.6 3.5 %collective-permute-done.22.high = bf16[256,768]{1,0:T(8,128)(2,1)S(1)} collective-permute-done((bf16[256,768]{1,0:T(8,128)(2,1)S(1)}, bf16[256,768]{1,0:T(8,128)(2,1)S(1)}, u32[]{:S(2)}, u32[]{:S(2)}) %collective-permute-start.22) | collective-permute-done | bytes 393248 | tf_op jit(solution)/shard_map/ppermute | solution.py:840
  233.1 2.9 collective-permute-done.21.low
  236.2 8.8 %collective-permute-start.28 = (bf16[1024,768]{1,0:T(8,128)(2,1)S(1)}, bf16[1024,768]{1,0:T(8,128)(2,1)S(1)}, u32[]{:S(2)}, u32[]{:S(2)}) collective-permute-start(bf16[1024,768]{1,0:T(8,128)(2,1)S(1)} %get-tuple-element.239), channel_id=1, source_target_pairs={{0,4},{4,0},{1,5},{5,1},{2,6},{6,2},{3,7},{7,3},{8,12},{12,8},{9,1... | collective-permute-start | bytes 4718600 | tf_op jit(solution)/shard_map/ppermute | solution.py:836
  246.7 4.0 %qkv_weight_grads.1 = (f32[4,96,576]{2,1,0:T(8,128)S(1)}, bf16[4,96,576]{2,1,0:T(8,128)(2,1)S(1)}) custom-call(s32[10]{0:T(128)S(1)} %copy-done.40, bf16[2,1024,768]{2,1,0:T(8,128)(2,1)S(1)} %copy-done.5, bf16[1024,768]{1,0:T(8,128)(2,1)S(1)} %copy-done.8, bf16[2048,768]{1,0:T(8,128)(2,1)S(1)} %get-tuple-element.248.refs_0_.refs_1_.refs_2_.g), custom_call_target="tpu_custom_call" | custom-call | tf_op jit(solution)/shard_map/qkv_weight_grads/pallas_call | solution.py:596
  251.5 1.5 collective-permute-done.25
  253.0 2.9 collective-permute-start.26
  255.9 1.8 collective-permute-done.26
  258.0 3.5 %collective-permute-done.27 = f32[16,768]{1,0:T(8,128)S(1)} collective-permute-done((f32[16,768]{1,0:T(8,128)S(1)}, f32[16,768]{1,0:T(8,128)S(1)}, u32[]{:S(2)}, u32[]{:S(2)}) %collective-permute-start.27) | collective-permute-done | bytes 49184 | tf_op jit(solution)/shard_map/ppermute | solution.py:844
  261.7 2.3 join_halves.2
  264.8 1.5 collective-permute-start.31
  267.7 3.7 %collective-permute-start.32 = (bf16[96,768]{1,0:T(8,128)(2,1)S(1)}, bf16[96,768]{1,0:T(8,128)(2,1)S(1)}, u32[]{:S(2)}, u32[]{:S(2)}) collective-permute-start(bf16[96,768]{1,0:T(8,128)(2,1)S(1)} %get-tuple-element.261), channel_id=1, source_target_pairs={{0,8},{8,0},{16,24},{24,16},{1,9},{9,1},{17,25},{25,17},{2,10},{10... | collective-permute-start | bytes 442376 | tf_op jit(solution)/shard_map/ppermute | solution.py:844
  271.4 12.1 %collective-permute-done.35 = f32[16,768]{1,0:T(8,128)S(1)} collective-permute-done((f32[16,768]{1,0:T(8,128)S(1)}, f32[16,768]{1,0:T(8,128)S(1)}, u32[]{:S(2)}, u32[]{:S(2)}) %collective-permute-start.35) | collective-permute-done | bytes 49184 | tf_op jit(solution)/shard_map/ppermute | solution.py:840
  283.6 3.9 %collective-permute-start.34 = (bf16[96,768]{1,0:T(8,128)(2,1)S(1)}, bf16[96,768]{1,0:T(8,128)(2,1)S(1)}, u32[]{:S(2)}, u32[]{:S(2)}) collective-permute-start(bf16[96,768]{1,0:T(8,128)(2,1)S(1)} %get-tuple-element.263), channel_id=1, source_target_pairs={{0,24},{8,16},{16,8},{24,0},{1,25},{9,17},{17,9},{25,1},{2,26},{10... | collective-permute-start | bytes 442376 | tf_op jit(solution)/shard_map/ppermute | solution.py:844
  287.4 2.6 collective-permute-done.34.refs_3_
  291.8 1.4 collective-permute-start.36
  293.3 5.7 %collective-permute-start.38 = (bf16[96,576]{1,0:T(8,128)(2,1)S(1)}, bf16[96,576]{1,0:T(8,128)(2,1)S(1)}, u32[]{:S(2)}, u32[]{:S(2)}) collective-permute-start(bf16[96,576]{1,0:T(8,128)(2,1)S(1)} %get-tuple-element.272), channel_id=1, source_target_pairs={{0,8},{8,0},{16,24},{24,16},{1,9},{9,1},{17,25},{25,17},{2,10},{10... | collective-permute-start | bytes 331784 | tf_op jit(solution)/shard_map/ppermute | solution.py:844
  299.5 3.4 %collective-permute-start.40 = (bf16[96,576]{1,0:T(8,128)(2,1)S(1)}, bf16[96,576]{1,0:T(8,128)(2,1)S(1)}, u32[]{:S(2)}, u32[]{:S(2)}) collective-permute-start(bf16[96,576]{1,0:T(8,128)(2,1)S(1)} %get-tuple-element.274), channel_id=1, source_target_pairs={{0,24},{8,16},{16,8},{24,0},{1,25},{9,17},{17,9},{25,1},{2,26},{10... | collective-permute-start | bytes 331784 | tf_op jit(solution)/shard_map/ppermute | solution.py:844
  302.9 4.1 %collective-permute-done.39.refs_2_ = bf16[96,576]{1,0:T(8,128)(2,1)S(1)} collective-permute-done((bf16[96,576]{1,0:T(8,128)(2,1)S(1)}, bf16[96,576]{1,0:T(8,128)(2,1)S(1)}, u32[]{:S(2)}, u32[]{:S(2)}) %collective-permute-start.39) | collective-permute-done | bytes 110624 | tf_op jit(solution)/shard_map/ppermute | solution.py:844
  307.9 2.9 split_halves.3
  310.9 1.3 copy-done.19
  312.1 5.4 %collective-permute-start.42 = (bf16[1024,768]{1,0:T(8,128)(2,1)}, bf16[1024,768]{1,0:T(8,128)(2,1)S(1)}, u32[]{:S(2)}, u32[]{:S(2)}) collective-permute-start(bf16[1024,768]{1,0:T(8,128)(2,1)} %get-tuple-element.280), channel_id=1, source_target_pairs={{0,4},{4,0},{1,5},{5,1},{2,6},{6,2},{3,7},{7,3},{8,12},{12,8},{9,1... | collective-permute-start | bytes 4718600 | tf_op jit(solution)/shard_map/ppermute | solution.py:836
  319.4 1.8 copy.42
  321.9 1.4 copy-done.20
  323.3 2.3 join_halves.3
  326.7 1.3 copy.43
  (242 shorter events, 39.8 us)
Async XLA Ops:
  7.2 8.7 %copy-start.54 = (s32[2,1024]{1,0:T(2,128)S(1)}, s32[2,1024]{1,0:T(2,128)}, u32[]{:S(2)}) copy-start(s32[2,1024]{1,0:T(2,128)} %param.15) | copy-start | bytes 24580
  7.2 8.7 %copy-start.55 = (s32[2,1024]{1,0:T(2,128)S(1)}, s32[2,1024]{1,0:T(2,128)}, u32[]{:S(2)}) copy-start(s32[2,1024]{1,0:T(2,128)} %param.14) | copy-start | bytes 24580
  7.2 104.3 %all-gather.2.cloned.1.call-start = ((), (), s32[]{:S(2)}) async-start(), calls=%async_computation.1 | async-start | bytes 11354112 | tf_op jit(solution)/shard_map/all_gather | solution.py:915
  10.9 314.7 %reduce-scatter.2.cloned.1.call-start = ((), (), s32[]{:S(2)}) async-start(), calls=%async_computation.2 | async-start | bytes 6488064 | tf_op jit(solution)/shard_map/reduce_scatter | solution.py:988
  11.3 12.9 %collective-permute-start.3 = (bf16[96,576]{1,0:T(8,128)(2,1)S(1)}, bf16[96,576]{1,0:T(8,128)(2,1)S(1)}, u32[]{:S(2)}, u32[]{:S(2)}) collective-permute-start(bf16[96,576]{1,0:T(8,128)(2,1)S(1)} %copy.34.refs_0_), channel_id=1, source_target_pairs={{0,24},{8,16},{16,8},{24,0},{1,25},{9,17},{17,9},{25,1},{2,26},{10... | collective-permute-start | bytes 331784 | tf_op jit(solution)/shard_map/ppermute | solution.py:844
  15.5 10.0 %collective-permute-start.2 = (bf16[96,576]{1,0:T(8,128)(2,1)S(1)}, bf16[96,576]{1,0:T(8,128)(2,1)S(1)}, u32[]{:S(2)}, u32[]{:S(2)}) collective-permute-start(bf16[96,576]{1,0:T(8,128)(2,1)S(1)} %copy.34.refs_0_), channel_id=1, source_target_pairs={{0,16},{8,24},{16,0},{24,8},{1,17},{9,25},{17,1},{25,9},{2,18},{10... | collective-permute-start | bytes 331784 | tf_op jit(solution)/shard_map/ppermute | solution.py:844
  15.5 10.0 %collective-permute-start.1 = (bf16[96,576]{1,0:T(8,128)(2,1)S(1)}, bf16[96,576]{1,0:T(8,128)(2,1)S(1)}, u32[]{:S(2)}, u32[]{:S(2)}) collective-permute-start(bf16[96,576]{1,0:T(8,128)(2,1)S(1)} %copy.34.refs_0_), channel_id=1, source_target_pairs={{0,8},{8,0},{16,24},{24,16},{1,9},{9,1},{17,25},{25,17},{2,10},{10... | collective-permute-start | bytes 331784 | tf_op jit(solution)/shard_map/ppermute | solution.py:844
  15.9 6.5 %collective-permute-start = (s32[2,1024]{1,0:T(2,128)S(1)}, s32[2,1024]{1,0:T(2,128)S(1)}, u32[]{:S(2)}, u32[]{:S(2)}) collective-permute-start(s32[2,1024]{1,0:T(2,128)S(1)} %bitcast.141), channel_id=1, source_target_pairs={{0,4},{4,0},{1,5},{5,1},{2,6},{6,2},{3,7},{7,3},{8,12},{12,8},{9,1... | collective-permute-start | bytes 24584 | tf_op jit(solution)/shard_map/ppermute | solution.py:836
  19.9 11.0 %collective-permute-start.5 = (bf16[1024,768]{1,0:T(8,128)(2,1)}, bf16[1024,768]{1,0:T(8,128)(2,1)S(1)}, u32[]{:S(2)}, u32[]{:S(2)}) collective-permute-start(bf16[1024,768]{1,0:T(8,128)(2,1)} %dynamic-slice_bitcast_fusion), channel_id=1, source_target_pairs={{0,4},{4,0},{1,5},{5,1},{2,6},{6,2},{3,7},{7,3},{8,12},{12,8},{9,1... | collective-permute-start | bytes 4718600 | tf_op jit(solution)/shard_map/ppermute | solution.py:836
  22.4 119.5 %copy-start.39 = (s32[10]{0:T(128)}, s32[10]{0:T(128)S(1)}, u32[]{:S(2)}) copy-start(s32[10]{0:T(128)S(1)} %stack.143.place) | copy-start | bytes 124
  22.4 35.6 %collective-permute-start.9 = (bf16[512,768]{1,0:T(8,128)(2,1)}, bf16[512,768]{1,0:T(8,128)(2,1)}, u32[]{:S(2)}, u32[]{:S(2)}) collective-permute-start(bf16[512,768]{1,0:T(8,128)(2,1)} %dynamic-slice_bitcast_fusion.1), channel_id=1, source_target_pairs={{0,4},{4,0},{1,5},{5,1},{2,6},{6,2},{3,7},{7,3},{8,12},{12,8},{9,1... | collective-permute-start | bytes 2359304 | tf_op jit(solution)/shard_map/ppermute | solution.py:836
  23.0 7.8 %copy-start.51 = (s32[1,8,2,128]{3,1,2,0:T(8,128)}, s32[1,8,2,128]{3,1,2,0:T(8,128)S(1)}, u32[]{:S(2)}) copy-start(s32[1,8,2,128]{3,1,2,0:T(8,128)S(1)} %copy.55) | copy-start | bytes 24580
  25.6 5.3 %collective-permute-start.4 = (bf16[4,96,576]{2,1,0:T(8,128)(2,1)S(1)}, bf16[4,96,576]{2,1,0:T(8,128)(2,1)S(1)}, u32[]{:S(2)}, u32[]{:S(2)}) collective-permute-start(bf16[4,96,576]{2,1,0:T(8,128)(2,1)S(1)} %pad_maximum_fusion.3), channel_id=1, source_target_pairs={{0,4},{4,0},{1,5},{5,1},{2,6},{6,2},{3,7},{7,3},{8,12},{12,8},{9,1... | collective-permute-start | bytes 1327112 | tf_op jit(solution)/shard_map/ppermute | solution.py:836
  36.2 7.1 %copy-start.52 = (s32[1,8,2,128]{3,1,2,0:T(8,128)S(1)}, s32[1,8,2,128]{3,1,2,0:T(8,128)}, u32[]{:S(2)}) copy-start(s32[1,8,2,128]{3,1,2,0:T(8,128)} %copy-done.51) | copy-start | bytes 24580
  43.3 27.3 %copy-start.2 = (bf16[2048,256]{1,0:T(8,128)(2,1)}, bf16[2048,256]{1,0:T(8,128)(2,1)S(1)}, u32[]{:S(2)}) copy-start(bf16[2048,256]{1,0:T(8,128)(2,1)S(1)} %get-tuple-element.150.v) | copy-start | bytes 3145732
  49.4 11.9 %collective-permute-start.6 = (bf16[512,192]{1,0:T(8,128)(2,1)S(1)}, bf16[512,192]{1,0:T(8,128)(2,1)S(1)}, u32[]{:S(2)}, u32[]{:S(2)}) collective-permute-start(bf16[512,192]{1,0:T(8,128)(2,1)S(1)} %get-tuple-element.154), channel_id=1, source_target_pairs={{0,3},{1,2},{2,1},{3,0},{4,7},{5,6},{6,5},{7,4},{8,11},{9,10},{10,... | collective-permute-start | bytes 589832 | tf_op jit(solution)/shard_map/ppermute | solution.py:840
  57.7 12.3 %collective-permute-start.7 = (bf16[512,192]{1,0:T(8,128)(2,1)S(1)}, bf16[512,192]{1,0:T(8,128)(2,1)S(1)}, u32[]{:S(2)}, u32[]{:S(2)}) collective-permute-start(bf16[512,192]{1,0:T(8,128)(2,1)S(1)} %get-tuple-element.157), channel_id=1, source_target_pairs={{0,1},{1,0},{2,3},{3,2},{4,5},{5,4},{6,7},{7,6},{8,9},{9,8},{10,11... | collective-permute-start | bytes 589832 | tf_op jit(solution)/shard_map/ppermute | solution.py:840
  70.6 42.6 %collective-permute-start.8 = (bf16[512,192]{1,0:T(8,128)(2,1)}, bf16[512,192]{1,0:T(8,128)(2,1)}, u32[]{:S(2)}, u32[]{:S(2)}) collective-permute-start(bf16[512,192]{1,0:T(8,128)(2,1)} %get-tuple-element.161), channel_id=1, source_target_pairs={{0,2},{1,3},{2,0},{3,1},{4,6},{5,7},{6,4},{7,5},{8,10},{9,11},{10,... | collective-permute-start | bytes 589832 | tf_op jit(solution)/shard_map/ppermute | solution.py:840
  76.7 36.6 %copy-start.47 = (f32[8,512]{1,0:T(8,128)}, f32[8,512]{1,0:T(8,128)S(1)}, u32[]{:S(2)}) copy-start(f32[8,512]{1,0:T(8,128)S(1)} %get-tuple-element.190) | copy-start | bytes 49156
  121.6 20.3 %copy-start.1 = (bf16[3072,1792]{1,0:T(8,128)(2,1)S(1)}, bf16[3072,1792]{1,0:T(8,128)(2,1)}, u32[]{:S(2)}) copy-start(bf16[3072,1792]{1,0:T(8,128)(2,1)} %all-gather.2.cloned.1.call-done) | copy-start | bytes 33030148
  140.8 34.5 %collective-permute-start.14 = (bf16[512,768]{1,0:T(8,128)(2,1)}, bf16[512,768]{1,0:T(8,128)(2,1)}, u32[]{:S(2)}, u32[]{:S(2)}) collective-permute-start(bf16[512,768]{1,0:T(8,128)(2,1)} %get-tuple-element.215.refs_0_), channel_id=1, source_target_pairs={{0,2},{1,3},{2,0},{3,1},{4,6},{5,7},{6,4},{7,5},{8,10},{9,11},{10,... | collective-permute-start | bytes 2359304 | tf_op jit(solution)/shard_map/ppermute | solution.py:840
  140.8 34.5 %collective-permute-start.13 = (bf16[512,768]{1,0:T(8,128)(2,1)}, bf16[512,768]{1,0:T(8,128)(2,1)}, u32[]{:S(2)}, u32[]{:S(2)}) collective-permute-start(bf16[512,768]{1,0:T(8,128)(2,1)} %get-tuple-element.215.refs_0_), channel_id=1, source_target_pairs={{0,1},{1,0},{2,3},{3,2},{4,5},{5,4},{6,7},{7,6},{8,9},{9,8},{10,11... | collective-permute-start | bytes 2359304 | tf_op jit(solution)/shard_map/ppermute | solution.py:840
  146.7 14.2 %copy-start.23 = (bf16[512,192]{1,0:T(8,128)(2,1)S(1)}, bf16[512,192]{1,0:T(8,128)(2,1)}, u32[]{:S(2)}) copy-start(bf16[512,192]{1,0:T(8,128)(2,1)} %copy-done.21) | copy-start | bytes 589828
  146.7 14.2 %copy-start.26 = (bf16[512,192]{1,0:T(8,128)(2,1)S(1)}, bf16[512,192]{1,0:T(8,128)(2,1)}, u32[]{:S(2)}) copy-start(bf16[512,192]{1,0:T(8,128)(2,1)} %copy-done.24) | copy-start | bytes 589828
  158.2 17.1 %collective-permute-start.10 = (bf16[512,192]{1,0:T(8,128)(2,1)}, bf16[512,192]{1,0:T(8,128)(2,1)}, u32[]{:S(2)}, u32[]{:S(2)}) collective-permute-start(bf16[512,192]{1,0:T(8,128)(2,1)} %get-tuple-element.177), channel_id=1, source_target_pairs={{0,1},{1,0},{2,3},{3,2},{4,5},{5,4},{6,7},{7,6},{8,9},{9,8},{10,11... | collective-permute-start | bytes 589832 | tf_op jit(solution)/shard_map/ppermute | solution.py:840
  158.7 16.6 %collective-permute-start.11 = (bf16[512,192]{1,0:T(8,128)(2,1)}, bf16[512,192]{1,0:T(8,128)(2,1)}, u32[]{:S(2)}, u32[]{:S(2)}) collective-permute-start(bf16[512,192]{1,0:T(8,128)(2,1)} %get-tuple-element.178), channel_id=1, source_target_pairs={{0,2},{1,3},{2,0},{3,1},{4,6},{5,7},{6,4},{7,5},{8,10},{9,11},{10,... | collective-permute-start | bytes 589832 | tf_op jit(solution)/shard_map/ppermute | solution.py:840
  160.2 15.1 %collective-permute-start.12 = (bf16[512,192]{1,0:T(8,128)(2,1)}, bf16[512,192]{1,0:T(8,128)(2,1)}, u32[]{:S(2)}, u32[]{:S(2)}) collective-permute-start(bf16[512,192]{1,0:T(8,128)(2,1)} %get-tuple-element.179), channel_id=1, source_target_pairs={{0,3},{1,2},{2,1},{3,0},{4,7},{5,6},{6,5},{7,4},{8,11},{9,10},{10,... | collective-permute-start | bytes 589832 | tf_op jit(solution)/shard_map/ppermute | solution.py:840
  175.3 6.2 %collective-permute-start.15 = (bf16[4,4,96,768]{3,2,1,0:T(8,128)(2,1)}, bf16[4,4,96,768]{3,2,1,0:T(8,128)(2,1)}, u32[]{:S(2)}, u32[]{:S(2)}) collective-permute-start(bf16[4,4,96,768]{3,2,1,0:T(8,128)(2,1)} %get-tuple-element.185), channel_id=1, source_target_pairs={{0,4},{4,0},{1,5},{5,1},{2,6},{6,2},{3,7},{7,3},{8,12},{12,8},{9,1... | collective-permute-start | bytes 7077896 | tf_op jit(solution)/shard_map/ppermute | solution.py:836
  181.5 10.0 %copy-start.10 = (f32[2048,128]{1,0:T(8,128)S(1)}, f32[2048,128]{1,0:T(8,128)}, u32[]{:S(2)}) copy-start(f32[2048,128]{1,0:T(8,128)} %copy-done.9) | copy-start | bytes 3145732
  181.5 10.0 %copy-start.12 = (f32[2048,128]{1,0:T(8,128)S(1)}, f32[2048,128]{1,0:T(8,128)}, u32[]{:S(2)}) copy-start(f32[2048,128]{1,0:T(8,128)} %copy-done.11) | copy-start | bytes 3145732
  181.5 10.0 %copy-start.28 = (bf16[256,2048]{1,0:T(8,128)(2,1)S(1)}, bf16[256,2048]{1,0:T(8,128)(2,1)}, u32[]{:S(2)}) copy-start(bf16[256,2048]{1,0:T(8,128)(2,1)} %copy-done.27) | copy-start | bytes 3145732
  184.7 6.8 %copy-start.44 = (f32[8,512]{1,0:T(8,128)S(1)}, f32[8,512]{1,0:T(8,128)}, u32[]{:S(2)}) copy-start(f32[8,512]{1,0:T(8,128)} %copy-done.43) | copy-start | bytes 49156
  184.8 6.8 %copy-start.3 = (bf16[2048,256]{1,0:T(8,128)(2,1)S(1)}, bf16[2048,256]{1,0:T(8,128)(2,1)}, u32[]{:S(2)}) copy-start(bf16[2048,256]{1,0:T(8,128)(2,1)} %copy-done.2) | copy-start | bytes 3145732
  184.8 35.9 %collective-permute-start.18 = (bf16[4,96,768]{2,1,0:T(8,128)(2,1)S(1)}, bf16[4,96,768]{2,1,0:T(8,128)(2,1)S(1)}, u32[]{:S(2)}, u32[]{:S(2)}) collective-permute-start(bf16[4,96,768]{2,1,0:T(8,128)(2,1)S(1)} %get-tuple-element.202), channel_id=1, source_target_pairs={{0,1},{1,0},{2,3},{3,2},{4,5},{5,4},{6,7},{7,6},{8,9},{9,8},{10,11... | collective-permute-start | bytes 1769480 | tf_op jit(solution)/shard_map/ppermute | solution.py:840
  185.2 35.5 %collective-permute-start.19 = (bf16[4,96,768]{2,1,0:T(8,128)(2,1)S(1)}, bf16[4,96,768]{2,1,0:T(8,128)(2,1)S(1)}, u32[]{:S(2)}, u32[]{:S(2)}) collective-permute-start(bf16[4,96,768]{2,1,0:T(8,128)(2,1)S(1)} %get-tuple-element.203), channel_id=1, source_target_pairs={{0,2},{1,3},{2,0},{3,1},{4,6},{5,7},{6,4},{7,5},{8,10},{9,11},{10,... | collective-permute-start | bytes 1769480 | tf_op jit(solution)/shard_map/ppermute | solution.py:840
  186.7 33.9 %collective-permute-start.20 = (bf16[4,96,768]{2,1,0:T(8,128)(2,1)S(1)}, bf16[4,96,768]{2,1,0:T(8,128)(2,1)S(1)}, u32[]{:S(2)}, u32[]{:S(2)}) collective-permute-start(bf16[4,96,768]{2,1,0:T(8,128)(2,1)S(1)} %get-tuple-element.204), channel_id=1, source_target_pairs={{0,3},{1,2},{2,1},{3,0},{4,7},{5,6},{6,5},{7,4},{8,11},{9,10},{10,... | collective-permute-start | bytes 1769480 | tf_op jit(solution)/shard_map/ppermute | solution.py:840
  189.6 30.9 %collective-permute-start.17 = (bf16[256,768]{1,0:T(8,128)(2,1)S(1)}, bf16[256,768]{1,0:T(8,128)(2,1)S(1)}, u32[]{:S(2)}, u32[]{:S(2)}) collective-permute-start(bf16[256,768]{1,0:T(8,128)(2,1)S(1)} %slice.99), channel_id=1, source_target_pairs={{0,1},{1,0},{2,3},{3,2},{4,5},{5,4},{6,7},{7,6},{8,9},{9,8},{10,11... | collective-permute-start | bytes 1179656 | tf_op jit(solution)/shard_map/ppermute | solution.py:840
  190.1 30.6 %collective-permute-start.16 = (bf16[256,768]{1,0:T(8,128)(2,1)S(1)}, bf16[256,768]{1,0:T(8,128)(2,1)S(1)}, u32[]{:S(2)}, u32[]{:S(2)}) collective-permute-start(bf16[256,768]{1,0:T(8,128)(2,1)S(1)} %slice.98), channel_id=1, source_target_pairs={{0,2},{1,3},{2,0},{3,1},{4,6},{5,7},{6,4},{7,5},{8,10},{9,11},{10,... | collective-permute-start | bytes 1179656 | tf_op jit(solution)/shard_map/ppermute | solution.py:840
  191.6 29.1 %copy-start.15 = (bf16[768,768]{1,0:T(8,128)(2,1)S(1)}, bf16[768,768]{1,0:T(8,128)(2,1)}, u32[]{:S(2)}) copy-start(bf16[768,768]{1,0:T(8,128)(2,1)} %copy-done.14) | copy-start | bytes 3538948
  191.6 29.1 %copy-start.40 = (s32[10]{0:T(128)S(1)}, s32[10]{0:T(128)}, u32[]{:S(2)}) copy-start(s32[10]{0:T(128)} %copy-done.39) | copy-start | bytes 124
  222.1 11.0 %collective-permute-start.22 = (bf16[256,768]{1,0:T(8,128)(2,1)S(1)}, bf16[256,768]{1,0:T(8,128)(2,1)S(1)}, u32[]{:S(2)}, u32[]{:S(2)}) collective-permute-start(bf16[256,768]{1,0:T(8,128)(2,1)S(1)} %get-tuple-element.309), channel_id=1, source_target_pairs={{0,1},{1,0},{2,3},{3,2},{4,5},{5,4},{6,7},{7,6},{8,9},{9,8},{10,11... | collective-permute-start | bytes 1179656 | tf_op jit(solution)/shard_map/ppermute | solution.py:840
  223.1 12.9 %collective-permute-start.21 = (bf16[256,768]{1,0:T(8,128)(2,1)S(1)}, bf16[256,768]{1,0:T(8,128)(2,1)S(1)}, u32[]{:S(2)}, u32[]{:S(2)}) collective-permute-start(bf16[256,768]{1,0:T(8,128)(2,1)S(1)} %get-tuple-element.310), channel_id=1, source_target_pairs={{0,2},{1,3},{2,0},{3,1},{4,6},{5,7},{6,4},{7,5},{8,10},{9,11},{10,... | collective-permute-start | bytes 1179656 | tf_op jit(solution)/shard_map/ppermute | solution.py:840
  226.5 20.2 %copy-start.8 = (bf16[1024,768]{1,0:T(8,128)(2,1)S(1)}, bf16[1024,768]{1,0:T(8,128)(2,1)}, u32[]{:S(2)}) copy-start(bf16[1024,768]{1,0:T(8,128)(2,1)} %copy-done.6) | copy-start | bytes 4718596
  236.0 10.7 %copy-start.5 = (bf16[2,1024,768]{2,1,0:T(8,128)(2,1)S(1)}, bf16[2,1024,768]{2,1,0:T(8,128)(2,1)}, u32[]{:S(2)}) copy-start(bf16[2,1024,768]{2,1,0:T(8,128)(2,1)} %own.1) | copy-start | bytes 9437188
  236.2 25.5 %collective-permute-start.28 = (bf16[1024,768]{1,0:T(8,128)(2,1)S(1)}, bf16[1024,768]{1,0:T(8,128)(2,1)S(1)}, u32[]{:S(2)}, u32[]{:S(2)}) collective-permute-start(bf16[1024,768]{1,0:T(8,128)(2,1)S(1)} %get-tuple-element.239), channel_id=1, source_target_pairs={{0,4},{4,0},{1,5},{5,1},{2,6},{6,2},{3,7},{7,3},{8,12},{12,8},{9,1... | collective-permute-start | bytes 4718600 | tf_op jit(solution)/shard_map/ppermute | solution.py:836
  245.0 19.1 %collective-permute-start.23 = (bf16[512,768]{1,0:T(8,128)(2,1)S(1)}, bf16[512,768]{1,0:T(8,128)(2,1)S(1)}, u32[]{:S(2)}, u32[]{:S(2)}) collective-permute-start(bf16[512,768]{1,0:T(8,128)(2,1)S(1)} %get-tuple-element.234), channel_id=1, source_target_pairs={{0,1},{1,0},{2,3},{3,2},{4,5},{5,4},{6,7},{7,6},{8,9},{9,8},{10,11... | collective-permute-start | bytes 2359304 | tf_op jit(solution)/shard_map/ppermute | solution.py:840
  245.6 18.8 %collective-permute-start.24 = (bf16[512,768]{1,0:T(8,128)(2,1)S(1)}, bf16[512,768]{1,0:T(8,128)(2,1)S(1)}, u32[]{:S(2)}, u32[]{:S(2)}) collective-permute-start(bf16[512,768]{1,0:T(8,128)(2,1)S(1)} %get-tuple-element.235), channel_id=1, source_target_pairs={{0,2},{1,3},{2,0},{3,1},{4,6},{5,7},{6,4},{7,5},{8,10},{9,11},{10,... | collective-permute-start | bytes 2359304 | tf_op jit(solution)/shard_map/ppermute | solution.py:840
  250.7 10.9 %collective-permute-start.29 = (bf16[4,96,576]{2,1,0:T(8,128)(2,1)S(1)}, bf16[4,96,576]{2,1,0:T(8,128)(2,1)S(1)}, u32[]{:S(2)}, u32[]{:S(2)}) collective-permute-start(bf16[4,96,576]{2,1,0:T(8,128)(2,1)S(1)} %get-tuple-element.250), channel_id=1, source_target_pairs={{0,4},{4,0},{1,5},{5,1},{2,6},{6,2},{3,7},{7,3},{8,12},{12,8},{9,1... | collective-permute-start | bytes 1327112 | tf_op jit(solution)/shard_map/ppermute | solution.py:836
  251.4 1.6 collective-permute-start.25
  253.0 4.7 %collective-permute-start.26 = (f32[16,768]{1,0:T(8,128)S(1)}, f32[16,768]{1,0:T(8,128)S(1)}, u32[]{:S(2)}, u32[]{:S(2)}) collective-permute-start(f32[16,768]{1,0:T(8,128)S(1)} %add.176), channel_id=1, source_target_pairs={{0,8},{8,0},{16,24},{24,16},{1,9},{9,1},{17,25},{25,17},{2,10},{10... | collective-permute-start | bytes 147464 | tf_op jit(solution)/shard_map/ppermute | solution.py:844
  257.7 3.9 %collective-permute-start.27 = (f32[16,768]{1,0:T(8,128)S(1)}, f32[16,768]{1,0:T(8,128)S(1)}, u32[]{:S(2)}, u32[]{:S(2)}) collective-permute-start(f32[16,768]{1,0:T(8,128)S(1)} %add.177), channel_id=1, source_target_pairs={{0,16},{8,24},{16,0},{24,8},{1,17},{9,25},{17,1},{25,9},{2,18},{10... | collective-permute-start | bytes 147464 | tf_op jit(solution)/shard_map/ppermute | solution.py:844
  264.8 25.3 %collective-permute-start.31 = (bf16[512,768]{1,0:T(8,128)(2,1)S(1)}, bf16[512,768]{1,0:T(8,128)(2,1)S(1)}, u32[]{:S(2)}, u32[]{:S(2)}) collective-permute-start(bf16[512,768]{1,0:T(8,128)(2,1)S(1)} %add_block.1.refs_0_), channel_id=1, source_target_pairs={{0,2},{1,3},{2,0},{3,1},{4,6},{5,7},{6,4},{7,5},{8,10},{9,11},{10,... | collective-permute-start | bytes 2359304 | tf_op jit(solution)/shard_map/ppermute | solution.py:840
  266.3 23.8 %collective-permute-start.30 = (bf16[512,768]{1,0:T(8,128)(2,1)S(1)}, bf16[512,768]{1,0:T(8,128)(2,1)S(1)}, u32[]{:S(2)}, u32[]{:S(2)}) collective-permute-start(bf16[512,768]{1,0:T(8,128)(2,1)S(1)} %add_block.1.refs_0_), channel_id=1, source_target_pairs={{0,1},{1,0},{2,3},{3,2},{4,5},{5,4},{6,7},{7,6},{8,9},{9,8},{10,11... | collective-permute-start | bytes 2359304 | tf_op jit(solution)/shard_map/ppermute | solution.py:840
  267.1 16.5 %collective-permute-start.35 = (f32[16,768]{1,0:T(8,128)S(1)}, f32[16,768]{1,0:T(8,128)S(1)}, u32[]{:S(2)}, u32[]{:S(2)}) collective-permute-start(f32[16,768]{1,0:T(8,128)S(1)} %add.178), channel_id=1, source_target_pairs={{0,1},{1,0},{2,3},{3,2},{4,5},{5,4},{6,7},{7,6},{8,9},{9,8},{10,11... | collective-permute-start | bytes 147464 | tf_op jit(solution)/shard_map/ppermute | solution.py:840
  267.7 19.7 %collective-permute-start.32 = (bf16[96,768]{1,0:T(8,128)(2,1)S(1)}, bf16[96,768]{1,0:T(8,128)(2,1)S(1)}, u32[]{:S(2)}, u32[]{:S(2)}) collective-permute-start(bf16[96,768]{1,0:T(8,128)(2,1)S(1)} %get-tuple-element.261), channel_id=1, source_target_pairs={{0,8},{8,0},{16,24},{24,16},{1,9},{9,1},{17,25},{25,17},{2,10},{10... | collective-permute-start | bytes 442376 | tf_op jit(solution)/shard_map/ppermute | solution.py:844
  271.4 16.0 %collective-permute-start.33 = (bf16[96,768]{1,0:T(8,128)(2,1)S(1)}, bf16[96,768]{1,0:T(8,128)(2,1)S(1)}, u32[]{:S(2)}, u32[]{:S(2)}) collective-permute-start(bf16[96,768]{1,0:T(8,128)(2,1)S(1)} %get-tuple-element.262), channel_id=1, source_target_pairs={{0,16},{8,24},{16,0},{24,8},{1,17},{9,25},{17,1},{25,9},{2,18},{10... | collective-permute-start | bytes 442376 | tf_op jit(solution)/shard_map/ppermute | solution.py:844
  283.6 6.5 %collective-permute-start.34 = (bf16[96,768]{1,0:T(8,128)(2,1)S(1)}, bf16[96,768]{1,0:T(8,128)(2,1)S(1)}, u32[]{:S(2)}, u32[]{:S(2)}) collective-permute-start(bf16[96,768]{1,0:T(8,128)(2,1)S(1)} %get-tuple-element.263), channel_id=1, source_target_pairs={{0,24},{8,16},{16,8},{24,0},{1,25},{9,17},{17,9},{25,1},{2,26},{10... | collective-permute-start | bytes 442376 | tf_op jit(solution)/shard_map/ppermute | solution.py:844
  291.7 16.3 %collective-permute-start.37 = (bf16[256,768]{1,0:T(8,128)(2,1)}, bf16[256,768]{1,0:T(8,128)(2,1)S(1)}, u32[]{:S(2)}, u32[]{:S(2)}) collective-permute-start(bf16[256,768]{1,0:T(8,128)(2,1)} %slice.105), channel_id=1, source_target_pairs={{0,1},{1,0},{2,3},{3,2},{4,5},{5,4},{6,7},{7,6},{8,9},{9,8},{10,11... | collective-permute-start | bytes 1179656 | tf_op jit(solution)/shard_map/ppermute | solution.py:840
  291.8 16.1 %collective-permute-start.36 = (bf16[256,768]{1,0:T(8,128)(2,1)}, bf16[256,768]{1,0:T(8,128)(2,1)}, u32[]{:S(2)}, u32[]{:S(2)}) collective-permute-start(bf16[256,768]{1,0:T(8,128)(2,1)} %slice.104), channel_id=1, source_target_pairs={{0,2},{1,3},{2,0},{3,1},{4,6},{5,7},{6,4},{7,5},{8,10},{9,11},{10,... | collective-permute-start | bytes 1179656 | tf_op jit(solution)/shard_map/ppermute | solution.py:840
  293.2 6.2 %collective-permute-start.41 = (f32[16,768]{1,0:T(8,128)S(1)}, f32[16,768]{1,0:T(8,128)S(1)}, u32[]{:S(2)}, u32[]{:S(2)}) collective-permute-start(f32[16,768]{1,0:T(8,128)S(1)} %add.179), channel_id=1, source_target_pairs={{0,2},{1,3},{2,0},{3,1},{4,6},{5,7},{6,4},{7,5},{8,10},{9,11},{10,... | collective-permute-start | bytes 147464 | tf_op jit(solution)/shard_map/ppermute | solution.py:840
  293.3 9.6 %collective-permute-start.38 = (bf16[96,576]{1,0:T(8,128)(2,1)S(1)}, bf16[96,576]{1,0:T(8,128)(2,1)S(1)}, u32[]{:S(2)}, u32[]{:S(2)}) collective-permute-start(bf16[96,576]{1,0:T(8,128)(2,1)S(1)} %get-tuple-element.272), channel_id=1, source_target_pairs={{0,8},{8,0},{16,24},{24,16},{1,9},{9,1},{17,25},{25,17},{2,10},{10... | collective-permute-start | bytes 331784 | tf_op jit(solution)/shard_map/ppermute | solution.py:844
  299.0 8.0 %collective-permute-start.39 = (bf16[96,576]{1,0:T(8,128)(2,1)S(1)}, bf16[96,576]{1,0:T(8,128)(2,1)S(1)}, u32[]{:S(2)}, u32[]{:S(2)}) collective-permute-start(bf16[96,576]{1,0:T(8,128)(2,1)S(1)} %get-tuple-element.273), channel_id=1, source_target_pairs={{0,16},{8,24},{16,0},{24,8},{1,17},{9,25},{17,1},{25,9},{2,18},{10... | collective-permute-start | bytes 331784 | tf_op jit(solution)/shard_map/ppermute | solution.py:844
  299.5 7.5 %collective-permute-start.40 = (bf16[96,576]{1,0:T(8,128)(2,1)S(1)}, bf16[96,576]{1,0:T(8,128)(2,1)S(1)}, u32[]{:S(2)}, u32[]{:S(2)}) collective-permute-start(bf16[96,576]{1,0:T(8,128)(2,1)S(1)} %get-tuple-element.274), channel_id=1, source_target_pairs={{0,24},{8,16},{16,8},{24,0},{1,25},{9,17},{17,9},{25,1},{2,26},{10... | collective-permute-start | bytes 331784 | tf_op jit(solution)/shard_map/ppermute | solution.py:844
  312.1 9.7 %collective-permute-start.42 = (bf16[1024,768]{1,0:T(8,128)(2,1)}, bf16[1024,768]{1,0:T(8,128)(2,1)S(1)}, u32[]{:S(2)}, u32[]{:S(2)}) collective-permute-start(bf16[1024,768]{1,0:T(8,128)(2,1)} %get-tuple-element.280), channel_id=1, source_target_pairs={{0,4},{4,0},{1,5},{5,1},{2,6},{6,2},{3,7},{7,3},{8,12},{12,8},{9,1... | collective-permute-start | bytes 4718600 | tf_op jit(solution)/shard_map/ppermute | solution.py:836
  (41 other events, 111.5 us)
Sparse Core Ops, SparseCore 0:
  11.6 99.8 all-gather.1
  177.2 125.9 reduce-scatter.1

commit v5 on v4

--- a/solution.py
+++ b/solution.py
@@ -58,7 +58,7 @@
     pieces = []
     for x in refs[:count]:
         pieces += [x] if len(x.shape) == 2 else [x.at[n] for n in range(x.shape[0])]
-    bias, own, other, cos, sin, q_o, k_o, v_o, kt_o, w_o = refs[count:]
+    bias, own, other, cos, sin, q_o, k_o, v_o, kt_o, qt_o, w_o = refs[count:]
     piece_rows = pieces[0].shape[0]
     pad = jnp.zeros((piece_rows, WIDE - part), BF)
     for n in range(per):
@@ -70,7 +70,9 @@
     def run(x, sl):
         c, s = twice(cos[sl, :]), twice(sin[sl, :])
         p = nn(x, w_o[:, 0:WIDE]) + bias[0:1, :]
-        q_o[sl, :] = ((p * c + swap_pairs(p) * s).astype(BF).astype(F32) * (HEAD**-0.5)).astype(BF)
+        q = ((p * c + swap_pairs(p) * s).astype(BF).astype(F32) * (HEAD**-0.5)).astype(BF)
+        q_o[sl, :] = q
+        qt_o[:, sl] = q.T
         p = nn(x, w_o[:, WIDE : 2 * WIDE]) + bias[1:2, :]
         k = (p * c + swap_pairs(p) * s).astype(BF)
         k_o[sl, :] = k
@@ -98,17 +100,18 @@
             in_specs=[whole_block(p.shape) for p in pieces]
             + [whole_block(bias.shape), pl.BlockSpec((1, half_len, width), lambda i, s: (s[per], 0, 0))]
             + [whole_block(x.shape) for x in (other, cos, sin)],
-            out_specs=[whole_block((length, WIDE))] * 3 + [whole_block((WIDE, length)), whole_block((width, 3 * WIDE))],
+            out_specs=[whole_block((length, WIDE))] * 3 + [whole_block((WIDE, length))] * 2 + [whole_block((width, 3 * WIDE))],
         ),
         out_shape=[jax.ShapeDtypeStruct((length, WIDE), BF)] * 3
-        + [jax.ShapeDtypeStruct((WIDE, length), BF), jax.ShapeDtypeStruct((width, 3 * WIDE), BF)],
+        + [jax.ShapeDtypeStruct((WIDE, length), BF)] * 2
+        + [jax.ShapeDtypeStruct((width, 3 * WIDE), BF)],
         compiler_params=params(32),
         cost_estimate=COST,
         name="project_qkv",
     )(place, *pieces, bias, tokens, other, cos, sin)
 
 
-def forward_kernel(heads, place, q, k, v, segc, segr, ctx_o, lse_o, acc, s_sc, m_sc, l_sc, qc_sc):
+def forward_kernel(heads, place, q, k, v, segc, segr, ctx_o, lse_o, full_o, acc, s_sc, m_sc, l_sc, qc_sc):
     i = place[0] + pl.program_id(0)
     start, count = place[1 + 2 * i], place[2 + 2 * i]
     qc_sc[...] = jnp.concatenate(lanes_of_heads(q[...], heads), axis=0)
@@ -151,14 +154,23 @@
         tile = jnp.where(lane == h, lse[of(h), :], tile)
     lse_o[...] = tile.T[0:8, :]
     acc[...] = jnp.zeros(acc.shape, F32)
+    full_o[...] = jnp.zeros(full_o.shape, F32)
 
     def pass3(j, _):
-        ps = [(s_sc[j, of(h), :] * twice(l_sc[of(h), :])).astype(BF) for h in range(heads)]
-        acc[...] += nn(jnp.concatenate(ps, axis=1), jnp.concatenate(lanes_of_heads(v[at(j), :], heads), axis=0))
+        ps, less = [], []
+        for h in range(heads):
+            p = s_sc[j, of(h), :] * twice(l_sc[of(h), :])
+            b = p.astype(BF)
+            ps.append(b)
+            less.append((p - b.astype(F32)).astype(BF))
+        vs = jnp.concatenate(lanes_of_heads(v[at(j), :], heads), axis=0)
+        acc[...] += nn(jnp.concatenate(ps, axis=1), vs)
+        full_o[...] += nn(jnp.concatenate(less, axis=1), vs)
         return 0
 
     lax.fori_loop(0, count, pass3, 0)
     ctx_o[...] = acc[:, : heads * HEAD].astype(BF)
+    full_o[...] += acc[...]
 
 
 def attention_forward(place, q, k, v, segc, segr, heads, share):
@@ -177,7 +189,11 @@
                 pl.BlockSpec((BLOCK, 1), rows),
                 whole_block(segr.shape),
             ],
-            out_specs=[pl.BlockSpec((BLOCK, heads * HEAD), lambda i, s: (i, 0)), pl.BlockSpec((8, BLOCK), lambda i, s: (0, i))],
+            out_specs=[
+                pl.BlockSpec((BLOCK, heads * HEAD), lambda i, s: (i, 0)),
+                pl.BlockSpec((8, BLOCK), lambda i, s: (0, i)),
+                pl.BlockSpec((BLOCK, WIDE), lambda i, s: (i, 0)),
+            ],
             scratch_shapes=[
                 pltpu.VMEM((BLOCK, WIDE), F32),
                 pltpu.VMEM((length // CHUNK, heads * BLOCK, CHUNK), F32),
@@ -186,67 +202,79 @@
                 pltpu.VMEM((heads * BLOCK, WIDE), BF),
             ],
         ),
-        out_shape=[jax.ShapeDtypeStruct((share, heads * HEAD), BF), jax.ShapeDtypeStruct((8, share), F32)],
+        out_shape=[
+            jax.ShapeDtypeStruct((share, heads * HEAD), BF),
+            jax.ShapeDtypeStruct((8, share), F32),
+            jax.ShapeDtypeStruct((share, WIDE), F32),
+        ],
         compiler_params=params(16),
         cost_estimate=COST,
         name="attention_forward",
     )(place, q, k, v, segc, segr)
 
 
-def backward_kernel(heads, place, q, k, kt, v, do, lse, segc, segr, cos, sin, g_o, gb_o, dk_sc, dv_sc, qc_sc, dc_sc, dq_sc, p_sc, dp_sc, dl_sc):
+def backward_kernel(heads, place, q, qt, k, kt, v, d0, d1, d2, d3, full, lse, segc, segr, cos, sin, g_o, gb_o, dk_sc, dv_sc, qc_sc, dc_sc, dq_sc, d_sc, dt_sc):
     step_at = pl.program_id(0)
     i = step_at ^ place[0]
     length = k.shape[0]
+    part = d0.shape[1]
+    per = d0.shape[0] // BLOCK
 
     @pl.when(step_at == 0)
     def _():
         dk_sc[...] = jnp.zeros(dk_sc.shape, F32)
         dv_sc[...] = jnp.zeros(dv_sc.shape, F32)
         gb_o[...] = jnp.zeros(gb_o.shape, F32)
+        d_sc[...] = jnp.zeros(d_sc.shape, BF)
+
+    for n, d in enumerate((d0, d1, d2, d3)):
+
+        @pl.when(step_at // per == n)
+        def _(d=d):
+            d_sc[:, 0:part] = d[pl.ds(pl.multiple_of(step_at % per * BLOCK, BLOCK), BLOCK), :]
 
     start, count = place[1 + 2 * i], place[2 + 2 * i]
     qc_sc[...] = jnp.concatenate(lanes_of_heads(q[...], heads), axis=0)
-    d = do[0]
-    d = jnp.concatenate([d, jnp.zeros((BLOCK, WIDE - d.shape[1]), BF)], axis=1)
-    dc_sc[...] = jnp.concatenate(lanes_of_heads(d, heads), axis=0)
+    dz = d_sc[...]
+    dc_sc[...] = jnp.concatenate(lanes_of_heads(dz, heads), axis=0)
+    dt_sc[...] = dz.T
     dq_sc[...] = jnp.zeros(dq_sc.shape, F32)
     own = pl.ds(pl.multiple_of(i * BLOCK, BLOCK), BLOCK)
     seg_q = segr[0:1, own]
-    dl_sc[...] = jnp.zeros(dl_sc.shape, F32)
-
-    def at(j):
-        return pl.ds(pl.multiple_of(start + j * CHUNK, 128), CHUNK)
+    row = lax.broadcasted_iota(jnp.int32, (8, WIDE), 0)
+    lane = lax.broadcasted_iota(jnp.int32, (8, WIDE), 1) // HEAD
+    pick = jnp.where(row == lane, 1.0, 0.0).astype(F32)
+    delta = lax.dot_general(
+        pick, dz.astype(F32) * full[...], (((1,), (1,)), ((), ())), preferred_element_type=F32, precision=lax.Precision.HIGHEST
+    )
 
     def of(h):
         return slice(h * BLOCK, (h + 1) * BLOCK)
 
-    def pass1(j, _):
-        s = nt(k[at(j), :], qc_sc[...])
-        dp = nt(v[at(j), :], dc_sc[...])
-        keep = segc[at(j), :] == seg_q
+    def step(j, _):
+        at = pl.ds(pl.multiple_of(start + j * CHUNK, 128), CHUNK)
+        s = nt(k[at, :], qc_sc[...])
+        dp = nt(v[at, :], dc_sc[...])
+        keep = segc[at, :] == seg_q
         for h in range(heads):
+            mine = slice(h * HEAD, (h + 1) * HEAD)
             p = jnp.exp(jnp.where(keep, s[:, of(h)], NEG) - lse[h : h + 1, :])
-            p_sc[j, :, of(h)] = p
-            dp_sc[j, :, of(h)] = dp[:, of(h)]
-            dl_sc[:, of(h)] += jnp.sum((p * dp[:, of(h)]).reshape(CHUNK // 8, 8, BLOCK), axis=0)
+            ds = (p * (dp[:, of(h)] - delta[h : h + 1, :])).astype(BF)
+            dq_sc[mine, :] += nn(kt[mine, at], ds)
+            dv_sc[mine, at] += nt(dt_sc[mine, :], p.astype(BF))
+            dk_sc[mine, at] += nt(qt[mine, :], ds)
         return 0
 
-    lax.fori_loop(0, count, pass1, 0)
-    delta = jnp.sum(dl_sc[...], axis=0, keepdims=True)
-
-    def pass2(j, _):
-        ps, dss = [], []
-        for h in range(heads):
-            p = p_sc[j, :, of(h)]
-            ds = (p * (dp_sc[j, :, of(h)] - delta[:, of(h)])).astype(BF)
-            ps.append(p.astype(BF))
-            dss.append(ds)
-            dq_sc[h * HEAD : (h + 1) * HEAD, :] += nn(kt[h * HEAD : (h + 1) * HEAD, at(j)], ds)
-        dv_sc[at(j), :] += nn(jnp.concatenate(ps, axis=1), dc_sc[...])
-        dk_sc[at(j), :] += nn(jnp.concatenate(dss, axis=1), qc_sc[...])
+    def pair(j, _):
+        step(2 * j, 0)
+        step(2 * j + 1, 0)
         return 0
 
-    lax.fori_loop(0, count, pass2, 0)
+    lax.fori_loop(0, count // 2, pair, 0)
+
+    @pl.when(count % 2 == 1)
+    def _():
+        step(count - 1, 0)
 
     def turn(x, sl):
         return (x * twice(cos[sl, :]) - swap_pairs(x) * twice(sin[sl, :])).astype(BF)
@@ -261,27 +289,28 @@
     def _():
         def last(r, _):
             sl = pl.ds(pl.multiple_of(r * BLOCK, BLOCK), BLOCK)
-            put(turn(dk_sc[sl, :], sl), sl, 1)
-            put(dv_sc[sl, :].astype(BF), sl, 2)
+            put(turn(dk_sc[:, sl].T, sl), sl, 1)
+            put(dv_sc[:, sl].astype(BF).T, sl, 2)
             return 0
 
         lax.fori_loop(0, length // BLOCK, last, 0)
 
 
-def attention_backward(place, q, k, kt, v, do, lse, segc, segr, cos, sin, heads):
+def attention_backward(place, q, qt, k, kt, v, do, full, lse, segc, segr, cos, sin, heads):
     length = k.shape[0]
-    steps, per = length // BLOCK, do.shape[1] // BLOCK
     return pl.pallas_call(
         partial(backward_kernel, heads),
         grid_spec=pltpu.PrefetchScalarGridSpec(
             num_scalar_prefetch=1,
-            grid=(steps,),
+            grid=(length // BLOCK,),
             in_specs=[
                 pl.BlockSpec((BLOCK, WIDE), lambda i, s: (i ^ s[0], 0)),
+                pl.BlockSpec((WIDE, BLOCK), lambda i, s: (0, i ^ s[0])),
                 whole_block(k.shape),
                 whole_block(kt.shape),
                 whole_block(v.shape),
-                pl.BlockSpec((1, BLOCK, heads * HEAD), lambda i, s: (i // per, i % per, 0)),
+                *[whole_block(d.shape) for d in do],
+                pl.BlockSpec((BLOCK, WIDE), lambda i, s: (i, 0)),
                 pl.BlockSpec((8, BLOCK), lambda i, s: (0, i)),
                 whole_block(segc.shape),
                 whole_block(segr.shape),
@@ -289,17 +318,15 @@
                 whole_block(sin.shape),
             ],
             out_specs=[whole_block((length, 3 * WIDE)), whole_block((8, 3 * WIDE))],
-            scratch_shapes=[pltpu.VMEM((length, WIDE), F32)] * 2
+            scratch_shapes=[pltpu.VMEM((WIDE, length), F32)] * 2
             + [pltpu.VMEM((heads * BLOCK, WIDE), BF)] * 2
-            + [pltpu.VMEM((WIDE, BLOCK), F32)]
-            + [pltpu.VMEM((length // CHUNK, CHUNK, heads * BLOCK), F32)] * 2
-            + [pltpu.VMEM((8, heads * BLOCK), F32)],
+            + [pltpu.VMEM((WIDE, BLOCK), F32), pltpu.VMEM((BLOCK, WIDE), BF), pltpu.VMEM((WIDE, BLOCK), BF)],
         ),
         out_shape=[jax.ShapeDtypeStruct((length, 3 * WIDE), BF), jax.ShapeDtypeStruct((8, 3 * WIDE), F32)],
-        compiler_params=params(32),
+        compiler_params=params(28),
         cost_estimate=COST,
         name="attention_backward",
-    )(place, q, k, kt, v, do, lse, segc, segr, cos, sin)
+    )(place, q, qt, k, kt, v, *do, full, lse, segc, segr, cos, sin)
 
 
 def out_copies(place, gathered, w_out, sems):
@@ -426,7 +453,7 @@
             sd((share, 128), F32),
             sd((8, width), F32),
         ],
-        compiler_params=params(32),
+        compiler_params=params(54),
         cost_estimate=COST,
         name="feed_forward",
     )(place, gathered, gathered, *contexts, tokb, gtop, vec, bias)
@@ -500,7 +527,7 @@
         out_shape=[far((share, width), F32), far((width, share), BF)]
         + [sd((share, part), BF)] * 4
         + [far((4, share, hidden), BF), sd((4, 8, hidden), F32), sd((8, width), F32)],
-        compiler_params=params(28),
+        compiler_params=params(54),
         cost_estimate=COST,
         name="feed_back",
     )(place, gathered, gathered, gs, gsb, fs, gp, root, vec)
@@ -636,75 +663,89 @@
     )(place, *[g] * len(blocks), w)
 
 
-def split_kernel(place, *refs):
-    keep, send, last = refs[5], refs[6], place.shape[0] - 1
-    share = refs[0].shape[0]
-    core, here = place[last - 1], place[last]
-
-    def put(out, sl, k):
-        if k < 3:
-            out[sl, :] = refs[k][...]
-        else:
-            half = share // 2
-            out[pl.ds(pl.multiple_of(sl.start, half), half), :] = refs[3][...]
-            out[pl.ds(pl.multiple_of(sl.start + half, half), half), :] = refs[4][...]
-
-    for k in range(4):
-        owner = here ^ k
-        sl = pl.ds(pl.multiple_of(owner % 2 * share, share), share)
-        mine = owner // 2 == core
-
-        @pl.when(mine)
-        def _(k=k, sl=sl):
-            put(keep, sl, k)
-
-        @pl.when(jnp.logical_not(mine))
-        def _(k=k, sl=sl):
-            put(send, sl, k)
-
-
-def split_halves(place, blocks):
-    share, width = blocks[0].shape
-    shape = (2 * share, width)
-    return pl.pallas_call(
-        split_kernel,
+def pick_kernel(place, near, *refs):
+    far, (keep, send) = refs[:-2], refs[-2:]
+    last = place.shape[0] - 1
+    mine = place[last] // 2 == place[last - 1]
+
+    def put(out, parts):
+        rows = out.shape[0] // len(parts)
+        for n, x in enumerate(parts):
+            out[n * rows : (n + 1) * rows, :] = x[...]
+
+    @pl.when(mine)
+    def _():
+        put(keep, [near])
+        put(send, far)
+
+    @pl.when(jnp.logical_not(mine))
+    def _():
+        put(keep, far)
+        put(send, [near])
+
+
+def pick(place, near, *far):
+    return pl.pallas_call(
+        pick_kernel,
         grid_spec=pltpu.PrefetchScalarGridSpec(
             num_scalar_prefetch=1,
             grid=(1,),
-            in_specs=[whole_block(x.shape) for x in blocks],
-            out_specs=[whole_block(shape)] * 2,
-        ),
-        out_shape=[jax.ShapeDtypeStruct(shape, blocks[0].dtype)] * 2,
-        compiler_params=params(12),
-        cost_estimate=COST,
-        name="split_halves",
-    )(place, *blocks)
-
-
-def join_kernel(place, keep, other, out):
-    @pl.when(pl.program_id(0) == place[place.shape[0] - 2])
-    def _():
-        out[0] = keep[...]
-
-    @pl.when(pl.program_id(0) != place[place.shape[0] - 2])
-    def _():
-        out[0] = other[...]
-
-
-def join_halves(place, keep, other):
+            in_specs=[whole_block(x.shape) for x in (near, *far)],
+            out_specs=[whole_block(near.shape)] * 2,
+        ),
+        out_shape=[jax.ShapeDtypeStruct(near.shape, near.dtype)] * 2,
+        compiler_params=params(8),
+        cost_estimate=COST,
+        name="pick",
+    )(place, near, *far)
+
+
+def join_kernel(place, keep_a, keep_b, other_a, other_b, out):
+    last = place.shape[0] - 1
+    mine = pl.program_id(0) == place[last - 1]
+    same = pl.program_id(1) == place[last] % 2
+    for x, own, even in ((keep_a, True, True), (keep_b, True, False), (other_a, False, True), (other_b, False, False)):
+
+        @pl.when(jnp.logical_and(mine == own, same == even))
+        def _(x=x):
+            out[0] = x[...]
+
+
+def join(place, keeps, others):
+    share, width = keeps[0].shape
     return pl.pallas_call(
         join_kernel,
         grid_spec=pltpu.PrefetchScalarGridSpec(
             num_scalar_prefetch=1,
-            grid=(2,),
-            in_specs=[whole_block(keep.shape), whole_block(other.shape)],
-            out_specs=pl.BlockSpec((1,) + keep.shape, lambda i, s: (i, 0, 0)),
-        ),
-        out_shape=jax.ShapeDtypeStruct((2,) + keep.shape, keep.dtype),
-        compiler_params=params(16),
-        cost_estimate=COST,
-        name="join_halves",
-    )(place, keep, other)
+            grid=(2, 2),
+            in_specs=[whole_block((share, width))] * 4,
+            out_specs=pl.BlockSpec((1, share, width), lambda i, j, s: (i, j, 0)),
+        ),
+        out_shape=jax.ShapeDtypeStruct((2, 2 * share, width), keeps[0].dtype),
+        compiler_params=pltpu.CompilerParams(dimension_semantics=("arbitrary", "arbitrary"), vmem_limit_bytes=12 * 1024 * 1024),
+        cost_estimate=COST,
+        name="join",
+    )(place, *keeps, *others)
+
+
+def relay_kernel(one, two, low, high, one_o, two_o):
+    half = low.shape[0]
+    one_o[0:half, :] = (one[0:half, :] + low[...].astype(F32)).astype(BF)
+    one_o[half:, :] = one[half:, :].astype(BF)
+    two_o[0:half, :] = two[0:half, :].astype(BF)
+    two_o[half:, :] = (two[half:, :] + high[...].astype(F32)).astype(BF)
+
+
+def relay(one, two, low, high):
+    return pl.pallas_call(
+        relay_kernel,
+        in_specs=[pl.BlockSpec(memory_space=pltpu.VMEM)] * 4,
+        out_specs=[pl.BlockSpec(memory_space=pltpu.VMEM)] * 2,
+        out_shape=[jax.ShapeDtypeStruct(one.shape, BF)] * 2,
+        compiler_params=pltpu.CompilerParams(vmem_limit_bytes=16 * 1024 * 1024),
+        cost_estimate=COST,
+        name="relay",
+    )(one, two, low, high)
 
 
 def collect_kernel(place, hidden_sums, one, two, bias, out):
@@ -756,25 +797,53 @@
     )(*stacks)
 
 
-def finish_kernel(*refs):
+def finish_kernel(parts, *refs):
     out = refs[-1]
     total = refs[0][...]
     for x in refs[1:-1]:
         total = total + x[...].astype(F32)
-    out[...] = total
-
-
-def finish(*parts):
+    if parts == 1:
+        out[...] = total
+    else:
+        cols = total.shape[1] // parts
+        for m in range(parts):
+            out[:, m, :] = total[:, m * cols : (m + 1) * cols]
+
+
+def finish(parts, *pieces):
     vmem = pl.BlockSpec(memory_space=pltpu.VMEM)
-    return pl.pallas_call(
-        finish_kernel,
-        in_specs=[vmem] * len(parts),
+    rows, cols = pieces[0].shape
+    return pl.pallas_call(
+        partial(finish_kernel, parts),
+        in_specs=[vmem] * len(pieces),
         out_specs=vmem,
-        out_shape=jax.ShapeDtypeStruct(parts[0].shape, F32),
+        out_shape=jax.ShapeDtypeStruct((rows, cols) if parts == 1 else (rows, parts, cols // parts), F32),
         compiler_params=pltpu.CompilerParams(vmem_limit_bytes=8 * 1024 * 1024),
         cost_estimate=COST,
         name="finish",
-    )(*parts)
+    )(*pieces)
+
+
+def place_kernel(whole, rest, feed_o, out_o):
+    hh = rest.shape[1] // 2
+    for m in range(2):
+        feed_o[:, m, 0:hh] = whole[:, m * hh : (m + 1) * hh].astype(F32)
+        feed_o[:, m, hh:] = rest[:, m * hh : (m + 1) * hh]
+    out_o[...] = whole[:, 2 * hh :].astype(F32)
+
+
+def place_feed(whole, rest):
+    vmem = pl.BlockSpec(memory_space=pltpu.VMEM)
+    rows, cols = rest.shape
+    return pl.pallas_call(
+        place_kernel,
+        in_specs=[vmem] * 2,
+        out_specs=[vmem] * 2,
+        out_shape=[jax.ShapeDtypeStruct((rows, 2, cols), F32), jax.ShapeDtypeStruct((rows, whole.shape[1] - cols), F32)],
+        compiler_params=pltpu.CompilerParams(vmem_limit_bytes=8 * 1024 * 1024),
+        cost_estimate=COST,
+        name="place_feed",
+    )(whole, rest)
 
 
 def block_kernel(own, first, one, two, out):
@@ -854,13 +923,6 @@
 
 def after(x, *others):
     return lax.optimization_barrier((x, others))[0]
-
-
-def sum_shard(x):
-    if lax.axis_size("shard") != 4:
-        return lax.psum(x, "shard")
-    x = x + swap_shard(x, 1)
-    return x + swap_shard(x, 2)
 
 
 def gather_tp(x, half):
@@ -908,11 +970,10 @@
         return jnp.where(first_core, jnp.stack([own, other]), jnp.stack([other, own]))
 
     hh = hidden // 2
-    row = z * 2 + c
-    bias_terms = lax.dynamic_slice_in_dim(three_rows(ffn_bias), row * rows, rows, 1).T
-    extra = jnp.pad(bias_terms, ((0, 0), (0, 256 - part - 3)))
-    gathered = jnp.concatenate([ffn_weight.reshape(rows, 2 * hidden), out_weight, extra], axis=1)
-    gathered = lax.all_gather(gathered, ("tp", "shard", "ctx"), axis=0, tiled=True).reshape(4, width, 2 * hidden + 256)
+    gathered = jnp.concatenate([ffn_weight.reshape(rows, 2 * hidden), out_weight], axis=1)
+    gathered = lax.all_gather(gathered, ("tp", "shard", "ctx"), axis=0, tiled=True).reshape(4, width, 2 * hidden + part)
+    bias_all = ffn_bias.reshape(1, hidden)
+    bias_all = jnp.concatenate([bias_all] + [swap_tp(bias_all, k) for k in (1, 2, 3)])
     qkv_rows = qkv_weight.reshape(rows, 3 * part)
     other_tokens = swap_ctx(take(tokens, 1 - c))
     if direct:
@@ -941,13 +1002,13 @@
     bounds = key_bounds(segment)
     seg_column = segment[:, None]
     seg_row = jnp.broadcast_to(segment[None, :], (8, length))
-    q, k_rows, v_rows, k_turned, qkv_wide = project_qkv(place, qkv_pieces, per, bias_pad, tokens, other_tokens, cosine, sine, part)
-
-    contexts, log_totals = [None] * 4, [None] * 4
+    q, k_rows, v_rows, k_turned, q_turned, qkv_wide = project_qkv(place, qkv_pieces, per, bias_pad, tokens, other_tokens, cosine, sine, part)
+
+    contexts, log_totals, fulls = [None] * 4, [None] * 4, [None] * 4
 
     def forward(j, q):
         spot = jnp.concatenate([((t ^ j) * (share // BLOCK))[None].astype(jnp.int32), bounds])
-        context, log_totals[j] = attention_forward(spot, q, k_rows, v_rows, seg_column, seg_row, heads, share)
+        context, log_totals[j], fulls[j] = attention_forward(spot, q, k_rows, v_rows, seg_column, seg_row, heads, share)
         contexts[j] = swap_tp(context, j) if j else context
 
     forward(3, q)
@@ -957,22 +1018,14 @@
     forward(2, q_next)
     q_next, log_totals[2], contexts[1] = lax.optimization_barrier((q, log_totals[2], contexts[1]))
     forward(0, q_next)
-    log_total = jnp.concatenate(log_totals, axis=1)
-    terms = gathered[:, :, 2 * hidden + part : 2 * hidden + part + 3].astype(F32)
-    bias_all = order_four(list(jnp.sum(terms, axis=2)), t)
-
-    (
-        layer_out,
-        grad_second,
-        grad_second_b,
-        first_scaled,
-        normed_t,
-        second_t,
-        activated,
-        slope,
-        root,
-        sums_two,
-    ) = feed_forward(place, gathered, contexts, tok_block, grad_top, vec, bias_all)
+    stacked = jnp.stack(contexts)
+    tok_block, log_total, full, stacked = lax.optimization_barrier(
+        (tok_block, jnp.concatenate(log_totals, axis=1), jnp.concatenate(fulls), stacked)
+    )
+
+    layer_out, grad_second, grad_second_b, first_scaled, normed_t, second_t, activated, slope, root, sums_two = feed_forward(
+        place, gathered, contexts, tok_block, grad_top, vec, bias_all
+    )
 
     barrier = lax.optimization_barrier
     out_blocks = [layer_out, swap_tp(layer_out, 1), swap_tp(layer_out, 2)]
@@ -982,23 +1035,23 @@
     )
     heads_grads = [g0, swap_tp(g1, 1), swap_tp(g2, 2), swap_tp(g3, 3)]
 
-    contexts = jnp.stack(contexts)
-    *made, whole = weight_grads(place, per, normed_t, second_t, first_t, contexts, grad_hidden, activated)
+    *made, whole = weight_grads(place, per, normed_t, second_t, first_t, stacked, grad_hidden, activated)
     made, whole, heads_grads, out_blocks = barrier((made, whole, heads_grads, out_blocks))
     whole = lax.psum_scatter(whole.reshape(-1, 2 * hh + part), ("tp", "shard", "ctx"), scatter_dimension=0, tiled=True)
-    corner = [swap_tp(out_blocks[1][: share // 2], 2), swap_tp(out_blocks[2][share // 2 :], 1)]
-    grad_heads = jnp.stack(heads_grads)
+    grad_heads = heads_grads
+    corner = [out_blocks[1][: share // 2], out_blocks[2][share // 2 :]]
     if direct:
         got = swap_ctx(made[1])
-        grad_heads, got = barrier((grad_heads, got))
+        grad_heads, got, corner = barrier((grad_heads, got, corner))
         packs = [made[0][k].astype(F32) + got[k].astype(F32) for k in range(4)]
         sent = [packs[k].astype(BF) for k in (1, 2, 3)]
         grad_heads, sent = barrier((grad_heads, sent))
         sent = [swap_tp(sent[k - 1], k) for k in (1, 2, 3)]
+    corner = [swap_tp(corner[0], 2), swap_tp(corner[1], 1)]
 
     spot = jnp.concatenate([(t * (share // BLOCK))[None].astype(jnp.int32), bounds])
     grad_proj, bias_sums = attention_backward(
-        spot, q, k_rows, k_turned, v_rows, grad_heads, log_total, seg_column, seg_row, cosine, sine, heads
+        spot, q, q_turned, k_rows, k_turned, v_rows, grad_heads, full, log_total, seg_column, seg_row, cosine, sine, heads
     )
     grad_proj, bias_sums, corner, hidden_sums, sums_one, sums_two = barrier((grad_proj, bias_sums, corner, hidden_sums, sums_one, sums_two))
     if direct:
@@ -1008,18 +1061,28 @@
     three, grad_proj, corner, bias_sums = barrier((three, grad_proj, corner, bias_sums))
     low, high = swap_tp(three[: share // 2], 2), swap_tp(three[share // 2 :], 1)
     one, two, own = branch(place, (1, 2, 0), (F32, F32, F32), grad_proj, qkv_wide)
-    keep, send = split_halves(place, [*out_blocks, *corner])
+    keep_a, send_a = pick(place, out_blocks[0], out_blocks[2])
+    keep_b, send_b = pick(place, out_blocks[1], *corner)
     small = collect(place, hidden_sums, sums_one, sums_two, bias_sums)
-    low, high, one, two, own, keep, send, grad_proj, small = barrier((low, high, one, two, own, keep, send, grad_proj, small))
+    outs = [keep_a, keep_b, send_a, send_b]
+    low, high, one, two, own, outs, grad_proj, small = barrier((low, high, one, two, own, outs, grad_proj, small))
 
     one, two = relay(one, two, low, high)
-    one, two, send, keep, grad_proj, small = barrier((one, two, send, keep, grad_proj, small))
+    one, two, outs, grad_proj, small = barrier((one, two, outs, grad_proj, small))
     one, two = swap_tp(one, 1), swap_tp(two, 2)
     grads = qkv_weight_grads(place, per, tokens, other_tokens, grad_proj, part)
-    outputs = join_halves(place, keep, swap_ctx(send))
-    small = sum_shard(small + swap_ctx(small))
+    outputs = join(place, outs[:2], [swap_ctx(outs[2]), swap_ctx(outs[3])])
+
+    def send_shards(pieces, small, k):
+        moved = [swap_shard(pieces[j - 1], j) for j in (1, 2, 3)]
+        moved[0], small = barrier((moved[0], small))
+        return moved, small + swap_tp(small, k)
+
     if direct:
         summed, *pieces = settle(packs[0], *sent)
+        small = small + swap_ctx(small)
+        small = small + swap_shard(small, 1)
+        small = small + swap_shard(small, 2)
         qkv_sum, *qkv_pieces = settle(grads[0], swap_ctx(grads[1]))
         one, two, own, small, outputs, summed, pieces, qkv_sum, qkv_pieces = barrier(
             (one, two, own, small, outputs, summed, pieces, qkv_sum, qkv_pieces)
@@ -1029,28 +1092,27 @@
 
     block = add_block(own, grad_first, one, two)
     ready = [block, swap_tp(block, 1), swap_tp(block, 2)]
-    small = small + swap_tp(small, 1)
     if direct:
-        total = finish(summed, *[swap_shard(pieces[j - 1], j) for j in (1, 2, 3)])
+        moved, small = send_shards(pieces, small, 1)
+        total = finish(1, summed, *moved)
         ready, total, small, qkv_pieces = barrier((ready, total, small, qkv_pieces))
+        moved, small = send_shards(qkv_pieces, small, 2)
+        qkv_total = finish(3, qkv_sum, *moved)
+    else:
+        qkv_total = lax.psum_scatter(grads[0], ("shard", "ctx"), scatter_dimension=0, tiled=True).reshape(rows, 3, part)
+        total = lax.psum_scatter(made[0].reshape(-1, 2 * hh), ("tp", "shard", "ctx"), scatter_dimension=0, tiled=True).astype(F32)
     corner = [swap_tp(ready[1][: share // 2], 2), swap_tp(ready[2][share // 2 :], 1)]
-    if direct:
-        qkv_total = finish(qkv_sum, *[swap_shard(qkv_pieces[j - 1], j) for j in (1, 2, 3)])
-    else:
-        qkv_total = lax.psum_scatter(grads[0], ("shard", "ctx"), scatter_dimension=0, tiled=True)
-        total = lax.psum_scatter(made[0].reshape(-1, 2 * hh), ("tp", "shard", "ctx"), scatter_dimension=0, tiled=True).astype(F32)
-    small = small + swap_tp(small, 2)
-    qkv_total = qkv_total.reshape(rows, 3, part)
-    corner, qkv_total, total, small = barrier((corner, qkv_total, total, small))
-    keep, send = split_halves(place, [*ready, *corner])
-    grad_tokens = join_halves(place, keep, swap_ctx(send))
+    keep_a, send_a = pick(place, ready[0], ready[2])
+    other_a = swap_ctx(send_a)
+    grad_ffn_weight, grad_out_weight = place_feed(whole, total)
+    small = small if direct else lax.psum(small, ("shard", "ctx", "tp"))
+    corner, grad_ffn_weight, grad_out_weight, small, keep_a, other_a, qkv_total = barrier(
+        (corner, grad_ffn_weight, grad_out_weight, small, keep_a, other_a, qkv_total)
+    )
+    keep_b, send_b = pick(place, ready[1], *corner)
+    grad_tokens = join(place, [keep_a, keep_b], [other_a, swap_ctx(send_b)])
 
     grad_qkv_weight = qkv_total
-    whole = whole.astype(F32)
-    grad_up = jnp.concatenate([whole[:, :hh], total[:, :hh]], axis=1)
-    grad_down = jnp.concatenate([whole[:, hh : 2 * hh], total[:, hh:]], axis=1)
-    grad_ffn_weight = jnp.stack([grad_up, grad_down], axis=1)
-    grad_out_weight = whole[:, 2 * hh :]
     grad_ffn_bias = take(small, t)
     vectors = small[4:10]
     grad_qkv_bias = take(small[10:14], t).reshape(3, WIDE)[:, :part]

time: 339 us -> 326 us (0.962); the launches traced: 335 us -> 326 us
  waiting for transfers between devices: 72 us -> 91 us
  local copies, waits for them, and re-layouts: 48.4 us -> 29.6 us
  starting transfers between devices: 62.5 us -> 54.5 us
    ppermute x11, waiting for transfers between devices: 13.3 us -> 35.5 us  [swap_shard(): return lax.ppermute(x, 'shard', [(i, i ^ k) for i in range(4)])]
    all_gather x1, waiting for transfers between devices: 34.8 us -> 17.2 us  [body(): lax.all_gather(gathered, ('tp', 'shard', 'ctx'), axis=0, tiled=True)]
    unnamed x130 -> x104, local copies, waits for them, and re-layouts: 32.6 us -> 16.6 us
    ppermute x23 -> x26, waiting for transfers between devices: 20.1 us -> 31.3 us  [swap_tp(): return lax.ppermute(x, 'tp', [(i, i ^ k) for i in range(4)])]
    ppermute x11, starting transfers between devices: 24.1 us -> 13.3 us  [swap_shard(): return lax.ppermute(x, 'shard', [(i, i ^ k) for i in range(4)])]
    pallas_call x1, Pallas kernels: 28.3 us -> 20.7 us  [attention_backward(): pl.pallas_call(partial(backward_kernel, heads), grid_spec=pltpu.PrefetchS...]
    pallas_call x4, Pallas kernels: 26.1 us -> 20.6 us  [attention_forward(): pl.pallas_call(partial(forward_kernel, heads), grid_spec=pltpu.PrefetchSc...]
    ppermute x23 -> x26, starting transfers between devices: 18.3 us -> 23 us  [swap_tp(): return lax.ppermute(x, 'tp', [(i, i ^ k) for i in range(4)])]
  transfers between devices with their start and end apart: 45 -> 50, of which waited for: 16 -> 22; matrix products, arithmetic and copies ran while one was open for 9% -> 10% of each run, Pallas kernels for 31% -> 28%
where the time goes in v5:
time: 326 us
  Pallas kernels  119 us (37%)
  waiting for transfers between devices  91 us (28%)
  starting transfers between devices  54.5 us (17%)
  local copies, waits for them, and re-layouts  29.6 us (9%)
  other arithmetic  17 us (5%)
  between operations  14.8 us (5%)
    ppermute x11, waiting for transfers between devices, swap_shard(): return lax.ppermute(x, 'shard', [(i, i ^ k) for i in range(4)])  35.5 us
    ppermute x26, waiting for transfers between devices, swap_tp(): return lax.ppermute(x, 'tp', [(i, i ^ k) for i in range(4)])  31.3 us
    ppermute x26, starting transfers between devices, swap_tp(): return lax.ppermute(x, 'tp', [(i, i ^ k) for i in range(4)])  23 us
    pallas_call x1, Pallas kernels, feed_forward(): pl.pallas_call(feed_kernel, grid_spec=pltpu.PrefetchScalarGridSpec(num_sc...  21.2 us
    pallas_call x1, Pallas kernels, attention_backward(): pl.pallas_call(partial(backward_kernel, heads), grid_spec=pltpu.PrefetchS...  20.7 us
    pallas_call x4, Pallas kernels, attention_forward(): pl.pallas_call(partial(forward_kernel, heads), grid_spec=pltpu.PrefetchSc...  20.6 us
    ppermute x11, starting transfers between devices, swap_ctx(): return lax.ppermute(x, 'ctx', [(0, 1), (1, 0)])  18.1 us
    all_gather x1, waiting for transfers between devices, body(): lax.all_gather(gathered, ('tp', 'shard', 'ctx'), axis=0, tiled=True)  17.2 us
  transfers between devices with their start and end apart: 50, of which 22 were waited for; matrix products, arithmetic and copies ran while one was open for 10% of the time, Pallas kernels for 28%

profile of v5, /device:TPU:1, one launch (start us, length us, event | category | flops | bytes accessed | tf_op | source)
XLA Modules:
  0.0 326.2 jit_solution(9799183309819417968)
XLA Ops:
  8.4 1.6 pad_maximum_fusion.3
  10.7 3.0 collective-permute-start.12
  14.0 1.7 copy.27
  16.8 3.6 %collective-permute-start.3 = (bf16[96,576]{1,0:T(8,128)(2,1)S(1)}, bf16[96,576]{1,0:T(8,128)(2,1)S(1)}, u32[]{:S(2)}, u32[]{:S(2)}) collective-permute-start(bf16[96,576]{1,0:T(8,128)(2,1)S(1)} %copy.33.refs_0_), channel_id=1, source_target_pairs={{0,24},{8,16},{16,8},{24,0},{1,25},{9,17},{17,9},{25,1},{2,26},{10... | collective-permute-start | bytes 331784 | tf_op jit(solution)/shard_map/ppermute | solution.py:913
  21.3 2.1 dynamic-slice_bitcast_fusion.1
  26.9 2.1 collective-permute-start
  29.1 1.3 pad_maximum_fusion.5.bias
  32.0 3.1 collective-permute-done.2.refs_2_
  35.1 4.4 %collective-permute-done.1.refs_1_ = bf16[96,576]{1,0:T(8,128)(2,1)S(1)} collective-permute-done((bf16[96,576]{1,0:T(8,128)(2,1)S(1)}, bf16[96,576]{1,0:T(8,128)(2,1)S(1)}, u32[]{:S(2)}, u32[]{:S(2)}) %collective-permute-start.1) | collective-permute-done | bytes 110624 | tf_op jit(solution)/shard_map/ppermute | solution.py:913
  40.5 3.7 %fusion = (f32[2048,128]{1,0:T(8,128)S(1)}, f32[2048,128]{1,0:T(8,128)S(1)}) fusion(f32[128]{0:T(128)S(1)} %copy-done.47, f32[128]{0:T(128)S(1)} %copy-done.46, f32[2048]{0:T(1024)S(1)} %bitcast.124), kind=kLoop, calls=%fused_computation.8 | loop fusion | flops 524288 | bytes 2106368 | tf_op jit(solution)/shard_map/mul | solution.py:891
  45.5 1.9 copy-done.3
  47.4 1.4 copy-done.6
  49.7 5.7 %project_qkv.1 = (bf16[2048,256]{1,0:T(8,128)(2,1)S(1)}, bf16[2048,256]{1,0:T(8,128)(2,1)S(1)}, bf16[2048,256]{1,0:T(8,128)(2,1)S(1)}, bf16[256,2048]{1,0:T(8,12...) custom-call(s32[10]{0:T(128)S(1)} %stack.96.place, bf16[96,576]{1,0:T(8,128)(2,1)S(1)} %copy.33.refs_0_, ...), custom_call_target="tpu_custom_call" | custom-call | tf_op jit(solution)/shard_map/project_qkv/pallas_call | solution.py:95
  57.4 5.2 %attention_forward.4 = (bf16[512,192]{1,0:T(8,128)(2,1)S(1)}, f32[8,512]{1,0:T(8,128)S(1)}, f32[512,256]{1,0:T(8,128)S(1)}) custom-call(s32[17]{0:T(128)S(1)} %get-tuple-element.390.place, bf16[2048,256]{1,0:T(8,128)(2,1)S(1)} %get-tuple-element.193.q, bf16[2048,256]{1,0:T(8,128)(2,1)S(1)} %get-tuple-element.183.k, ...), custom_call_target="tpu_custom_call" | custom-call | tf_op jit(solution)/shard_map/attention_forward/pallas_call | solution.py:180
  62.6 2.2 collective-permute-start.6
  64.8 5.2 %attention_forward.5 = (bf16[512,192]{1,0:T(8,128)(2,1)S(1)}, f32[8,512]{1,0:T(8,128)S(1)}, f32[512,256]{1,0:T(8,128)S(1)}) custom-call(s32[17]{0:T(128)S(1)} %get-tuple-element.392.place, bf16[2048,256]{1,0:T(8,128)(2,1)S(1)} %get-tuple-element.193.q, bf16[2048,256]{1,0:T(8,128)(2,1)S(1)} %get-tuple-element.183.k, ...), custom_call_target="tpu_custom_call" | custom-call | tf_op jit(solution)/shard_map/attention_forward/pallas_call | solution.py:180
  70.3 2.4 bitcast_select_fusion.gtop
  73.7 5.2 %attention_forward.6 = (bf16[512,192]{1,0:T(8,128)(2,1)S(1)}, f32[8,512]{1,0:T(8,128)S(1)}, f32[512,256]{1,0:T(8,128)S(1)}) custom-call(s32[17]{0:T(128)S(1)} %get-tuple-element.391.place, bf16[2048,256]{1,0:T(8,128)(2,1)S(1)} %get-tuple-element.193.q, bf16[2048,256]{1,0:T(8,128)(2,1)S(1)} %get-tuple-element.183.k, ...), custom_call_target="tpu_custom_call" | custom-call | tf_op jit(solution)/shard_map/attention_forward/pallas_call | solution.py:180
  78.8 4.8 %collective-permute-done.7.c1 = bf16[512,192]{1,0:T(8,128)(2,1)S(1)} collective-permute-done((bf16[512,192]{1,0:T(8,128)(2,1)S(1)}, bf16[512,192]{1,0:T(8,128)(2,1)S(1)}, u32[]{:S(2)}, u32[]{:S(2)}) %collective-permute-start.7) | collective-permute-done | bytes 196640 | tf_op jit(solution)/shard_map/ppermute | solution.py:909
  83.7 5.2 %attention_forward.7 = (bf16[512,192]{1,0:T(8,128)(2,1)S(1)}, f32[8,512]{1,0:T(8,128)S(1)}, f32[512,256]{1,0:T(8,128)S(1)}) custom-call(s32[17]{0:T(128)S(1)} %get-tuple-element.393.place, bf16[2048,256]{1,0:T(8,128)(2,1)S(1)} %get-tuple-element.193.q, bf16[2048,256]{1,0:T(8,128)(2,1)S(1)} %get-tuple-element.183.k, ...), custom_call_target="tpu_custom_call" | custom-call | tf_op jit(solution)/shard_map/attention_forward/pallas_call | solution.py:180
  88.8 1.5 pad_maximum_fusion.full
  90.3 5.0 %collective-permute-done.8.c2 = bf16[512,192]{1,0:T(8,128)(2,1)S(1)} collective-permute-done((bf16[512,192]{1,0:T(8,128)(2,1)S(1)}, bf16[512,192]{1,0:T(8,128)(2,1)S(1)}, u32[]{:S(2)}, u32[]{:S(2)}) %collective-permute-start.8) | collective-permute-done | bytes 196640 | tf_op jit(solution)/shard_map/ppermute | solution.py:909
  97.2 17.2 %all-gather.2.cloned.1.call-done = bf16[3072,1728]{1,0:T(8,128)(2,1)} async-done(((bf16[96,1728]{1,0:T(8,128)(2,1)}), bf16[3072,1728]{1,0:T(8,128)(2,1)}) %all-gather.2.cloned.1.call-update) | async-done | bytes 10616848 | tf_op jit(solution)/shard_map/all_gather | solution.py:974
  114.4 21.2 %feed_forward.1 = (bf16[512,768]{1,0:T(8,128)(2,1)}, f32[512,768]{1,0:T(8,128)}, bf16[512,768]{1,0:T(8,128)(2,1)}, f32[512,768]{1,0:T(8,128)}, bf16[768,512]{1,0...) custom-call(s32[10]{0:T(128)} %copy-done.34, ...), custom_call_target="tpu_custom_call" | custom-call | tf_op jit(solution)/shard_map/feed_forward/pallas_call | solution.py:427
  135.9 15.2 %feed_back.1 = (f32[512,768]{1,0:T(8,128)}, bf16[768,512]{1,0:T(8,128)(2,1)}, bf16[512,192]{1,0:T(8,128)(2,1)}, bf16[512,192]{1,0:T(8,128)(2,1)}, bf16[512,192]{...) custom-call(s32[10]{0:T(128)} %copy-done.34, ...), custom_call_target="tpu_custom_call" | custom-call | tf_op jit(solution)/shard_map/feed_back/pallas_call | solution.py:511
  151.1 1.4 collective-permute-start.13
  152.5 1.4 collective-permute-start.14
  153.9 12.1 %weight_grads.1 = (bf16[4,4,96,768]{3,2,1,0:T(8,128)(2,1)}, bf16[4,4,96,768]{3,2,1,0:T(8,128)(2,1)}, bf16[4,768,960]{2,1,0:T(8,128)(2,1)}) custom-call(s32[10]{0:T(128)} %copy-done.34, bf16[768,512]{1,0:T(8,128)(2,1)} %get-tuple-element.207.nbt, bf16[768,512]{1,0:T(8,128)(2,1)} %get-tuple-element.208.gst, bf16[768,512]{1,0:T(8,128)(2,1)} %get-tuple-element.214.gft, ...), custom_call_target="tpu_custom_call" | custom-call | tf_op jit(solution)/shard_map/weight_grads/pallas_call | solution.py:579
  167.6 1.6 collective-permute-start.18
  171.5 2.1 collective-permute-done.18
  173.6 2.4 add_bitcast_fusion
  177.1 1.7 collective-permute-start.22
  180.1 1.4 collective-permute-start.20
  181.5 20.7 %attention_backward.1 = (bf16[2048,768]{1,0:T(8,128)(2,1)S(1)}, f32[8,768]{1,0:T(8,128)S(1)}) custom-call(s32[17]{0:T(128)S(1)} %get-tuple-element.393.place, bf16[2048,256]{1,0:T(8,128)(2,1)S(1)} %get-tuple-element.193.q, bf16[256,2048]{1,0:T(8,128)(2,1)S(1)} %copy-done.20, bf16[2048,256]{1,0:T(8,128)(2,1)S(1)} %get-tuple-element.183.k, ...), custom_call_target="tpu_custom_call" | custom-call | tf_op jit(solution)/shard_map/attention_backward/pallas_call | solution.py:301
  202.2 10.8 %collective-permute-done.19.refs_0_ = bf16[256,768]{1,0:T(8,128)(2,1)S(1)} collective-permute-done((bf16[256,768]{1,0:T(8,128)(2,1)S(1)}, bf16[256,768]{1,0:T(8,128)(2,1)S(1)}, u32[]{:S(2)}, u32[]{:S(2)}) %collective-permute-start.19) | collective-permute-done | bytes 393248 | tf_op jit(solution)/shard_map/ppermute | solution.py:909
  213.0 1.3 branch.2
  214.5 1.6 collective-permute-start.24
  216.2 1.8 pick.4
  218.0 2.6 branch.3
  220.6 2.0 pick.5
  223.2 4.7 %collective-permute-done.25.high = bf16[256,768]{1,0:T(8,128)(2,1)S(1)} collective-permute-done((bf16[256,768]{1,0:T(8,128)(2,1)S(1)}, bf16[256,768]{1,0:T(8,128)(2,1)S(1)}, u32[]{:S(2)}, u32[]{:S(2)}) %collective-permute-start.25) | collective-permute-done | bytes 393248 | tf_op jit(solution)/shard_map/ppermute | solution.py:909
  227.9 1.7 collective-permute-done.24.low
  229.9 4.4 %collective-permute-start.31 = (bf16[512,768]{1,0:T(8,128)(2,1)S(1)}, bf16[512,768]{1,0:T(8,128)(2,1)S(1)}, u32[]{:S(2)}, u32[]{:S(2)}) collective-permute-start(bf16[512,768]{1,0:T(8,128)(2,1)S(1)} %get-tuple-element.295), channel_id=1, source_target_pairs={{0,4},{4,0},{1,5},{5,1},{2,6},{6,2},{3,7},{7,3},{8,12},{12,8},{9,1... | collective-permute-start | bytes 2359304 | tf_op jit(solution)/shard_map/ppermute | solution.py:905
  235.6 1.9 collective-permute-start.27
  240.3 6.5 %collective-permute-done.29 = f32[16,768]{1,0:T(8,128)S(1)} collective-permute-done((f32[16,768]{1,0:T(8,128)S(1)}, f32[16,768]{1,0:T(8,128)S(1)}, u32[]{:S(2)}, u32[]{:S(2)}) %collective-permute-start.29) | collective-permute-done | bytes 49184 | tf_op jit(solution)/shard_map/ppermute | solution.py:913
  246.8 3.8 %qkv_weight_grads.1 = (f32[4,96,576]{2,1,0:T(8,128)S(1)}, bf16[4,96,576]{2,1,0:T(8,128)(2,1)S(1)}) custom-call(s32[10]{0:T(128)S(1)} %copy-done.35, bf16[2,1024,768]{2,1,0:T(8,128)(2,1)S(1)} %copy-done.4, bf16[1024,768]{1,0:T(8,128)(2,1)S(1)} %copy-done.7, bf16[2048,768]{1,0:T(8,128)(2,1)S(1)} %get-tuple-element.305.refs_0_.refs_1_.refs_2_.g), custom_call_target="tpu_custom_call" | custom-call | tf_op jit(solution)/shard_map/qkv_weight_grads/pallas_call | solution.py:623
  251.4 2.1 collective-permute-start.33
  255.1 2.7 join.2
  260.7 2.0 collective-permute-start.38
  262.7 5.9 %collective-permute-done.36.refs_1_ = bf16[96,768]{1,0:T(8,128)(2,1)S(1)} collective-permute-done((bf16[96,768]{1,0:T(8,128)(2,1)S(1)}, bf16[96,768]{1,0:T(8,128)(2,1)S(1)}, u32[]{:S(2)}, u32[]{:S(2)}) %collective-permute-start.36) | collective-permute-done | bytes 147488 | tf_op jit(solution)/shard_map/ppermute | solution.py:913
  269.2 6.2 %collective-permute-done.38.refs_3_ = bf16[96,768]{1,0:T(8,128)(2,1)S(1)} collective-permute-done((bf16[96,768]{1,0:T(8,128)(2,1)S(1)}, bf16[96,768]{1,0:T(8,128)(2,1)S(1)}, u32[]{:S(2)}, u32[]{:S(2)}) %collective-permute-start.38) | collective-permute-done | bytes 147488 | tf_op jit(solution)/shard_map/ppermute | solution.py:913
  275.5 2.5 collective-permute-done.39
  278.0 1.7 collective-permute-done.35.refs_0_
  279.8 1.5 pick.6
  285.0 2.2 collective-permute-start.42
  288.3 2.6 collective-permute-done.42.refs_1_
  291.0 1.5 collective-permute-start.46
  292.5 1.8 collective-permute-done.45.refs_2_
  294.3 1.4 collective-permute-start.43
  295.7 3.6 %collective-permute-done.46.refs_3_ = bf16[96,576]{1,0:T(8,128)(2,1)S(1)} collective-permute-done((bf16[96,576]{1,0:T(8,128)(2,1)S(1)}, bf16[96,576]{1,0:T(8,128)(2,1)S(1)}, u32[]{:S(2)}, u32[]{:S(2)}) %collective-permute-start.46) | collective-permute-done | bytes 110624 | tf_op jit(solution)/shard_map/ppermute | solution.py:913
  299.5 2.7 reduce-scatter.2.cloned.1.call-done.whole
  304.1 2.5 pick.7
  307.5 4.7 %collective-permute-start.47 = (bf16[512,768]{1,0:T(8,128)(2,1)}, bf16[512,768]{1,0:T(8,128)(2,1)S(1)}, u32[]{:S(2)}, u32[]{:S(2)}) collective-permute-start(bf16[512,768]{1,0:T(8,128)(2,1)} %get-tuple-element.348), channel_id=1, source_target_pairs={{0,4},{4,0},{1,5},{5,1},{2,6},{6,2},{3,7},{7,3},{8,12},{12,8},{9,1... | collective-permute-start | bytes 2359304 | tf_op jit(solution)/shard_map/ppermute | solution.py:905
  316.6 2.7 join.3
  (216 shorter events, 47.1 us)
Async XLA Ops:
  7.2 13.2 %copy-start.43 = (s32[2,1024]{1,0:T(2,128)S(1)}, s32[2,1024]{1,0:T(2,128)}, u32[]{:S(2)}) copy-start(s32[2,1024]{1,0:T(2,128)} %param.15) | copy-start | bytes 24580
  7.2 16.2 %copy-start.2 = (bf16[2,1024,768]{2,1,0:T(8,128)(2,1)S(1)}, bf16[2,1024,768]{2,1,0:T(8,128)(2,1)}, u32[]{:S(2)}) copy-start(bf16[2,1024,768]{2,1,0:T(8,128)(2,1)} %own.1) | copy-start | bytes 9437188
  7.2 107.2 %all-gather.2.cloned.1.call-start = ((), (), s32[]{:S(2)}) async-start(), calls=%async_computation.1 | async-start | bytes 11354112 | tf_op jit(solution)/shard_map/all_gather | solution.py:974
  10.0 292.2 %reduce-scatter.2.cloned.1.call-start = ((), (), s32[]{:S(2)}) async-start(), calls=%async_computation.2 | async-start | bytes 6488064 | tf_op jit(solution)/shard_map/reduce_scatter | solution.py:1040
  10.7 15.8 %collective-permute-start.12 = (f32[1,768]{1,0:T(1,128)S(1)}, f32[1,768]{1,0:T(1,128)}, u32[]{:S(2)}, u32[]{:S(2)}) collective-permute-start(f32[1,768]{1,0:T(1,128)S(1)} %reshape.214), channel_id=1, source_target_pairs={{0,3},{1,2},{2,1},{3,0},{4,7},{5,6},{6,5},{7,4},{8,11},{9,10},{10,... | collective-permute-start | bytes 9224 | tf_op jit(solution)/shard_map/ppermute | solution.py:909
  13.7 13.2 %collective-permute-start.11 = (f32[1,768]{1,0:T(1,128)S(1)}, f32[1,768]{1,0:T(1,128)}, u32[]{:S(2)}, u32[]{:S(2)}) collective-permute-start(f32[1,768]{1,0:T(1,128)S(1)} %reshape.214), channel_id=1, source_target_pairs={{0,2},{1,3},{2,0},{3,1},{4,6},{5,7},{6,4},{7,5},{8,10},{9,11},{10,... | collective-permute-start | bytes 9224 | tf_op jit(solution)/shard_map/ppermute | solution.py:909
  13.9 15.1 %collective-permute-start.10 = (f32[1,768]{1,0:T(1,128)S(1)}, f32[1,768]{1,0:T(1,128)}, u32[]{:S(2)}, u32[]{:S(2)}) collective-permute-start(f32[1,768]{1,0:T(1,128)S(1)} %reshape.214), channel_id=1, source_target_pairs={{0,1},{1,0},{2,3},{3,2},{4,5},{5,4},{6,7},{7,6},{8,9},{9,8},{10,11... | collective-permute-start | bytes 9224 | tf_op jit(solution)/shard_map/ppermute | solution.py:909
  16.8 15.3 %collective-permute-start.3 = (bf16[96,576]{1,0:T(8,128)(2,1)S(1)}, bf16[96,576]{1,0:T(8,128)(2,1)S(1)}, u32[]{:S(2)}, u32[]{:S(2)}) collective-permute-start(bf16[96,576]{1,0:T(8,128)(2,1)S(1)} %copy.33.refs_0_), channel_id=1, source_target_pairs={{0,24},{8,16},{16,8},{24,0},{1,25},{9,17},{17,9},{25,1},{2,26},{10... | collective-permute-start | bytes 331784 | tf_op jit(solution)/shard_map/ppermute | solution.py:913
  20.3 14.7 %collective-permute-start.2 = (bf16[96,576]{1,0:T(8,128)(2,1)S(1)}, bf16[96,576]{1,0:T(8,128)(2,1)S(1)}, u32[]{:S(2)}, u32[]{:S(2)}) collective-permute-start(bf16[96,576]{1,0:T(8,128)(2,1)S(1)} %copy.33.refs_0_), channel_id=1, source_target_pairs={{0,16},{8,24},{16,0},{24,8},{1,17},{9,25},{17,1},{25,9},{2,18},{10... | collective-permute-start | bytes 331784 | tf_op jit(solution)/shard_map/ppermute | solution.py:913
  24.6 15.9 %copy-start.46 = (f32[128]{0:T(128)S(1)}, f32[128]{0:T(128)}, u32[]{:S(2)}) copy-start(f32[128]{0:T(128)} %constant.195) | copy-start | bytes 1540
  24.6 15.9 %copy-start.47 = (f32[128]{0:T(128)S(1)}, f32[128]{0:T(128)}, u32[]{:S(2)}) copy-start(f32[128]{0:T(128)} %constant.188.clone) | copy-start | bytes 1540
  26.5 19.0 %copy-start.34 = (s32[10]{0:T(128)}, s32[10]{0:T(128)S(1)}, u32[]{:S(2)}) copy-start(s32[10]{0:T(128)S(1)} %stack.96.place) | copy-start | bytes 124
  26.5 13.0 %collective-permute-start.1 = (bf16[96,576]{1,0:T(8,128)(2,1)S(1)}, bf16[96,576]{1,0:T(8,128)(2,1)S(1)}, u32[]{:S(2)}, u32[]{:S(2)}) collective-permute-start(bf16[96,576]{1,0:T(8,128)(2,1)S(1)} %copy.33.refs_0_), channel_id=1, source_target_pairs={{0,8},{8,0},{16,24},{24,16},{1,9},{9,1},{17,25},{25,17},{2,10},{10... | collective-permute-start | bytes 331784 | tf_op jit(solution)/shard_map/ppermute | solution.py:913
  26.9 3.5 %collective-permute-start = (s32[2,1024]{1,0:T(2,128)S(1)}, s32[2,1024]{1,0:T(2,128)S(1)}, u32[]{:S(2)}, u32[]{:S(2)}) collective-permute-start(s32[2,1024]{1,0:T(2,128)S(1)} %bitcast.126), channel_id=1, source_target_pairs={{0,4},{4,0},{1,5},{5,1},{2,6},{6,2},{3,7},{7,3},{8,12},{12,8},{9,1... | collective-permute-start | bytes 24584 | tf_op jit(solution)/shard_map/ppermute | solution.py:905
  29.0 15.3 %collective-permute-start.5 = (bf16[1024,768]{1,0:T(8,128)(2,1)}, bf16[1024,768]{1,0:T(8,128)(2,1)S(1)}, u32[]{:S(2)}, u32[]{:S(2)}) collective-permute-start(bf16[1024,768]{1,0:T(8,128)(2,1)} %dynamic-slice_bitcast_fusion), channel_id=1, source_target_pairs={{0,4},{4,0},{1,5},{5,1},{2,6},{6,2},{3,7},{7,3},{8,12},{12,8},{9,1... | collective-permute-start | bytes 4718600 | tf_op jit(solution)/shard_map/ppermute | solution.py:905
  30.4 39.9 %collective-permute-start.9 = (bf16[512,768]{1,0:T(8,128)(2,1)}, bf16[512,768]{1,0:T(8,128)(2,1)}, u32[]{:S(2)}, u32[]{:S(2)}) collective-permute-start(bf16[512,768]{1,0:T(8,128)(2,1)} %dynamic-slice_bitcast_fusion.1), channel_id=1, source_target_pairs={{0,4},{4,0},{1,5},{5,1},{2,6},{6,2},{3,7},{7,3},{8,12},{12,8},{9,1... | collective-permute-start | bytes 2359304 | tf_op jit(solution)/shard_map/ppermute | solution.py:905
  39.6 4.6 %collective-permute-start.4 = (bf16[4,96,576]{2,1,0:T(8,128)(2,1)S(1)}, bf16[4,96,576]{2,1,0:T(8,128)(2,1)S(1)}, u32[]{:S(2)}, u32[]{:S(2)}) collective-permute-start(bf16[4,96,576]{2,1,0:T(8,128)(2,1)S(1)} %pad_maximum_fusion.2), channel_id=1, source_target_pairs={{0,4},{4,0},{1,5},{5,1},{2,6},{6,2},{3,7},{7,3},{8,12},{12,8},{9,1... | collective-permute-start | bytes 1327112 | tf_op jit(solution)/shard_map/ppermute | solution.py:905
  57.4 26.2 %copy-start = (bf16[2048,256]{1,0:T(8,128)(2,1)}, bf16[2048,256]{1,0:T(8,128)(2,1)S(1)}, u32[]{:S(2)}) copy-start(bf16[2048,256]{1,0:T(8,128)(2,1)S(1)} %get-tuple-element.185.v) | copy-start | bytes 3145732
  62.6 11.0 %collective-permute-start.6 = (bf16[512,192]{1,0:T(8,128)(2,1)S(1)}, bf16[512,192]{1,0:T(8,128)(2,1)S(1)}, u32[]{:S(2)}, u32[]{:S(2)}) collective-permute-start(bf16[512,192]{1,0:T(8,128)(2,1)S(1)} %get-tuple-element.189), channel_id=1, source_target_pairs={{0,3},{1,2},{2,1},{3,0},{4,7},{5,6},{6,5},{7,4},{8,11},{9,10},{10,... | collective-permute-start | bytes 589832 | tf_op jit(solution)/shard_map/ppermute | solution.py:909
  70.0 13.6 %collective-permute-start.7 = (bf16[512,192]{1,0:T(8,128)(2,1)S(1)}, bf16[512,192]{1,0:T(8,128)(2,1)S(1)}, u32[]{:S(2)}, u32[]{:S(2)}) collective-permute-start(bf16[512,192]{1,0:T(8,128)(2,1)S(1)} %get-tuple-element.192), channel_id=1, source_target_pairs={{0,1},{1,0},{2,3},{3,2},{4,5},{5,4},{6,7},{7,6},{8,9},{9,8},{10,11... | collective-permute-start | bytes 589832 | tf_op jit(solution)/shard_map/ppermute | solution.py:909
  73.7 21.7 %copy-start.39 = (bf16[512,192]{1,0:T(8,128)(2,1)}, bf16[512,192]{1,0:T(8,128)(2,1)S(1)}, u32[]{:S(2)}) copy-start(bf16[512,192]{1,0:T(8,128)(2,1)S(1)} %collective-permute-done.6.c3) | copy-start | bytes 589828
  83.6 11.7 %copy-start.40 = (bf16[512,192]{1,0:T(8,128)(2,1)}, bf16[512,192]{1,0:T(8,128)(2,1)S(1)}, u32[]{:S(2)}) copy-start(bf16[512,192]{1,0:T(8,128)(2,1)S(1)} %collective-permute-done.7.c1) | copy-start | bytes 589828
  83.6 11.7 %collective-permute-start.8 = (bf16[512,192]{1,0:T(8,128)(2,1)S(1)}, bf16[512,192]{1,0:T(8,128)(2,1)S(1)}, u32[]{:S(2)}, u32[]{:S(2)}) collective-permute-start(bf16[512,192]{1,0:T(8,128)(2,1)S(1)} %get-tuple-element.196), channel_id=1, source_target_pairs={{0,2},{1,3},{2,0},{3,1},{4,6},{5,7},{6,4},{7,5},{8,10},{9,11},{10,... | collective-permute-start | bytes 589832 | tf_op jit(solution)/shard_map/ppermute | solution.py:909
  135.6 32.0 %collective-permute-start.17 = (bf16[512,768]{1,0:T(8,128)(2,1)}, bf16[512,768]{1,0:T(8,128)(2,1)}, u32[]{:S(2)}, u32[]{:S(2)}) collective-permute-start(bf16[512,768]{1,0:T(8,128)(2,1)} %get-tuple-element.266.near), channel_id=1, source_target_pairs={{0,2},{1,3},{2,0},{3,1},{4,6},{5,7},{6,4},{7,5},{8,10},{9,11},{10,... | collective-permute-start | bytes 2359304 | tf_op jit(solution)/shard_map/ppermute | solution.py:909
  135.7 31.9 %collective-permute-start.16 = (bf16[512,768]{1,0:T(8,128)(2,1)}, bf16[512,768]{1,0:T(8,128)(2,1)}, u32[]{:S(2)}, u32[]{:S(2)}) collective-permute-start(bf16[512,768]{1,0:T(8,128)(2,1)} %get-tuple-element.266.near), channel_id=1, source_target_pairs={{0,1},{1,0},{2,3},{3,2},{4,5},{5,4},{6,7},{7,6},{8,9},{9,8},{10,11... | collective-permute-start | bytes 2359304 | tf_op jit(solution)/shard_map/ppermute | solution.py:909
  151.1 14.9 %collective-permute-start.13 = (bf16[512,192]{1,0:T(8,128)(2,1)}, bf16[512,192]{1,0:T(8,128)(2,1)S(1)}, u32[]{:S(2)}, u32[]{:S(2)}) collective-permute-start(bf16[512,192]{1,0:T(8,128)(2,1)} %get-tuple-element.222), channel_id=1, source_target_pairs={{0,1},{1,0},{2,3},{3,2},{4,5},{5,4},{6,7},{7,6},{8,9},{9,8},{10,11... | collective-permute-start | bytes 589832 | tf_op jit(solution)/shard_map/ppermute | solution.py:909
  152.5 13.5 %collective-permute-start.14 = (bf16[512,192]{1,0:T(8,128)(2,1)}, bf16[512,192]{1,0:T(8,128)(2,1)S(1)}, u32[]{:S(2)}, u32[]{:S(2)}) collective-permute-start(bf16[512,192]{1,0:T(8,128)(2,1)} %get-tuple-element.223), channel_id=1, source_target_pairs={{0,2},{1,3},{2,0},{3,1},{4,6},{5,7},{6,4},{7,5},{8,10},{9,11},{10,... | collective-permute-start | bytes 589832 | tf_op jit(solution)/shard_map/ppermute | solution.py:909
  153.9 13.0 %collective-permute-start.15 = (bf16[512,192]{1,0:T(8,128)(2,1)}, bf16[512,192]{1,0:T(8,128)(2,1)S(1)}, u32[]{:S(2)}, u32[]{:S(2)}) collective-permute-start(bf16[512,192]{1,0:T(8,128)(2,1)} %get-tuple-element.224), channel_id=1, source_target_pairs={{0,3},{1,2},{2,1},{3,0},{4,7},{5,6},{6,5},{7,4},{8,11},{9,10},{10,... | collective-permute-start | bytes 589832 | tf_op jit(solution)/shard_map/ppermute | solution.py:909
  167.6 6.0 %collective-permute-start.18 = (bf16[4,4,96,768]{3,2,1,0:T(8,128)(2,1)}, bf16[4,4,96,768]{3,2,1,0:T(8,128)(2,1)S(1)}, u32[]{:S(2)}, u32[]{:S(2)}) collective-permute-start(bf16[4,4,96,768]{3,2,1,0:T(8,128)(2,1)} %get-tuple-element.230), channel_id=1, source_target_pairs={{0,4},{4,0},{1,5},{5,1},{2,6},{6,2},{3,7},{7,3},{8,12},{12,8},{9,1... | collective-permute-start | bytes 7077896 | tf_op jit(solution)/shard_map/ppermute | solution.py:905
  170.3 11.2 %copy-start.28 = (bf16[512,192]{1,0:T(8,128)(2,1)S(1)}, bf16[512,192]{1,0:T(8,128)(2,1)}, u32[]{:S(2)}) copy-start(bf16[512,192]{1,0:T(8,128)(2,1)} %copy-done.27) | copy-start | bytes 589828
  170.3 11.2 %copy-start.30 = (bf16[512,192]{1,0:T(8,128)(2,1)S(1)}, bf16[512,192]{1,0:T(8,128)(2,1)}, u32[]{:S(2)}) copy-start(bf16[512,192]{1,0:T(8,128)(2,1)} %copy-done.29) | copy-start | bytes 589828
  176.0 37.0 %collective-permute-start.21 = (bf16[4,96,768]{2,1,0:T(8,128)(2,1)S(1)}, bf16[4,96,768]{2,1,0:T(8,128)(2,1)S(1)}, u32[]{:S(2)}, u32[]{:S(2)}) collective-permute-start(bf16[4,96,768]{2,1,0:T(8,128)(2,1)S(1)} %get-tuple-element.253), channel_id=1, source_target_pairs={{0,1},{1,0},{2,3},{3,2},{4,5},{5,4},{6,7},{7,6},{8,9},{9,8},{10,11... | collective-permute-start | bytes 1769480 | tf_op jit(solution)/shard_map/ppermute | solution.py:909
  177.1 35.9 %collective-permute-start.22 = (bf16[4,96,768]{2,1,0:T(8,128)(2,1)S(1)}, bf16[4,96,768]{2,1,0:T(8,128)(2,1)S(1)}, u32[]{:S(2)}, u32[]{:S(2)}) collective-permute-start(bf16[4,96,768]{2,1,0:T(8,128)(2,1)S(1)} %get-tuple-element.254), channel_id=1, source_target_pairs={{0,2},{1,3},{2,0},{3,1},{4,6},{5,7},{6,4},{7,5},{8,10},{9,11},{10,... | collective-permute-start | bytes 1769480 | tf_op jit(solution)/shard_map/ppermute | solution.py:909
  178.8 34.2 %collective-permute-start.23 = (bf16[4,96,768]{2,1,0:T(8,128)(2,1)S(1)}, bf16[4,96,768]{2,1,0:T(8,128)(2,1)S(1)}, u32[]{:S(2)}, u32[]{:S(2)}) collective-permute-start(bf16[4,96,768]{2,1,0:T(8,128)(2,1)S(1)} %get-tuple-element.255), channel_id=1, source_target_pairs={{0,3},{1,2},{2,1},{3,0},{4,7},{5,6},{6,5},{7,4},{8,11},{9,10},{10,... | collective-permute-start | bytes 1769480 | tf_op jit(solution)/shard_map/ppermute | solution.py:909
  178.8 34.2 %collective-permute-start.19 = (bf16[256,768]{1,0:T(8,128)(2,1)S(1)}, bf16[256,768]{1,0:T(8,128)(2,1)S(1)}, u32[]{:S(2)}, u32[]{:S(2)}) collective-permute-start(bf16[256,768]{1,0:T(8,128)(2,1)S(1)} %slice.73), channel_id=1, source_target_pairs={{0,2},{1,3},{2,0},{3,1},{4,6},{5,7},{6,4},{7,5},{8,10},{9,11},{10,... | collective-permute-start | bytes 1179656 | tf_op jit(solution)/shard_map/ppermute | solution.py:909
  180.1 32.9 %collective-permute-start.20 = (bf16[256,768]{1,0:T(8,128)(2,1)S(1)}, bf16[256,768]{1,0:T(8,128)(2,1)S(1)}, u32[]{:S(2)}, u32[]{:S(2)}) collective-permute-start(bf16[256,768]{1,0:T(8,128)(2,1)S(1)} %slice.74), channel_id=1, source_target_pairs={{0,1},{1,0},{2,3},{3,2},{4,5},{5,4},{6,7},{7,6},{8,9},{9,8},{10,11... | collective-permute-start | bytes 1179656 | tf_op jit(solution)/shard_map/ppermute | solution.py:909
  181.5 31.5 %copy-start.14 = (bf16[768,768]{1,0:T(8,128)(2,1)S(1)}, bf16[768,768]{1,0:T(8,128)(2,1)}, u32[]{:S(2)}) copy-start(bf16[768,768]{1,0:T(8,128)(2,1)} %copy-done.13) | copy-start | bytes 3538948
  181.5 31.5 %copy-start.35 = (s32[10]{0:T(128)S(1)}, s32[10]{0:T(128)}, u32[]{:S(2)}) copy-start(s32[10]{0:T(128)} %copy-done.34) | copy-start | bytes 124
  214.5 13.5 %collective-permute-start.25 = (bf16[256,768]{1,0:T(8,128)(2,1)S(1)}, bf16[256,768]{1,0:T(8,128)(2,1)S(1)}, u32[]{:S(2)}, u32[]{:S(2)}) collective-permute-start(bf16[256,768]{1,0:T(8,128)(2,1)S(1)} %get-tuple-element.377), channel_id=1, source_target_pairs={{0,1},{1,0},{2,3},{3,2},{4,5},{5,4},{6,7},{7,6},{8,9},{9,8},{10,11... | collective-permute-start | bytes 1179656 | tf_op jit(solution)/shard_map/ppermute | solution.py:909
  214.5 15.1 %collective-permute-start.24 = (bf16[256,768]{1,0:T(8,128)(2,1)S(1)}, bf16[256,768]{1,0:T(8,128)(2,1)S(1)}, u32[]{:S(2)}, u32[]{:S(2)}) collective-permute-start(bf16[256,768]{1,0:T(8,128)(2,1)S(1)} %get-tuple-element.378), channel_id=1, source_target_pairs={{0,2},{1,3},{2,0},{3,1},{4,6},{5,7},{6,4},{7,5},{8,10},{9,11},{10,... | collective-permute-start | bytes 1179656 | tf_op jit(solution)/shard_map/ppermute | solution.py:909
  220.6 26.3 %copy-start.7 = (bf16[1024,768]{1,0:T(8,128)(2,1)S(1)}, bf16[1024,768]{1,0:T(8,128)(2,1)}, u32[]{:S(2)}) copy-start(bf16[1024,768]{1,0:T(8,128)(2,1)} %copy-done.5) | copy-start | bytes 4718596
  229.6 17.2 %copy-start.4 = (bf16[2,1024,768]{2,1,0:T(8,128)(2,1)S(1)}, bf16[2,1024,768]{2,1,0:T(8,128)(2,1)}, u32[]{:S(2)}) copy-start(bf16[2,1024,768]{2,1,0:T(8,128)(2,1)} %own.1) | copy-start | bytes 9437188
  229.9 25.3 %collective-permute-start.31 = (bf16[512,768]{1,0:T(8,128)(2,1)S(1)}, bf16[512,768]{1,0:T(8,128)(2,1)S(1)}, u32[]{:S(2)}, u32[]{:S(2)}) collective-permute-start(bf16[512,768]{1,0:T(8,128)(2,1)S(1)} %get-tuple-element.295), channel_id=1, source_target_pairs={{0,4},{4,0},{1,5},{5,1},{2,6},{6,2},{3,7},{7,3},{8,12},{12,8},{9,1... | collective-permute-start | bytes 2359304 | tf_op jit(solution)/shard_map/ppermute | solution.py:905
  234.3 20.8 %collective-permute-start.32 = (bf16[512,768]{1,0:T(8,128)(2,1)S(1)}, bf16[512,768]{1,0:T(8,128)(2,1)S(1)}, u32[]{:S(2)}, u32[]{:S(2)}) collective-permute-start(bf16[512,768]{1,0:T(8,128)(2,1)S(1)} %get-tuple-element.296), channel_id=1, source_target_pairs={{0,4},{4,0},{1,5},{5,1},{2,6},{6,2},{3,7},{7,3},{8,12},{12,8},{9,1... | collective-permute-start | bytes 2359304 | tf_op jit(solution)/shard_map/ppermute | solution.py:905
  234.4 23.5 %collective-permute-start.26 = (bf16[512,768]{1,0:T(8,128)(2,1)S(1)}, bf16[512,768]{1,0:T(8,128)(2,1)S(1)}, u32[]{:S(2)}, u32[]{:S(2)}) collective-permute-start(bf16[512,768]{1,0:T(8,128)(2,1)S(1)} %get-tuple-element.289), channel_id=1, source_target_pairs={{0,1},{1,0},{2,3},{3,2},{4,5},{5,4},{6,7},{7,6},{8,9},{9,8},{10,11... | collective-permute-start | bytes 2359304 | tf_op jit(solution)/shard_map/ppermute | solution.py:909
  235.6 22.2 %collective-permute-start.27 = (bf16[512,768]{1,0:T(8,128)(2,1)S(1)}, bf16[512,768]{1,0:T(8,128)(2,1)S(1)}, u32[]{:S(2)}, u32[]{:S(2)}) collective-permute-start(bf16[512,768]{1,0:T(8,128)(2,1)S(1)} %get-tuple-element.290), channel_id=1, source_target_pairs={{0,2},{1,3},{2,0},{3,1},{4,6},{5,7},{6,4},{7,5},{8,10},{9,11},{10,... | collective-permute-start | bytes 2359304 | tf_op jit(solution)/shard_map/ppermute | solution.py:909
  237.6 1.9 collective-permute-start.28
  239.4 7.3 %collective-permute-start.29 = (f32[16,768]{1,0:T(8,128)S(1)}, f32[16,768]{1,0:T(8,128)S(1)}, u32[]{:S(2)}, u32[]{:S(2)}) collective-permute-start(f32[16,768]{1,0:T(8,128)S(1)} %add.168), channel_id=1, source_target_pairs={{0,8},{8,0},{16,24},{24,16},{1,9},{9,1},{17,25},{25,17},{2,10},{10... | collective-permute-start | bytes 147464 | tf_op jit(solution)/shard_map/ppermute | solution.py:913
  246.7 4.7 %collective-permute-start.30 = (f32[16,768]{1,0:T(8,128)S(1)}, f32[16,768]{1,0:T(8,128)S(1)}, u32[]{:S(2)}, u32[]{:S(2)}) collective-permute-start(f32[16,768]{1,0:T(8,128)S(1)} %add.169), channel_id=1, source_target_pairs={{0,16},{8,24},{16,0},{24,8},{1,17},{9,25},{17,1},{25,9},{2,18},{10... | collective-permute-start | bytes 147464 | tf_op jit(solution)/shard_map/ppermute | solution.py:913
  251.4 3.6 %collective-permute-start.33 = (bf16[4,96,576]{2,1,0:T(8,128)(2,1)S(1)}, bf16[4,96,576]{2,1,0:T(8,128)(2,1)S(1)}, u32[]{:S(2)}, u32[]{:S(2)}) collective-permute-start(bf16[4,96,576]{2,1,0:T(8,128)(2,1)S(1)} %get-tuple-element.307), channel_id=1, source_target_pairs={{0,4},{4,0},{1,5},{5,1},{2,6},{6,2},{3,7},{7,3},{8,12},{12,8},{9,1... | collective-permute-start | bytes 1327112 | tf_op jit(solution)/shard_map/ppermute | solution.py:905
  258.2 21.5 %collective-permute-start.35 = (bf16[512,768]{1,0:T(8,128)(2,1)S(1)}, bf16[512,768]{1,0:T(8,128)(2,1)S(1)}, u32[]{:S(2)}, u32[]{:S(2)}) collective-permute-start(bf16[512,768]{1,0:T(8,128)(2,1)S(1)} %add_block.1.near), channel_id=1, source_target_pairs={{0,2},{1,3},{2,0},{3,1},{4,6},{5,7},{6,4},{7,5},{8,10},{9,11},{10,... | collective-permute-start | bytes 2359304 | tf_op jit(solution)/shard_map/ppermute | solution.py:909
  258.4 21.4 %collective-permute-start.34 = (bf16[512,768]{1,0:T(8,128)(2,1)S(1)}, bf16[512,768]{1,0:T(8,128)(2,1)S(1)}, u32[]{:S(2)}, u32[]{:S(2)}) collective-permute-start(bf16[512,768]{1,0:T(8,128)(2,1)S(1)} %add_block.1.near), channel_id=1, source_target_pairs={{0,1},{1,0},{2,3},{3,2},{4,5},{5,4},{6,7},{7,6},{8,9},{9,8},{10,11... | collective-permute-start | bytes 2359304 | tf_op jit(solution)/shard_map/ppermute | solution.py:909
  259.2 9.5 %collective-permute-start.36 = (bf16[96,768]{1,0:T(8,128)(2,1)S(1)}, bf16[96,768]{1,0:T(8,128)(2,1)S(1)}, u32[]{:S(2)}, u32[]{:S(2)}) collective-permute-start(bf16[96,768]{1,0:T(8,128)(2,1)S(1)} %get-tuple-element.318), channel_id=1, source_target_pairs={{0,8},{8,0},{16,24},{24,16},{1,9},{9,1},{17,25},{25,17},{2,10},{10... | collective-permute-start | bytes 442376 | tf_op jit(solution)/shard_map/ppermute | solution.py:913
  259.8 9.4 %collective-permute-start.37 = (bf16[96,768]{1,0:T(8,128)(2,1)S(1)}, bf16[96,768]{1,0:T(8,128)(2,1)S(1)}, u32[]{:S(2)}, u32[]{:S(2)}) collective-permute-start(bf16[96,768]{1,0:T(8,128)(2,1)S(1)} %get-tuple-element.321), channel_id=1, source_target_pairs={{0,16},{8,24},{16,0},{24,8},{1,17},{9,25},{17,1},{25,9},{2,18},{10... | collective-permute-start | bytes 442376 | tf_op jit(solution)/shard_map/ppermute | solution.py:913
  260.7 14.8 %collective-permute-start.38 = (bf16[96,768]{1,0:T(8,128)(2,1)S(1)}, bf16[96,768]{1,0:T(8,128)(2,1)S(1)}, u32[]{:S(2)}, u32[]{:S(2)}) collective-permute-start(bf16[96,768]{1,0:T(8,128)(2,1)S(1)} %get-tuple-element.322), channel_id=1, source_target_pairs={{0,24},{8,16},{16,8},{24,0},{1,25},{9,17},{17,9},{25,1},{2,26},{10... | collective-permute-start | bytes 442376 | tf_op jit(solution)/shard_map/ppermute | solution.py:913
  268.6 9.4 %collective-permute-start.39 = (f32[16,768]{1,0:T(8,128)S(1)}, f32[16,768]{1,0:T(8,128)S(1)}, u32[]{:S(2)}, u32[]{:S(2)}) collective-permute-start(f32[16,768]{1,0:T(8,128)S(1)} %add.170), channel_id=1, source_target_pairs={{0,1},{1,0},{2,3},{3,2},{4,5},{5,4},{6,7},{7,6},{8,9},{9,8},{10,11... | collective-permute-start | bytes 147464 | tf_op jit(solution)/shard_map/ppermute | solution.py:909
  281.3 22.8 %collective-permute-start.44 = (bf16[512,768]{1,0:T(8,128)(2,1)}, bf16[512,768]{1,0:T(8,128)(2,1)S(1)}, u32[]{:S(2)}, u32[]{:S(2)}) collective-permute-start(bf16[512,768]{1,0:T(8,128)(2,1)} %get-tuple-element.338), channel_id=1, source_target_pairs={{0,4},{4,0},{1,5},{5,1},{2,6},{6,2},{3,7},{7,3},{8,12},{12,8},{9,1... | collective-permute-start | bytes 2359304 | tf_op jit(solution)/shard_map/ppermute | solution.py:905
  283.5 20.6 %collective-permute-start.41 = (bf16[256,768]{1,0:T(8,128)(2,1)}, bf16[256,768]{1,0:T(8,128)(2,1)S(1)}, u32[]{:S(2)}, u32[]{:S(2)}) collective-permute-start(bf16[256,768]{1,0:T(8,128)(2,1)} %slice.86), channel_id=1, source_target_pairs={{0,1},{1,0},{2,3},{3,2},{4,5},{5,4},{6,7},{7,6},{8,9},{9,8},{10,11... | collective-permute-start | bytes 1179656 | tf_op jit(solution)/shard_map/ppermute | solution.py:909
  284.7 19.4 %collective-permute-start.40 = (bf16[256,768]{1,0:T(8,128)(2,1)}, bf16[256,768]{1,0:T(8,128)(2,1)}, u32[]{:S(2)}, u32[]{:S(2)}) collective-permute-start(bf16[256,768]{1,0:T(8,128)(2,1)} %slice.85), channel_id=1, source_target_pairs={{0,2},{1,3},{2,0},{3,1},{4,6},{5,7},{6,4},{7,5},{8,10},{9,11},{10,... | collective-permute-start | bytes 1179656 | tf_op jit(solution)/shard_map/ppermute | solution.py:909
  285.0 6.0 %collective-permute-start.42 = (bf16[96,576]{1,0:T(8,128)(2,1)S(1)}, bf16[96,576]{1,0:T(8,128)(2,1)S(1)}, u32[]{:S(2)}, u32[]{:S(2)}) collective-permute-start(bf16[96,576]{1,0:T(8,128)(2,1)S(1)} %get-tuple-element.333), channel_id=1, source_target_pairs={{0,8},{8,0},{16,24},{24,16},{1,9},{9,1},{17,25},{25,17},{2,10},{10... | collective-permute-start | bytes 331784 | tf_op jit(solution)/shard_map/ppermute | solution.py:913
  287.2 7.1 %collective-permute-start.45 = (bf16[96,576]{1,0:T(8,128)(2,1)S(1)}, bf16[96,576]{1,0:T(8,128)(2,1)S(1)}, u32[]{:S(2)}, u32[]{:S(2)}) collective-permute-start(bf16[96,576]{1,0:T(8,128)(2,1)S(1)} %get-tuple-element.341), channel_id=1, source_target_pairs={{0,16},{8,24},{16,0},{24,8},{1,17},{9,25},{17,1},{25,9},{2,18},{10... | collective-permute-start | bytes 331784 | tf_op jit(solution)/shard_map/ppermute | solution.py:913
  291.0 8.3 %collective-permute-start.46 = (bf16[96,576]{1,0:T(8,128)(2,1)S(1)}, bf16[96,576]{1,0:T(8,128)(2,1)S(1)}, u32[]{:S(2)}, u32[]{:S(2)}) collective-permute-start(bf16[96,576]{1,0:T(8,128)(2,1)S(1)} %get-tuple-element.342), channel_id=1, source_target_pairs={{0,24},{8,16},{16,8},{24,0},{1,25},{9,17},{17,9},{25,1},{2,26},{10... | collective-permute-start | bytes 331784 | tf_op jit(solution)/shard_map/ppermute | solution.py:913
  294.3 5.2 %collective-permute-start.43 = (f32[16,768]{1,0:T(8,128)S(1)}, f32[16,768]{1,0:T(8,128)S(1)}, u32[]{:S(2)}, u32[]{:S(2)}) collective-permute-start(f32[16,768]{1,0:T(8,128)S(1)} %add.171), channel_id=1, source_target_pairs={{0,2},{1,3},{2,0},{3,1},{4,6},{5,7},{6,4},{7,5},{8,10},{9,11},{10,... | collective-permute-start | bytes 147464 | tf_op jit(solution)/shard_map/ppermute | solution.py:909
  307.5 8.0 %collective-permute-start.47 = (bf16[512,768]{1,0:T(8,128)(2,1)}, bf16[512,768]{1,0:T(8,128)(2,1)S(1)}, u32[]{:S(2)}, u32[]{:S(2)}) collective-permute-start(bf16[512,768]{1,0:T(8,128)(2,1)} %get-tuple-element.348), channel_id=1, source_target_pairs={{0,4},{4,0},{1,5},{5,1},{2,6},{6,2},{3,7},{7,3},{8,12},{12,8},{9,1... | collective-permute-start | bytes 2359304 | tf_op jit(solution)/shard_map/ppermute | solution.py:905
  (34 other events, 154.4 us)
Sparse Core Ops, SparseCore 0:
  11.6 102.7 all-gather.1
  167.7 134.4 reduce-scatter.1

commit v6 on v5

--- a/solution.py
+++ b/solution.py
@@ -213,21 +213,47 @@
     )(place, q, k, v, segc, segr)
 
 
-def backward_kernel(heads, place, q, qt, k, kt, v, d0, d1, d2, d3, full, lse, segc, segr, cos, sin, g_o, gb_o, dk_sc, dv_sc, qc_sc, dc_sc, dq_sc, d_sc, dt_sc):
+def backward_kernel(heads, place, q, qt, k, kt, v, d0, d1, d2, d3, full, lse, segc, segr, cos, sin, g_o, gb_o, dk_sc, dv_sc, qc_sc, dc_sc, dq_sc, d_sc, dt_sc, qs_sc):
+    step_at = pl.program_id(0)
+    blocks = k.shape[0] // BLOCK
+
+    @pl.when(step_at < blocks)
+    def _():
+        backward_rows(heads, place, q, qt, k, kt, v, (d0, d1, d2, d3), full, lse, segc, segr, dk_sc, dv_sc, qc_sc, dc_sc, dq_sc, d_sc, dt_sc, qs_sc)
+
+    @pl.when(step_at == 0)
+    def _():
+        gb_o[...] = jnp.zeros(gb_o.shape, F32)
+
+    @pl.when(step_at >= blocks)
+    def _():
+        at = pl.ds(pl.multiple_of((step_at - blocks) * BLOCK, BLOCK), BLOCK)
+
+        def turn(x):
+            return (x * twice(cos[...]) - swap_pairs(x) * twice(sin[...])).astype(BF)
+
+        def put(x, m):
+            g_o[:, m * WIDE : (m + 1) * WIDE] = x
+            gb_o[0:1, m * WIDE : (m + 1) * WIDE] += jnp.sum(x.astype(F32), axis=0, keepdims=True)
+
+        put(turn(qs_sc[:, at].T * (HEAD**-0.5)), 0)
+        put(turn(dk_sc[:, at].T), 1)
+        put(dv_sc[:, at].astype(BF).T, 2)
+
+
+def backward_rows(heads, place, q, qt, k, kt, v, do, full, lse, segc, segr, dk_sc, dv_sc, qc_sc, dc_sc, dq_sc, d_sc, dt_sc, qs_sc):
     step_at = pl.program_id(0)
     i = step_at ^ place[0]
-    length = k.shape[0]
-    part = d0.shape[1]
-    per = d0.shape[0] // BLOCK
+    part = do[0].shape[1]
+    per = do[0].shape[0] // BLOCK
 
     @pl.when(step_at == 0)
     def _():
         dk_sc[...] = jnp.zeros(dk_sc.shape, F32)
         dv_sc[...] = jnp.zeros(dv_sc.shape, F32)
-        gb_o[...] = jnp.zeros(gb_o.shape, F32)
         d_sc[...] = jnp.zeros(d_sc.shape, BF)
 
-    for n, d in enumerate((d0, d1, d2, d3)):
+    for n, d in enumerate(do):
 
         @pl.when(step_at // per == n)
         def _(d=d):
@@ -276,51 +302,38 @@
     def _():
         step(count - 1, 0)
 
-    def turn(x, sl):
-        return (x * twice(cos[sl, :]) - swap_pairs(x) * twice(sin[sl, :])).astype(BF)
-
-    def put(x, sl, m):
-        g_o[sl, m * WIDE : (m + 1) * WIDE] = x
-        gb_o[0:1, m * WIDE : (m + 1) * WIDE] += jnp.sum(x.astype(F32), axis=0, keepdims=True)
-
-    put(turn(dq_sc[...].T * (HEAD**-0.5), own), own, 0)
-
-    @pl.when(step_at == pl.num_programs(0) - 1)
-    def _():
-        def last(r, _):
-            sl = pl.ds(pl.multiple_of(r * BLOCK, BLOCK), BLOCK)
-            put(turn(dk_sc[:, sl].T, sl), sl, 1)
-            put(dv_sc[:, sl].astype(BF).T, sl, 2)
-            return 0
-
-        lax.fori_loop(0, length // BLOCK, last, 0)
+    qs_sc[:, own] = dq_sc[...]
 
 
 def attention_backward(place, q, qt, k, kt, v, do, full, lse, segc, segr, cos, sin, heads):
     length = k.shape[0]
+    blocks = length // BLOCK
+    first = lambda i: jnp.minimum(i, blocks - 1)
+    second = lambda i: jnp.maximum(i - blocks, 0)
     return pl.pallas_call(
         partial(backward_kernel, heads),
         grid_spec=pltpu.PrefetchScalarGridSpec(
             num_scalar_prefetch=1,
-            grid=(length // BLOCK,),
+            grid=(2 * blocks,),
             in_specs=[
-                pl.BlockSpec((BLOCK, WIDE), lambda i, s: (i ^ s[0], 0)),
-                pl.BlockSpec((WIDE, BLOCK), lambda i, s: (0, i ^ s[0])),
+                pl.BlockSpec((BLOCK, WIDE), lambda i, s: (first(i) ^ s[0], 0)),
+                pl.BlockSpec((WIDE, BLOCK), lambda i, s: (0, first(i) ^ s[0])),
                 whole_block(k.shape),
                 whole_block(kt.shape),
                 whole_block(v.shape),
                 *[whole_block(d.shape) for d in do],
-                pl.BlockSpec((BLOCK, WIDE), lambda i, s: (i, 0)),
-                pl.BlockSpec((8, BLOCK), lambda i, s: (0, i)),
+                pl.BlockSpec((BLOCK, WIDE), lambda i, s: (first(i), 0)),
+                pl.BlockSpec((8, BLOCK), lambda i, s: (0, first(i))),
                 whole_block(segc.shape),
                 whole_block(segr.shape),
-                whole_block(cos.shape),
-                whole_block(sin.shape),
+                pl.BlockSpec((BLOCK, 128), lambda i, s: (second(i), 0)),
+                pl.BlockSpec((BLOCK, 128), lambda i, s: (second(i), 0)),
             ],
-            out_specs=[whole_block((length, 3 * WIDE)), whole_block((8, 3 * WIDE))],
+            out_specs=[pl.BlockSpec((BLOCK, 3 * WIDE), lambda i, s: (second(i), 0)), whole_block((8, 3 * WIDE))],
             scratch_shapes=[pltpu.VMEM((WIDE, length), F32)] * 2
             + [pltpu.VMEM((heads * BLOCK, WIDE), BF)] * 2
-            + [pltpu.VMEM((WIDE, BLOCK), F32), pltpu.VMEM((BLOCK, WIDE), BF), pltpu.VMEM((WIDE, BLOCK), BF)],
+            + [pltpu.VMEM((WIDE, BLOCK), F32), pltpu.VMEM((BLOCK, WIDE), BF), pltpu.VMEM((WIDE, BLOCK), BF)]
+            + [pltpu.VMEM((WIDE, length), F32)],
         ),
         out_shape=[jax.ShapeDtypeStruct((length, 3 * WIDE), BF), jax.ShapeDtypeStruct((8, 3 * WIDE), F32)],
         compiler_params=params(28),
@@ -340,15 +353,15 @@
 
 
 def gelu_parts(x):
-    e = jnp.exp(x * x * -0.5)
+    e = jnp.exp2(x * x * (-0.5 * 1.4426950408889634))
     t = 1.0 / (1.0 + (0.3275911 * 0.7071067811865476) * jnp.abs(x))
-    p = t * (0.254829592 + t * (-0.284496736 + t * (1.421413741 + t * (-1.453152027 + t * 1.061405429))))
-    tail = 0.5 * p * e
+    p = t * (0.127414796 + t * (-0.142248368 + t * (0.7107068705 + t * (-0.7265760135 + t * 0.5307027145))))
+    tail = p * e
     phi = jnp.where(x >= 0, 1.0 - tail, tail)
     return phi, phi + x * e * 0.3989422804014327
 
 
-ROWS = 256
+ROWS = 512
 
 
 def feed_kernel(place, gathered, w, c0, c1, c2, c3, tokb, gtop, vec, bias, *refs):
@@ -1053,51 +1066,49 @@
     grad_proj, bias_sums = attention_backward(
         spot, q, q_turned, k_rows, k_turned, v_rows, grad_heads, full, log_total, seg_column, seg_row, cosine, sine, heads
     )
-    grad_proj, bias_sums, corner, hidden_sums, sums_one, sums_two = barrier((grad_proj, bias_sums, corner, hidden_sums, sums_one, sums_two))
+    grad_proj, bias_sums, corner, hidden_sums, sums_one, sums_two, out_blocks = barrier(
+        (grad_proj, bias_sums, corner, hidden_sums, sums_one, sums_two, out_blocks)
+    )
     if direct:
         grad_proj, sent, packs[0] = barrier((grad_proj, sent, packs[0]))
 
     three = branch(place, (3,), (BF,), grad_proj, qkv_wide)[0]
-    three, grad_proj, corner, bias_sums = barrier((three, grad_proj, corner, bias_sums))
+    three, grad_proj, corner, bias_sums, out_blocks = barrier((three, grad_proj, corner, bias_sums, out_blocks))
     low, high = swap_tp(three[: share // 2], 2), swap_tp(three[share // 2 :], 1)
     one, two, own = branch(place, (1, 2, 0), (F32, F32, F32), grad_proj, qkv_wide)
+    grads = qkv_weight_grads(place, per, tokens, other_tokens, grad_proj, part)
     keep_a, send_a = pick(place, out_blocks[0], out_blocks[2])
     keep_b, send_b = pick(place, out_blocks[1], *corner)
     small = collect(place, hidden_sums, sums_one, sums_two, bias_sums)
-    outs = [keep_a, keep_b, send_a, send_b]
-    low, high, one, two, own, outs, grad_proj, small = barrier((low, high, one, two, own, outs, grad_proj, small))
-
-    one, two = relay(one, two, low, high)
-    one, two, outs, grad_proj, small = barrier((one, two, outs, grad_proj, small))
-    one, two = swap_tp(one, 1), swap_tp(two, 2)
-    grads = qkv_weight_grads(place, per, tokens, other_tokens, grad_proj, part)
-    outputs = join(place, outs[:2], [swap_ctx(outs[2]), swap_ctx(outs[3])])
+    outs = [keep_a, keep_b, swap_ctx(send_a), swap_ctx(send_b)]
+    if direct:
+        qkv_sum, *qkv_pieces = settle(grads[0], swap_ctx(grads[1]))
+        qkv_sum, qkv_pieces, low = barrier((qkv_sum, qkv_pieces, low))
+    low, high, one, two, own, outs, small = barrier((low, high, one, two, own, outs, small))
 
     def send_shards(pieces, small, k):
         moved = [swap_shard(pieces[j - 1], j) for j in (1, 2, 3)]
         moved[0], small = barrier((moved[0], small))
         return moved, small + swap_tp(small, k)
 
+    one, two = relay(one, two, low, high)
+    one, two, outs, small = barrier((one, two, outs, small))
+    one, two = swap_tp(one, 1), swap_tp(two, 2)
+    outputs = join(place, outs[:2], outs[2:])
     if direct:
+        moved, small = send_shards(qkv_pieces, small, 1)
+        qkv_total = finish(3, qkv_sum, *moved)
         summed, *pieces = settle(packs[0], *sent)
-        small = small + swap_ctx(small)
-        small = small + swap_shard(small, 1)
-        small = small + swap_shard(small, 2)
-        qkv_sum, *qkv_pieces = settle(grads[0], swap_ctx(grads[1]))
-        one, two, own, small, outputs, summed, pieces, qkv_sum, qkv_pieces = barrier(
-            (one, two, own, small, outputs, summed, pieces, qkv_sum, qkv_pieces)
-        )
+        one, two, own, small, outputs, summed, pieces, qkv_total = barrier((one, two, own, small, outputs, summed, pieces, qkv_total))
     else:
         one, two, own, small, outputs = barrier((one, two, own, small, outputs))
 
     block = add_block(own, grad_first, one, two)
     ready = [block, swap_tp(block, 1), swap_tp(block, 2)]
     if direct:
-        moved, small = send_shards(pieces, small, 1)
+        moved, small = send_shards(pieces, small, 2)
         total = finish(1, summed, *moved)
-        ready, total, small, qkv_pieces = barrier((ready, total, small, qkv_pieces))
-        moved, small = send_shards(qkv_pieces, small, 2)
-        qkv_total = finish(3, qkv_sum, *moved)
+        ready, total, small = barrier((ready, total, small))
     else:
         qkv_total = lax.psum_scatter(grads[0], ("shard", "ctx"), scatter_dimension=0, tiled=True).reshape(rows, 3, part)
         total = lax.psum_scatter(made[0].reshape(-1, 2 * hh), ("tp", "shard", "ctx"), scatter_dimension=0, tiled=True).astype(F32)
@@ -1105,7 +1116,12 @@
     keep_a, send_a = pick(place, ready[0], ready[2])
     other_a = swap_ctx(send_a)
     grad_ffn_weight, grad_out_weight = place_feed(whole, total)
-    small = small if direct else lax.psum(small, ("shard", "ctx", "tp"))
+    if direct:
+        small = small + swap_shard(small, 1)
+        small = small + swap_shard(small, 2)
+        small = small + swap_ctx(small)
+    else:
+        small = lax.psum(small, ("shard", "ctx", "tp"))
     corner, grad_ffn_weight, grad_out_weight, small, keep_a, other_a, qkv_total = barrier(
         (corner, grad_ffn_weight, grad_out_weight, small, keep_a, other_a, qkv_total)
     )

time: 326 us -> 324 us (level)
  Pallas kernels: 119 us -> 136 us
  waiting for transfers between devices: 91 us -> 74.6 us
    pallas_call x4, Pallas kernels: 20.6 us -> 29.4 us  [attention_forward(): pl.pallas_call(partial(forward_kernel, heads), grid_spec=pltpu.PrefetchSc...]
    pallas_call x1, Pallas kernels: 20.7 us -> 28.3 us  [attention_backward(): pl.pallas_call(partial(backward_kernel, heads), grid_spec=pltpu.PrefetchS...]
    all_gather x1, waiting for transfers between devices: 17.2 us -> 10.9 us  [body(): lax.all_gather(gathered, ('tp', 'shard', 'ctx'), axis=0, tiled=True)]
    ppermute x11, starting transfers between devices: 18.1 us -> 12.4 us  [swap_ctx(): return lax.ppermute(x, 'ctx', [(0, 1), (1, 0)])]
    ppermute x11, waiting for transfers between devices: 35.5 us -> 30.1 us  [swap_shard(): return lax.ppermute(x, 'shard', [(i, i ^ k) for i in range(4)])]
    ppermute x26, starting transfers between devices: 23 us -> 27.6 us  [swap_tp(): return lax.ppermute(x, 'tp', [(i, i ^ k) for i in range(4)])]
  transfers between devices with their start and end apart: 50 -> 50, of which waited for: 22 -> 17; matrix products, arithmetic and copies ran while one was open for 10% -> 10% of each run, Pallas kernels for 28% -> 34%
where the time goes in v6:
time: 324 us; the launch traced here: 326 us
  Pallas kernels  136 us (42%)
  waiting for transfers between devices  74.6 us (23%)
  starting transfers between devices  54.3 us (17%)
  local copies, waits for them, and re-layouts  29.5 us (9%)
  other arithmetic  16.9 us (5%)
  between operations  14.8 us (5%)
    ppermute x26, waiting for transfers between devices, swap_tp(): return lax.ppermute(x, 'tp', [(i, i ^ k) for i in range(4)])  30.4 us
    ppermute x11, waiting for transfers between devices, swap_shard(): return lax.ppermute(x, 'shard', [(i, i ^ k) for i in range(4)])  30.1 us
    pallas_call x4, Pallas kernels, attention_forward(): pl.pallas_call(partial(forward_kernel, heads), grid_spec=pltpu.PrefetchSc...  29.4 us
    pallas_call x1, Pallas kernels, attention_backward(): pl.pallas_call(partial(backward_kernel, heads), grid_spec=pltpu.PrefetchS...  28.3 us
    ppermute x26, starting transfers between devices, swap_tp(): return lax.ppermute(x, 'tp', [(i, i ^ k) for i in range(4)])  27.6 us
    pallas_call x1, Pallas kernels, feed_forward(): pl.pallas_call(feed_kernel, grid_spec=pltpu.PrefetchScalarGridSpec(num_sc...  21 us
    unnamed x104, local copies, waits for them, and re-layouts  16.6 us
    pallas_call x1, Pallas kernels, feed_back(): pl.pallas_call(feed_back_kernel, grid_spec=pltpu.PrefetchScalarGridSpec(n...  15.3 us
  transfers between devices with their start and end apart: 50, of which 17 were waited for; matrix products, arithmetic and copies ran while one was open for 10% of the time, Pallas kernels for 34%

profile of v6, /device:TPU:1, one launch (start us, length us, event | category | flops | bytes accessed | tf_op | source)
XLA Modules:
  0.0 326.0 jit_solution(6571161580083946073)
XLA Ops:
  8.4 1.6 pad_maximum_fusion.3
  10.7 3.0 collective-permute-start.12
  14.0 1.7 copy.27
  16.8 3.6 %collective-permute-start.4 = (bf16[96,576]{1,0:T(8,128)(2,1)S(1)}, bf16[96,576]{1,0:T(8,128)(2,1)S(1)}, u32[]{:S(2)}, u32[]{:S(2)}) collective-permute-start(bf16[96,576]{1,0:T(8,128)(2,1)S(1)} %copy.33.refs_0_), channel_id=1, source_target_pairs={{0,24},{8,16},{16,8},{24,0},{1,25},{9,17},{17,9},{25,1},{2,26},{10... | collective-permute-start | bytes 331784 | tf_op jit(solution)/shard_map/ppermute | solution.py:926
  21.3 2.1 dynamic-slice_bitcast_fusion.1
  23.4 1.2 dynamic-slice_bitcast_fusion
  26.9 2.1 collective-permute-start.1
  29.1 1.3 pad_maximum_fusion.5.bias
  32.0 3.1 collective-permute-done.3.refs_2_
  35.1 4.4 %collective-permute-done.2.refs_1_ = bf16[96,576]{1,0:T(8,128)(2,1)S(1)} collective-permute-done((bf16[96,576]{1,0:T(8,128)(2,1)S(1)}, bf16[96,576]{1,0:T(8,128)(2,1)S(1)}, u32[]{:S(2)}, u32[]{:S(2)}) %collective-permute-start.2) | collective-permute-done | bytes 110624 | tf_op jit(solution)/shard_map/ppermute | solution.py:926
  40.5 3.7 %fusion = (f32[2048,128]{1,0:T(8,128)S(1)}, f32[2048,128]{1,0:T(8,128)S(1)}) fusion(f32[128]{0:T(128)S(1)} %copy-done.47, f32[128]{0:T(128)S(1)} %copy-done.46, f32[2048]{0:T(1024)S(1)} %bitcast.124), kind=kLoop, calls=%fused_computation.8 | loop fusion | flops 524288 | bytes 2106368 | tf_op jit(solution)/shard_map/mul | solution.py:904
  45.5 1.9 copy-done.3
  47.4 1.4 copy-done.6
  49.7 5.7 %project_qkv.1 = (bf16[2048,256]{1,0:T(8,128)(2,1)S(1)}, bf16[2048,256]{1,0:T(8,128)(2,1)S(1)}, bf16[2048,256]{1,0:T(8,128)(2,1)S(1)}, bf16[256,2048]{1,0:T(8,12...) custom-call(s32[10]{0:T(128)S(1)} %stack.96.place, bf16[96,576]{1,0:T(8,128)(2,1)S(1)} %copy.33.refs_0_, ...), custom_call_target="tpu_custom_call" | custom-call | tf_op jit(solution)/shard_map/project_qkv/pallas_call | solution.py:95
  57.4 6.8 %attention_forward.4 = (bf16[512,192]{1,0:T(8,128)(2,1)S(1)}, f32[8,512]{1,0:T(8,128)S(1)}, f32[512,256]{1,0:T(8,128)S(1)}) custom-call(s32[17]{0:T(128)S(1)} %get-tuple-element.396.place, bf16[2048,256]{1,0:T(8,128)(2,1)S(1)} %get-tuple-element.196.q, bf16[2048,256]{1,0:T(8,128)(2,1)S(1)} %get-tuple-element.186.k, ...), custom_call_target="tpu_custom_call" | custom-call | tf_op jit(solution)/shard_map/attention_forward/pallas_call | solution.py:180
  64.2 2.2 collective-permute-start.6
  66.5 9.2 %attention_forward.5 = (bf16[512,192]{1,0:T(8,128)(2,1)S(1)}, f32[8,512]{1,0:T(8,128)S(1)}, f32[512,256]{1,0:T(8,128)S(1)}) custom-call(s32[17]{0:T(128)S(1)} %get-tuple-element.398.place, bf16[2048,256]{1,0:T(8,128)(2,1)S(1)} %get-tuple-element.196.q, bf16[2048,256]{1,0:T(8,128)(2,1)S(1)} %get-tuple-element.186.k, ...), custom_call_target="tpu_custom_call" | custom-call | tf_op jit(solution)/shard_map/attention_forward/pallas_call | solution.py:180
  76.0 2.4 bitcast_select_fusion.gtop
  79.3 6.7 %attention_forward.6 = (bf16[512,192]{1,0:T(8,128)(2,1)S(1)}, f32[8,512]{1,0:T(8,128)S(1)}, f32[512,256]{1,0:T(8,128)S(1)}) custom-call(s32[17]{0:T(128)S(1)} %get-tuple-element.397.place, bf16[2048,256]{1,0:T(8,128)(2,1)S(1)} %get-tuple-element.196.q, bf16[2048,256]{1,0:T(8,128)(2,1)S(1)} %get-tuple-element.186.k, ...), custom_call_target="tpu_custom_call" | custom-call | tf_op jit(solution)/shard_map/attention_forward/pallas_call | solution.py:180
  86.1 5.2 %collective-permute-done.7.c1 = bf16[512,192]{1,0:T(8,128)(2,1)S(1)} collective-permute-done((bf16[512,192]{1,0:T(8,128)(2,1)S(1)}, bf16[512,192]{1,0:T(8,128)(2,1)S(1)}, u32[]{:S(2)}, u32[]{:S(2)}) %collective-permute-start.7) | collective-permute-done | bytes 196640 | tf_op jit(solution)/shard_map/ppermute | solution.py:922
  91.3 6.8 %attention_forward.7 = (bf16[512,192]{1,0:T(8,128)(2,1)S(1)}, f32[8,512]{1,0:T(8,128)S(1)}, f32[512,256]{1,0:T(8,128)S(1)}) custom-call(s32[17]{0:T(128)S(1)} %get-tuple-element.399.place, bf16[2048,256]{1,0:T(8,128)(2,1)S(1)} %get-tuple-element.196.q, bf16[2048,256]{1,0:T(8,128)(2,1)S(1)} %get-tuple-element.186.k, ...), custom_call_target="tpu_custom_call" | custom-call | tf_op jit(solution)/shard_map/attention_forward/pallas_call | solution.py:180
  98.1 1.5 pad_maximum_fusion.full
  100.3 1.2 pad_maximum_fusion.1.ctx
  101.5 10.9 %all-gather.2.cloned.1.call-done = bf16[3072,1728]{1,0:T(8,128)(2,1)} async-done(((bf16[96,1728]{1,0:T(8,128)(2,1)}), bf16[3072,1728]{1,0:T(8,128)(2,1)}) %all-gather.2.cloned.1.call-update) | async-done | bytes 10616848 | tf_op jit(solution)/shard_map/all_gather | solution.py:987
  112.4 21.0 %feed_forward.1 = (bf16[512,768]{1,0:T(8,128)(2,1)}, f32[512,768]{1,0:T(8,128)}, bf16[512,768]{1,0:T(8,128)(2,1)}, f32[512,768]{1,0:T(8,128)}, bf16[768,512]{1,0...) custom-call(s32[10]{0:T(128)} %copy-done.34, ...), custom_call_target="tpu_custom_call" | custom-call | tf_op jit(solution)/shard_map/feed_forward/pallas_call | solution.py:440
  135.1 15.3 %feed_back.1 = (f32[512,768]{1,0:T(8,128)}, bf16[768,512]{1,0:T(8,128)(2,1)}, bf16[512,192]{1,0:T(8,128)(2,1)}, bf16[512,192]{1,0:T(8,128)(2,1)}, bf16[512,192]{...) custom-call(s32[10]{0:T(128)} %copy-done.34, ...), custom_call_target="tpu_custom_call" | custom-call | tf_op jit(solution)/shard_map/feed_back/pallas_call | solution.py:524
  151.8 1.3 collective-permute-start.15
  153.2 12.1 %weight_grads.1 = (bf16[4,4,96,768]{3,2,1,0:T(8,128)(2,1)}, bf16[4,4,96,768]{3,2,1,0:T(8,128)(2,1)}, bf16[4,768,960]{2,1,0:T(8,128)(2,1)}) custom-call(s32[10]{0:T(128)} %copy-done.34, bf16[768,512]{1,0:T(8,128)(2,1)} %get-tuple-element.210.nbt, bf16[768,512]{1,0:T(8,128)(2,1)} %get-tuple-element.211.gst, bf16[768,512]{1,0:T(8,128)(2,1)} %get-tuple-element.217.gft, ...), custom_call_target="tpu_custom_call" | custom-call | tf_op jit(solution)/shard_map/weight_grads/pallas_call | solution.py:592
  166.8 1.7 collective-permute-start.18
  170.8 2.1 collective-permute-done.18
  172.9 2.3 add_bitcast_fusion
  176.6 1.3 collective-permute-start.23
  179.4 28.3 %attention_backward.1 = (bf16[2048,768]{1,0:T(8,128)(2,1)S(1)}, f32[8,768]{1,0:T(8,128)S(1)}) custom-call(s32[17]{0:T(128)S(1)} %get-tuple-element.399.place, bf16[2048,256]{1,0:T(8,128)(2,1)S(1)} %get-tuple-element.196.q, bf16[256,2048]{1,0:T(8,128)(2,1)S(1)} %copy-done.20, bf16[2048,256]{1,0:T(8,128)(2,1)S(1)} %get-tuple-element.186.k, ...), custom_call_target="tpu_custom_call" | custom-call | tf_op jit(solution)/shard_map/attention_backward/pallas_call | solution.py:313
  207.7 3.9 %collective-permute-done.19.refs_0_ = bf16[256,768]{1,0:T(8,128)(2,1)S(1)} collective-permute-done((bf16[256,768]{1,0:T(8,128)(2,1)S(1)}, bf16[256,768]{1,0:T(8,128)(2,1)S(1)}, u32[]{:S(2)}, u32[]{:S(2)}) %collective-permute-start.19) | collective-permute-done | bytes 393248 | tf_op jit(solution)/shard_map/ppermute | solution.py:922
  211.6 1.3 branch.2
  213.0 2.0 pick.4
  215.0 1.6 collective-permute-start.27
  216.6 1.8 pick.5
  218.5 4.0 %qkv_weight_grads.1 = (f32[4,96,576]{2,1,0:T(8,128)S(1)}, bf16[4,96,576]{2,1,0:T(8,128)(2,1)S(1)}) custom-call(s32[10]{0:T(128)S(1)} %copy-done.35, bf16[2,1024,768]{2,1,0:T(8,128)(2,1)S(1)} %copy-done.4, bf16[1024,768]{1,0:T(8,128)(2,1)S(1)} %copy-done.7, bf16[2048,768]{1,0:T(8,128)(2,1)S(1)} %get-tuple-element.268.refs_0_.g.refs_1_.refs_2_), custom_call_target="tpu_custom_call" | custom-call | tf_op jit(solution)/shard_map/qkv_weight_grads/pallas_call | solution.py:636
  224.8 2.6 branch.3
  228.0 13.0 %collective-permute-done.25.low = bf16[256,768]{1,0:T(8,128)(2,1)S(1)} collective-permute-done((bf16[256,768]{1,0:T(8,128)(2,1)S(1)}, bf16[256,768]{1,0:T(8,128)(2,1)S(1)}, u32[]{:S(2)}, u32[]{:S(2)}) %collective-permute-start.25) | collective-permute-done | bytes 393248 | tf_op jit(solution)/shard_map/ppermute | solution.py:922
  242.7 1.2 collective-permute-start.31
  243.9 2.2 collective-permute-start.33
  246.2 2.4 collective-permute-done.31.refs_1_
  248.7 5.8 %collective-permute-start.32 = (f32[16,768]{1,0:T(8,128)S(1)}, f32[16,768]{1,0:T(8,128)S(1)}, u32[]{:S(2)}, u32[]{:S(2)}) collective-permute-start(f32[16,768]{1,0:T(8,128)S(1)} %collect.1), channel_id=1, source_target_pairs={{0,1},{1,0},{2,3},{3,2},{4,5},{5,4},{6,7},{7,6},{8,9},{9,8},{10,11... | collective-permute-start | bytes 147464 | tf_op jit(solution)/shard_map/ppermute | solution.py:922
  254.8 2.7 join.2
  257.5 1.7 collective-permute-done.34.refs_3_
  259.4 1.6 collective-permute-done.32
  262.7 1.2 collective-permute-start.37
  264.0 2.3 collective-permute-start.38
  266.3 7.5 %collective-permute-done.37.refs_1_ = bf16[96,768]{1,0:T(8,128)(2,1)S(1)} collective-permute-done((bf16[96,768]{1,0:T(8,128)(2,1)S(1)}, bf16[96,768]{1,0:T(8,128)(2,1)S(1)}, u32[]{:S(2)}, u32[]{:S(2)}) %collective-permute-start.37) | collective-permute-done | bytes 147488 | tf_op jit(solution)/shard_map/ppermute | solution.py:926
  273.8 1.8 collective-permute-start.40
  275.7 4.5 %collective-permute-done.39.refs_3_ = bf16[96,768]{1,0:T(8,128)(2,1)S(1)} collective-permute-done((bf16[96,768]{1,0:T(8,128)(2,1)S(1)}, bf16[96,768]{1,0:T(8,128)(2,1)S(1)}, u32[]{:S(2)}, u32[]{:S(2)}) %collective-permute-start.39) | collective-permute-done | bytes 147488 | tf_op jit(solution)/shard_map/ppermute | solution.py:926
  280.2 6.6 %collective-permute-done.40 = f32[16,768]{1,0:T(8,128)S(1)} collective-permute-done((f32[16,768]{1,0:T(8,128)S(1)}, f32[16,768]{1,0:T(8,128)S(1)}, u32[]{:S(2)}, u32[]{:S(2)}) %collective-permute-start.40) | collective-permute-done | bytes 49184 | tf_op jit(solution)/shard_map/ppermute | solution.py:922
  286.9 1.5 pick.6
  288.4 1.3 collective-permute-start.46
  292.6 1.2 collective-permute-start.43
  293.8 2.5 collective-permute-done.43
  296.3 1.9 collective-permute-start.44
  298.2 3.9 %collective-permute-done.44 = f32[16,768]{1,0:T(8,128)S(1)} collective-permute-done((f32[16,768]{1,0:T(8,128)S(1)}, f32[16,768]{1,0:T(8,128)S(1)}, u32[]{:S(2)}, u32[]{:S(2)}) %collective-permute-start.44) | collective-permute-done | bytes 49184 | tf_op jit(solution)/shard_map/ppermute | solution.py:926
  302.1 2.1 collective-permute-start.45
  307.1 2.5 pick.7
  310.5 1.6 collective-permute-start.47
  316.4 2.7 join.3
  (216 shorter events, 42.7 us)
Async XLA Ops:
  7.2 13.2 %copy-start.43 = (s32[2,1024]{1,0:T(2,128)S(1)}, s32[2,1024]{1,0:T(2,128)}, u32[]{:S(2)}) copy-start(s32[2,1024]{1,0:T(2,128)} %param.15) | copy-start | bytes 24580
  7.2 16.2 %copy-start.2 = (bf16[2,1024,768]{2,1,0:T(8,128)(2,1)S(1)}, bf16[2,1024,768]{2,1,0:T(8,128)(2,1)}, u32[]{:S(2)}) copy-start(bf16[2,1024,768]{2,1,0:T(8,128)(2,1)} %own.1) | copy-start | bytes 9437188
  7.2 105.2 %all-gather.2.cloned.1.call-start = ((), (), s32[]{:S(2)}) async-start(), calls=%async_computation.1 | async-start | bytes 11354112 | tf_op jit(solution)/shard_map/all_gather | solution.py:987
  10.0 295.2 %reduce-scatter.2.cloned.1.call-start = ((), (), s32[]{:S(2)}) async-start(), calls=%async_computation.2 | async-start | bytes 6488064 | tf_op jit(solution)/shard_map/reduce_scatter | solution.py:1053
  10.7 15.8 %collective-permute-start.12 = (f32[1,768]{1,0:T(1,128)S(1)}, f32[1,768]{1,0:T(1,128)}, u32[]{:S(2)}, u32[]{:S(2)}) collective-permute-start(f32[1,768]{1,0:T(1,128)S(1)} %reshape.214), channel_id=1, source_target_pairs={{0,3},{1,2},{2,1},{3,0},{4,7},{5,6},{6,5},{7,4},{8,11},{9,10},{10,... | collective-permute-start | bytes 9224 | tf_op jit(solution)/shard_map/ppermute | solution.py:922
  13.7 13.2 %collective-permute-start.11 = (f32[1,768]{1,0:T(1,128)S(1)}, f32[1,768]{1,0:T(1,128)}, u32[]{:S(2)}, u32[]{:S(2)}) collective-permute-start(f32[1,768]{1,0:T(1,128)S(1)} %reshape.214), channel_id=1, source_target_pairs={{0,2},{1,3},{2,0},{3,1},{4,6},{5,7},{6,4},{7,5},{8,10},{9,11},{10,... | collective-permute-start | bytes 9224 | tf_op jit(solution)/shard_map/ppermute | solution.py:922
  13.9 15.1 %collective-permute-start.10 = (f32[1,768]{1,0:T(1,128)S(1)}, f32[1,768]{1,0:T(1,128)}, u32[]{:S(2)}, u32[]{:S(2)}) collective-permute-start(f32[1,768]{1,0:T(1,128)S(1)} %reshape.214), channel_id=1, source_target_pairs={{0,1},{1,0},{2,3},{3,2},{4,5},{5,4},{6,7},{7,6},{8,9},{9,8},{10,11... | collective-permute-start | bytes 9224 | tf_op jit(solution)/shard_map/ppermute | solution.py:922
  16.8 15.3 %collective-permute-start.4 = (bf16[96,576]{1,0:T(8,128)(2,1)S(1)}, bf16[96,576]{1,0:T(8,128)(2,1)S(1)}, u32[]{:S(2)}, u32[]{:S(2)}) collective-permute-start(bf16[96,576]{1,0:T(8,128)(2,1)S(1)} %copy.33.refs_0_), channel_id=1, source_target_pairs={{0,24},{8,16},{16,8},{24,0},{1,25},{9,17},{17,9},{25,1},{2,26},{10... | collective-permute-start | bytes 331784 | tf_op jit(solution)/shard_map/ppermute | solution.py:926
  20.3 14.7 %collective-permute-start.3 = (bf16[96,576]{1,0:T(8,128)(2,1)S(1)}, bf16[96,576]{1,0:T(8,128)(2,1)S(1)}, u32[]{:S(2)}, u32[]{:S(2)}) collective-permute-start(bf16[96,576]{1,0:T(8,128)(2,1)S(1)} %copy.33.refs_0_), channel_id=1, source_target_pairs={{0,16},{8,24},{16,0},{24,8},{1,17},{9,25},{17,1},{25,9},{2,18},{10... | collective-permute-start | bytes 331784 | tf_op jit(solution)/shard_map/ppermute | solution.py:926
  24.6 15.9 %copy-start.46 = (f32[128]{0:T(128)S(1)}, f32[128]{0:T(128)}, u32[]{:S(2)}) copy-start(f32[128]{0:T(128)} %constant.195) | copy-start | bytes 1540
  24.6 15.9 %copy-start.47 = (f32[128]{0:T(128)S(1)}, f32[128]{0:T(128)}, u32[]{:S(2)}) copy-start(f32[128]{0:T(128)} %constant.188.clone) | copy-start | bytes 1540
  26.5 19.0 %copy-start.34 = (s32[10]{0:T(128)}, s32[10]{0:T(128)S(1)}, u32[]{:S(2)}) copy-start(s32[10]{0:T(128)S(1)} %stack.96.place) | copy-start | bytes 124
  26.5 13.0 %collective-permute-start.2 = (bf16[96,576]{1,0:T(8,128)(2,1)S(1)}, bf16[96,576]{1,0:T(8,128)(2,1)S(1)}, u32[]{:S(2)}, u32[]{:S(2)}) collective-permute-start(bf16[96,576]{1,0:T(8,128)(2,1)S(1)} %copy.33.refs_0_), channel_id=1, source_target_pairs={{0,8},{8,0},{16,24},{24,16},{1,9},{9,1},{17,25},{25,17},{2,10},{10... | collective-permute-start | bytes 331784 | tf_op jit(solution)/shard_map/ppermute | solution.py:926
  26.9 3.5 %collective-permute-start.1 = (s32[2,1024]{1,0:T(2,128)S(1)}, s32[2,1024]{1,0:T(2,128)S(1)}, u32[]{:S(2)}, u32[]{:S(2)}) collective-permute-start(s32[2,1024]{1,0:T(2,128)S(1)} %bitcast.126), channel_id=1, source_target_pairs={{0,4},{4,0},{1,5},{5,1},{2,6},{6,2},{3,7},{7,3},{8,12},{12,8},{9,1... | collective-permute-start | bytes 24584 | tf_op jit(solution)/shard_map/ppermute | solution.py:918
  29.0 15.3 %collective-permute-start = (bf16[1024,768]{1,0:T(8,128)(2,1)}, bf16[1024,768]{1,0:T(8,128)(2,1)S(1)}, u32[]{:S(2)}, u32[]{:S(2)}) collective-permute-start(bf16[1024,768]{1,0:T(8,128)(2,1)} %dynamic-slice_bitcast_fusion), channel_id=1, source_target_pairs={{0,4},{4,0},{1,5},{5,1},{2,6},{6,2},{3,7},{7,3},{8,12},{12,8},{9,1... | collective-permute-start | bytes 4718600 | tf_op jit(solution)/shard_map/ppermute | solution.py:918
  30.4 45.6 %collective-permute-start.9 = (bf16[512,768]{1,0:T(8,128)(2,1)}, bf16[512,768]{1,0:T(8,128)(2,1)}, u32[]{:S(2)}, u32[]{:S(2)}) collective-permute-start(bf16[512,768]{1,0:T(8,128)(2,1)} %dynamic-slice_bitcast_fusion.1), channel_id=1, source_target_pairs={{0,4},{4,0},{1,5},{5,1},{2,6},{6,2},{3,7},{7,3},{8,12},{12,8},{9,1... | collective-permute-start | bytes 2359304 | tf_op jit(solution)/shard_map/ppermute | solution.py:918
  39.6 4.6 %collective-permute-start.5 = (bf16[4,96,576]{2,1,0:T(8,128)(2,1)S(1)}, bf16[4,96,576]{2,1,0:T(8,128)(2,1)S(1)}, u32[]{:S(2)}, u32[]{:S(2)}) collective-permute-start(bf16[4,96,576]{2,1,0:T(8,128)(2,1)S(1)} %pad_maximum_fusion.2), channel_id=1, source_target_pairs={{0,4},{4,0},{1,5},{5,1},{2,6},{6,2},{3,7},{7,3},{8,12},{12,8},{9,1... | collective-permute-start | bytes 1327112 | tf_op jit(solution)/shard_map/ppermute | solution.py:918
  57.4 33.9 %copy-start = (bf16[2048,256]{1,0:T(8,128)(2,1)}, bf16[2048,256]{1,0:T(8,128)(2,1)S(1)}, u32[]{:S(2)}) copy-start(bf16[2048,256]{1,0:T(8,128)(2,1)S(1)} %get-tuple-element.188.v) | copy-start | bytes 3145732
  64.2 15.1 %collective-permute-start.6 = (bf16[512,192]{1,0:T(8,128)(2,1)S(1)}, bf16[512,192]{1,0:T(8,128)(2,1)S(1)}, u32[]{:S(2)}, u32[]{:S(2)}) collective-permute-start(bf16[512,192]{1,0:T(8,128)(2,1)S(1)} %get-tuple-element.192), channel_id=1, source_target_pairs={{0,3},{1,2},{2,1},{3,0},{4,7},{5,6},{6,5},{7,4},{8,11},{9,10},{10,... | collective-permute-start | bytes 589832 | tf_op jit(solution)/shard_map/ppermute | solution.py:922
  75.6 15.6 %collective-permute-start.7 = (bf16[512,192]{1,0:T(8,128)(2,1)S(1)}, bf16[512,192]{1,0:T(8,128)(2,1)S(1)}, u32[]{:S(2)}, u32[]{:S(2)}) collective-permute-start(bf16[512,192]{1,0:T(8,128)(2,1)S(1)} %get-tuple-element.195), channel_id=1, source_target_pairs={{0,1},{1,0},{2,3},{3,2},{4,5},{5,4},{6,7},{7,6},{8,9},{9,8},{10,11... | collective-permute-start | bytes 589832 | tf_op jit(solution)/shard_map/ppermute | solution.py:922
  79.3 20.3 %copy-start.39 = (bf16[512,192]{1,0:T(8,128)(2,1)}, bf16[512,192]{1,0:T(8,128)(2,1)S(1)}, u32[]{:S(2)}) copy-start(bf16[512,192]{1,0:T(8,128)(2,1)S(1)} %collective-permute-done.6.c3) | copy-start | bytes 589828
  91.3 8.3 %collective-permute-start.8 = (bf16[512,192]{1,0:T(8,128)(2,1)S(1)}, bf16[512,192]{1,0:T(8,128)(2,1)S(1)}, u32[]{:S(2)}, u32[]{:S(2)}) collective-permute-start(bf16[512,192]{1,0:T(8,128)(2,1)S(1)} %get-tuple-element.199), channel_id=1, source_target_pairs={{0,2},{1,3},{2,0},{3,1},{4,6},{5,7},{6,4},{7,5},{8,10},{9,11},{10,... | collective-permute-start | bytes 589832 | tf_op jit(solution)/shard_map/ppermute | solution.py:922
  133.4 33.4 %collective-permute-start.17 = (bf16[512,768]{1,0:T(8,128)(2,1)}, bf16[512,768]{1,0:T(8,128)(2,1)}, u32[]{:S(2)}, u32[]{:S(2)}) collective-permute-start(bf16[512,768]{1,0:T(8,128)(2,1)} %get-tuple-element.280.near), channel_id=1, source_target_pairs={{0,2},{1,3},{2,0},{3,1},{4,6},{5,7},{6,4},{7,5},{8,10},{9,11},{10,... | collective-permute-start | bytes 2359304 | tf_op jit(solution)/shard_map/ppermute | solution.py:922
  134.6 32.2 %collective-permute-start.16 = (bf16[512,768]{1,0:T(8,128)(2,1)}, bf16[512,768]{1,0:T(8,128)(2,1)}, u32[]{:S(2)}, u32[]{:S(2)}) collective-permute-start(bf16[512,768]{1,0:T(8,128)(2,1)} %get-tuple-element.280.near), channel_id=1, source_target_pairs={{0,1},{1,0},{2,3},{3,2},{4,5},{5,4},{6,7},{7,6},{8,9},{9,8},{10,11... | collective-permute-start | bytes 2359304 | tf_op jit(solution)/shard_map/ppermute | solution.py:922
  150.4 14.8 %collective-permute-start.13 = (bf16[512,192]{1,0:T(8,128)(2,1)}, bf16[512,192]{1,0:T(8,128)(2,1)S(1)}, u32[]{:S(2)}, u32[]{:S(2)}) collective-permute-start(bf16[512,192]{1,0:T(8,128)(2,1)} %get-tuple-element.225), channel_id=1, source_target_pairs={{0,1},{1,0},{2,3},{3,2},{4,5},{5,4},{6,7},{7,6},{8,9},{9,8},{10,11... | collective-permute-start | bytes 589832 | tf_op jit(solution)/shard_map/ppermute | solution.py:922
  151.4 13.9 %collective-permute-start.14 = (bf16[512,192]{1,0:T(8,128)(2,1)}, bf16[512,192]{1,0:T(8,128)(2,1)S(1)}, u32[]{:S(2)}, u32[]{:S(2)}) collective-permute-start(bf16[512,192]{1,0:T(8,128)(2,1)} %get-tuple-element.226), channel_id=1, source_target_pairs={{0,2},{1,3},{2,0},{3,1},{4,6},{5,7},{6,4},{7,5},{8,10},{9,11},{10,... | collective-permute-start | bytes 589832 | tf_op jit(solution)/shard_map/ppermute | solution.py:922
  151.8 14.3 %collective-permute-start.15 = (bf16[512,192]{1,0:T(8,128)(2,1)}, bf16[512,192]{1,0:T(8,128)(2,1)S(1)}, u32[]{:S(2)}, u32[]{:S(2)}) collective-permute-start(bf16[512,192]{1,0:T(8,128)(2,1)} %get-tuple-element.227), channel_id=1, source_target_pairs={{0,3},{1,2},{2,1},{3,0},{4,7},{5,6},{6,5},{7,4},{8,11},{9,10},{10,... | collective-permute-start | bytes 589832 | tf_op jit(solution)/shard_map/ppermute | solution.py:922
  166.8 6.1 %collective-permute-start.18 = (bf16[4,4,96,768]{3,2,1,0:T(8,128)(2,1)}, bf16[4,4,96,768]{3,2,1,0:T(8,128)(2,1)S(1)}, u32[]{:S(2)}, u32[]{:S(2)}) collective-permute-start(bf16[4,4,96,768]{3,2,1,0:T(8,128)(2,1)} %get-tuple-element.233), channel_id=1, source_target_pairs={{0,4},{4,0},{1,5},{5,1},{2,6},{6,2},{3,7},{7,3},{8,12},{12,8},{9,1... | collective-permute-start | bytes 7077896 | tf_op jit(solution)/shard_map/ppermute | solution.py:918
  169.6 9.7 %copy-start.28 = (bf16[512,192]{1,0:T(8,128)(2,1)S(1)}, bf16[512,192]{1,0:T(8,128)(2,1)}, u32[]{:S(2)}) copy-start(bf16[512,192]{1,0:T(8,128)(2,1)} %copy-done.27) | copy-start | bytes 589828
  169.6 9.7 %copy-start.30 = (bf16[512,192]{1,0:T(8,128)(2,1)S(1)}, bf16[512,192]{1,0:T(8,128)(2,1)}, u32[]{:S(2)}) copy-start(bf16[512,192]{1,0:T(8,128)(2,1)} %copy-done.29) | copy-start | bytes 589828
  169.6 9.7 %copy-start.32 = (bf16[512,192]{1,0:T(8,128)(2,1)S(1)}, bf16[512,192]{1,0:T(8,128)(2,1)}, u32[]{:S(2)}) copy-start(bf16[512,192]{1,0:T(8,128)(2,1)} %copy-done.31) | copy-start | bytes 589828
  170.7 8.6 %copy-start.1 = (bf16[2048,256]{1,0:T(8,128)(2,1)S(1)}, bf16[2048,256]{1,0:T(8,128)(2,1)}, u32[]{:S(2)}) copy-start(bf16[2048,256]{1,0:T(8,128)(2,1)} %copy-done) | copy-start | bytes 3145732
  170.7 8.6 %copy-start.9 = (f32[2048,128]{1,0:T(8,128)S(1)}, f32[2048,128]{1,0:T(8,128)}, u32[]{:S(2)}) copy-start(f32[2048,128]{1,0:T(8,128)} %copy-done.8) | copy-start | bytes 3145732
  175.2 36.4 %collective-permute-start.21 = (bf16[4,96,768]{2,1,0:T(8,128)(2,1)S(1)}, bf16[4,96,768]{2,1,0:T(8,128)(2,1)S(1)}, u32[]{:S(2)}, u32[]{:S(2)}) collective-permute-start(bf16[4,96,768]{2,1,0:T(8,128)(2,1)S(1)} %get-tuple-element.257), channel_id=1, source_target_pairs={{0,1},{1,0},{2,3},{3,2},{4,5},{5,4},{6,7},{7,6},{8,9},{9,8},{10,11... | collective-permute-start | bytes 1769480 | tf_op jit(solution)/shard_map/ppermute | solution.py:922
  176.2 35.3 %collective-permute-start.22 = (bf16[4,96,768]{2,1,0:T(8,128)(2,1)S(1)}, bf16[4,96,768]{2,1,0:T(8,128)(2,1)S(1)}, u32[]{:S(2)}, u32[]{:S(2)}) collective-permute-start(bf16[4,96,768]{2,1,0:T(8,128)(2,1)S(1)} %get-tuple-element.258), channel_id=1, source_target_pairs={{0,2},{1,3},{2,0},{3,1},{4,6},{5,7},{6,4},{7,5},{8,10},{9,11},{10,... | collective-permute-start | bytes 1769480 | tf_op jit(solution)/shard_map/ppermute | solution.py:922
  176.6 34.9 %collective-permute-start.23 = (bf16[4,96,768]{2,1,0:T(8,128)(2,1)S(1)}, bf16[4,96,768]{2,1,0:T(8,128)(2,1)S(1)}, u32[]{:S(2)}, u32[]{:S(2)}) collective-permute-start(bf16[4,96,768]{2,1,0:T(8,128)(2,1)S(1)} %get-tuple-element.259), channel_id=1, source_target_pairs={{0,3},{1,2},{2,1},{3,0},{4,7},{5,6},{6,5},{7,4},{8,11},{9,10},{10,... | collective-permute-start | bytes 1769480 | tf_op jit(solution)/shard_map/ppermute | solution.py:922
  177.9 33.6 %collective-permute-start.19 = (bf16[256,768]{1,0:T(8,128)(2,1)S(1)}, bf16[256,768]{1,0:T(8,128)(2,1)S(1)}, u32[]{:S(2)}, u32[]{:S(2)}) collective-permute-start(bf16[256,768]{1,0:T(8,128)(2,1)S(1)} %slice.73), channel_id=1, source_target_pairs={{0,2},{1,3},{2,0},{3,1},{4,6},{5,7},{6,4},{7,5},{8,10},{9,11},{10,... | collective-permute-start | bytes 1179656 | tf_op jit(solution)/shard_map/ppermute | solution.py:922
  179.0 32.6 %collective-permute-start.20 = (bf16[256,768]{1,0:T(8,128)(2,1)S(1)}, bf16[256,768]{1,0:T(8,128)(2,1)S(1)}, u32[]{:S(2)}, u32[]{:S(2)}) collective-permute-start(bf16[256,768]{1,0:T(8,128)(2,1)S(1)} %slice.74), channel_id=1, source_target_pairs={{0,1},{1,0},{2,3},{3,2},{4,5},{5,4},{6,7},{7,6},{8,9},{9,8},{10,11... | collective-permute-start | bytes 1179656 | tf_op jit(solution)/shard_map/ppermute | solution.py:922
  179.4 32.2 %copy-start.14 = (bf16[768,768]{1,0:T(8,128)(2,1)S(1)}, bf16[768,768]{1,0:T(8,128)(2,1)}, u32[]{:S(2)}) copy-start(bf16[768,768]{1,0:T(8,128)(2,1)} %copy-done.13) | copy-start | bytes 3538948
  179.4 32.2 %copy-start.35 = (s32[10]{0:T(128)S(1)}, s32[10]{0:T(128)}, u32[]{:S(2)}) copy-start(s32[10]{0:T(128)} %copy-done.34) | copy-start | bytes 124
  215.0 26.0 %collective-permute-start.27 = (bf16[512,768]{1,0:T(8,128)(2,1)S(1)}, bf16[512,768]{1,0:T(8,128)(2,1)S(1)}, u32[]{:S(2)}, u32[]{:S(2)}) collective-permute-start(bf16[512,768]{1,0:T(8,128)(2,1)S(1)} %get-tuple-element.287), channel_id=1, source_target_pairs={{0,4},{4,0},{1,5},{5,1},{2,6},{6,2},{3,7},{7,3},{8,12},{12,8},{9,1... | collective-permute-start | bytes 2359304 | tf_op jit(solution)/shard_map/ppermute | solution.py:918
  218.4 22.7 %collective-permute-start.28 = (bf16[512,768]{1,0:T(8,128)(2,1)S(1)}, bf16[512,768]{1,0:T(8,128)(2,1)S(1)}, u32[]{:S(2)}, u32[]{:S(2)}) collective-permute-start(bf16[512,768]{1,0:T(8,128)(2,1)S(1)} %get-tuple-element.288), channel_id=1, source_target_pairs={{0,4},{4,0},{1,5},{5,1},{2,6},{6,2},{3,7},{7,3},{8,12},{12,8},{9,1... | collective-permute-start | bytes 2359304 | tf_op jit(solution)/shard_map/ppermute | solution.py:918
  222.5 5.4 %collective-permute-start.24 = (bf16[4,96,576]{2,1,0:T(8,128)(2,1)S(1)}, bf16[4,96,576]{2,1,0:T(8,128)(2,1)S(1)}, u32[]{:S(2)}, u32[]{:S(2)}) collective-permute-start(bf16[4,96,576]{2,1,0:T(8,128)(2,1)S(1)} %get-tuple-element.270), channel_id=1, source_target_pairs={{0,4},{4,0},{1,5},{5,1},{2,6},{6,2},{3,7},{7,3},{8,12},{12,8},{9,1... | collective-permute-start | bytes 1327112 | tf_op jit(solution)/shard_map/ppermute | solution.py:918
  223.1 17.9 %collective-permute-start.25 = (bf16[256,768]{1,0:T(8,128)(2,1)S(1)}, bf16[256,768]{1,0:T(8,128)(2,1)S(1)}, u32[]{:S(2)}, u32[]{:S(2)}) collective-permute-start(bf16[256,768]{1,0:T(8,128)(2,1)S(1)} %get-tuple-element.384), channel_id=1, source_target_pairs={{0,2},{1,3},{2,0},{3,1},{4,6},{5,7},{6,4},{7,5},{8,10},{9,11},{10,... | collective-permute-start | bytes 1179656 | tf_op jit(solution)/shard_map/ppermute | solution.py:922
  223.6 17.4 %collective-permute-start.26 = (bf16[256,768]{1,0:T(8,128)(2,1)S(1)}, bf16[256,768]{1,0:T(8,128)(2,1)S(1)}, u32[]{:S(2)}, u32[]{:S(2)}) collective-permute-start(bf16[256,768]{1,0:T(8,128)(2,1)S(1)} %get-tuple-element.383), channel_id=1, source_target_pairs={{0,1},{1,0},{2,3},{3,2},{4,5},{5,4},{6,7},{7,6},{8,9},{9,8},{10,11... | collective-permute-start | bytes 1179656 | tf_op jit(solution)/shard_map/ppermute | solution.py:922
  241.3 19.8 %collective-permute-start.29 = (bf16[512,768]{1,0:T(8,128)(2,1)S(1)}, bf16[512,768]{1,0:T(8,128)(2,1)S(1)}, u32[]{:S(2)}, u32[]{:S(2)}) collective-permute-start(bf16[512,768]{1,0:T(8,128)(2,1)S(1)} %get-tuple-element.304), channel_id=1, source_target_pairs={{0,1},{1,0},{2,3},{3,2},{4,5},{5,4},{6,7},{7,6},{8,9},{9,8},{10,11... | collective-permute-start | bytes 2359304 | tf_op jit(solution)/shard_map/ppermute | solution.py:922
  242.4 18.6 %collective-permute-start.30 = (bf16[512,768]{1,0:T(8,128)(2,1)S(1)}, bf16[512,768]{1,0:T(8,128)(2,1)S(1)}, u32[]{:S(2)}, u32[]{:S(2)}) collective-permute-start(bf16[512,768]{1,0:T(8,128)(2,1)S(1)} %get-tuple-element.305), channel_id=1, source_target_pairs={{0,2},{1,3},{2,0},{3,1},{4,6},{5,7},{6,4},{7,5},{8,10},{9,11},{10,... | collective-permute-start | bytes 2359304 | tf_op jit(solution)/shard_map/ppermute | solution.py:922
  242.7 6.0 %collective-permute-start.31 = (bf16[96,576]{1,0:T(8,128)(2,1)S(1)}, bf16[96,576]{1,0:T(8,128)(2,1)S(1)}, u32[]{:S(2)}, u32[]{:S(2)}) collective-permute-start(bf16[96,576]{1,0:T(8,128)(2,1)S(1)} %get-tuple-element.307), channel_id=1, source_target_pairs={{0,8},{8,0},{16,24},{24,16},{1,9},{9,1},{17,25},{25,17},{2,10},{10... | collective-permute-start | bytes 331784 | tf_op jit(solution)/shard_map/ppermute | solution.py:926
  243.9 13.6 %collective-permute-start.33 = (bf16[96,576]{1,0:T(8,128)(2,1)S(1)}, bf16[96,576]{1,0:T(8,128)(2,1)S(1)}, u32[]{:S(2)}, u32[]{:S(2)}) collective-permute-start(bf16[96,576]{1,0:T(8,128)(2,1)S(1)} %get-tuple-element.324), channel_id=1, source_target_pairs={{0,16},{8,24},{16,0},{24,8},{1,17},{9,25},{17,1},{25,9},{2,18},{10... | collective-permute-start | bytes 331784 | tf_op jit(solution)/shard_map/ppermute | solution.py:926
  246.1 13.1 %collective-permute-start.34 = (bf16[96,576]{1,0:T(8,128)(2,1)S(1)}, bf16[96,576]{1,0:T(8,128)(2,1)S(1)}, u32[]{:S(2)}, u32[]{:S(2)}) collective-permute-start(bf16[96,576]{1,0:T(8,128)(2,1)S(1)} %get-tuple-element.325), channel_id=1, source_target_pairs={{0,24},{8,16},{16,8},{24,0},{1,25},{9,17},{17,9},{25,1},{2,26},{10... | collective-permute-start | bytes 331784 | tf_op jit(solution)/shard_map/ppermute | solution.py:926
  248.7 12.4 %collective-permute-start.32 = (f32[16,768]{1,0:T(8,128)S(1)}, f32[16,768]{1,0:T(8,128)S(1)}, u32[]{:S(2)}, u32[]{:S(2)}) collective-permute-start(f32[16,768]{1,0:T(8,128)S(1)} %collect.1), channel_id=1, source_target_pairs={{0,1},{1,0},{2,3},{3,2},{4,5},{5,4},{6,7},{7,6},{8,9},{9,8},{10,11... | collective-permute-start | bytes 147464 | tf_op jit(solution)/shard_map/ppermute | solution.py:922
  261.4 25.5 %collective-permute-start.36 = (bf16[512,768]{1,0:T(8,128)(2,1)S(1)}, bf16[512,768]{1,0:T(8,128)(2,1)S(1)}, u32[]{:S(2)}, u32[]{:S(2)}) collective-permute-start(bf16[512,768]{1,0:T(8,128)(2,1)S(1)} %add_block.1.near), channel_id=1, source_target_pairs={{0,2},{1,3},{2,0},{3,1},{4,6},{5,7},{6,4},{7,5},{8,10},{9,11},{10,... | collective-permute-start | bytes 2359304 | tf_op jit(solution)/shard_map/ppermute | solution.py:922
  262.5 24.4 %collective-permute-start.35 = (bf16[512,768]{1,0:T(8,128)(2,1)S(1)}, bf16[512,768]{1,0:T(8,128)(2,1)S(1)}, u32[]{:S(2)}, u32[]{:S(2)}) collective-permute-start(bf16[512,768]{1,0:T(8,128)(2,1)S(1)} %add_block.1.near), channel_id=1, source_target_pairs={{0,1},{1,0},{2,3},{3,2},{4,5},{5,4},{6,7},{7,6},{8,9},{9,8},{10,11... | collective-permute-start | bytes 2359304 | tf_op jit(solution)/shard_map/ppermute | solution.py:922
  262.7 11.1 %collective-permute-start.37 = (bf16[96,768]{1,0:T(8,128)(2,1)S(1)}, bf16[96,768]{1,0:T(8,128)(2,1)S(1)}, u32[]{:S(2)}, u32[]{:S(2)}) collective-permute-start(bf16[96,768]{1,0:T(8,128)(2,1)S(1)} %get-tuple-element.332), channel_id=1, source_target_pairs={{0,8},{8,0},{16,24},{24,16},{1,9},{9,1},{17,25},{25,17},{2,10},{10... | collective-permute-start | bytes 442376 | tf_op jit(solution)/shard_map/ppermute | solution.py:926
  264.0 11.7 %collective-permute-start.38 = (bf16[96,768]{1,0:T(8,128)(2,1)S(1)}, bf16[96,768]{1,0:T(8,128)(2,1)S(1)}, u32[]{:S(2)}, u32[]{:S(2)}) collective-permute-start(bf16[96,768]{1,0:T(8,128)(2,1)S(1)} %get-tuple-element.335), channel_id=1, source_target_pairs={{0,16},{8,24},{16,0},{24,8},{1,17},{9,25},{17,1},{25,9},{2,18},{10... | collective-permute-start | bytes 442376 | tf_op jit(solution)/shard_map/ppermute | solution.py:926
  266.3 13.9 %collective-permute-start.39 = (bf16[96,768]{1,0:T(8,128)(2,1)S(1)}, bf16[96,768]{1,0:T(8,128)(2,1)S(1)}, u32[]{:S(2)}, u32[]{:S(2)}) collective-permute-start(bf16[96,768]{1,0:T(8,128)(2,1)S(1)} %get-tuple-element.336), channel_id=1, source_target_pairs={{0,24},{8,16},{16,8},{24,0},{1,25},{9,17},{17,9},{25,1},{2,26},{10... | collective-permute-start | bytes 442376 | tf_op jit(solution)/shard_map/ppermute | solution.py:926
  273.8 13.0 %collective-permute-start.40 = (f32[16,768]{1,0:T(8,128)S(1)}, f32[16,768]{1,0:T(8,128)S(1)}, u32[]{:S(2)}, u32[]{:S(2)}) collective-permute-start(f32[16,768]{1,0:T(8,128)S(1)} %add.168), channel_id=1, source_target_pairs={{0,2},{1,3},{2,0},{3,1},{4,6},{5,7},{6,4},{7,5},{8,10},{9,11},{10,... | collective-permute-start | bytes 147464 | tf_op jit(solution)/shard_map/ppermute | solution.py:922
  288.4 18.6 %collective-permute-start.46 = (bf16[512,768]{1,0:T(8,128)(2,1)}, bf16[512,768]{1,0:T(8,128)(2,1)S(1)}, u32[]{:S(2)}, u32[]{:S(2)}) collective-permute-start(bf16[512,768]{1,0:T(8,128)(2,1)} %get-tuple-element.347), channel_id=1, source_target_pairs={{0,4},{4,0},{1,5},{5,1},{2,6},{6,2},{3,7},{7,3},{8,12},{12,8},{9,1... | collective-permute-start | bytes 2359304 | tf_op jit(solution)/shard_map/ppermute | solution.py:918
  291.3 15.7 %collective-permute-start.42 = (bf16[256,768]{1,0:T(8,128)(2,1)}, bf16[256,768]{1,0:T(8,128)(2,1)S(1)}, u32[]{:S(2)}, u32[]{:S(2)}) collective-permute-start(bf16[256,768]{1,0:T(8,128)(2,1)} %slice.86), channel_id=1, source_target_pairs={{0,1},{1,0},{2,3},{3,2},{4,5},{5,4},{6,7},{7,6},{8,9},{9,8},{10,11... | collective-permute-start | bytes 1179656 | tf_op jit(solution)/shard_map/ppermute | solution.py:922
  292.3 14.8 %collective-permute-start.41 = (bf16[256,768]{1,0:T(8,128)(2,1)}, bf16[256,768]{1,0:T(8,128)(2,1)}, u32[]{:S(2)}, u32[]{:S(2)}) collective-permute-start(bf16[256,768]{1,0:T(8,128)(2,1)} %slice.85), channel_id=1, source_target_pairs={{0,2},{1,3},{2,0},{3,1},{4,6},{5,7},{6,4},{7,5},{8,10},{9,11},{10,... | collective-permute-start | bytes 1179656 | tf_op jit(solution)/shard_map/ppermute | solution.py:922
  292.6 3.7 %collective-permute-start.43 = (f32[16,768]{1,0:T(8,128)S(1)}, f32[16,768]{1,0:T(8,128)S(1)}, u32[]{:S(2)}, u32[]{:S(2)}) collective-permute-start(f32[16,768]{1,0:T(8,128)S(1)} %add.169), channel_id=1, source_target_pairs={{0,8},{8,0},{16,24},{24,16},{1,9},{9,1},{17,25},{25,17},{2,10},{10... | collective-permute-start | bytes 147464 | tf_op jit(solution)/shard_map/ppermute | solution.py:926
  296.3 5.8 %collective-permute-start.44 = (f32[16,768]{1,0:T(8,128)S(1)}, f32[16,768]{1,0:T(8,128)S(1)}, u32[]{:S(2)}, u32[]{:S(2)}) collective-permute-start(f32[16,768]{1,0:T(8,128)S(1)} %add.170), channel_id=1, source_target_pairs={{0,16},{8,24},{16,0},{24,8},{1,17},{9,25},{17,1},{25,9},{2,18},{10... | collective-permute-start | bytes 147464 | tf_op jit(solution)/shard_map/ppermute | solution.py:926
  302.1 3.0 collective-permute-start.45
  310.5 4.8 %collective-permute-start.47 = (bf16[512,768]{1,0:T(8,128)(2,1)}, bf16[512,768]{1,0:T(8,128)(2,1)S(1)}, u32[]{:S(2)}, u32[]{:S(2)}) collective-permute-start(bf16[512,768]{1,0:T(8,128)(2,1)} %get-tuple-element.354), channel_id=1, source_target_pairs={{0,4},{4,0},{1,5},{5,1},{2,6},{6,2},{3,7},{7,3},{8,12},{12,8},{9,1... | collective-permute-start | bytes 2359304 | tf_op jit(solution)/shard_map/ppermute | solution.py:918
  (34 other events, 135.3 us)
Sparse Core Ops, SparseCore 0:
  11.6 100.7 all-gather.1
  166.9 138.1 reduce-scatter.1

commit v7 on v6

--- a/solution.py
+++ b/solution.py
@@ -713,32 +713,56 @@
     )(place, near, *far)
 
 
-def join_kernel(place, keep_a, keep_b, other_a, other_b, out):
+def join_kernel(second, place, *refs):
     last = place.shape[0] - 1
-    mine = pl.program_id(0) == place[last - 1]
-    same = pl.program_id(1) == place[last] % 2
-    for x, own, even in ((keep_a, True, True), (keep_b, True, False), (other_a, False, True), (other_b, False, False)):
-
-        @pl.when(jnp.logical_and(mine == own, same == even))
-        def _(x=x):
-            out[0] = x[...]
-
-
-def join(place, keeps, others):
-    share, width = keeps[0].shape
-    return pl.pallas_call(
-        join_kernel,
+    mine = place[last] // 2 == place[last - 1]
+    if second:
+        near, *far, other, _, out = refs
+    else:
+        near, *far, other, out = refs
+    here = pl.program_id(0) == place[last - 1]
+
+    def put(parts):
+        rows = out.shape[1] // len(parts)
+        for n, x in enumerate(parts):
+            out[0, n * rows : (n + 1) * rows, :] = x[...]
+
+    @pl.when(jnp.logical_and(here, mine))
+    def _():
+        put([near])
+
+    @pl.when(jnp.logical_and(here, jnp.logical_not(mine)))
+    def _():
+        put(far)
+
+    @pl.when(jnp.logical_not(here))
+    def _():
+        put([other])
+
+
+def join(place, near, far, other, before=None):
+    share, width = near.shape
+    second = before is not None
+    last = place.shape[0] - 1
+    ins = [near, *far, other]
+    specs = [whole_block(x.shape) for x in ins]
+    if second:
+        ins.append(before)
+        specs.append(pl.BlockSpec(memory_space=pl.ANY))
+    return pl.pallas_call(
+        partial(join_kernel, second),
         grid_spec=pltpu.PrefetchScalarGridSpec(
             num_scalar_prefetch=1,
-            grid=(2, 2),
-            in_specs=[whole_block((share, width))] * 4,
-            out_specs=pl.BlockSpec((1, share, width), lambda i, j, s: (i, j, 0)),
+            grid=(2,),
+            in_specs=specs,
+            out_specs=pl.BlockSpec((1, share, width), lambda i, s: (i, (s[last] + int(second)) % 2, 0)),
         ),
-        out_shape=jax.ShapeDtypeStruct((2, 2 * share, width), keeps[0].dtype),
-        compiler_params=pltpu.CompilerParams(dimension_semantics=("arbitrary", "arbitrary"), vmem_limit_bytes=12 * 1024 * 1024),
+        out_shape=jax.ShapeDtypeStruct((2, 2 * share, width), near.dtype),
+        input_output_aliases={len(ins): 0} if second else {},
+        compiler_params=params(12),
         cost_estimate=COST,
         name="join",
-    )(place, *keeps, *others)
+    )(place, *ins)
 
 
 def relay_kernel(one, two, low, high, one_o, two_o):
@@ -1066,8 +1090,8 @@
     grad_proj, bias_sums = attention_backward(
         spot, q, q_turned, k_rows, k_turned, v_rows, grad_heads, full, log_total, seg_column, seg_row, cosine, sine, heads
     )
-    grad_proj, bias_sums, corner, hidden_sums, sums_one, sums_two, out_blocks = barrier(
-        (grad_proj, bias_sums, corner, hidden_sums, sums_one, sums_two, out_blocks)
+    grad_proj, bias_sums, hidden_sums, sums_one, sums_two, out_blocks = barrier(
+        (grad_proj, bias_sums, hidden_sums, sums_one, sums_two, out_blocks)
     )
     if direct:
         grad_proj, sent, packs[0] = barrier((grad_proj, sent, packs[0]))
@@ -1080,7 +1104,7 @@
     keep_a, send_a = pick(place, out_blocks[0], out_blocks[2])
     keep_b, send_b = pick(place, out_blocks[1], *corner)
     small = collect(place, hidden_sums, sums_one, sums_two, bias_sums)
-    outs = [keep_a, keep_b, swap_ctx(send_a), swap_ctx(send_b)]
+    outs = [swap_ctx(send_a), swap_ctx(send_b)]
     if direct:
         qkv_sum, *qkv_pieces = settle(grads[0], swap_ctx(grads[1]))
         qkv_sum, qkv_pieces, low = barrier((qkv_sum, qkv_pieces, low))
@@ -1094,7 +1118,8 @@
     one, two = relay(one, two, low, high)
     one, two, outs, small = barrier((one, two, outs, small))
     one, two = swap_tp(one, 1), swap_tp(two, 2)
-    outputs = join(place, outs[:2], outs[2:])
+    outputs = join(place, out_blocks[0], [out_blocks[2]], outs[0])
+    outputs = join(place, out_blocks[1], corner, outs[1], outputs)
     if direct:
         moved, small = send_shards(qkv_pieces, small, 1)
         qkv_total = finish(3, qkv_sum, *moved)
@@ -1113,20 +1138,20 @@
         qkv_total = lax.psum_scatter(grads[0], ("shard", "ctx"), scatter_dimension=0, tiled=True).reshape(rows, 3, part)
         total = lax.psum_scatter(made[0].reshape(-1, 2 * hh), ("tp", "shard", "ctx"), scatter_dimension=0, tiled=True).astype(F32)
     corner = [swap_tp(ready[1][: share // 2], 2), swap_tp(ready[2][share // 2 :], 1)]
-    keep_a, send_a = pick(place, ready[0], ready[2])
-    other_a = swap_ctx(send_a)
+    _, send_a = pick(place, ready[0], ready[2])
+    grad_tokens = join(place, ready[0], [ready[2]], swap_ctx(send_a))
     grad_ffn_weight, grad_out_weight = place_feed(whole, total)
     if direct:
         small = small + swap_shard(small, 1)
+        small, grad_tokens = barrier((small, grad_tokens))
         small = small + swap_shard(small, 2)
-        small = small + swap_ctx(small)
     else:
         small = lax.psum(small, ("shard", "ctx", "tp"))
-    corner, grad_ffn_weight, grad_out_weight, small, keep_a, other_a, qkv_total = barrier(
-        (corner, grad_ffn_weight, grad_out_weight, small, keep_a, other_a, qkv_total)
-    )
-    keep_b, send_b = pick(place, ready[1], *corner)
-    grad_tokens = join(place, [keep_a, keep_b], [other_a, swap_ctx(send_b)])
+    corner, small, grad_tokens, qkv_total = barrier((corner, small, grad_tokens, qkv_total))
+    if direct:
+        small = small + swap_ctx(small)
+    send_b = jnp.where(here, jnp.concatenate(corner), ready[1])
+    grad_tokens = join(place, ready[1], corner, swap_ctx(send_b), grad_tokens)
 
     grad_qkv_weight = qkv_total
     grad_ffn_bias = take(small, t)

time: 324 us -> 317 us (0.978)
  waiting for transfers between devices: 74.6 us -> 66.2 us
  local copies, waits for them, and re-layouts: 29.5 us -> 25.9 us
    ppermute x26, waiting for transfers between devices: 30.4 us -> 24.2 us  [swap_tp(): return lax.ppermute(x, 'tp', [(i, i ^ k) for i in range(4)])]
    ppermute x11, waiting for transfers between devices: 30.1 us -> 26.1 us  [swap_shard(): return lax.ppermute(x, 'shard', [(i, i ^ k) for i in range(4)])]
    pallas_call x2 -> x4, Pallas kernels: 5.46 us -> 9.35 us  [join(): pl.pallas_call(partial(join_kernel, second), grid_spec=pltpu.PrefetchScal...]
    unnamed x104 -> x100, local copies, waits for them, and re-layouts: 16.6 us -> 14.6 us
    pallas_call x4 -> x3, Pallas kernels: 7.88 us -> 6.84 us  [pick(): pl.pallas_call(pick_kernel, grid_spec=pltpu.PrefetchScalarGridSpec(num_sc...]
  transfers between devices with their start and end apart: 50 -> 50, of which waited for: 17 -> 18; matrix products, arithmetic and copies ran while one was open for 10% -> 10% of each run, Pallas kernels for 34% -> 37%
where the time goes in v7:
time: 317 us; the launch traced here: 316 us
  Pallas kernels  137 us (43%)
  waiting for transfers between devices  66.2 us (21%)
  starting transfers between devices  53.6 us (17%)
  local copies, waits for them, and re-layouts  25.9 us (8%)
  other arithmetic  18.1 us (6%)
  between operations  14.8 us (5%)
    pallas_call x4, Pallas kernels, attention_forward(): pl.pallas_call(partial(forward_kernel, heads), grid_spec=pltpu.PrefetchSc...  28.7 us
    pallas_call x1, Pallas kernels, attention_backward(): pl.pallas_call(partial(backward_kernel, heads), grid_spec=pltpu.PrefetchS...  27.8 us
    ppermute x26, starting transfers between devices, swap_tp(): return lax.ppermute(x, 'tp', [(i, i ^ k) for i in range(4)])  27.3 us
    ppermute x11, waiting for transfers between devices, swap_shard(): return lax.ppermute(x, 'shard', [(i, i ^ k) for i in range(4)])  26.1 us
    ppermute x26, waiting for transfers between devices, swap_tp(): return lax.ppermute(x, 'tp', [(i, i ^ k) for i in range(4)])  24.2 us
    pallas_call x1, Pallas kernels, feed_forward(): pl.pallas_call(feed_kernel, grid_spec=pltpu.PrefetchScalarGridSpec(num_sc...  21 us
    pallas_call x1, Pallas kernels, feed_back(): pl.pallas_call(feed_back_kernel, grid_spec=pltpu.PrefetchScalarGridSpec(n...  15.3 us
    ppermute x11, starting transfers between devices, swap_shard(): return lax.ppermute(x, 'shard', [(i, i ^ k) for i in range(4)])  14.8 us
  transfers between devices with their start and end apart: 50, of which 18 were waited for; matrix products, arithmetic and copies ran while one was open for 10% of the time, Pallas kernels for 37%

profile of v7, /device:TPU:1, one launch (start us, length us, event | category | flops | bytes accessed | tf_op | source)
XLA Modules:
  0.0 316.2 jit_solution(2260183978729155389)
XLA Ops:
  8.4 1.6 pad_maximum_fusion.3
  10.7 3.0 collective-permute-start.12
  14.0 1.7 copy.29
  16.8 3.6 %collective-permute-start.4 = (bf16[96,576]{1,0:T(8,128)(2,1)S(1)}, bf16[96,576]{1,0:T(8,128)(2,1)S(1)}, u32[]{:S(2)}, u32[]{:S(2)}) collective-permute-start(bf16[96,576]{1,0:T(8,128)(2,1)S(1)} %copy.35.refs_0_), channel_id=1, source_target_pairs={{0,24},{8,16},{16,8},{24,0},{1,25},{9,17},{17,9},{25,1},{2,26},{10... | collective-permute-start | bytes 331784 | tf_op jit(solution)/shard_map/ppermute | solution.py:950
  21.3 2.1 dynamic-slice_bitcast_fusion.1
  23.4 1.2 dynamic-slice_bitcast_fusion
  26.9 2.1 collective-permute-start.1
  29.1 1.3 pad_maximum_fusion.5.bias
  32.0 3.1 collective-permute-done.3.refs_2_
  35.1 4.4 %collective-permute-done.2.refs_1_ = bf16[96,576]{1,0:T(8,128)(2,1)S(1)} collective-permute-done((bf16[96,576]{1,0:T(8,128)(2,1)S(1)}, bf16[96,576]{1,0:T(8,128)(2,1)S(1)}, u32[]{:S(2)}, u32[]{:S(2)}) %collective-permute-start.2) | collective-permute-done | bytes 110624 | tf_op jit(solution)/shard_map/ppermute | solution.py:950
  40.5 3.7 %fusion = (f32[2048,128]{1,0:T(8,128)S(1)}, f32[2048,128]{1,0:T(8,128)S(1)}) fusion(f32[128]{0:T(128)S(1)} %copy-done.45, f32[128]{0:T(128)S(1)} %copy-done.44, f32[2048]{0:T(1024)S(1)} %bitcast.124), kind=kLoop, calls=%fused_computation.8 | loop fusion | flops 524288 | bytes 2106368 | tf_op jit(solution)/shard_map/mul | solution.py:928
  45.5 1.9 copy-done.3
  47.4 1.4 copy-done.6
  49.7 5.7 %project_qkv.1 = (bf16[2048,256]{1,0:T(8,128)(2,1)S(1)}, bf16[2048,256]{1,0:T(8,128)(2,1)S(1)}, bf16[2048,256]{1,0:T(8,128)(2,1)S(1)}, bf16[256,2048]{1,0:T(8,12...) custom-call(s32[10]{0:T(128)S(1)} %stack.96.place, bf16[96,576]{1,0:T(8,128)(2,1)S(1)} %copy.35.refs_0_, ...), custom_call_target="tpu_custom_call" | custom-call | tf_op jit(solution)/shard_map/project_qkv/pallas_call | solution.py:95
  57.4 6.8 %attention_forward.4 = (bf16[512,192]{1,0:T(8,128)(2,1)S(1)}, f32[8,512]{1,0:T(8,128)S(1)}, f32[512,256]{1,0:T(8,128)S(1)}) custom-call(s32[17]{0:T(128)S(1)} %get-tuple-element.372.place, bf16[2048,256]{1,0:T(8,128)(2,1)S(1)} %get-tuple-element.184.q, bf16[2048,256]{1,0:T(8,128)(2,1)S(1)} %get-tuple-element.174.k, ...), custom_call_target="tpu_custom_call" | custom-call | tf_op jit(solution)/shard_map/attention_forward/pallas_call | solution.py:180
  64.2 2.2 collective-permute-start.6
  66.4 7.6 %attention_forward.5 = (bf16[512,192]{1,0:T(8,128)(2,1)S(1)}, f32[8,512]{1,0:T(8,128)S(1)}, f32[512,256]{1,0:T(8,128)S(1)}) custom-call(s32[17]{0:T(128)S(1)} %get-tuple-element.374.place, bf16[2048,256]{1,0:T(8,128)(2,1)S(1)} %get-tuple-element.184.q, bf16[2048,256]{1,0:T(8,128)(2,1)S(1)} %get-tuple-element.174.k, ...), custom_call_target="tpu_custom_call" | custom-call | tf_op jit(solution)/shard_map/attention_forward/pallas_call | solution.py:180
  74.3 2.4 bitcast_select_fusion.gtop
  77.7 7.6 %attention_forward.6 = (bf16[512,192]{1,0:T(8,128)(2,1)S(1)}, f32[8,512]{1,0:T(8,128)S(1)}, f32[512,256]{1,0:T(8,128)S(1)}) custom-call(s32[17]{0:T(128)S(1)} %get-tuple-element.373.place, bf16[2048,256]{1,0:T(8,128)(2,1)S(1)} %get-tuple-element.184.q, bf16[2048,256]{1,0:T(8,128)(2,1)S(1)} %get-tuple-element.174.k, ...), custom_call_target="tpu_custom_call" | custom-call | tf_op jit(solution)/shard_map/attention_forward/pallas_call | solution.py:180
  85.3 2.9 collective-permute-done.7.c1
  88.1 6.8 %attention_forward.7 = (bf16[512,192]{1,0:T(8,128)(2,1)S(1)}, f32[8,512]{1,0:T(8,128)S(1)}, f32[512,256]{1,0:T(8,128)S(1)}) custom-call(s32[17]{0:T(128)S(1)} %get-tuple-element.375.place, bf16[2048,256]{1,0:T(8,128)(2,1)S(1)} %get-tuple-element.184.q, bf16[2048,256]{1,0:T(8,128)(2,1)S(1)} %get-tuple-element.174.k, ...), custom_call_target="tpu_custom_call" | custom-call | tf_op jit(solution)/shard_map/attention_forward/pallas_call | solution.py:180
  94.9 1.5 pad_maximum_fusion.full
  96.4 1.6 collective-permute-done.8.c2
  98.7 1.3 pad_maximum_fusion.1.ctx
  100.0 12.6 %all-gather.2.cloned.1.call-done = bf16[3072,1728]{1,0:T(8,128)(2,1)} async-done(((bf16[96,1728]{1,0:T(8,128)(2,1)}), bf16[3072,1728]{1,0:T(8,128)(2,1)}) %all-gather.2.cloned.1.call-update) | async-done | bytes 10616848 | tf_op jit(solution)/shard_map/all_gather | solution.py:1011
  112.6 21.0 %feed_forward.1 = (bf16[512,768]{1,0:T(8,128)(2,1)}, f32[512,768]{1,0:T(8,128)}, bf16[512,768]{1,0:T(8,128)(2,1)}, f32[512,768]{1,0:T(8,128)}, bf16[768,512]{1,0...) custom-call(s32[10]{0:T(128)} %copy-done.32, ...), custom_call_target="tpu_custom_call" | custom-call | tf_op jit(solution)/shard_map/feed_forward/pallas_call | solution.py:440
  134.0 1.3 collective-permute-start.16
  135.2 15.3 %feed_back.1 = (f32[512,768]{1,0:T(8,128)}, bf16[768,512]{1,0:T(8,128)(2,1)}, bf16[512,192]{1,0:T(8,128)(2,1)}, bf16[512,192]{1,0:T(8,128)(2,1)}, bf16[512,192]{...) custom-call(s32[10]{0:T(128)} %copy-done.32, ...), custom_call_target="tpu_custom_call" | custom-call | tf_op jit(solution)/shard_map/feed_back/pallas_call | solution.py:524
  153.2 12.1 %weight_grads.1 = (bf16[4,4,96,768]{3,2,1,0:T(8,128)(2,1)}, bf16[4,4,96,768]{3,2,1,0:T(8,128)(2,1)}, bf16[4,768,960]{2,1,0:T(8,128)(2,1)}) custom-call(s32[10]{0:T(128)} %copy-done.32, bf16[768,512]{1,0:T(8,128)(2,1)} %get-tuple-element.198.nbt, bf16[768,512]{1,0:T(8,128)(2,1)} %get-tuple-element.199.gst, bf16[768,512]{1,0:T(8,128)(2,1)} %get-tuple-element.205.gft, ...), custom_call_target="tpu_custom_call" | custom-call | tf_op jit(solution)/shard_map/weight_grads/pallas_call | solution.py:592
  166.9 1.7 collective-permute-start.18
  170.9 2.1 collective-permute-done.18
  173.0 2.3 add_bitcast_fusion
  176.8 1.3 collective-permute-start.21
  179.5 27.8 %attention_backward.1 = (bf16[2048,768]{1,0:T(8,128)(2,1)S(1)}, f32[8,768]{1,0:T(8,128)S(1)}) custom-call(s32[17]{0:T(128)S(1)} %get-tuple-element.375.place, bf16[2048,256]{1,0:T(8,128)(2,1)S(1)} %get-tuple-element.184.q, bf16[256,2048]{1,0:T(8,128)(2,1)S(1)} %copy-done.21, bf16[2048,256]{1,0:T(8,128)(2,1)S(1)} %get-tuple-element.174.k, ...), custom_call_target="tpu_custom_call" | custom-call | tf_op jit(solution)/shard_map/attention_backward/pallas_call | solution.py:313
  207.4 1.3 branch.2
  208.8 2.1 collective-permute-done.22.refs_0_.refs_1_
  211.0 2.7 pick.3
  213.7 1.4 collective-permute-start.27
  215.1 2.7 pick.4
  217.7 4.0 %qkv_weight_grads.1 = (f32[4,96,576]{2,1,0:T(8,128)S(1)}, bf16[4,96,576]{2,1,0:T(8,128)(2,1)S(1)}) custom-call(s32[10]{0:T(128)S(1)} %copy-done.33, bf16[2,1024,768]{2,1,0:T(8,128)(2,1)S(1)} %copy-done.4, bf16[1024,768]{1,0:T(8,128)(2,1)S(1)} %copy-done.7, bf16[2048,768]{1,0:T(8,128)(2,1)S(1)} %get-tuple-element.254.refs_0_.g.refs_1_.refs_2_), custom_call_target="tpu_custom_call" | custom-call | tf_op jit(solution)/shard_map/qkv_weight_grads/pallas_call | solution.py:636
  224.8 2.6 branch.3
  228.0 12.3 %collective-permute-done.25.low = bf16[256,768]{1,0:T(8,128)(2,1)S(1)} collective-permute-done((bf16[256,768]{1,0:T(8,128)(2,1)S(1)}, bf16[256,768]{1,0:T(8,128)(2,1)S(1)}, u32[]{:S(2)}, u32[]{:S(2)}) %collective-permute-start.25) | collective-permute-done | bytes 393248 | tf_op jit(solution)/shard_map/ppermute | solution.py:946
  240.6 1.3 collective-permute-start.29
  243.1 2.4 collective-permute-start.33
  245.6 5.9 %collective-permute-done.31.refs_1_ = bf16[96,576]{1,0:T(8,128)(2,1)S(1)} collective-permute-done((bf16[96,576]{1,0:T(8,128)(2,1)S(1)}, bf16[96,576]{1,0:T(8,128)(2,1)S(1)}, u32[]{:S(2)}, u32[]{:S(2)}) %collective-permute-start.31) | collective-permute-done | bytes 110624 | tf_op jit(solution)/shard_map/ppermute | solution.py:950
  251.5 2.3 collective-permute-start.32
  254.1 2.9 join.4.refs_4_
  257.0 2.9 join.5
  260.1 1.3 collective-permute-done.32
  262.5 1.7 collective-permute-start.35
  264.7 2.8 collective-permute-start.38
  267.7 1.8 collective-permute-done.37.refs_1_
  269.5 3.0 collective-permute-start.40
  272.6 7.2 %collective-permute-done.39.refs_3_ = bf16[96,768]{1,0:T(8,128)(2,1)S(1)} collective-permute-done((bf16[96,768]{1,0:T(8,128)(2,1)S(1)}, bf16[96,768]{1,0:T(8,128)(2,1)S(1)}, u32[]{:S(2)}, u32[]{:S(2)}) %collective-permute-start.39) | collective-permute-done | bytes 147488 | tf_op jit(solution)/shard_map/ppermute | solution.py:950
  279.9 3.1 collective-permute-done.40
  283.0 1.5 pick.5
  284.6 2.3 collective-permute-start.44
  288.3 1.5 collective-permute-start.43
  289.8 1.8 collective-permute-done.43
  291.6 1.8 join.6.refs_4_
  293.4 2.3 collective-permute-start.45
  295.6 1.9 collective-permute-done.45
  299.4 2.0 collective-permute-start.46
  305.6 1.8 join.7
  (214 shorter events, 41.9 us)
Async XLA Ops:
  7.2 13.2 %copy-start.41 = (s32[2,1024]{1,0:T(2,128)S(1)}, s32[2,1024]{1,0:T(2,128)}, u32[]{:S(2)}) copy-start(s32[2,1024]{1,0:T(2,128)} %param.15) | copy-start | bytes 24580
  7.2 16.2 %copy-start.2 = (bf16[2,1024,768]{2,1,0:T(8,128)(2,1)S(1)}, bf16[2,1024,768]{2,1,0:T(8,128)(2,1)}, u32[]{:S(2)}) copy-start(bf16[2,1024,768]{2,1,0:T(8,128)(2,1)} %own.1) | copy-start | bytes 9437188
  7.2 105.4 %all-gather.2.cloned.1.call-start = ((), (), s32[]{:S(2)}) async-start(), calls=%async_computation.1 | async-start | bytes 11354112 | tf_op jit(solution)/shard_map/all_gather | solution.py:1011
  10.0 297.4 %reduce-scatter.2.cloned.1.call-start = ((), (), s32[]{:S(2)}) async-start(), calls=%async_computation.2 | async-start | bytes 6488064 | tf_op jit(solution)/shard_map/reduce_scatter | solution.py:1077
  10.7 15.8 %collective-permute-start.12 = (f32[1,768]{1,0:T(1,128)S(1)}, f32[1,768]{1,0:T(1,128)}, u32[]{:S(2)}, u32[]{:S(2)}) collective-permute-start(f32[1,768]{1,0:T(1,128)S(1)} %reshape.214), channel_id=1, source_target_pairs={{0,3},{1,2},{2,1},{3,0},{4,7},{5,6},{6,5},{7,4},{8,11},{9,10},{10,... | collective-permute-start | bytes 9224 | tf_op jit(solution)/shard_map/ppermute | solution.py:946
  13.7 13.2 %collective-permute-start.11 = (f32[1,768]{1,0:T(1,128)S(1)}, f32[1,768]{1,0:T(1,128)}, u32[]{:S(2)}, u32[]{:S(2)}) collective-permute-start(f32[1,768]{1,0:T(1,128)S(1)} %reshape.214), channel_id=1, source_target_pairs={{0,2},{1,3},{2,0},{3,1},{4,6},{5,7},{6,4},{7,5},{8,10},{9,11},{10,... | collective-permute-start | bytes 9224 | tf_op jit(solution)/shard_map/ppermute | solution.py:946
  13.9 15.1 %collective-permute-start.10 = (f32[1,768]{1,0:T(1,128)S(1)}, f32[1,768]{1,0:T(1,128)}, u32[]{:S(2)}, u32[]{:S(2)}) collective-permute-start(f32[1,768]{1,0:T(1,128)S(1)} %reshape.214), channel_id=1, source_target_pairs={{0,1},{1,0},{2,3},{3,2},{4,5},{5,4},{6,7},{7,6},{8,9},{9,8},{10,11... | collective-permute-start | bytes 9224 | tf_op jit(solution)/shard_map/ppermute | solution.py:946
  16.8 15.3 %collective-permute-start.4 = (bf16[96,576]{1,0:T(8,128)(2,1)S(1)}, bf16[96,576]{1,0:T(8,128)(2,1)S(1)}, u32[]{:S(2)}, u32[]{:S(2)}) collective-permute-start(bf16[96,576]{1,0:T(8,128)(2,1)S(1)} %copy.35.refs_0_), channel_id=1, source_target_pairs={{0,24},{8,16},{16,8},{24,0},{1,25},{9,17},{17,9},{25,1},{2,26},{10... | collective-permute-start | bytes 331784 | tf_op jit(solution)/shard_map/ppermute | solution.py:950
  20.3 14.7 %collective-permute-start.3 = (bf16[96,576]{1,0:T(8,128)(2,1)S(1)}, bf16[96,576]{1,0:T(8,128)(2,1)S(1)}, u32[]{:S(2)}, u32[]{:S(2)}) collective-permute-start(bf16[96,576]{1,0:T(8,128)(2,1)S(1)} %copy.35.refs_0_), channel_id=1, source_target_pairs={{0,16},{8,24},{16,0},{24,8},{1,17},{9,25},{17,1},{25,9},{2,18},{10... | collective-permute-start | bytes 331784 | tf_op jit(solution)/shard_map/ppermute | solution.py:950
  24.6 15.9 %copy-start.44 = (f32[128]{0:T(128)S(1)}, f32[128]{0:T(128)}, u32[]{:S(2)}) copy-start(f32[128]{0:T(128)} %constant.195) | copy-start | bytes 1540
  24.6 15.9 %copy-start.45 = (f32[128]{0:T(128)S(1)}, f32[128]{0:T(128)}, u32[]{:S(2)}) copy-start(f32[128]{0:T(128)} %constant.188.clone) | copy-start | bytes 1540
  26.5 19.0 %copy-start.32 = (s32[10]{0:T(128)}, s32[10]{0:T(128)S(1)}, u32[]{:S(2)}) copy-start(s32[10]{0:T(128)S(1)} %stack.96.place) | copy-start | bytes 124
  26.5 13.0 %collective-permute-start.2 = (bf16[96,576]{1,0:T(8,128)(2,1)S(1)}, bf16[96,576]{1,0:T(8,128)(2,1)S(1)}, u32[]{:S(2)}, u32[]{:S(2)}) collective-permute-start(bf16[96,576]{1,0:T(8,128)(2,1)S(1)} %copy.35.refs_0_), channel_id=1, source_target_pairs={{0,8},{8,0},{16,24},{24,16},{1,9},{9,1},{17,25},{25,17},{2,10},{10... | collective-permute-start | bytes 331784 | tf_op jit(solution)/shard_map/ppermute | solution.py:950
  26.9 3.5 %collective-permute-start.1 = (s32[2,1024]{1,0:T(2,128)S(1)}, s32[2,1024]{1,0:T(2,128)S(1)}, u32[]{:S(2)}, u32[]{:S(2)}) collective-permute-start(s32[2,1024]{1,0:T(2,128)S(1)} %bitcast.126), channel_id=1, source_target_pairs={{0,4},{4,0},{1,5},{5,1},{2,6},{6,2},{3,7},{7,3},{8,12},{12,8},{9,1... | collective-permute-start | bytes 24584 | tf_op jit(solution)/shard_map/ppermute | solution.py:942
  29.0 15.3 %collective-permute-start = (bf16[1024,768]{1,0:T(8,128)(2,1)}, bf16[1024,768]{1,0:T(8,128)(2,1)S(1)}, u32[]{:S(2)}, u32[]{:S(2)}) collective-permute-start(bf16[1024,768]{1,0:T(8,128)(2,1)} %dynamic-slice_bitcast_fusion), channel_id=1, source_target_pairs={{0,4},{4,0},{1,5},{5,1},{2,6},{6,2},{3,7},{7,3},{8,12},{12,8},{9,1... | collective-permute-start | bytes 4718600 | tf_op jit(solution)/shard_map/ppermute | solution.py:942
  30.4 44.0 %collective-permute-start.9 = (bf16[512,768]{1,0:T(8,128)(2,1)}, bf16[512,768]{1,0:T(8,128)(2,1)}, u32[]{:S(2)}, u32[]{:S(2)}) collective-permute-start(bf16[512,768]{1,0:T(8,128)(2,1)} %dynamic-slice_bitcast_fusion.1), channel_id=1, source_target_pairs={{0,4},{4,0},{1,5},{5,1},{2,6},{6,2},{3,7},{7,3},{8,12},{12,8},{9,1... | collective-permute-start | bytes 2359304 | tf_op jit(solution)/shard_map/ppermute | solution.py:942
  39.6 4.6 %collective-permute-start.5 = (bf16[4,96,576]{2,1,0:T(8,128)(2,1)S(1)}, bf16[4,96,576]{2,1,0:T(8,128)(2,1)S(1)}, u32[]{:S(2)}, u32[]{:S(2)}) collective-permute-start(bf16[4,96,576]{2,1,0:T(8,128)(2,1)S(1)} %pad_maximum_fusion.2), channel_id=1, source_target_pairs={{0,4},{4,0},{1,5},{5,1},{2,6},{6,2},{3,7},{7,3},{8,12},{12,8},{9,1... | collective-permute-start | bytes 1327112 | tf_op jit(solution)/shard_map/ppermute | solution.py:942
  57.4 30.7 %copy-start = (bf16[2048,256]{1,0:T(8,128)(2,1)}, bf16[2048,256]{1,0:T(8,128)(2,1)S(1)}, u32[]{:S(2)}) copy-start(bf16[2048,256]{1,0:T(8,128)(2,1)S(1)} %get-tuple-element.176.v) | copy-start | bytes 3145732
  64.2 13.5 %collective-permute-start.6 = (bf16[512,192]{1,0:T(8,128)(2,1)S(1)}, bf16[512,192]{1,0:T(8,128)(2,1)S(1)}, u32[]{:S(2)}, u32[]{:S(2)}) collective-permute-start(bf16[512,192]{1,0:T(8,128)(2,1)S(1)} %get-tuple-element.180), channel_id=1, source_target_pairs={{0,3},{1,2},{2,1},{3,0},{4,7},{5,6},{6,5},{7,4},{8,11},{9,10},{10,... | collective-permute-start | bytes 589832 | tf_op jit(solution)/shard_map/ppermute | solution.py:946
  74.0 14.1 %collective-permute-start.7 = (bf16[512,192]{1,0:T(8,128)(2,1)S(1)}, bf16[512,192]{1,0:T(8,128)(2,1)S(1)}, u32[]{:S(2)}, u32[]{:S(2)}) collective-permute-start(bf16[512,192]{1,0:T(8,128)(2,1)S(1)} %get-tuple-element.183), channel_id=1, source_target_pairs={{0,1},{1,0},{2,3},{3,2},{4,5},{5,4},{6,7},{7,6},{8,9},{9,8},{10,11... | collective-permute-start | bytes 589832 | tf_op jit(solution)/shard_map/ppermute | solution.py:946
  77.7 20.4 %copy-start.37 = (bf16[512,192]{1,0:T(8,128)(2,1)}, bf16[512,192]{1,0:T(8,128)(2,1)S(1)}, u32[]{:S(2)}) copy-start(bf16[512,192]{1,0:T(8,128)(2,1)S(1)} %collective-permute-done.6.c3) | copy-start | bytes 589828
  88.1 9.9 %copy-start.38 = (bf16[512,192]{1,0:T(8,128)(2,1)}, bf16[512,192]{1,0:T(8,128)(2,1)S(1)}, u32[]{:S(2)}) copy-start(bf16[512,192]{1,0:T(8,128)(2,1)S(1)} %collective-permute-done.7.c1) | copy-start | bytes 589828
  88.1 9.9 %collective-permute-start.8 = (bf16[512,192]{1,0:T(8,128)(2,1)S(1)}, bf16[512,192]{1,0:T(8,128)(2,1)S(1)}, u32[]{:S(2)}, u32[]{:S(2)}) collective-permute-start(bf16[512,192]{1,0:T(8,128)(2,1)S(1)} %get-tuple-element.187), channel_id=1, source_target_pairs={{0,2},{1,3},{2,0},{3,1},{4,6},{5,7},{6,4},{7,5},{8,10},{9,11},{10,... | collective-permute-start | bytes 589832 | tf_op jit(solution)/shard_map/ppermute | solution.py:946
  133.6 33.2 %collective-permute-start.17 = (bf16[512,768]{1,0:T(8,128)(2,1)}, bf16[512,768]{1,0:T(8,128)(2,1)}, u32[]{:S(2)}, u32[]{:S(2)}) collective-permute-start(bf16[512,768]{1,0:T(8,128)(2,1)} %get-tuple-element.266.near.refs_0_), channel_id=1, source_target_pairs={{0,2},{1,3},{2,0},{3,1},{4,6},{5,7},{6,4},{7,5},{8,10},{9,11},{10,... | collective-permute-start | bytes 2359304 | tf_op jit(solution)/shard_map/ppermute | solution.py:946
  134.0 32.9 %collective-permute-start.16 = (bf16[512,768]{1,0:T(8,128)(2,1)}, bf16[512,768]{1,0:T(8,128)(2,1)}, u32[]{:S(2)}, u32[]{:S(2)}) collective-permute-start(bf16[512,768]{1,0:T(8,128)(2,1)} %get-tuple-element.266.near.refs_0_), channel_id=1, source_target_pairs={{0,1},{1,0},{2,3},{3,2},{4,5},{5,4},{6,7},{7,6},{8,9},{9,8},{10,11... | collective-permute-start | bytes 2359304 | tf_op jit(solution)/shard_map/ppermute | solution.py:946
  150.5 14.8 %collective-permute-start.13 = (bf16[512,192]{1,0:T(8,128)(2,1)}, bf16[512,192]{1,0:T(8,128)(2,1)S(1)}, u32[]{:S(2)}, u32[]{:S(2)}) collective-permute-start(bf16[512,192]{1,0:T(8,128)(2,1)} %get-tuple-element.213), channel_id=1, source_target_pairs={{0,1},{1,0},{2,3},{3,2},{4,5},{5,4},{6,7},{7,6},{8,9},{9,8},{10,11... | collective-permute-start | bytes 589832 | tf_op jit(solution)/shard_map/ppermute | solution.py:946
  150.8 14.6 %collective-permute-start.14 = (bf16[512,192]{1,0:T(8,128)(2,1)}, bf16[512,192]{1,0:T(8,128)(2,1)S(1)}, u32[]{:S(2)}, u32[]{:S(2)}) collective-permute-start(bf16[512,192]{1,0:T(8,128)(2,1)} %get-tuple-element.214), channel_id=1, source_target_pairs={{0,2},{1,3},{2,0},{3,1},{4,6},{5,7},{6,4},{7,5},{8,10},{9,11},{10,... | collective-permute-start | bytes 589832 | tf_op jit(solution)/shard_map/ppermute | solution.py:946
  152.0 14.2 %collective-permute-start.15 = (bf16[512,192]{1,0:T(8,128)(2,1)}, bf16[512,192]{1,0:T(8,128)(2,1)S(1)}, u32[]{:S(2)}, u32[]{:S(2)}) collective-permute-start(bf16[512,192]{1,0:T(8,128)(2,1)} %get-tuple-element.215), channel_id=1, source_target_pairs={{0,3},{1,2},{2,1},{3,0},{4,7},{5,6},{6,5},{7,4},{8,11},{9,10},{10,... | collective-permute-start | bytes 589832 | tf_op jit(solution)/shard_map/ppermute | solution.py:946
  166.9 6.1 %collective-permute-start.18 = (bf16[4,4,96,768]{3,2,1,0:T(8,128)(2,1)}, bf16[4,4,96,768]{3,2,1,0:T(8,128)(2,1)S(1)}, u32[]{:S(2)}, u32[]{:S(2)}) collective-permute-start(bf16[4,4,96,768]{3,2,1,0:T(8,128)(2,1)} %get-tuple-element.221), channel_id=1, source_target_pairs={{0,4},{4,0},{1,5},{5,1},{2,6},{6,2},{3,7},{7,3},{8,12},{12,8},{9,1... | collective-permute-start | bytes 7077896 | tf_op jit(solution)/shard_map/ppermute | solution.py:942
  169.7 9.8 %copy-start.26 = (bf16[512,192]{1,0:T(8,128)(2,1)S(1)}, bf16[512,192]{1,0:T(8,128)(2,1)}, u32[]{:S(2)}) copy-start(bf16[512,192]{1,0:T(8,128)(2,1)} %copy-done.25) | copy-start | bytes 589828
  169.7 9.8 %copy-start.28 = (bf16[512,192]{1,0:T(8,128)(2,1)S(1)}, bf16[512,192]{1,0:T(8,128)(2,1)}, u32[]{:S(2)}) copy-start(bf16[512,192]{1,0:T(8,128)(2,1)} %copy-done.27) | copy-start | bytes 589828
  169.7 9.7 %copy-start.30 = (bf16[512,192]{1,0:T(8,128)(2,1)S(1)}, bf16[512,192]{1,0:T(8,128)(2,1)}, u32[]{:S(2)}) copy-start(bf16[512,192]{1,0:T(8,128)(2,1)} %copy-done.29) | copy-start | bytes 589828
  175.3 32.0 %collective-permute-start.19 = (bf16[4,96,768]{2,1,0:T(8,128)(2,1)S(1)}, bf16[4,96,768]{2,1,0:T(8,128)(2,1)S(1)}, u32[]{:S(2)}, u32[]{:S(2)}) collective-permute-start(bf16[4,96,768]{2,1,0:T(8,128)(2,1)S(1)} %get-tuple-element.243), channel_id=1, source_target_pairs={{0,1},{1,0},{2,3},{3,2},{4,5},{5,4},{6,7},{7,6},{8,9},{9,8},{10,11... | collective-permute-start | bytes 1769480 | tf_op jit(solution)/shard_map/ppermute | solution.py:946
  175.6 31.8 %collective-permute-start.20 = (bf16[4,96,768]{2,1,0:T(8,128)(2,1)S(1)}, bf16[4,96,768]{2,1,0:T(8,128)(2,1)S(1)}, u32[]{:S(2)}, u32[]{:S(2)}) collective-permute-start(bf16[4,96,768]{2,1,0:T(8,128)(2,1)S(1)} %get-tuple-element.244), channel_id=1, source_target_pairs={{0,2},{1,3},{2,0},{3,1},{4,6},{5,7},{6,4},{7,5},{8,10},{9,11},{10,... | collective-permute-start | bytes 1769480 | tf_op jit(solution)/shard_map/ppermute | solution.py:946
  176.8 30.6 %collective-permute-start.21 = (bf16[4,96,768]{2,1,0:T(8,128)(2,1)S(1)}, bf16[4,96,768]{2,1,0:T(8,128)(2,1)S(1)}, u32[]{:S(2)}, u32[]{:S(2)}) collective-permute-start(bf16[4,96,768]{2,1,0:T(8,128)(2,1)S(1)} %get-tuple-element.245), channel_id=1, source_target_pairs={{0,3},{1,2},{2,1},{3,0},{4,7},{5,6},{6,5},{7,4},{8,11},{9,10},{10,... | collective-permute-start | bytes 1769480 | tf_op jit(solution)/shard_map/ppermute | solution.py:946
  178.0 32.9 %collective-permute-start.22 = (bf16[256,768]{1,0:T(8,128)(2,1)S(1)}, bf16[256,768]{1,0:T(8,128)(2,1)S(1)}, u32[]{:S(2)}, u32[]{:S(2)}) collective-permute-start(bf16[256,768]{1,0:T(8,128)(2,1)S(1)} %slice.73), channel_id=1, source_target_pairs={{0,2},{1,3},{2,0},{3,1},{4,6},{5,7},{6,4},{7,5},{8,10},{9,11},{10,... | collective-permute-start | bytes 1179656 | tf_op jit(solution)/shard_map/ppermute | solution.py:946
  179.1 31.9 %collective-permute-start.23 = (bf16[256,768]{1,0:T(8,128)(2,1)S(1)}, bf16[256,768]{1,0:T(8,128)(2,1)S(1)}, u32[]{:S(2)}, u32[]{:S(2)}) collective-permute-start(bf16[256,768]{1,0:T(8,128)(2,1)S(1)} %slice.74), channel_id=1, source_target_pairs={{0,1},{1,0},{2,3},{3,2},{4,5},{5,4},{6,7},{7,6},{8,9},{9,8},{10,11... | collective-permute-start | bytes 1179656 | tf_op jit(solution)/shard_map/ppermute | solution.py:946
  179.5 27.9 %copy-start.14 = (bf16[768,768]{1,0:T(8,128)(2,1)S(1)}, bf16[768,768]{1,0:T(8,128)(2,1)}, u32[]{:S(2)}) copy-start(bf16[768,768]{1,0:T(8,128)(2,1)} %copy-done.13) | copy-start | bytes 3538948
  179.5 27.9 %copy-start.33 = (s32[10]{0:T(128)S(1)}, s32[10]{0:T(128)}, u32[]{:S(2)}) copy-start(s32[10]{0:T(128)} %copy-done.32) | copy-start | bytes 124
  207.4 10.3 %copy-start.7 = (bf16[1024,768]{1,0:T(8,128)(2,1)S(1)}, bf16[1024,768]{1,0:T(8,128)(2,1)}, u32[]{:S(2)}) copy-start(bf16[1024,768]{1,0:T(8,128)(2,1)} %copy-done.5) | copy-start | bytes 4718596
  213.7 26.7 %collective-permute-start.27 = (bf16[512,768]{1,0:T(8,128)(2,1)S(1)}, bf16[512,768]{1,0:T(8,128)(2,1)S(1)}, u32[]{:S(2)}, u32[]{:S(2)}) collective-permute-start(bf16[512,768]{1,0:T(8,128)(2,1)S(1)} %get-tuple-element.268), channel_id=1, source_target_pairs={{0,4},{4,0},{1,5},{5,1},{2,6},{6,2},{3,7},{7,3},{8,12},{12,8},{9,1... | collective-permute-start | bytes 2359304 | tf_op jit(solution)/shard_map/ppermute | solution.py:942
  217.7 22.6 %collective-permute-start.28 = (bf16[512,768]{1,0:T(8,128)(2,1)S(1)}, bf16[512,768]{1,0:T(8,128)(2,1)S(1)}, u32[]{:S(2)}, u32[]{:S(2)}) collective-permute-start(bf16[512,768]{1,0:T(8,128)(2,1)S(1)} %get-tuple-element.272), channel_id=1, source_target_pairs={{0,4},{4,0},{1,5},{5,1},{2,6},{6,2},{3,7},{7,3},{8,12},{12,8},{9,1... | collective-permute-start | bytes 2359304 | tf_op jit(solution)/shard_map/ppermute | solution.py:942
  221.8 6.2 %collective-permute-start.24 = (bf16[4,96,576]{2,1,0:T(8,128)(2,1)S(1)}, bf16[4,96,576]{2,1,0:T(8,128)(2,1)S(1)}, u32[]{:S(2)}, u32[]{:S(2)}) collective-permute-start(bf16[4,96,576]{2,1,0:T(8,128)(2,1)S(1)} %get-tuple-element.256), channel_id=1, source_target_pairs={{0,4},{4,0},{1,5},{5,1},{2,6},{6,2},{3,7},{7,3},{8,12},{12,8},{9,1... | collective-permute-start | bytes 1327112 | tf_op jit(solution)/shard_map/ppermute | solution.py:942
  222.4 17.9 %collective-permute-start.25 = (bf16[256,768]{1,0:T(8,128)(2,1)S(1)}, bf16[256,768]{1,0:T(8,128)(2,1)S(1)}, u32[]{:S(2)}, u32[]{:S(2)}) collective-permute-start(bf16[256,768]{1,0:T(8,128)(2,1)S(1)} %get-tuple-element.360), channel_id=1, source_target_pairs={{0,2},{1,3},{2,0},{3,1},{4,6},{5,7},{6,4},{7,5},{8,10},{9,11},{10,... | collective-permute-start | bytes 1179656 | tf_op jit(solution)/shard_map/ppermute | solution.py:946
  223.6 16.7 %collective-permute-start.26 = (bf16[256,768]{1,0:T(8,128)(2,1)S(1)}, bf16[256,768]{1,0:T(8,128)(2,1)S(1)}, u32[]{:S(2)}, u32[]{:S(2)}) collective-permute-start(bf16[256,768]{1,0:T(8,128)(2,1)S(1)} %get-tuple-element.359), channel_id=1, source_target_pairs={{0,1},{1,0},{2,3},{3,2},{4,5},{5,4},{6,7},{7,6},{8,9},{9,8},{10,11... | collective-permute-start | bytes 1179656 | tf_op jit(solution)/shard_map/ppermute | solution.py:946
  240.6 20.8 %collective-permute-start.29 = (bf16[512,768]{1,0:T(8,128)(2,1)S(1)}, bf16[512,768]{1,0:T(8,128)(2,1)S(1)}, u32[]{:S(2)}, u32[]{:S(2)}) collective-permute-start(bf16[512,768]{1,0:T(8,128)(2,1)S(1)} %get-tuple-element.286), channel_id=1, source_target_pairs={{0,1},{1,0},{2,3},{3,2},{4,5},{5,4},{6,7},{7,6},{8,9},{9,8},{10,11... | collective-permute-start | bytes 2359304 | tf_op jit(solution)/shard_map/ppermute | solution.py:946
  241.8 19.6 %collective-permute-start.30 = (bf16[512,768]{1,0:T(8,128)(2,1)S(1)}, bf16[512,768]{1,0:T(8,128)(2,1)S(1)}, u32[]{:S(2)}, u32[]{:S(2)}) collective-permute-start(bf16[512,768]{1,0:T(8,128)(2,1)S(1)} %get-tuple-element.287), channel_id=1, source_target_pairs={{0,2},{1,3},{2,0},{3,1},{4,6},{5,7},{6,4},{7,5},{8,10},{9,11},{10,... | collective-permute-start | bytes 2359304 | tf_op jit(solution)/shard_map/ppermute | solution.py:946
  242.1 9.4 %collective-permute-start.31 = (bf16[96,576]{1,0:T(8,128)(2,1)S(1)}, bf16[96,576]{1,0:T(8,128)(2,1)S(1)}, u32[]{:S(2)}, u32[]{:S(2)}) collective-permute-start(bf16[96,576]{1,0:T(8,128)(2,1)S(1)} %get-tuple-element.289), channel_id=1, source_target_pairs={{0,8},{8,0},{16,24},{24,16},{1,9},{9,1},{17,25},{25,17},{2,10},{10... | collective-permute-start | bytes 331784 | tf_op jit(solution)/shard_map/ppermute | solution.py:950
  243.1 16.7 %collective-permute-start.33 = (bf16[96,576]{1,0:T(8,128)(2,1)S(1)}, bf16[96,576]{1,0:T(8,128)(2,1)S(1)}, u32[]{:S(2)}, u32[]{:S(2)}) collective-permute-start(bf16[96,576]{1,0:T(8,128)(2,1)S(1)} %get-tuple-element.304), channel_id=1, source_target_pairs={{0,16},{8,24},{16,0},{24,8},{1,17},{9,25},{17,1},{25,9},{2,18},{10... | collective-permute-start | bytes 331784 | tf_op jit(solution)/shard_map/ppermute | solution.py:950
  245.5 14.3 %collective-permute-start.34 = (bf16[96,576]{1,0:T(8,128)(2,1)S(1)}, bf16[96,576]{1,0:T(8,128)(2,1)S(1)}, u32[]{:S(2)}, u32[]{:S(2)}) collective-permute-start(bf16[96,576]{1,0:T(8,128)(2,1)S(1)} %get-tuple-element.305), channel_id=1, source_target_pairs={{0,24},{8,16},{16,8},{24,0},{1,25},{9,17},{17,9},{25,1},{2,26},{10... | collective-permute-start | bytes 331784 | tf_op jit(solution)/shard_map/ppermute | solution.py:950
  251.5 9.9 %collective-permute-start.32 = (f32[16,768]{1,0:T(8,128)S(1)}, f32[16,768]{1,0:T(8,128)S(1)}, u32[]{:S(2)}, u32[]{:S(2)}) collective-permute-start(f32[16,768]{1,0:T(8,128)S(1)} %collect.1), channel_id=1, source_target_pairs={{0,1},{1,0},{2,3},{3,2},{4,5},{5,4},{6,7},{7,6},{8,9},{9,8},{10,11... | collective-permute-start | bytes 147464 | tf_op jit(solution)/shard_map/ppermute | solution.py:946
  261.7 21.3 %collective-permute-start.36 = (bf16[512,768]{1,0:T(8,128)(2,1)S(1)}, bf16[512,768]{1,0:T(8,128)(2,1)S(1)}, u32[]{:S(2)}, u32[]{:S(2)}) collective-permute-start(bf16[512,768]{1,0:T(8,128)(2,1)S(1)} %add_block.1.near.refs_0_), channel_id=1, source_target_pairs={{0,2},{1,3},{2,0},{3,1},{4,6},{5,7},{6,4},{7,5},{8,10},{9,11},{10,... | collective-permute-start | bytes 2359304 | tf_op jit(solution)/shard_map/ppermute | solution.py:946
  262.5 20.5 %collective-permute-start.35 = (bf16[512,768]{1,0:T(8,128)(2,1)S(1)}, bf16[512,768]{1,0:T(8,128)(2,1)S(1)}, u32[]{:S(2)}, u32[]{:S(2)}) collective-permute-start(bf16[512,768]{1,0:T(8,128)(2,1)S(1)} %add_block.1.near.refs_0_), channel_id=1, source_target_pairs={{0,1},{1,0},{2,3},{3,2},{4,5},{5,4},{6,7},{7,6},{8,9},{9,8},{10,11... | collective-permute-start | bytes 2359304 | tf_op jit(solution)/shard_map/ppermute | solution.py:946
  264.2 5.4 %collective-permute-start.37 = (bf16[96,768]{1,0:T(8,128)(2,1)S(1)}, bf16[96,768]{1,0:T(8,128)(2,1)S(1)}, u32[]{:S(2)}, u32[]{:S(2)}) collective-permute-start(bf16[96,768]{1,0:T(8,128)(2,1)S(1)} %get-tuple-element.312), channel_id=1, source_target_pairs={{0,8},{8,0},{16,24},{24,16},{1,9},{9,1},{17,25},{25,17},{2,10},{10... | collective-permute-start | bytes 442376 | tf_op jit(solution)/shard_map/ppermute | solution.py:950
  264.7 7.9 %collective-permute-start.38 = (bf16[96,768]{1,0:T(8,128)(2,1)S(1)}, bf16[96,768]{1,0:T(8,128)(2,1)S(1)}, u32[]{:S(2)}, u32[]{:S(2)}) collective-permute-start(bf16[96,768]{1,0:T(8,128)(2,1)S(1)} %get-tuple-element.315), channel_id=1, source_target_pairs={{0,16},{8,24},{16,0},{24,8},{1,17},{9,25},{17,1},{25,9},{2,18},{10... | collective-permute-start | bytes 442376 | tf_op jit(solution)/shard_map/ppermute | solution.py:950
  267.5 12.3 %collective-permute-start.39 = (bf16[96,768]{1,0:T(8,128)(2,1)S(1)}, bf16[96,768]{1,0:T(8,128)(2,1)S(1)}, u32[]{:S(2)}, u32[]{:S(2)}) collective-permute-start(bf16[96,768]{1,0:T(8,128)(2,1)S(1)} %get-tuple-element.316), channel_id=1, source_target_pairs={{0,24},{8,16},{16,8},{24,0},{1,25},{9,17},{17,9},{25,1},{2,26},{10... | collective-permute-start | bytes 442376 | tf_op jit(solution)/shard_map/ppermute | solution.py:950
  269.5 13.5 %collective-permute-start.40 = (f32[16,768]{1,0:T(8,128)S(1)}, f32[16,768]{1,0:T(8,128)S(1)}, u32[]{:S(2)}, u32[]{:S(2)}) collective-permute-start(f32[16,768]{1,0:T(8,128)S(1)} %add.168), channel_id=1, source_target_pairs={{0,2},{1,3},{2,0},{3,1},{4,6},{5,7},{6,4},{7,5},{8,10},{9,11},{10,... | collective-permute-start | bytes 147464 | tf_op jit(solution)/shard_map/ppermute | solution.py:946
  284.6 7.0 %collective-permute-start.44 = (bf16[512,768]{1,0:T(8,128)(2,1)S(1)}, bf16[512,768]{1,0:T(8,128)(2,1)S(1)}, u32[]{:S(2)}, u32[]{:S(2)}) collective-permute-start(bf16[512,768]{1,0:T(8,128)(2,1)S(1)} %get-tuple-element.322), channel_id=1, source_target_pairs={{0,4},{4,0},{1,5},{5,1},{2,6},{6,2},{3,7},{7,3},{8,12},{12,8},{9,1... | collective-permute-start | bytes 2359304 | tf_op jit(solution)/shard_map/ppermute | solution.py:942
  286.9 11.3 %collective-permute-start.42 = (bf16[256,768]{1,0:T(8,128)(2,1)S(1)}, bf16[256,768]{1,0:T(8,128)(2,1)S(1)}, u32[]{:S(2)}, u32[]{:S(2)}) collective-permute-start(bf16[256,768]{1,0:T(8,128)(2,1)S(1)} %slice.86), channel_id=1, source_target_pairs={{0,1},{1,0},{2,3},{3,2},{4,5},{5,4},{6,7},{7,6},{8,9},{9,8},{10,11... | collective-permute-start | bytes 1179656 | tf_op jit(solution)/shard_map/ppermute | solution.py:946
  287.3 11.0 %collective-permute-start.41 = (bf16[256,768]{1,0:T(8,128)(2,1)S(1)}, bf16[256,768]{1,0:T(8,128)(2,1)S(1)}, u32[]{:S(2)}, u32[]{:S(2)}) collective-permute-start(bf16[256,768]{1,0:T(8,128)(2,1)S(1)} %slice.85), channel_id=1, source_target_pairs={{0,2},{1,3},{2,0},{3,1},{4,6},{5,7},{6,4},{7,5},{8,10},{9,11},{10,... | collective-permute-start | bytes 1179656 | tf_op jit(solution)/shard_map/ppermute | solution.py:946
  288.3 3.2 %collective-permute-start.43 = (f32[16,768]{1,0:T(8,128)S(1)}, f32[16,768]{1,0:T(8,128)S(1)}, u32[]{:S(2)}, u32[]{:S(2)}) collective-permute-start(f32[16,768]{1,0:T(8,128)S(1)} %add.169), channel_id=1, source_target_pairs={{0,8},{8,0},{16,24},{24,16},{1,9},{9,1},{17,25},{25,17},{2,10},{10... | collective-permute-start | bytes 147464 | tf_op jit(solution)/shard_map/ppermute | solution.py:950
  293.4 4.2 %collective-permute-start.45 = (f32[16,768]{1,0:T(8,128)S(1)}, f32[16,768]{1,0:T(8,128)S(1)}, u32[]{:S(2)}, u32[]{:S(2)}) collective-permute-start(f32[16,768]{1,0:T(8,128)S(1)} %add.170), channel_id=1, source_target_pairs={{0,16},{8,24},{16,0},{24,8},{1,17},{9,25},{17,1},{25,9},{2,18},{10... | collective-permute-start | bytes 147464 | tf_op jit(solution)/shard_map/ppermute | solution.py:950
  299.4 6.3 %collective-permute-start.46 = (bf16[512,768]{1,0:T(8,128)(2,1)}, bf16[512,768]{1,0:T(8,128)(2,1)S(1)}, u32[]{:S(2)}, u32[]{:S(2)}) collective-permute-start(bf16[512,768]{1,0:T(8,128)(2,1)} %maximum_select_fusion), channel_id=1, source_target_pairs={{0,4},{4,0},{1,5},{5,1},{2,6},{6,2},{3,7},{7,3},{8,12},{12,8},{9,1... | collective-permute-start | bytes 2359304 | tf_op jit(solution)/shard_map/ppermute | solution.py:942
  301.3 1.8 collective-permute-start.47
  (32 other events, 141.0 us)
Sparse Core Ops, SparseCore 0:
  11.6 100.9 all-gather.1
  167.0 131.6 reduce-scatter.1

commit v8 on v7

--- a/solution.py
+++ b/solution.py
@@ -1106,6 +1106,9 @@
     small = collect(place, hidden_sums, sums_one, sums_two, bias_sums)
     outs = [swap_ctx(send_a), swap_ctx(send_b)]
     if direct:
+        small = small + swap_ctx(small)
+        small = small + swap_shard(small, 1)
+    if direct:
         qkv_sum, *qkv_pieces = settle(grads[0], swap_ctx(grads[1]))
         qkv_sum, qkv_pieces, low = barrier((qkv_sum, qkv_pieces, low))
     low, high, one, two, own, outs, small = barrier((low, high, one, two, own, outs, small))
@@ -1142,14 +1145,11 @@
     grad_tokens = join(place, ready[0], [ready[2]], swap_ctx(send_a))
     grad_ffn_weight, grad_out_weight = place_feed(whole, total)
     if direct:
-        small = small + swap_shard(small, 1)
         small, grad_tokens = barrier((small, grad_tokens))
         small = small + swap_shard(small, 2)
     else:
         small = lax.psum(small, ("shard", "ctx", "tp"))
     corner, small, grad_tokens, qkv_total = barrier((corner, small, grad_tokens, qkv_total))
-    if direct:
-        small = small + swap_ctx(small)
     send_b = jnp.where(here, jnp.concatenate(corner), ready[1])
     grad_tokens = join(place, ready[1], corner, swap_ctx(send_b), grad_tokens)
 

time: 317 us -> 316 us (level)
    ppermute x11, waiting for transfers between devices: 26.1 us -> 21 us  [swap_shard(): return lax.ppermute(x, 'shard', [(i, i ^ k) for i in range(4)])]
    ppermute x26, starting transfers between devices: 27.3 us -> 22.9 us  [swap_tp(): return lax.ppermute(x, 'tp', [(i, i ^ k) for i in range(4)])]
    unnamed x100 -> x102, local copies, waits for them, and re-layouts: 14.6 us -> 14.6 us
  transfers between devices with their start and end apart: 50 -> 50, of which waited for: 18 -> 20; matrix products, arithmetic and copies ran while one was open for 10% -> 10% of each run, Pallas kernels for 37% -> 37%
where the time goes in v8:
time: 316 us; the launch traced here: 314 us
  Pallas kernels  138 us (44%)
  waiting for transfers between devices  65 us (21%)
  starting transfers between devices  51.8 us (16%)
  local copies, waits for them, and re-layouts  26 us (8%)
  other arithmetic  18.9 us (6%)
  between operations  14.8 us (5%)
    pallas_call x4, Pallas kernels, attention_forward(): pl.pallas_call(partial(forward_kernel, heads), grid_spec=pltpu.PrefetchSc...  28.7 us
    pallas_call x1, Pallas kernels, attention_backward(): pl.pallas_call(partial(backward_kernel, heads), grid_spec=pltpu.PrefetchS...  27.7 us
    ppermute x26, waiting for transfers between devices, swap_tp(): return lax.ppermute(x, 'tp', [(i, i ^ k) for i in range(4)])  27 us
    ppermute x26, starting transfers between devices, swap_tp(): return lax.ppermute(x, 'tp', [(i, i ^ k) for i in range(4)])  22.9 us
    pallas_call x1, Pallas kernels, feed_forward(): pl.pallas_call(feed_kernel, grid_spec=pltpu.PrefetchScalarGridSpec(num_sc...  21 us
    ppermute x11, waiting for transfers between devices, swap_shard(): return lax.ppermute(x, 'shard', [(i, i ^ k) for i in range(4)])  21 us
    ppermute x11, starting transfers between devices, swap_shard(): return lax.ppermute(x, 'shard', [(i, i ^ k) for i in range(4)])  16.3 us
    pallas_call x1, Pallas kernels, feed_back(): pl.pallas_call(feed_back_kernel, grid_spec=pltpu.PrefetchScalarGridSpec(n...  15.3 us
  transfers between devices with their start and end apart: 50, of which 20 were waited for; matrix products, arithmetic and copies ran while one was open for 10% of the time, Pallas kernels for 37%

profile of v8, /device:TPU:1, one launch (start us, length us, event | category | flops | bytes accessed | tf_op | source)
XLA Modules:
  0.0 314.3 jit_solution(7379292763692704365)
XLA Ops:
  8.4 1.6 pad_maximum_fusion.3
  10.7 3.0 collective-permute-start.12
  14.0 1.7 copy.29
  16.8 3.6 %collective-permute-start.4 = (bf16[96,576]{1,0:T(8,128)(2,1)S(1)}, bf16[96,576]{1,0:T(8,128)(2,1)S(1)}, u32[]{:S(2)}, u32[]{:S(2)}) collective-permute-start(bf16[96,576]{1,0:T(8,128)(2,1)S(1)} %copy.35.refs_0_), channel_id=1, source_target_pairs={{0,24},{8,16},{16,8},{24,0},{1,25},{9,17},{17,9},{25,1},{2,26},{10... | collective-permute-start | bytes 331784 | tf_op jit(solution)/shard_map/ppermute | solution.py:950
  21.3 2.1 dynamic-slice_bitcast_fusion.1
  23.4 1.2 dynamic-slice_bitcast_fusion
  26.9 2.1 collective-permute-start.1
  29.1 1.3 pad_maximum_fusion.5.bias
  32.0 3.0 collective-permute-done.3.refs_2_
  35.1 4.4 %collective-permute-done.2.refs_1_ = bf16[96,576]{1,0:T(8,128)(2,1)S(1)} collective-permute-done((bf16[96,576]{1,0:T(8,128)(2,1)S(1)}, bf16[96,576]{1,0:T(8,128)(2,1)S(1)}, u32[]{:S(2)}, u32[]{:S(2)}) %collective-permute-start.2) | collective-permute-done | bytes 110624 | tf_op jit(solution)/shard_map/ppermute | solution.py:950
  40.5 3.7 %fusion = (f32[2048,128]{1,0:T(8,128)S(1)}, f32[2048,128]{1,0:T(8,128)S(1)}) fusion(f32[128]{0:T(128)S(1)} %copy-done.46, f32[128]{0:T(128)S(1)} %copy-done.45, f32[2048]{0:T(1024)S(1)} %bitcast.124), kind=kLoop, calls=%fused_computation.8 | loop fusion | flops 524288 | bytes 2106368 | tf_op jit(solution)/shard_map/mul | solution.py:928
  44.3 1.2 copy-done.5
  45.5 1.9 copy-done.3
  47.4 1.4 copy-done.6
  49.7 5.7 %project_qkv.1 = (bf16[2048,256]{1,0:T(8,128)(2,1)S(1)}, bf16[2048,256]{1,0:T(8,128)(2,1)S(1)}, bf16[2048,256]{1,0:T(8,128)(2,1)S(1)}, bf16[256,2048]{1,0:T(8,12...) custom-call(s32[10]{0:T(128)S(1)} %stack.96.place, bf16[96,576]{1,0:T(8,128)(2,1)S(1)} %copy.35.refs_0_, ...), custom_call_target="tpu_custom_call" | custom-call | tf_op jit(solution)/shard_map/project_qkv/pallas_call | solution.py:95
  57.4 6.8 %attention_forward.4 = (bf16[512,192]{1,0:T(8,128)(2,1)S(1)}, f32[8,512]{1,0:T(8,128)S(1)}, f32[512,256]{1,0:T(8,128)S(1)}) custom-call(s32[17]{0:T(128)S(1)} %get-tuple-element.372.place, bf16[2048,256]{1,0:T(8,128)(2,1)S(1)} %get-tuple-element.184.q, bf16[2048,256]{1,0:T(8,128)(2,1)S(1)} %get-tuple-element.174.k, ...), custom_call_target="tpu_custom_call" | custom-call | tf_op jit(solution)/shard_map/attention_forward/pallas_call | solution.py:180
  64.2 2.2 collective-permute-start.6
  66.4 6.8 %attention_forward.5 = (bf16[512,192]{1,0:T(8,128)(2,1)S(1)}, f32[8,512]{1,0:T(8,128)S(1)}, f32[512,256]{1,0:T(8,128)S(1)}) custom-call(s32[17]{0:T(128)S(1)} %get-tuple-element.374.place, bf16[2048,256]{1,0:T(8,128)(2,1)S(1)} %get-tuple-element.184.q, bf16[2048,256]{1,0:T(8,128)(2,1)S(1)} %get-tuple-element.174.k, ...), custom_call_target="tpu_custom_call" | custom-call | tf_op jit(solution)/shard_map/attention_forward/pallas_call | solution.py:180
  74.0 2.4 bitcast_select_fusion.gtop
  77.3 8.4 %attention_forward.6 = (bf16[512,192]{1,0:T(8,128)(2,1)S(1)}, f32[8,512]{1,0:T(8,128)S(1)}, f32[512,256]{1,0:T(8,128)S(1)}) custom-call(s32[17]{0:T(128)S(1)} %get-tuple-element.373.place, bf16[2048,256]{1,0:T(8,128)(2,1)S(1)} %get-tuple-element.184.q, bf16[2048,256]{1,0:T(8,128)(2,1)S(1)} %get-tuple-element.174.k, ...), custom_call_target="tpu_custom_call" | custom-call | tf_op jit(solution)/shard_map/attention_forward/pallas_call | solution.py:180
  85.7 1.6 collective-permute-done.7.c1
  87.3 1.6 collective-permute-start.8
  88.9 6.8 %attention_forward.7 = (bf16[512,192]{1,0:T(8,128)(2,1)S(1)}, f32[8,512]{1,0:T(8,128)S(1)}, f32[512,256]{1,0:T(8,128)S(1)}) custom-call(s32[17]{0:T(128)S(1)} %get-tuple-element.375.place, bf16[2048,256]{1,0:T(8,128)(2,1)S(1)} %get-tuple-element.184.q, bf16[2048,256]{1,0:T(8,128)(2,1)S(1)} %get-tuple-element.174.k, ...), custom_call_target="tpu_custom_call" | custom-call | tf_op jit(solution)/shard_map/attention_forward/pallas_call | solution.py:180
  95.7 1.5 pad_maximum_fusion.full
  98.1 1.2 pad_maximum_fusion.1.ctx
  99.3 13.8 %all-gather.2.cloned.1.call-done = bf16[3072,1728]{1,0:T(8,128)(2,1)} async-done(((bf16[96,1728]{1,0:T(8,128)(2,1)}), bf16[3072,1728]{1,0:T(8,128)(2,1)}) %all-gather.2.cloned.1.call-update) | async-done | bytes 10616848 | tf_op jit(solution)/shard_map/all_gather | solution.py:1011
  113.1 21.0 %feed_forward.1 = (bf16[512,768]{1,0:T(8,128)(2,1)}, f32[512,768]{1,0:T(8,128)}, bf16[512,768]{1,0:T(8,128)(2,1)}, f32[512,768]{1,0:T(8,128)}, bf16[768,512]{1,0...) custom-call(s32[10]{0:T(128)} %copy-done.32, ...), custom_call_target="tpu_custom_call" | custom-call | tf_op jit(solution)/shard_map/feed_forward/pallas_call | solution.py:440
  134.2 1.6 collective-permute-start.17
  135.7 15.3 %feed_back.1 = (f32[512,768]{1,0:T(8,128)}, bf16[768,512]{1,0:T(8,128)(2,1)}, bf16[512,192]{1,0:T(8,128)(2,1)}, bf16[512,192]{1,0:T(8,128)(2,1)}, bf16[512,192]{...) custom-call(s32[10]{0:T(128)} %copy-done.32, ...), custom_call_target="tpu_custom_call" | custom-call | tf_op jit(solution)/shard_map/feed_back/pallas_call | solution.py:524
  151.0 1.5 collective-permute-start.13
  153.8 12.2 %weight_grads.1 = (bf16[4,4,96,768]{3,2,1,0:T(8,128)(2,1)}, bf16[4,4,96,768]{3,2,1,0:T(8,128)(2,1)}, bf16[4,768,960]{2,1,0:T(8,128)(2,1)}) custom-call(s32[10]{0:T(128)} %copy-done.32, bf16[768,512]{1,0:T(8,128)(2,1)} %get-tuple-element.198.nbt, bf16[768,512]{1,0:T(8,128)(2,1)} %get-tuple-element.199.gst, bf16[768,512]{1,0:T(8,128)(2,1)} %get-tuple-element.205.gft, ...), custom_call_target="tpu_custom_call" | custom-call | tf_op jit(solution)/shard_map/weight_grads/pallas_call | solution.py:592
  167.5 1.4 collective-permute-start.18
  171.2 2.1 collective-permute-done.18
  173.3 2.4 add_bitcast_fusion
  175.8 1.8 collective-permute-start.19
  177.6 1.3 collective-permute-start.21
  180.3 27.7 %attention_backward.1 = (bf16[2048,768]{1,0:T(8,128)(2,1)S(1)}, f32[8,768]{1,0:T(8,128)S(1)}) custom-call(s32[17]{0:T(128)S(1)} %get-tuple-element.375.place, bf16[2048,256]{1,0:T(8,128)(2,1)S(1)} %get-tuple-element.184.q, bf16[256,2048]{1,0:T(8,128)(2,1)S(1)} %copy-done.21, bf16[2048,256]{1,0:T(8,128)(2,1)S(1)} %get-tuple-element.174.k, ...), custom_call_target="tpu_custom_call" | custom-call | tf_op jit(solution)/shard_map/attention_backward/pallas_call | solution.py:313
  208.1 1.3 branch.2
  209.4 3.6 %collective-permute-done.22.refs_0_.refs_1_ = bf16[256,768]{1,0:T(8,128)(2,1)S(1)} collective-permute-done((bf16[256,768]{1,0:T(8,128)(2,1)S(1)}, bf16[256,768]{1,0:T(8,128)(2,1)S(1)}, u32[]{:S(2)}, u32[]{:S(2)}) %collective-permute-start.22) | collective-permute-done | bytes 393248 | tf_op jit(solution)/shard_map/ppermute | solution.py:946
  213.0 2.7 pick.3
  215.7 1.3 collective-permute-start.27
  217.0 2.9 pick.4
  221.1 4.0 %qkv_weight_grads.1 = (f32[4,96,576]{2,1,0:T(8,128)S(1)}, bf16[4,96,576]{2,1,0:T(8,128)(2,1)S(1)}) custom-call(s32[10]{0:T(128)S(1)} %copy-done.33, bf16[2,1024,768]{2,1,0:T(8,128)(2,1)S(1)} %copy-done.4, bf16[1024,768]{1,0:T(8,128)(2,1)S(1)} %copy-done.7, bf16[2048,768]{1,0:T(8,128)(2,1)S(1)} %get-tuple-element.254.refs_0_.g.refs_1_.refs_2_), custom_call_target="tpu_custom_call" | custom-call | tf_op jit(solution)/shard_map/qkv_weight_grads/pallas_call | solution.py:636
  225.2 1.4 collective-permute-start.30
  227.6 1.5 collective-permute-done.30
  230.3 2.6 branch.3
  233.0 6.0 %collective-permute-done.25.low = bf16[256,768]{1,0:T(8,128)(2,1)S(1)} collective-permute-done((bf16[256,768]{1,0:T(8,128)(2,1)S(1)}, bf16[256,768]{1,0:T(8,128)(2,1)S(1)}, u32[]{:S(2)}, u32[]{:S(2)}) %collective-permute-start.25) | collective-permute-done | bytes 393248 | tf_op jit(solution)/shard_map/ppermute | solution.py:946
  239.2 1.3 collective-permute-start.31
  242.1 3.3 %collective-permute-start.35 = (bf16[96,576]{1,0:T(8,128)(2,1)S(1)}, bf16[96,576]{1,0:T(8,128)(2,1)S(1)}, u32[]{:S(2)}, u32[]{:S(2)}) collective-permute-start(bf16[96,576]{1,0:T(8,128)(2,1)S(1)} %get-tuple-element.304), channel_id=1, source_target_pairs={{0,16},{8,24},{16,0},{24,8},{1,17},{9,25},{17,1},{25,9},{2,18},{10... | collective-permute-start | bytes 331784 | tf_op jit(solution)/shard_map/ppermute | solution.py:950
  246.2 2.9 join.4.refs_4_
  249.0 3.1 join.5
  252.5 8.1 %collective-permute-done.34 = f32[16,768]{1,0:T(8,128)S(1)} collective-permute-done((f32[16,768]{1,0:T(8,128)S(1)}, f32[16,768]{1,0:T(8,128)S(1)}, u32[]{:S(2)}, u32[]{:S(2)}) %collective-permute-start.34) | collective-permute-done | bytes 49184 | tf_op jit(solution)/shard_map/ppermute | solution.py:946
  260.6 2.7 collective-permute-done.32.two
  264.6 4.3 %collective-permute-start.40 = (bf16[96,768]{1,0:T(8,128)(2,1)S(1)}, bf16[96,768]{1,0:T(8,128)(2,1)S(1)}, u32[]{:S(2)}, u32[]{:S(2)}) collective-permute-start(bf16[96,768]{1,0:T(8,128)(2,1)S(1)} %get-tuple-element.315), channel_id=1, source_target_pairs={{0,16},{8,24},{16,0},{24,8},{1,17},{9,25},{17,1},{25,9},{2,18},{10... | collective-permute-start | bytes 442376 | tf_op jit(solution)/shard_map/ppermute | solution.py:950
  268.9 4.9 %collective-permute-done.39.refs_1_ = bf16[96,768]{1,0:T(8,128)(2,1)S(1)} collective-permute-done((bf16[96,768]{1,0:T(8,128)(2,1)S(1)}, bf16[96,768]{1,0:T(8,128)(2,1)S(1)}, u32[]{:S(2)}, u32[]{:S(2)}) %collective-permute-start.39) | collective-permute-done | bytes 147488 | tf_op jit(solution)/shard_map/ppermute | solution.py:950
  273.9 5.4 %collective-permute-done.41.refs_3_ = bf16[96,768]{1,0:T(8,128)(2,1)S(1)} collective-permute-done((bf16[96,768]{1,0:T(8,128)(2,1)S(1)}, bf16[96,768]{1,0:T(8,128)(2,1)S(1)}, u32[]{:S(2)}, u32[]{:S(2)}) %collective-permute-start.41) | collective-permute-done | bytes 147488 | tf_op jit(solution)/shard_map/ppermute | solution.py:950
  279.3 2.0 collective-permute-done.42
  281.4 1.5 pick.5
  282.9 4.7 %collective-permute-start.45 = (bf16[512,768]{1,0:T(8,128)(2,1)S(1)}, bf16[512,768]{1,0:T(8,128)(2,1)S(1)}, u32[]{:S(2)}, u32[]{:S(2)}) collective-permute-start(bf16[512,768]{1,0:T(8,128)(2,1)S(1)} %get-tuple-element.322), channel_id=1, source_target_pairs={{0,4},{4,0},{1,5},{5,1},{2,6},{6,2},{3,7},{7,3},{8,12},{12,8},{9,1... | collective-permute-start | bytes 2359304 | tf_op jit(solution)/shard_map/ppermute | solution.py:942
  289.6 1.8 join.6.refs_4_
  291.3 2.5 collective-permute-start.46
  293.8 1.5 collective-permute-done.46
  295.9 2.6 collective-permute-done.44.refs_2_
  303.7 1.8 join.7
  (216 shorter events, 38.4 us)
Async XLA Ops:
  7.2 13.2 %copy-start.42 = (s32[2,1024]{1,0:T(2,128)S(1)}, s32[2,1024]{1,0:T(2,128)}, u32[]{:S(2)}) copy-start(s32[2,1024]{1,0:T(2,128)} %param.15) | copy-start | bytes 24580
  7.2 16.2 %copy-start.2 = (bf16[2,1024,768]{2,1,0:T(8,128)(2,1)S(1)}, bf16[2,1024,768]{2,1,0:T(8,128)(2,1)}, u32[]{:S(2)}) copy-start(bf16[2,1024,768]{2,1,0:T(8,128)(2,1)} %own.1) | copy-start | bytes 9437188
  7.2 105.9 %all-gather.2.cloned.1.call-start = ((), (), s32[]{:S(2)}) async-start(), calls=%async_computation.1 | async-start | bytes 11354112 | tf_op jit(solution)/shard_map/all_gather | solution.py:1011
  10.0 295.5 %reduce-scatter.2.cloned.1.call-start = ((), (), s32[]{:S(2)}) async-start(), calls=%async_computation.2 | async-start | bytes 6488064 | tf_op jit(solution)/shard_map/reduce_scatter | solution.py:1077
  10.7 15.8 %collective-permute-start.12 = (f32[1,768]{1,0:T(1,128)S(1)}, f32[1,768]{1,0:T(1,128)}, u32[]{:S(2)}, u32[]{:S(2)}) collective-permute-start(f32[1,768]{1,0:T(1,128)S(1)} %reshape.214), channel_id=1, source_target_pairs={{0,3},{1,2},{2,1},{3,0},{4,7},{5,6},{6,5},{7,4},{8,11},{9,10},{10,... | collective-permute-start | bytes 9224 | tf_op jit(solution)/shard_map/ppermute | solution.py:946
  13.7 13.2 %collective-permute-start.11 = (f32[1,768]{1,0:T(1,128)S(1)}, f32[1,768]{1,0:T(1,128)}, u32[]{:S(2)}, u32[]{:S(2)}) collective-permute-start(f32[1,768]{1,0:T(1,128)S(1)} %reshape.214), channel_id=1, source_target_pairs={{0,2},{1,3},{2,0},{3,1},{4,6},{5,7},{6,4},{7,5},{8,10},{9,11},{10,... | collective-permute-start | bytes 9224 | tf_op jit(solution)/shard_map/ppermute | solution.py:946
  13.9 15.1 %collective-permute-start.10 = (f32[1,768]{1,0:T(1,128)S(1)}, f32[1,768]{1,0:T(1,128)}, u32[]{:S(2)}, u32[]{:S(2)}) collective-permute-start(f32[1,768]{1,0:T(1,128)S(1)} %reshape.214), channel_id=1, source_target_pairs={{0,1},{1,0},{2,3},{3,2},{4,5},{5,4},{6,7},{7,6},{8,9},{9,8},{10,11... | collective-permute-start | bytes 9224 | tf_op jit(solution)/shard_map/ppermute | solution.py:946
  16.8 15.3 %collective-permute-start.4 = (bf16[96,576]{1,0:T(8,128)(2,1)S(1)}, bf16[96,576]{1,0:T(8,128)(2,1)S(1)}, u32[]{:S(2)}, u32[]{:S(2)}) collective-permute-start(bf16[96,576]{1,0:T(8,128)(2,1)S(1)} %copy.35.refs_0_), channel_id=1, source_target_pairs={{0,24},{8,16},{16,8},{24,0},{1,25},{9,17},{17,9},{25,1},{2,26},{10... | collective-permute-start | bytes 331784 | tf_op jit(solution)/shard_map/ppermute | solution.py:950
  20.3 14.7 %collective-permute-start.3 = (bf16[96,576]{1,0:T(8,128)(2,1)S(1)}, bf16[96,576]{1,0:T(8,128)(2,1)S(1)}, u32[]{:S(2)}, u32[]{:S(2)}) collective-permute-start(bf16[96,576]{1,0:T(8,128)(2,1)S(1)} %copy.35.refs_0_), channel_id=1, source_target_pairs={{0,16},{8,24},{16,0},{24,8},{1,17},{9,25},{17,1},{25,9},{2,18},{10... | collective-permute-start | bytes 331784 | tf_op jit(solution)/shard_map/ppermute | solution.py:950
  24.6 15.9 %copy-start.45 = (f32[128]{0:T(128)S(1)}, f32[128]{0:T(128)}, u32[]{:S(2)}) copy-start(f32[128]{0:T(128)} %constant.195) | copy-start | bytes 1540
  24.6 15.9 %copy-start.46 = (f32[128]{0:T(128)S(1)}, f32[128]{0:T(128)}, u32[]{:S(2)}) copy-start(f32[128]{0:T(128)} %constant.188.clone) | copy-start | bytes 1540
  26.5 19.0 %copy-start.32 = (s32[10]{0:T(128)}, s32[10]{0:T(128)S(1)}, u32[]{:S(2)}) copy-start(s32[10]{0:T(128)S(1)} %stack.96.place) | copy-start | bytes 124
  26.5 13.0 %collective-permute-start.2 = (bf16[96,576]{1,0:T(8,128)(2,1)S(1)}, bf16[96,576]{1,0:T(8,128)(2,1)S(1)}, u32[]{:S(2)}, u32[]{:S(2)}) collective-permute-start(bf16[96,576]{1,0:T(8,128)(2,1)S(1)} %copy.35.refs_0_), channel_id=1, source_target_pairs={{0,8},{8,0},{16,24},{24,16},{1,9},{9,1},{17,25},{25,17},{2,10},{10... | collective-permute-start | bytes 331784 | tf_op jit(solution)/shard_map/ppermute | solution.py:950
  26.9 3.5 %collective-permute-start.1 = (s32[2,1024]{1,0:T(2,128)S(1)}, s32[2,1024]{1,0:T(2,128)S(1)}, u32[]{:S(2)}, u32[]{:S(2)}) collective-permute-start(s32[2,1024]{1,0:T(2,128)S(1)} %bitcast.126), channel_id=1, source_target_pairs={{0,4},{4,0},{1,5},{5,1},{2,6},{6,2},{3,7},{7,3},{8,12},{12,8},{9,1... | collective-permute-start | bytes 24584 | tf_op jit(solution)/shard_map/ppermute | solution.py:942
  29.0 15.3 %collective-permute-start = (bf16[1024,768]{1,0:T(8,128)(2,1)}, bf16[1024,768]{1,0:T(8,128)(2,1)S(1)}, u32[]{:S(2)}, u32[]{:S(2)}) collective-permute-start(bf16[1024,768]{1,0:T(8,128)(2,1)} %dynamic-slice_bitcast_fusion), channel_id=1, source_target_pairs={{0,4},{4,0},{1,5},{5,1},{2,6},{6,2},{3,7},{7,3},{8,12},{12,8},{9,1... | collective-permute-start | bytes 4718600 | tf_op jit(solution)/shard_map/ppermute | solution.py:942
  30.4 43.6 %collective-permute-start.9 = (bf16[512,768]{1,0:T(8,128)(2,1)}, bf16[512,768]{1,0:T(8,128)(2,1)}, u32[]{:S(2)}, u32[]{:S(2)}) collective-permute-start(bf16[512,768]{1,0:T(8,128)(2,1)} %dynamic-slice_bitcast_fusion.1), channel_id=1, source_target_pairs={{0,4},{4,0},{1,5},{5,1},{2,6},{6,2},{3,7},{7,3},{8,12},{12,8},{9,1... | collective-permute-start | bytes 2359304 | tf_op jit(solution)/shard_map/ppermute | solution.py:942
  39.6 4.6 %collective-permute-start.5 = (bf16[4,96,576]{2,1,0:T(8,128)(2,1)S(1)}, bf16[4,96,576]{2,1,0:T(8,128)(2,1)S(1)}, u32[]{:S(2)}, u32[]{:S(2)}) collective-permute-start(bf16[4,96,576]{2,1,0:T(8,128)(2,1)S(1)} %pad_maximum_fusion.2), channel_id=1, source_target_pairs={{0,4},{4,0},{1,5},{5,1},{2,6},{6,2},{3,7},{7,3},{8,12},{12,8},{9,1... | collective-permute-start | bytes 1327112 | tf_op jit(solution)/shard_map/ppermute | solution.py:942
  57.4 31.5 %copy-start = (bf16[2048,256]{1,0:T(8,128)(2,1)}, bf16[2048,256]{1,0:T(8,128)(2,1)S(1)}, u32[]{:S(2)}) copy-start(bf16[2048,256]{1,0:T(8,128)(2,1)S(1)} %get-tuple-element.176.v) | copy-start | bytes 3145732
  64.2 13.1 %collective-permute-start.6 = (bf16[512,192]{1,0:T(8,128)(2,1)S(1)}, bf16[512,192]{1,0:T(8,128)(2,1)S(1)}, u32[]{:S(2)}, u32[]{:S(2)}) collective-permute-start(bf16[512,192]{1,0:T(8,128)(2,1)S(1)} %get-tuple-element.180), channel_id=1, source_target_pairs={{0,3},{1,2},{2,1},{3,0},{4,7},{5,6},{6,5},{7,4},{8,11},{9,10},{10,... | collective-permute-start | bytes 589832 | tf_op jit(solution)/shard_map/ppermute | solution.py:946
  73.2 14.1 %collective-permute-start.7 = (bf16[512,192]{1,0:T(8,128)(2,1)S(1)}, bf16[512,192]{1,0:T(8,128)(2,1)S(1)}, u32[]{:S(2)}, u32[]{:S(2)}) collective-permute-start(bf16[512,192]{1,0:T(8,128)(2,1)S(1)} %get-tuple-element.183), channel_id=1, source_target_pairs={{0,1},{1,0},{2,3},{3,2},{4,5},{5,4},{6,7},{7,6},{8,9},{9,8},{10,11... | collective-permute-start | bytes 589832 | tf_op jit(solution)/shard_map/ppermute | solution.py:946
  77.3 20.1 %copy-start.37 = (bf16[512,192]{1,0:T(8,128)(2,1)}, bf16[512,192]{1,0:T(8,128)(2,1)S(1)}, u32[]{:S(2)}) copy-start(bf16[512,192]{1,0:T(8,128)(2,1)S(1)} %collective-permute-done.6.c3) | copy-start | bytes 589828
  87.3 10.1 %collective-permute-start.8 = (bf16[512,192]{1,0:T(8,128)(2,1)S(1)}, bf16[512,192]{1,0:T(8,128)(2,1)S(1)}, u32[]{:S(2)}, u32[]{:S(2)}) collective-permute-start(bf16[512,192]{1,0:T(8,128)(2,1)S(1)} %get-tuple-element.187), channel_id=1, source_target_pairs={{0,2},{1,3},{2,0},{3,1},{4,6},{5,7},{6,4},{7,5},{8,10},{9,11},{10,... | collective-permute-start | bytes 589832 | tf_op jit(solution)/shard_map/ppermute | solution.py:946
  134.2 33.3 %collective-permute-start.17 = (bf16[512,768]{1,0:T(8,128)(2,1)}, bf16[512,768]{1,0:T(8,128)(2,1)}, u32[]{:S(2)}, u32[]{:S(2)}) collective-permute-start(bf16[512,768]{1,0:T(8,128)(2,1)} %get-tuple-element.266.near.refs_0_), channel_id=1, source_target_pairs={{0,2},{1,3},{2,0},{3,1},{4,6},{5,7},{6,4},{7,5},{8,10},{9,11},{10,... | collective-permute-start | bytes 2359304 | tf_op jit(solution)/shard_map/ppermute | solution.py:946
  135.7 31.8 %collective-permute-start.16 = (bf16[512,768]{1,0:T(8,128)(2,1)}, bf16[512,768]{1,0:T(8,128)(2,1)}, u32[]{:S(2)}, u32[]{:S(2)}) collective-permute-start(bf16[512,768]{1,0:T(8,128)(2,1)} %get-tuple-element.266.near.refs_0_), channel_id=1, source_target_pairs={{0,1},{1,0},{2,3},{3,2},{4,5},{5,4},{6,7},{7,6},{8,9},{9,8},{10,11... | collective-permute-start | bytes 2359304 | tf_op jit(solution)/shard_map/ppermute | solution.py:946
  151.0 14.9 %collective-permute-start.13 = (bf16[512,192]{1,0:T(8,128)(2,1)}, bf16[512,192]{1,0:T(8,128)(2,1)S(1)}, u32[]{:S(2)}, u32[]{:S(2)}) collective-permute-start(bf16[512,192]{1,0:T(8,128)(2,1)} %get-tuple-element.213), channel_id=1, source_target_pairs={{0,1},{1,0},{2,3},{3,2},{4,5},{5,4},{6,7},{7,6},{8,9},{9,8},{10,11... | collective-permute-start | bytes 589832 | tf_op jit(solution)/shard_map/ppermute | solution.py:946
  152.6 13.4 %collective-permute-start.14 = (bf16[512,192]{1,0:T(8,128)(2,1)}, bf16[512,192]{1,0:T(8,128)(2,1)S(1)}, u32[]{:S(2)}, u32[]{:S(2)}) collective-permute-start(bf16[512,192]{1,0:T(8,128)(2,1)} %get-tuple-element.214), channel_id=1, source_target_pairs={{0,2},{1,3},{2,0},{3,1},{4,6},{5,7},{6,4},{7,5},{8,10},{9,11},{10,... | collective-permute-start | bytes 589832 | tf_op jit(solution)/shard_map/ppermute | solution.py:946
  152.6 14.1 %collective-permute-start.15 = (bf16[512,192]{1,0:T(8,128)(2,1)}, bf16[512,192]{1,0:T(8,128)(2,1)S(1)}, u32[]{:S(2)}, u32[]{:S(2)}) collective-permute-start(bf16[512,192]{1,0:T(8,128)(2,1)} %get-tuple-element.215), channel_id=1, source_target_pairs={{0,3},{1,2},{2,1},{3,0},{4,7},{5,6},{6,5},{7,4},{8,11},{9,10},{10,... | collective-permute-start | bytes 589832 | tf_op jit(solution)/shard_map/ppermute | solution.py:946
  167.5 5.8 %collective-permute-start.18 = (bf16[4,4,96,768]{3,2,1,0:T(8,128)(2,1)}, bf16[4,4,96,768]{3,2,1,0:T(8,128)(2,1)S(1)}, u32[]{:S(2)}, u32[]{:S(2)}) collective-permute-start(bf16[4,4,96,768]{3,2,1,0:T(8,128)(2,1)} %get-tuple-element.221), channel_id=1, source_target_pairs={{0,4},{4,0},{1,5},{5,1},{2,6},{6,2},{3,7},{7,3},{8,12},{12,8},{9,1... | collective-permute-start | bytes 7077896 | tf_op jit(solution)/shard_map/ppermute | solution.py:942
  175.8 32.2 %collective-permute-start.19 = (bf16[4,96,768]{2,1,0:T(8,128)(2,1)S(1)}, bf16[4,96,768]{2,1,0:T(8,128)(2,1)S(1)}, u32[]{:S(2)}, u32[]{:S(2)}) collective-permute-start(bf16[4,96,768]{2,1,0:T(8,128)(2,1)S(1)} %get-tuple-element.243), channel_id=1, source_target_pairs={{0,1},{1,0},{2,3},{3,2},{4,5},{5,4},{6,7},{7,6},{8,9},{9,8},{10,11... | collective-permute-start | bytes 1769480 | tf_op jit(solution)/shard_map/ppermute | solution.py:946
  177.5 30.4 %collective-permute-start.20 = (bf16[4,96,768]{2,1,0:T(8,128)(2,1)S(1)}, bf16[4,96,768]{2,1,0:T(8,128)(2,1)S(1)}, u32[]{:S(2)}, u32[]{:S(2)}) collective-permute-start(bf16[4,96,768]{2,1,0:T(8,128)(2,1)S(1)} %get-tuple-element.244), channel_id=1, source_target_pairs={{0,2},{1,3},{2,0},{3,1},{4,6},{5,7},{6,4},{7,5},{8,10},{9,11},{10,... | collective-permute-start | bytes 1769480 | tf_op jit(solution)/shard_map/ppermute | solution.py:946
  177.6 30.5 %collective-permute-start.21 = (bf16[4,96,768]{2,1,0:T(8,128)(2,1)S(1)}, bf16[4,96,768]{2,1,0:T(8,128)(2,1)S(1)}, u32[]{:S(2)}, u32[]{:S(2)}) collective-permute-start(bf16[4,96,768]{2,1,0:T(8,128)(2,1)S(1)} %get-tuple-element.245), channel_id=1, source_target_pairs={{0,3},{1,2},{2,1},{3,0},{4,7},{5,6},{6,5},{7,4},{8,11},{9,10},{10,... | collective-permute-start | bytes 1769480 | tf_op jit(solution)/shard_map/ppermute | solution.py:946
  178.8 34.2 %collective-permute-start.22 = (bf16[256,768]{1,0:T(8,128)(2,1)S(1)}, bf16[256,768]{1,0:T(8,128)(2,1)S(1)}, u32[]{:S(2)}, u32[]{:S(2)}) collective-permute-start(bf16[256,768]{1,0:T(8,128)(2,1)S(1)} %slice.73), channel_id=1, source_target_pairs={{0,2},{1,3},{2,0},{3,1},{4,6},{5,7},{6,4},{7,5},{8,10},{9,11},{10,... | collective-permute-start | bytes 1179656 | tf_op jit(solution)/shard_map/ppermute | solution.py:946
  179.0 34.0 %collective-permute-start.23 = (bf16[256,768]{1,0:T(8,128)(2,1)S(1)}, bf16[256,768]{1,0:T(8,128)(2,1)S(1)}, u32[]{:S(2)}, u32[]{:S(2)}) collective-permute-start(bf16[256,768]{1,0:T(8,128)(2,1)S(1)} %slice.74), channel_id=1, source_target_pairs={{0,1},{1,0},{2,3},{3,2},{4,5},{5,4},{6,7},{7,6},{8,9},{9,8},{10,11... | collective-permute-start | bytes 1179656 | tf_op jit(solution)/shard_map/ppermute | solution.py:946
  180.3 27.7 %copy-start.14 = (bf16[768,768]{1,0:T(8,128)(2,1)S(1)}, bf16[768,768]{1,0:T(8,128)(2,1)}, u32[]{:S(2)}) copy-start(bf16[768,768]{1,0:T(8,128)(2,1)} %copy-done.13) | copy-start | bytes 3538948
  180.3 27.7 %copy-start.33 = (s32[10]{0:T(128)S(1)}, s32[10]{0:T(128)}, u32[]{:S(2)}) copy-start(s32[10]{0:T(128)} %copy-done.32) | copy-start | bytes 124
  208.0 11.9 %copy-start.34 = (f32[4,8,768]{2,1,0:T(8,128)S(1)}, f32[4,8,768]{2,1,0:T(8,128)}, u32[]{:S(2)}) copy-start(f32[4,8,768]{2,1,0:T(8,128)} %get-tuple-element.273.hidden_sums) | copy-start | bytes 294916
  208.1 11.9 %copy-start.35 = (f32[8,768]{1,0:T(8,128)S(1)}, f32[8,768]{1,0:T(8,128)}, u32[]{:S(2)}) copy-start(f32[8,768]{1,0:T(8,128)} %get-tuple-element.275.two) | copy-start | bytes 73732
  208.1 11.9 %copy-start.36 = (f32[8,768]{1,0:T(8,128)S(1)}, f32[8,768]{1,0:T(8,128)}, u32[]{:S(2)}) copy-start(f32[8,768]{1,0:T(8,128)} %get-tuple-element.274.one) | copy-start | bytes 73732
  208.1 13.0 %copy-start.7 = (bf16[1024,768]{1,0:T(8,128)(2,1)S(1)}, bf16[1024,768]{1,0:T(8,128)(2,1)}, u32[]{:S(2)}) copy-start(bf16[1024,768]{1,0:T(8,128)(2,1)} %copy-done.5) | copy-start | bytes 4718596
  215.7 23.3 %collective-permute-start.27 = (bf16[512,768]{1,0:T(8,128)(2,1)S(1)}, bf16[512,768]{1,0:T(8,128)(2,1)S(1)}, u32[]{:S(2)}, u32[]{:S(2)}) collective-permute-start(bf16[512,768]{1,0:T(8,128)(2,1)S(1)} %get-tuple-element.268), channel_id=1, source_target_pairs={{0,4},{4,0},{1,5},{5,1},{2,6},{6,2},{3,7},{7,3},{8,12},{12,8},{9,1... | collective-permute-start | bytes 2359304 | tf_op jit(solution)/shard_map/ppermute | solution.py:942
  219.9 19.1 %collective-permute-start.28 = (bf16[512,768]{1,0:T(8,128)(2,1)S(1)}, bf16[512,768]{1,0:T(8,128)(2,1)S(1)}, u32[]{:S(2)}, u32[]{:S(2)}) collective-permute-start(bf16[512,768]{1,0:T(8,128)(2,1)S(1)} %get-tuple-element.272), channel_id=1, source_target_pairs={{0,4},{4,0},{1,5},{5,1},{2,6},{6,2},{3,7},{7,3},{8,12},{12,8},{9,1... | collective-permute-start | bytes 2359304 | tf_op jit(solution)/shard_map/ppermute | solution.py:942
  220.5 4.7 %collective-permute-start.29 = (f32[16,768]{1,0:T(8,128)S(1)}, f32[16,768]{1,0:T(8,128)S(1)}, u32[]{:S(2)}, u32[]{:S(2)}) collective-permute-start(f32[16,768]{1,0:T(8,128)S(1)} %collect.1), channel_id=1, source_target_pairs={{0,4},{4,0},{1,5},{5,1},{2,6},{6,2},{3,7},{7,3},{8,12},{12,8},{9,1... | collective-permute-start | bytes 147464 | tf_op jit(solution)/shard_map/ppermute | solution.py:942
  225.1 7.7 %collective-permute-start.24 = (bf16[4,96,576]{2,1,0:T(8,128)(2,1)S(1)}, bf16[4,96,576]{2,1,0:T(8,128)(2,1)S(1)}, u32[]{:S(2)}, u32[]{:S(2)}) collective-permute-start(bf16[4,96,576]{2,1,0:T(8,128)(2,1)S(1)} %get-tuple-element.256), channel_id=1, source_target_pairs={{0,4},{4,0},{1,5},{5,1},{2,6},{6,2},{3,7},{7,3},{8,12},{12,8},{9,1... | collective-permute-start | bytes 1327112 | tf_op jit(solution)/shard_map/ppermute | solution.py:942
  225.2 3.9 %collective-permute-start.30 = (f32[16,768]{1,0:T(8,128)S(1)}, f32[16,768]{1,0:T(8,128)S(1)}, u32[]{:S(2)}, u32[]{:S(2)}) collective-permute-start(f32[16,768]{1,0:T(8,128)S(1)} %add.168), channel_id=1, source_target_pairs={{0,8},{8,0},{16,24},{24,16},{1,9},{9,1},{17,25},{25,17},{2,10},{10... | collective-permute-start | bytes 147464 | tf_op jit(solution)/shard_map/ppermute | solution.py:950
  226.7 12.4 %collective-permute-start.25 = (bf16[256,768]{1,0:T(8,128)(2,1)S(1)}, bf16[256,768]{1,0:T(8,128)(2,1)S(1)}, u32[]{:S(2)}, u32[]{:S(2)}) collective-permute-start(bf16[256,768]{1,0:T(8,128)(2,1)S(1)} %get-tuple-element.360), channel_id=1, source_target_pairs={{0,2},{1,3},{2,0},{3,1},{4,6},{5,7},{6,4},{7,5},{8,10},{9,11},{10,... | collective-permute-start | bytes 1179656 | tf_op jit(solution)/shard_map/ppermute | solution.py:946
  229.2 9.9 %collective-permute-start.26 = (bf16[256,768]{1,0:T(8,128)(2,1)S(1)}, bf16[256,768]{1,0:T(8,128)(2,1)S(1)}, u32[]{:S(2)}, u32[]{:S(2)}) collective-permute-start(bf16[256,768]{1,0:T(8,128)(2,1)S(1)} %get-tuple-element.359), channel_id=1, source_target_pairs={{0,1},{1,0},{2,3},{3,2},{4,5},{5,4},{6,7},{7,6},{8,9},{9,8},{10,11... | collective-permute-start | bytes 1179656 | tf_op jit(solution)/shard_map/ppermute | solution.py:946
  239.2 21.4 %collective-permute-start.31 = (bf16[512,768]{1,0:T(8,128)(2,1)S(1)}, bf16[512,768]{1,0:T(8,128)(2,1)S(1)}, u32[]{:S(2)}, u32[]{:S(2)}) collective-permute-start(bf16[512,768]{1,0:T(8,128)(2,1)S(1)} %get-tuple-element.286), channel_id=1, source_target_pairs={{0,1},{1,0},{2,3},{3,2},{4,5},{5,4},{6,7},{7,6},{8,9},{9,8},{10,11... | collective-permute-start | bytes 2359304 | tf_op jit(solution)/shard_map/ppermute | solution.py:946
  240.5 22.8 %collective-permute-start.32 = (bf16[512,768]{1,0:T(8,128)(2,1)S(1)}, bf16[512,768]{1,0:T(8,128)(2,1)S(1)}, u32[]{:S(2)}, u32[]{:S(2)}) collective-permute-start(bf16[512,768]{1,0:T(8,128)(2,1)S(1)} %get-tuple-element.287), channel_id=1, source_target_pairs={{0,2},{1,3},{2,0},{3,1},{4,6},{5,7},{6,4},{7,5},{8,10},{9,11},{10,... | collective-permute-start | bytes 2359304 | tf_op jit(solution)/shard_map/ppermute | solution.py:946
  241.5 4.0 %collective-permute-start.33 = (bf16[96,576]{1,0:T(8,128)(2,1)S(1)}, bf16[96,576]{1,0:T(8,128)(2,1)S(1)}, u32[]{:S(2)}, u32[]{:S(2)}) collective-permute-start(bf16[96,576]{1,0:T(8,128)(2,1)S(1)} %get-tuple-element.289), channel_id=1, source_target_pairs={{0,8},{8,0},{16,24},{24,16},{1,9},{9,1},{17,25},{25,17},{2,10},{10... | collective-permute-start | bytes 331784 | tf_op jit(solution)/shard_map/ppermute | solution.py:950
  242.1 10.1 %collective-permute-start.35 = (bf16[96,576]{1,0:T(8,128)(2,1)S(1)}, bf16[96,576]{1,0:T(8,128)(2,1)S(1)}, u32[]{:S(2)}, u32[]{:S(2)}) collective-permute-start(bf16[96,576]{1,0:T(8,128)(2,1)S(1)} %get-tuple-element.304), channel_id=1, source_target_pairs={{0,16},{8,24},{16,0},{24,8},{1,17},{9,25},{17,1},{25,9},{2,18},{10... | collective-permute-start | bytes 331784 | tf_op jit(solution)/shard_map/ppermute | solution.py:950
  245.4 6.9 %collective-permute-start.36 = (bf16[96,576]{1,0:T(8,128)(2,1)S(1)}, bf16[96,576]{1,0:T(8,128)(2,1)S(1)}, u32[]{:S(2)}, u32[]{:S(2)}) collective-permute-start(bf16[96,576]{1,0:T(8,128)(2,1)S(1)} %get-tuple-element.305), channel_id=1, source_target_pairs={{0,24},{8,16},{16,8},{24,0},{1,25},{9,17},{17,9},{25,1},{2,26},{10... | collective-permute-start | bytes 331784 | tf_op jit(solution)/shard_map/ppermute | solution.py:950
  245.6 15.1 %collective-permute-start.34 = (f32[16,768]{1,0:T(8,128)S(1)}, f32[16,768]{1,0:T(8,128)S(1)}, u32[]{:S(2)}, u32[]{:S(2)}) collective-permute-start(f32[16,768]{1,0:T(8,128)S(1)} %add.169), channel_id=1, source_target_pairs={{0,1},{1,0},{2,3},{3,2},{4,5},{5,4},{6,7},{7,6},{8,9},{9,8},{10,11... | collective-permute-start | bytes 147464 | tf_op jit(solution)/shard_map/ppermute | solution.py:946
  249.0 14.3 %copy-start.16 = (f32[512,768]{1,0:T(8,128)S(1)}, f32[512,768]{1,0:T(8,128)}, u32[]{:S(2)}) copy-start(f32[512,768]{1,0:T(8,128)} %get-tuple-element.308.first) | copy-start | bytes 4718596
  263.6 17.7 %collective-permute-start.38 = (bf16[512,768]{1,0:T(8,128)(2,1)S(1)}, bf16[512,768]{1,0:T(8,128)(2,1)S(1)}, u32[]{:S(2)}, u32[]{:S(2)}) collective-permute-start(bf16[512,768]{1,0:T(8,128)(2,1)S(1)} %add_block.1.near.refs_0_), channel_id=1, source_target_pairs={{0,2},{1,3},{2,0},{3,1},{4,6},{5,7},{6,4},{7,5},{8,10},{9,11},{10,... | collective-permute-start | bytes 2359304 | tf_op jit(solution)/shard_map/ppermute | solution.py:946
  264.3 17.1 %collective-permute-start.37 = (bf16[512,768]{1,0:T(8,128)(2,1)S(1)}, bf16[512,768]{1,0:T(8,128)(2,1)S(1)}, u32[]{:S(2)}, u32[]{:S(2)}) collective-permute-start(bf16[512,768]{1,0:T(8,128)(2,1)S(1)} %add_block.1.near.refs_0_), channel_id=1, source_target_pairs={{0,1},{1,0},{2,3},{3,2},{4,5},{5,4},{6,7},{7,6},{8,9},{9,8},{10,11... | collective-permute-start | bytes 2359304 | tf_op jit(solution)/shard_map/ppermute | solution.py:946
  264.3 9.5 %collective-permute-start.39 = (bf16[96,768]{1,0:T(8,128)(2,1)S(1)}, bf16[96,768]{1,0:T(8,128)(2,1)S(1)}, u32[]{:S(2)}, u32[]{:S(2)}) collective-permute-start(bf16[96,768]{1,0:T(8,128)(2,1)S(1)} %get-tuple-element.312), channel_id=1, source_target_pairs={{0,8},{8,0},{16,24},{24,16},{1,9},{9,1},{17,25},{25,17},{2,10},{10... | collective-permute-start | bytes 442376 | tf_op jit(solution)/shard_map/ppermute | solution.py:950
  264.6 9.3 %collective-permute-start.40 = (bf16[96,768]{1,0:T(8,128)(2,1)S(1)}, bf16[96,768]{1,0:T(8,128)(2,1)S(1)}, u32[]{:S(2)}, u32[]{:S(2)}) collective-permute-start(bf16[96,768]{1,0:T(8,128)(2,1)S(1)} %get-tuple-element.315), channel_id=1, source_target_pairs={{0,16},{8,24},{16,0},{24,8},{1,17},{9,25},{17,1},{25,9},{2,18},{10... | collective-permute-start | bytes 442376 | tf_op jit(solution)/shard_map/ppermute | solution.py:950
  268.9 10.3 %collective-permute-start.41 = (bf16[96,768]{1,0:T(8,128)(2,1)S(1)}, bf16[96,768]{1,0:T(8,128)(2,1)S(1)}, u32[]{:S(2)}, u32[]{:S(2)}) collective-permute-start(bf16[96,768]{1,0:T(8,128)(2,1)S(1)} %get-tuple-element.316), channel_id=1, source_target_pairs={{0,24},{8,16},{16,8},{24,0},{1,25},{9,17},{17,9},{25,1},{2,26},{10... | collective-permute-start | bytes 442376 | tf_op jit(solution)/shard_map/ppermute | solution.py:950
  273.8 7.5 %collective-permute-start.42 = (f32[16,768]{1,0:T(8,128)S(1)}, f32[16,768]{1,0:T(8,128)S(1)}, u32[]{:S(2)}, u32[]{:S(2)}) collective-permute-start(f32[16,768]{1,0:T(8,128)S(1)} %add.170), channel_id=1, source_target_pairs={{0,2},{1,3},{2,0},{3,1},{4,6},{5,7},{6,4},{7,5},{8,10},{9,11},{10,... | collective-permute-start | bytes 147464 | tf_op jit(solution)/shard_map/ppermute | solution.py:946
  282.9 6.7 %collective-permute-start.45 = (bf16[512,768]{1,0:T(8,128)(2,1)S(1)}, bf16[512,768]{1,0:T(8,128)(2,1)S(1)}, u32[]{:S(2)}, u32[]{:S(2)}) collective-permute-start(bf16[512,768]{1,0:T(8,128)(2,1)S(1)} %get-tuple-element.322), channel_id=1, source_target_pairs={{0,4},{4,0},{1,5},{5,1},{2,6},{6,2},{3,7},{7,3},{8,12},{12,8},{9,1... | collective-permute-start | bytes 2359304 | tf_op jit(solution)/shard_map/ppermute | solution.py:942
  287.7 10.8 %collective-permute-start.44 = (bf16[256,768]{1,0:T(8,128)(2,1)S(1)}, bf16[256,768]{1,0:T(8,128)(2,1)S(1)}, u32[]{:S(2)}, u32[]{:S(2)}) collective-permute-start(bf16[256,768]{1,0:T(8,128)(2,1)S(1)} %slice.86), channel_id=1, source_target_pairs={{0,1},{1,0},{2,3},{3,2},{4,5},{5,4},{6,7},{7,6},{8,9},{9,8},{10,11... | collective-permute-start | bytes 1179656 | tf_op jit(solution)/shard_map/ppermute | solution.py:946
  287.8 10.8 %collective-permute-start.43 = (bf16[256,768]{1,0:T(8,128)(2,1)S(1)}, bf16[256,768]{1,0:T(8,128)(2,1)S(1)}, u32[]{:S(2)}, u32[]{:S(2)}) collective-permute-start(bf16[256,768]{1,0:T(8,128)(2,1)S(1)} %slice.85), channel_id=1, source_target_pairs={{0,2},{1,3},{2,0},{3,1},{4,6},{5,7},{6,4},{7,5},{8,10},{9,11},{10,... | collective-permute-start | bytes 1179656 | tf_op jit(solution)/shard_map/ppermute | solution.py:946
  291.3 4.0 %collective-permute-start.46 = (f32[16,768]{1,0:T(8,128)S(1)}, f32[16,768]{1,0:T(8,128)S(1)}, u32[]{:S(2)}, u32[]{:S(2)}) collective-permute-start(f32[16,768]{1,0:T(8,128)S(1)} %add.171), channel_id=1, source_target_pairs={{0,16},{8,24},{16,0},{24,8},{1,17},{9,25},{17,1},{25,9},{2,18},{10... | collective-permute-start | bytes 147464 | tf_op jit(solution)/shard_map/ppermute | solution.py:950
  299.7 4.0 %collective-permute-start.47 = (bf16[512,768]{1,0:T(8,128)(2,1)}, bf16[512,768]{1,0:T(8,128)(2,1)S(1)}, u32[]{:S(2)}, u32[]{:S(2)}) collective-permute-start(bf16[512,768]{1,0:T(8,128)(2,1)} %maximum_select_fusion), channel_id=1, source_target_pairs={{0,4},{4,0},{1,5},{5,1},{2,6},{6,2},{3,7},{7,3},{8,12},{12,8},{9,1... | collective-permute-start | bytes 2359304 | tf_op jit(solution)/shard_map/ppermute | solution.py:942
  (33 other events, 176.6 us)
Sparse Core Ops, SparseCore 0:
  11.6 101.4 all-gather.1
  167.6 123.7 reduce-scatter.1

commit v9 on v8

--- a/solution.py
+++ b/solution.py
@@ -1125,6 +1125,7 @@
     outputs = join(place, out_blocks[1], corner, outs[1], outputs)
     if direct:
         moved, small = send_shards(qkv_pieces, small, 1)
+        small = small + swap_shard(small, 2)
         qkv_total = finish(3, qkv_sum, *moved)
         summed, *pieces = settle(packs[0], *sent)
         one, two, own, small, outputs, summed, pieces, qkv_total = barrier((one, two, own, small, outputs, summed, pieces, qkv_total))
@@ -1146,7 +1147,6 @@
     grad_ffn_weight, grad_out_weight = place_feed(whole, total)
     if direct:
         small, grad_tokens = barrier((small, grad_tokens))
-        small = small + swap_shard(small, 2)
     else:
         small = lax.psum(small, ("shard", "ctx", "tp"))
     corner, small, grad_tokens, qkv_total = barrier((corner, small, grad_tokens, qkv_total))

time: 316 us -> 324 us (1.025)
  waiting for transfers between devices: 65 us -> 92.2 us
  Pallas kernels: 138 us -> 122 us
    ppermute x26, waiting for transfers between devices: 27 us -> 52.5 us  [swap_tp(): return lax.ppermute(x, 'tp', [(i, i ^ k) for i in range(4)])]
    pallas_call x4, Pallas kernels: 28.7 us -> 20.5 us  [attention_forward(): pl.pallas_call(partial(forward_kernel, heads), grid_spec=pltpu.PrefetchSc...]
    pallas_call x1, Pallas kernels: 27.7 us -> 20.6 us  [attention_backward(): pl.pallas_call(partial(backward_kernel, heads), grid_spec=pltpu.PrefetchS...]
    unnamed x102 -> x100, local copies, waits for them, and re-layouts: 14.6 us -> 14.6 us
  transfers between devices with their start and end apart: 50 -> 50, of which waited for: 20 -> 19; matrix products, arithmetic and copies ran while one was open for 10% -> 10% of each run, Pallas kernels for 37% -> 31%
where the time goes in v9:
time: 324 us; the launch traced here: 323 us
  Pallas kernels  122 us (38%)
  waiting for transfers between devices  92.2 us (28%)
  starting transfers between devices  49.4 us (15%)
  local copies, waits for them, and re-layouts  25.9 us (8%)
  other arithmetic  18.2 us (6%)
  between operations  14.8 us (5%)
    ppermute x26, waiting for transfers between devices, swap_tp(): return lax.ppermute(x, 'tp', [(i, i ^ k) for i in range(4)])  52.5 us
    ppermute x26, starting transfers between devices, swap_tp(): return lax.ppermute(x, 'tp', [(i, i ^ k) for i in range(4)])  23.9 us
    ppermute x11, waiting for transfers between devices, swap_shard(): return lax.ppermute(x, 'shard', [(i, i ^ k) for i in range(4)])  21.6 us
    pallas_call x1, Pallas kernels, feed_forward(): pl.pallas_call(feed_kernel, grid_spec=pltpu.PrefetchScalarGridSpec(num_sc...  21 us
    pallas_call x1, Pallas kernels, attention_backward(): pl.pallas_call(partial(backward_kernel, heads), grid_spec=pltpu.PrefetchS...  20.6 us
    pallas_call x4, Pallas kernels, attention_forward(): pl.pallas_call(partial(forward_kernel, heads), grid_spec=pltpu.PrefetchSc...  20.5 us
    all_gather x1, waiting for transfers between devices, body(): lax.all_gather(gathered, ('tp', 'shard', 'ctx'), axis=0, tiled=True)  15.7 us
    pallas_call x1, Pallas kernels, feed_back(): pl.pallas_call(feed_back_kernel, grid_spec=pltpu.PrefetchScalarGridSpec(n...  15.3 us
  transfers between devices with their start and end apart: 50, of which 19 were waited for; matrix products, arithmetic and copies ran while one was open for 10% of the time, Pallas kernels for 31%

profile of v9, /device:TPU:1, one launch (start us, length us, event | category | flops | bytes accessed | tf_op | source)
XLA Modules:
  0.0 322.6 jit_solution(12547259871604134046)
XLA Ops:
  8.4 1.6 pad_maximum_fusion.3
  10.7 3.0 collective-permute-start.12
  14.0 1.7 copy.29
  16.8 3.6 %collective-permute-start.4 = (bf16[96,576]{1,0:T(8,128)(2,1)S(1)}, bf16[96,576]{1,0:T(8,128)(2,1)S(1)}, u32[]{:S(2)}, u32[]{:S(2)}) collective-permute-start(bf16[96,576]{1,0:T(8,128)(2,1)S(1)} %copy.35.refs_0_), channel_id=1, source_target_pairs={{0,24},{8,16},{16,8},{24,0},{1,25},{9,17},{17,9},{25,1},{2,26},{10... | collective-permute-start | bytes 331784 | tf_op jit(solution)/shard_map/ppermute | solution.py:950
  21.3 2.1 dynamic-slice_bitcast_fusion.1
  23.4 1.2 dynamic-slice_bitcast_fusion
  26.9 2.1 collective-permute-start.1
  29.1 1.3 pad_maximum_fusion.5.bias
  32.0 3.1 collective-permute-done.3.refs_2_
  35.1 4.4 %collective-permute-done.2.refs_1_ = bf16[96,576]{1,0:T(8,128)(2,1)S(1)} collective-permute-done((bf16[96,576]{1,0:T(8,128)(2,1)S(1)}, bf16[96,576]{1,0:T(8,128)(2,1)S(1)}, u32[]{:S(2)}, u32[]{:S(2)}) %collective-permute-start.2) | collective-permute-done | bytes 110624 | tf_op jit(solution)/shard_map/ppermute | solution.py:950
  40.5 3.7 %fusion = (f32[2048,128]{1,0:T(8,128)S(1)}, f32[2048,128]{1,0:T(8,128)S(1)}) fusion(f32[128]{0:T(128)S(1)} %copy-done.45, f32[128]{0:T(128)S(1)} %copy-done.44, f32[2048]{0:T(1024)S(1)} %bitcast.124), kind=kLoop, calls=%fused_computation.8 | loop fusion | flops 524288 | bytes 2106368 | tf_op jit(solution)/shard_map/mul | solution.py:928
  45.5 1.9 copy-done.3
  47.4 1.4 copy-done.6
  49.7 5.7 %project_qkv.1 = (bf16[2048,256]{1,0:T(8,128)(2,1)S(1)}, bf16[2048,256]{1,0:T(8,128)(2,1)S(1)}, bf16[2048,256]{1,0:T(8,128)(2,1)S(1)}, bf16[256,2048]{1,0:T(8,12...) custom-call(s32[10]{0:T(128)S(1)} %stack.96.place, bf16[96,576]{1,0:T(8,128)(2,1)S(1)} %copy.35.refs_0_, ...), custom_call_target="tpu_custom_call" | custom-call | tf_op jit(solution)/shard_map/project_qkv/pallas_call | solution.py:95
  57.4 5.1 %attention_forward.4 = (bf16[512,192]{1,0:T(8,128)(2,1)S(1)}, f32[8,512]{1,0:T(8,128)S(1)}, f32[512,256]{1,0:T(8,128)S(1)}) custom-call(s32[17]{0:T(128)S(1)} %get-tuple-element.372.place, bf16[2048,256]{1,0:T(8,128)(2,1)S(1)} %get-tuple-element.184.q, bf16[2048,256]{1,0:T(8,128)(2,1)S(1)} %get-tuple-element.174.k, ...), custom_call_target="tpu_custom_call" | custom-call | tf_op jit(solution)/shard_map/attention_forward/pallas_call | solution.py:180
  62.6 2.2 collective-permute-start.6
  64.8 5.1 %attention_forward.5 = (bf16[512,192]{1,0:T(8,128)(2,1)S(1)}, f32[8,512]{1,0:T(8,128)S(1)}, f32[512,256]{1,0:T(8,128)S(1)}) custom-call(s32[17]{0:T(128)S(1)} %get-tuple-element.374.place, bf16[2048,256]{1,0:T(8,128)(2,1)S(1)} %get-tuple-element.184.q, bf16[2048,256]{1,0:T(8,128)(2,1)S(1)} %get-tuple-element.174.k, ...), custom_call_target="tpu_custom_call" | custom-call | tf_op jit(solution)/shard_map/attention_forward/pallas_call | solution.py:180
  70.3 2.4 bitcast_select_fusion.gtop
  73.6 5.1 %attention_forward.6 = (bf16[512,192]{1,0:T(8,128)(2,1)S(1)}, f32[8,512]{1,0:T(8,128)S(1)}, f32[512,256]{1,0:T(8,128)S(1)}) custom-call(s32[17]{0:T(128)S(1)} %get-tuple-element.373.place, bf16[2048,256]{1,0:T(8,128)(2,1)S(1)} %get-tuple-element.184.q, bf16[2048,256]{1,0:T(8,128)(2,1)S(1)} %get-tuple-element.174.k, ...), custom_call_target="tpu_custom_call" | custom-call | tf_op jit(solution)/shard_map/attention_forward/pallas_call | solution.py:180
  78.7 5.0 %collective-permute-done.7.c1 = bf16[512,192]{1,0:T(8,128)(2,1)S(1)} collective-permute-done((bf16[512,192]{1,0:T(8,128)(2,1)S(1)}, bf16[512,192]{1,0:T(8,128)(2,1)S(1)}, u32[]{:S(2)}, u32[]{:S(2)}) %collective-permute-start.7) | collective-permute-done | bytes 196640 | tf_op jit(solution)/shard_map/ppermute | solution.py:946
  83.8 5.2 %attention_forward.7 = (bf16[512,192]{1,0:T(8,128)(2,1)S(1)}, f32[8,512]{1,0:T(8,128)S(1)}, f32[512,256]{1,0:T(8,128)S(1)}) custom-call(s32[17]{0:T(128)S(1)} %get-tuple-element.375.place, bf16[2048,256]{1,0:T(8,128)(2,1)S(1)} %get-tuple-element.184.q, bf16[2048,256]{1,0:T(8,128)(2,1)S(1)} %get-tuple-element.174.k, ...), custom_call_target="tpu_custom_call" | custom-call | tf_op jit(solution)/shard_map/attention_forward/pallas_call | solution.py:180
  88.9 1.5 pad_maximum_fusion.full
  90.4 4.5 %collective-permute-done.8.c2 = bf16[512,192]{1,0:T(8,128)(2,1)S(1)} collective-permute-done((bf16[512,192]{1,0:T(8,128)(2,1)S(1)}, bf16[512,192]{1,0:T(8,128)(2,1)S(1)}, u32[]{:S(2)}, u32[]{:S(2)}) %collective-permute-start.8) | collective-permute-done | bytes 196640 | tf_op jit(solution)/shard_map/ppermute | solution.py:946
  95.7 1.3 pad_maximum_fusion.1.ctx
  96.9 15.7 %all-gather.2.cloned.1.call-done = bf16[3072,1728]{1,0:T(8,128)(2,1)} async-done(((bf16[96,1728]{1,0:T(8,128)(2,1)}), bf16[3072,1728]{1,0:T(8,128)(2,1)}) %all-gather.2.cloned.1.call-update) | async-done | bytes 10616848 | tf_op jit(solution)/shard_map/all_gather | solution.py:1011
  112.6 21.0 %feed_forward.1 = (bf16[512,768]{1,0:T(8,128)(2,1)}, f32[512,768]{1,0:T(8,128)}, bf16[512,768]{1,0:T(8,128)(2,1)}, f32[512,768]{1,0:T(8,128)}, bf16[768,512]{1,0...) custom-call(s32[10]{0:T(128)} %copy-done.32, ...), custom_call_target="tpu_custom_call" | custom-call | tf_op jit(solution)/shard_map/feed_forward/pallas_call | solution.py:440
  134.6 1.4 collective-permute-start.16
  136.0 15.3 %feed_back.1 = (f32[512,768]{1,0:T(8,128)}, bf16[768,512]{1,0:T(8,128)(2,1)}, bf16[512,192]{1,0:T(8,128)(2,1)}, bf16[512,192]{1,0:T(8,128)(2,1)}, bf16[512,192]{...) custom-call(s32[10]{0:T(128)} %copy-done.32, ...), custom_call_target="tpu_custom_call" | custom-call | tf_op jit(solution)/shard_map/feed_back/pallas_call | solution.py:524
  152.0 2.0 collective-permute-start.15
  154.0 12.1 %weight_grads.1 = (bf16[4,4,96,768]{3,2,1,0:T(8,128)(2,1)}, bf16[4,4,96,768]{3,2,1,0:T(8,128)(2,1)}, bf16[4,768,960]{2,1,0:T(8,128)(2,1)}) custom-call(s32[10]{0:T(128)} %copy-done.32, bf16[768,512]{1,0:T(8,128)(2,1)} %get-tuple-element.198.nbt, bf16[768,512]{1,0:T(8,128)(2,1)} %get-tuple-element.199.gst, bf16[768,512]{1,0:T(8,128)(2,1)} %get-tuple-element.205.gft, ...), custom_call_target="tpu_custom_call" | custom-call | tf_op jit(solution)/shard_map/weight_grads/pallas_call | solution.py:592
  167.7 1.7 collective-permute-start.18
  171.6 2.1 collective-permute-done.18
  173.8 2.4 add_bitcast_fusion
  176.8 2.1 collective-permute-start.21
  179.5 20.6 %attention_backward.1 = (bf16[2048,768]{1,0:T(8,128)(2,1)S(1)}, f32[8,768]{1,0:T(8,128)S(1)}) custom-call(s32[17]{0:T(128)S(1)} %get-tuple-element.375.place, bf16[2048,256]{1,0:T(8,128)(2,1)S(1)} %get-tuple-element.184.q, bf16[256,2048]{1,0:T(8,128)(2,1)S(1)} %copy-done.21, bf16[2048,256]{1,0:T(8,128)(2,1)S(1)} %get-tuple-element.174.k, ...), custom_call_target="tpu_custom_call" | custom-call | tf_op jit(solution)/shard_map/attention_backward/pallas_call | solution.py:313
  200.2 2.7 collective-permute-done.21.refs_3_
  202.9 1.3 branch.2
  204.3 7.5 %collective-permute-done.22.refs_0_.refs_1_ = bf16[256,768]{1,0:T(8,128)(2,1)S(1)} collective-permute-done((bf16[256,768]{1,0:T(8,128)(2,1)S(1)}, bf16[256,768]{1,0:T(8,128)(2,1)S(1)}, u32[]{:S(2)}, u32[]{:S(2)}) %collective-permute-start.22) | collective-permute-done | bytes 393248 | tf_op jit(solution)/shard_map/ppermute | solution.py:946
  212.1 2.7 pick.3
  214.8 1.2 collective-permute-start.27
  216.0 2.7 pick.4
  219.8 4.0 %qkv_weight_grads.1 = (f32[4,96,576]{2,1,0:T(8,128)S(1)}, bf16[4,96,576]{2,1,0:T(8,128)(2,1)S(1)}) custom-call(s32[10]{0:T(128)S(1)} %copy-done.33, bf16[2,1024,768]{2,1,0:T(8,128)(2,1)S(1)} %copy-done.4, bf16[1024,768]{1,0:T(8,128)(2,1)S(1)} %copy-done.7, bf16[2048,768]{1,0:T(8,128)(2,1)S(1)} %get-tuple-element.254.refs_0_.g.refs_1_.refs_2_), custom_call_target="tpu_custom_call" | custom-call | tf_op jit(solution)/shard_map/qkv_weight_grads/pallas_call | solution.py:636
  225.2 1.5 collective-permute-start.25
  226.7 1.6 collective-permute-done.30
  228.3 1.6 collective-permute-start.26
  229.9 2.6 branch.3
  232.6 6.9 %collective-permute-done.25.low = bf16[256,768]{1,0:T(8,128)(2,1)S(1)} collective-permute-done((bf16[256,768]{1,0:T(8,128)(2,1)S(1)}, bf16[256,768]{1,0:T(8,128)(2,1)S(1)}, u32[]{:S(2)}, u32[]{:S(2)}) %collective-permute-start.25) | collective-permute-done | bytes 393248 | tf_op jit(solution)/shard_map/ppermute | solution.py:946
  239.7 1.3 collective-permute-start.31
  242.3 2.2 collective-permute-start.36
  244.7 4.6 %collective-permute-done.33.refs_1_ = bf16[96,576]{1,0:T(8,128)(2,1)S(1)} collective-permute-done((bf16[96,576]{1,0:T(8,128)(2,1)S(1)}, bf16[96,576]{1,0:T(8,128)(2,1)S(1)}, u32[]{:S(2)}, u32[]{:S(2)}) %collective-permute-start.33) | collective-permute-done | bytes 110624 | tf_op jit(solution)/shard_map/ppermute | solution.py:950
  250.1 11.9 %collective-permute-done.34 = f32[16,768]{1,0:T(8,128)S(1)} collective-permute-done((f32[16,768]{1,0:T(8,128)S(1)}, f32[16,768]{1,0:T(8,128)S(1)}, u32[]{:S(2)}, u32[]{:S(2)}) %collective-permute-start.34) | collective-permute-done | bytes 49184 | tf_op jit(solution)/shard_map/ppermute | solution.py:946
  262.1 2.2 collective-permute-start.35
  264.5 2.9 join.4.refs_4_
  267.4 2.9 join.5
  272.4 1.2 collective-permute-start.40
  273.6 2.3 collective-permute-start.42
  277.9 7.2 %collective-permute-done.41.refs_2_ = bf16[96,768]{1,0:T(8,128)(2,1)S(1)} collective-permute-done((bf16[96,768]{1,0:T(8,128)(2,1)S(1)}, bf16[96,768]{1,0:T(8,128)(2,1)S(1)}, u32[]{:S(2)}, u32[]{:S(2)}) %collective-permute-start.41) | collective-permute-done | bytes 147488 | tf_op jit(solution)/shard_map/ppermute | solution.py:950
  285.2 5.5 %collective-permute-done.43 = f32[16,768]{1,0:T(8,128)S(1)} collective-permute-done((f32[16,768]{1,0:T(8,128)S(1)}, f32[16,768]{1,0:T(8,128)S(1)}, u32[]{:S(2)}, u32[]{:S(2)}) %collective-permute-start.43) | collective-permute-done | bytes 49184 | tf_op jit(solution)/shard_map/ppermute | solution.py:946
  290.7 1.5 pick.5
  292.2 2.7 collective-permute-start.46
  295.0 1.2 collective-permute-start.45
  296.8 1.8 join.6.refs_4_
  298.6 7.2 %collective-permute-done.45.refs_2_ = bf16[256,768]{1,0:T(8,128)(2,1)S(1)} collective-permute-done((bf16[256,768]{1,0:T(8,128)(2,1)S(1)}, bf16[256,768]{1,0:T(8,128)(2,1)S(1)}, u32[]{:S(2)}, u32[]{:S(2)}) %collective-permute-start.45) | collective-permute-done | bytes 393248 | tf_op jit(solution)/shard_map/ppermute | solution.py:946
  312.1 1.8 join.7
  (214 shorter events, 40.2 us)
Async XLA Ops:
  7.2 13.2 %copy-start.41 = (s32[2,1024]{1,0:T(2,128)S(1)}, s32[2,1024]{1,0:T(2,128)}, u32[]{:S(2)}) copy-start(s32[2,1024]{1,0:T(2,128)} %param.15) | copy-start | bytes 24580
  7.2 16.2 %copy-start.2 = (bf16[2,1024,768]{2,1,0:T(8,128)(2,1)S(1)}, bf16[2,1024,768]{2,1,0:T(8,128)(2,1)}, u32[]{:S(2)}) copy-start(bf16[2,1024,768]{2,1,0:T(8,128)(2,1)} %own.1) | copy-start | bytes 9437188
  7.2 105.4 %all-gather.2.cloned.1.call-start = ((), (), s32[]{:S(2)}) async-start(), calls=%async_computation.1 | async-start | bytes 11354112 | tf_op jit(solution)/shard_map/all_gather | solution.py:1011
  10.0 303.9 %reduce-scatter.2.cloned.1.call-start = ((), (), s32[]{:S(2)}) async-start(), calls=%async_computation.2 | async-start | bytes 6488064 | tf_op jit(solution)/shard_map/reduce_scatter | solution.py:1077
  10.7 15.8 %collective-permute-start.12 = (f32[1,768]{1,0:T(1,128)S(1)}, f32[1,768]{1,0:T(1,128)}, u32[]{:S(2)}, u32[]{:S(2)}) collective-permute-start(f32[1,768]{1,0:T(1,128)S(1)} %reshape.214), channel_id=1, source_target_pairs={{0,3},{1,2},{2,1},{3,0},{4,7},{5,6},{6,5},{7,4},{8,11},{9,10},{10,... | collective-permute-start | bytes 9224 | tf_op jit(solution)/shard_map/ppermute | solution.py:946
  13.7 13.2 %collective-permute-start.11 = (f32[1,768]{1,0:T(1,128)S(1)}, f32[1,768]{1,0:T(1,128)}, u32[]{:S(2)}, u32[]{:S(2)}) collective-permute-start(f32[1,768]{1,0:T(1,128)S(1)} %reshape.214), channel_id=1, source_target_pairs={{0,2},{1,3},{2,0},{3,1},{4,6},{5,7},{6,4},{7,5},{8,10},{9,11},{10,... | collective-permute-start | bytes 9224 | tf_op jit(solution)/shard_map/ppermute | solution.py:946
  13.9 15.1 %collective-permute-start.10 = (f32[1,768]{1,0:T(1,128)S(1)}, f32[1,768]{1,0:T(1,128)}, u32[]{:S(2)}, u32[]{:S(2)}) collective-permute-start(f32[1,768]{1,0:T(1,128)S(1)} %reshape.214), channel_id=1, source_target_pairs={{0,1},{1,0},{2,3},{3,2},{4,5},{5,4},{6,7},{7,6},{8,9},{9,8},{10,11... | collective-permute-start | bytes 9224 | tf_op jit(solution)/shard_map/ppermute | solution.py:946
  16.8 15.3 %collective-permute-start.4 = (bf16[96,576]{1,0:T(8,128)(2,1)S(1)}, bf16[96,576]{1,0:T(8,128)(2,1)S(1)}, u32[]{:S(2)}, u32[]{:S(2)}) collective-permute-start(bf16[96,576]{1,0:T(8,128)(2,1)S(1)} %copy.35.refs_0_), channel_id=1, source_target_pairs={{0,24},{8,16},{16,8},{24,0},{1,25},{9,17},{17,9},{25,1},{2,26},{10... | collective-permute-start | bytes 331784 | tf_op jit(solution)/shard_map/ppermute | solution.py:950
  20.3 14.7 %collective-permute-start.3 = (bf16[96,576]{1,0:T(8,128)(2,1)S(1)}, bf16[96,576]{1,0:T(8,128)(2,1)S(1)}, u32[]{:S(2)}, u32[]{:S(2)}) collective-permute-start(bf16[96,576]{1,0:T(8,128)(2,1)S(1)} %copy.35.refs_0_), channel_id=1, source_target_pairs={{0,16},{8,24},{16,0},{24,8},{1,17},{9,25},{17,1},{25,9},{2,18},{10... | collective-permute-start | bytes 331784 | tf_op jit(solution)/shard_map/ppermute | solution.py:950
  24.6 15.9 %copy-start.44 = (f32[128]{0:T(128)S(1)}, f32[128]{0:T(128)}, u32[]{:S(2)}) copy-start(f32[128]{0:T(128)} %constant.195) | copy-start | bytes 1540
  24.6 15.9 %copy-start.45 = (f32[128]{0:T(128)S(1)}, f32[128]{0:T(128)}, u32[]{:S(2)}) copy-start(f32[128]{0:T(128)} %constant.188.clone) | copy-start | bytes 1540
  26.5 19.0 %copy-start.32 = (s32[10]{0:T(128)}, s32[10]{0:T(128)S(1)}, u32[]{:S(2)}) copy-start(s32[10]{0:T(128)S(1)} %stack.96.place) | copy-start | bytes 124
  26.5 13.0 %collective-permute-start.2 = (bf16[96,576]{1,0:T(8,128)(2,1)S(1)}, bf16[96,576]{1,0:T(8,128)(2,1)S(1)}, u32[]{:S(2)}, u32[]{:S(2)}) collective-permute-start(bf16[96,576]{1,0:T(8,128)(2,1)S(1)} %copy.35.refs_0_), channel_id=1, source_target_pairs={{0,8},{8,0},{16,24},{24,16},{1,9},{9,1},{17,25},{25,17},{2,10},{10... | collective-permute-start | bytes 331784 | tf_op jit(solution)/shard_map/ppermute | solution.py:950
  26.9 3.5 %collective-permute-start.1 = (s32[2,1024]{1,0:T(2,128)S(1)}, s32[2,1024]{1,0:T(2,128)S(1)}, u32[]{:S(2)}, u32[]{:S(2)}) collective-permute-start(s32[2,1024]{1,0:T(2,128)S(1)} %bitcast.126), channel_id=1, source_target_pairs={{0,4},{4,0},{1,5},{5,1},{2,6},{6,2},{3,7},{7,3},{8,12},{12,8},{9,1... | collective-permute-start | bytes 24584 | tf_op jit(solution)/shard_map/ppermute | solution.py:942
  29.0 15.3 %collective-permute-start = (bf16[1024,768]{1,0:T(8,128)(2,1)}, bf16[1024,768]{1,0:T(8,128)(2,1)S(1)}, u32[]{:S(2)}, u32[]{:S(2)}) collective-permute-start(bf16[1024,768]{1,0:T(8,128)(2,1)} %dynamic-slice_bitcast_fusion), channel_id=1, source_target_pairs={{0,4},{4,0},{1,5},{5,1},{2,6},{6,2},{3,7},{7,3},{8,12},{12,8},{9,1... | collective-permute-start | bytes 4718600 | tf_op jit(solution)/shard_map/ppermute | solution.py:942
  30.4 39.9 %collective-permute-start.9 = (bf16[512,768]{1,0:T(8,128)(2,1)}, bf16[512,768]{1,0:T(8,128)(2,1)}, u32[]{:S(2)}, u32[]{:S(2)}) collective-permute-start(bf16[512,768]{1,0:T(8,128)(2,1)} %dynamic-slice_bitcast_fusion.1), channel_id=1, source_target_pairs={{0,4},{4,0},{1,5},{5,1},{2,6},{6,2},{3,7},{7,3},{8,12},{12,8},{9,1... | collective-permute-start | bytes 2359304 | tf_op jit(solution)/shard_map/ppermute | solution.py:942
  39.6 4.6 %collective-permute-start.5 = (bf16[4,96,576]{2,1,0:T(8,128)(2,1)S(1)}, bf16[4,96,576]{2,1,0:T(8,128)(2,1)S(1)}, u32[]{:S(2)}, u32[]{:S(2)}) collective-permute-start(bf16[4,96,576]{2,1,0:T(8,128)(2,1)S(1)} %pad_maximum_fusion.2), channel_id=1, source_target_pairs={{0,4},{4,0},{1,5},{5,1},{2,6},{6,2},{3,7},{7,3},{8,12},{12,8},{9,1... | collective-permute-start | bytes 1327112 | tf_op jit(solution)/shard_map/ppermute | solution.py:942
  57.4 26.4 %copy-start = (bf16[2048,256]{1,0:T(8,128)(2,1)}, bf16[2048,256]{1,0:T(8,128)(2,1)S(1)}, u32[]{:S(2)}) copy-start(bf16[2048,256]{1,0:T(8,128)(2,1)S(1)} %get-tuple-element.176.v) | copy-start | bytes 3145732
  62.6 11.0 %collective-permute-start.6 = (bf16[512,192]{1,0:T(8,128)(2,1)S(1)}, bf16[512,192]{1,0:T(8,128)(2,1)S(1)}, u32[]{:S(2)}, u32[]{:S(2)}) collective-permute-start(bf16[512,192]{1,0:T(8,128)(2,1)S(1)} %get-tuple-element.180), channel_id=1, source_target_pairs={{0,3},{1,2},{2,1},{3,0},{4,7},{5,6},{6,5},{7,4},{8,11},{9,10},{10,... | collective-permute-start | bytes 589832 | tf_op jit(solution)/shard_map/ppermute | solution.py:946
  70.0 13.8 %collective-permute-start.7 = (bf16[512,192]{1,0:T(8,128)(2,1)S(1)}, bf16[512,192]{1,0:T(8,128)(2,1)S(1)}, u32[]{:S(2)}, u32[]{:S(2)}) collective-permute-start(bf16[512,192]{1,0:T(8,128)(2,1)S(1)} %get-tuple-element.183), channel_id=1, source_target_pairs={{0,1},{1,0},{2,3},{3,2},{4,5},{5,4},{6,7},{7,6},{8,9},{9,8},{10,11... | collective-permute-start | bytes 589832 | tf_op jit(solution)/shard_map/ppermute | solution.py:946
  73.6 21.4 %copy-start.37 = (bf16[512,192]{1,0:T(8,128)(2,1)}, bf16[512,192]{1,0:T(8,128)(2,1)S(1)}, u32[]{:S(2)}) copy-start(bf16[512,192]{1,0:T(8,128)(2,1)S(1)} %collective-permute-done.6.c3) | copy-start | bytes 589828
  83.7 11.2 %collective-permute-start.8 = (bf16[512,192]{1,0:T(8,128)(2,1)S(1)}, bf16[512,192]{1,0:T(8,128)(2,1)S(1)}, u32[]{:S(2)}, u32[]{:S(2)}) collective-permute-start(bf16[512,192]{1,0:T(8,128)(2,1)S(1)} %get-tuple-element.187), channel_id=1, source_target_pairs={{0,2},{1,3},{2,0},{3,1},{4,6},{5,7},{6,4},{7,5},{8,10},{9,11},{10,... | collective-permute-start | bytes 589832 | tf_op jit(solution)/shard_map/ppermute | solution.py:946
  133.7 34.0 %collective-permute-start.17 = (bf16[512,768]{1,0:T(8,128)(2,1)}, bf16[512,768]{1,0:T(8,128)(2,1)}, u32[]{:S(2)}, u32[]{:S(2)}) collective-permute-start(bf16[512,768]{1,0:T(8,128)(2,1)} %get-tuple-element.266.near.refs_0_), channel_id=1, source_target_pairs={{0,2},{1,3},{2,0},{3,1},{4,6},{5,7},{6,4},{7,5},{8,10},{9,11},{10,... | collective-permute-start | bytes 2359304 | tf_op jit(solution)/shard_map/ppermute | solution.py:946
  134.6 33.1 %collective-permute-start.16 = (bf16[512,768]{1,0:T(8,128)(2,1)}, bf16[512,768]{1,0:T(8,128)(2,1)}, u32[]{:S(2)}, u32[]{:S(2)}) collective-permute-start(bf16[512,768]{1,0:T(8,128)(2,1)} %get-tuple-element.266.near.refs_0_), channel_id=1, source_target_pairs={{0,1},{1,0},{2,3},{3,2},{4,5},{5,4},{6,7},{7,6},{8,9},{9,8},{10,11... | collective-permute-start | bytes 2359304 | tf_op jit(solution)/shard_map/ppermute | solution.py:946
  151.3 14.8 %collective-permute-start.13 = (bf16[512,192]{1,0:T(8,128)(2,1)}, bf16[512,192]{1,0:T(8,128)(2,1)S(1)}, u32[]{:S(2)}, u32[]{:S(2)}) collective-permute-start(bf16[512,192]{1,0:T(8,128)(2,1)} %get-tuple-element.213), channel_id=1, source_target_pairs={{0,1},{1,0},{2,3},{3,2},{4,5},{5,4},{6,7},{7,6},{8,9},{9,8},{10,11... | collective-permute-start | bytes 589832 | tf_op jit(solution)/shard_map/ppermute | solution.py:946
  151.4 14.8 %collective-permute-start.14 = (bf16[512,192]{1,0:T(8,128)(2,1)}, bf16[512,192]{1,0:T(8,128)(2,1)S(1)}, u32[]{:S(2)}, u32[]{:S(2)}) collective-permute-start(bf16[512,192]{1,0:T(8,128)(2,1)} %get-tuple-element.214), channel_id=1, source_target_pairs={{0,2},{1,3},{2,0},{3,1},{4,6},{5,7},{6,4},{7,5},{8,10},{9,11},{10,... | collective-permute-start | bytes 589832 | tf_op jit(solution)/shard_map/ppermute | solution.py:946
  152.0 14.9 %collective-permute-start.15 = (bf16[512,192]{1,0:T(8,128)(2,1)}, bf16[512,192]{1,0:T(8,128)(2,1)S(1)}, u32[]{:S(2)}, u32[]{:S(2)}) collective-permute-start(bf16[512,192]{1,0:T(8,128)(2,1)} %get-tuple-element.215), channel_id=1, source_target_pairs={{0,3},{1,2},{2,1},{3,0},{4,7},{5,6},{6,5},{7,4},{8,11},{9,10},{10,... | collective-permute-start | bytes 589832 | tf_op jit(solution)/shard_map/ppermute | solution.py:946
  167.7 6.1 %collective-permute-start.18 = (bf16[4,4,96,768]{3,2,1,0:T(8,128)(2,1)}, bf16[4,4,96,768]{3,2,1,0:T(8,128)(2,1)S(1)}, u32[]{:S(2)}, u32[]{:S(2)}) collective-permute-start(bf16[4,4,96,768]{3,2,1,0:T(8,128)(2,1)} %get-tuple-element.221), channel_id=1, source_target_pairs={{0,4},{4,0},{1,5},{5,1},{2,6},{6,2},{3,7},{7,3},{8,12},{12,8},{9,1... | collective-permute-start | bytes 7077896 | tf_op jit(solution)/shard_map/ppermute | solution.py:942
  176.2 23.9 %collective-permute-start.19 = (bf16[4,96,768]{2,1,0:T(8,128)(2,1)S(1)}, bf16[4,96,768]{2,1,0:T(8,128)(2,1)S(1)}, u32[]{:S(2)}, u32[]{:S(2)}) collective-permute-start(bf16[4,96,768]{2,1,0:T(8,128)(2,1)S(1)} %get-tuple-element.243), channel_id=1, source_target_pairs={{0,1},{1,0},{2,3},{3,2},{4,5},{5,4},{6,7},{7,6},{8,9},{9,8},{10,11... | collective-permute-start | bytes 1769480 | tf_op jit(solution)/shard_map/ppermute | solution.py:946
  176.3 23.9 %collective-permute-start.20 = (bf16[4,96,768]{2,1,0:T(8,128)(2,1)S(1)}, bf16[4,96,768]{2,1,0:T(8,128)(2,1)S(1)}, u32[]{:S(2)}, u32[]{:S(2)}) collective-permute-start(bf16[4,96,768]{2,1,0:T(8,128)(2,1)S(1)} %get-tuple-element.244), channel_id=1, source_target_pairs={{0,2},{1,3},{2,0},{3,1},{4,6},{5,7},{6,4},{7,5},{8,10},{9,11},{10,... | collective-permute-start | bytes 1769480 | tf_op jit(solution)/shard_map/ppermute | solution.py:946
  176.8 26.1 %collective-permute-start.21 = (bf16[4,96,768]{2,1,0:T(8,128)(2,1)S(1)}, bf16[4,96,768]{2,1,0:T(8,128)(2,1)S(1)}, u32[]{:S(2)}, u32[]{:S(2)}) collective-permute-start(bf16[4,96,768]{2,1,0:T(8,128)(2,1)S(1)} %get-tuple-element.245), channel_id=1, source_target_pairs={{0,3},{1,2},{2,1},{3,0},{4,7},{5,6},{6,5},{7,4},{8,11},{9,10},{10,... | collective-permute-start | bytes 1769480 | tf_op jit(solution)/shard_map/ppermute | solution.py:946
  178.9 32.8 %collective-permute-start.22 = (bf16[256,768]{1,0:T(8,128)(2,1)S(1)}, bf16[256,768]{1,0:T(8,128)(2,1)S(1)}, u32[]{:S(2)}, u32[]{:S(2)}) collective-permute-start(bf16[256,768]{1,0:T(8,128)(2,1)S(1)} %slice.73), channel_id=1, source_target_pairs={{0,2},{1,3},{2,0},{3,1},{4,6},{5,7},{6,4},{7,5},{8,10},{9,11},{10,... | collective-permute-start | bytes 1179656 | tf_op jit(solution)/shard_map/ppermute | solution.py:946
  178.9 33.2 %collective-permute-start.23 = (bf16[256,768]{1,0:T(8,128)(2,1)S(1)}, bf16[256,768]{1,0:T(8,128)(2,1)S(1)}, u32[]{:S(2)}, u32[]{:S(2)}) collective-permute-start(bf16[256,768]{1,0:T(8,128)(2,1)S(1)} %slice.74), channel_id=1, source_target_pairs={{0,1},{1,0},{2,3},{3,2},{4,5},{5,4},{6,7},{7,6},{8,9},{9,8},{10,11... | collective-permute-start | bytes 1179656 | tf_op jit(solution)/shard_map/ppermute | solution.py:946
  179.5 23.3 %copy-start.14 = (bf16[768,768]{1,0:T(8,128)(2,1)S(1)}, bf16[768,768]{1,0:T(8,128)(2,1)}, u32[]{:S(2)}) copy-start(bf16[768,768]{1,0:T(8,128)(2,1)} %copy-done.13) | copy-start | bytes 3538948
  179.5 23.3 %copy-start.33 = (s32[10]{0:T(128)S(1)}, s32[10]{0:T(128)}, u32[]{:S(2)}) copy-start(s32[10]{0:T(128)} %copy-done.32) | copy-start | bytes 124
  202.9 15.8 %copy-start.34 = (f32[4,8,768]{2,1,0:T(8,128)S(1)}, f32[4,8,768]{2,1,0:T(8,128)}, u32[]{:S(2)}) copy-start(f32[4,8,768]{2,1,0:T(8,128)} %get-tuple-element.273.hidden_sums) | copy-start | bytes 294916
  202.9 15.8 %copy-start.35 = (f32[8,768]{1,0:T(8,128)S(1)}, f32[8,768]{1,0:T(8,128)}, u32[]{:S(2)}) copy-start(f32[8,768]{1,0:T(8,128)} %get-tuple-element.275.two) | copy-start | bytes 73732
  202.9 15.8 %copy-start.36 = (f32[8,768]{1,0:T(8,128)S(1)}, f32[8,768]{1,0:T(8,128)}, u32[]{:S(2)}) copy-start(f32[8,768]{1,0:T(8,128)} %get-tuple-element.274.one) | copy-start | bytes 73732
  202.9 16.9 %copy-start.7 = (bf16[1024,768]{1,0:T(8,128)(2,1)S(1)}, bf16[1024,768]{1,0:T(8,128)(2,1)}, u32[]{:S(2)}) copy-start(bf16[1024,768]{1,0:T(8,128)(2,1)} %copy-done.5) | copy-start | bytes 4718596
  204.3 15.5 %copy-start.4 = (bf16[2,1024,768]{2,1,0:T(8,128)(2,1)S(1)}, bf16[2,1024,768]{2,1,0:T(8,128)(2,1)}, u32[]{:S(2)}) copy-start(bf16[2,1024,768]{2,1,0:T(8,128)(2,1)} %own.1) | copy-start | bytes 9437188
  214.8 24.7 %collective-permute-start.27 = (bf16[512,768]{1,0:T(8,128)(2,1)S(1)}, bf16[512,768]{1,0:T(8,128)(2,1)S(1)}, u32[]{:S(2)}, u32[]{:S(2)}) collective-permute-start(bf16[512,768]{1,0:T(8,128)(2,1)S(1)} %get-tuple-element.268), channel_id=1, source_target_pairs={{0,4},{4,0},{1,5},{5,1},{2,6},{6,2},{3,7},{7,3},{8,12},{12,8},{9,1... | collective-permute-start | bytes 2359304 | tf_op jit(solution)/shard_map/ppermute | solution.py:942
  218.7 20.8 %collective-permute-start.28 = (bf16[512,768]{1,0:T(8,128)(2,1)S(1)}, bf16[512,768]{1,0:T(8,128)(2,1)S(1)}, u32[]{:S(2)}, u32[]{:S(2)}) collective-permute-start(bf16[512,768]{1,0:T(8,128)(2,1)S(1)} %get-tuple-element.272), channel_id=1, source_target_pairs={{0,4},{4,0},{1,5},{5,1},{2,6},{6,2},{3,7},{7,3},{8,12},{12,8},{9,1... | collective-permute-start | bytes 2359304 | tf_op jit(solution)/shard_map/ppermute | solution.py:942
  219.2 4.7 %collective-permute-start.29 = (f32[16,768]{1,0:T(8,128)S(1)}, f32[16,768]{1,0:T(8,128)S(1)}, u32[]{:S(2)}, u32[]{:S(2)}) collective-permute-start(f32[16,768]{1,0:T(8,128)S(1)} %collect.1), channel_id=1, source_target_pairs={{0,4},{4,0},{1,5},{5,1},{2,6},{6,2},{3,7},{7,3},{8,12},{12,8},{9,1... | collective-permute-start | bytes 147464 | tf_op jit(solution)/shard_map/ppermute | solution.py:942
  223.8 8.6 %collective-permute-start.24 = (bf16[4,96,576]{2,1,0:T(8,128)(2,1)S(1)}, bf16[4,96,576]{2,1,0:T(8,128)(2,1)S(1)}, u32[]{:S(2)}, u32[]{:S(2)}) collective-permute-start(bf16[4,96,576]{2,1,0:T(8,128)(2,1)S(1)} %get-tuple-element.256), channel_id=1, source_target_pairs={{0,4},{4,0},{1,5},{5,1},{2,6},{6,2},{3,7},{7,3},{8,12},{12,8},{9,1... | collective-permute-start | bytes 1327112 | tf_op jit(solution)/shard_map/ppermute | solution.py:942
  224.0 4.3 %collective-permute-start.30 = (f32[16,768]{1,0:T(8,128)S(1)}, f32[16,768]{1,0:T(8,128)S(1)}, u32[]{:S(2)}, u32[]{:S(2)}) collective-permute-start(f32[16,768]{1,0:T(8,128)S(1)} %add.168), channel_id=1, source_target_pairs={{0,8},{8,0},{16,24},{24,16},{1,9},{9,1},{17,25},{25,17},{2,10},{10... | collective-permute-start | bytes 147464 | tf_op jit(solution)/shard_map/ppermute | solution.py:950
  225.2 14.3 %collective-permute-start.25 = (bf16[256,768]{1,0:T(8,128)(2,1)S(1)}, bf16[256,768]{1,0:T(8,128)(2,1)S(1)}, u32[]{:S(2)}, u32[]{:S(2)}) collective-permute-start(bf16[256,768]{1,0:T(8,128)(2,1)S(1)} %get-tuple-element.360), channel_id=1, source_target_pairs={{0,2},{1,3},{2,0},{3,1},{4,6},{5,7},{6,4},{7,5},{8,10},{9,11},{10,... | collective-permute-start | bytes 1179656 | tf_op jit(solution)/shard_map/ppermute | solution.py:946
  228.3 11.2 %collective-permute-start.26 = (bf16[256,768]{1,0:T(8,128)(2,1)S(1)}, bf16[256,768]{1,0:T(8,128)(2,1)S(1)}, u32[]{:S(2)}, u32[]{:S(2)}) collective-permute-start(bf16[256,768]{1,0:T(8,128)(2,1)S(1)} %get-tuple-element.359), channel_id=1, source_target_pairs={{0,1},{1,0},{2,3},{3,2},{4,5},{5,4},{6,7},{7,6},{8,9},{9,8},{10,11... | collective-permute-start | bytes 1179656 | tf_op jit(solution)/shard_map/ppermute | solution.py:946
  239.7 30.9 %collective-permute-start.31 = (bf16[512,768]{1,0:T(8,128)(2,1)S(1)}, bf16[512,768]{1,0:T(8,128)(2,1)S(1)}, u32[]{:S(2)}, u32[]{:S(2)}) collective-permute-start(bf16[512,768]{1,0:T(8,128)(2,1)S(1)} %get-tuple-element.286), channel_id=1, source_target_pairs={{0,1},{1,0},{2,3},{3,2},{4,5},{5,4},{6,7},{7,6},{8,9},{9,8},{10,11... | collective-permute-start | bytes 2359304 | tf_op jit(solution)/shard_map/ppermute | solution.py:946
  240.9 29.7 %collective-permute-start.32 = (bf16[512,768]{1,0:T(8,128)(2,1)S(1)}, bf16[512,768]{1,0:T(8,128)(2,1)S(1)}, u32[]{:S(2)}, u32[]{:S(2)}) collective-permute-start(bf16[512,768]{1,0:T(8,128)(2,1)S(1)} %get-tuple-element.287), channel_id=1, source_target_pairs={{0,2},{1,3},{2,0},{3,1},{4,6},{5,7},{6,4},{7,5},{8,10},{9,11},{10,... | collective-permute-start | bytes 2359304 | tf_op jit(solution)/shard_map/ppermute | solution.py:946
  241.2 8.1 %collective-permute-start.33 = (bf16[96,576]{1,0:T(8,128)(2,1)S(1)}, bf16[96,576]{1,0:T(8,128)(2,1)S(1)}, u32[]{:S(2)}, u32[]{:S(2)}) collective-permute-start(bf16[96,576]{1,0:T(8,128)(2,1)S(1)} %get-tuple-element.289), channel_id=1, source_target_pairs={{0,8},{8,0},{16,24},{24,16},{1,9},{9,1},{17,25},{25,17},{2,10},{10... | collective-permute-start | bytes 331784 | tf_op jit(solution)/shard_map/ppermute | solution.py:950
  242.3 28.0 %collective-permute-start.36 = (bf16[96,576]{1,0:T(8,128)(2,1)S(1)}, bf16[96,576]{1,0:T(8,128)(2,1)S(1)}, u32[]{:S(2)}, u32[]{:S(2)}) collective-permute-start(bf16[96,576]{1,0:T(8,128)(2,1)S(1)} %get-tuple-element.304), channel_id=1, source_target_pairs={{0,16},{8,24},{16,0},{24,8},{1,17},{9,25},{17,1},{25,9},{2,18},{10... | collective-permute-start | bytes 331784 | tf_op jit(solution)/shard_map/ppermute | solution.py:950
  244.5 25.8 %collective-permute-start.37 = (bf16[96,576]{1,0:T(8,128)(2,1)S(1)}, bf16[96,576]{1,0:T(8,128)(2,1)S(1)}, u32[]{:S(2)}, u32[]{:S(2)}) collective-permute-start(bf16[96,576]{1,0:T(8,128)(2,1)S(1)} %get-tuple-element.305), channel_id=1, source_target_pairs={{0,24},{8,16},{16,8},{24,0},{1,25},{9,17},{17,9},{25,1},{2,26},{10... | collective-permute-start | bytes 331784 | tf_op jit(solution)/shard_map/ppermute | solution.py:950
  249.3 12.8 %collective-permute-start.34 = (f32[16,768]{1,0:T(8,128)S(1)}, f32[16,768]{1,0:T(8,128)S(1)}, u32[]{:S(2)}, u32[]{:S(2)}) collective-permute-start(f32[16,768]{1,0:T(8,128)S(1)} %add.169), channel_id=1, source_target_pairs={{0,1},{1,0},{2,3},{3,2},{4,5},{5,4},{6,7},{7,6},{8,9},{9,8},{10,11... | collective-permute-start | bytes 147464 | tf_op jit(solution)/shard_map/ppermute | solution.py:946
  262.1 8.5 %collective-permute-start.35 = (f32[16,768]{1,0:T(8,128)S(1)}, f32[16,768]{1,0:T(8,128)S(1)}, u32[]{:S(2)}, u32[]{:S(2)}) collective-permute-start(f32[16,768]{1,0:T(8,128)S(1)} %add.170), channel_id=1, source_target_pairs={{0,16},{8,24},{16,0},{24,8},{1,17},{9,25},{17,1},{25,9},{2,18},{10... | collective-permute-start | bytes 147464 | tf_op jit(solution)/shard_map/ppermute | solution.py:950
  270.9 19.8 %collective-permute-start.39 = (bf16[512,768]{1,0:T(8,128)(2,1)S(1)}, bf16[512,768]{1,0:T(8,128)(2,1)S(1)}, u32[]{:S(2)}, u32[]{:S(2)}) collective-permute-start(bf16[512,768]{1,0:T(8,128)(2,1)S(1)} %add_block.1.near.refs_0_), channel_id=1, source_target_pairs={{0,2},{1,3},{2,0},{3,1},{4,6},{5,7},{6,4},{7,5},{8,10},{9,11},{10,... | collective-permute-start | bytes 2359304 | tf_op jit(solution)/shard_map/ppermute | solution.py:946
  271.3 19.4 %collective-permute-start.38 = (bf16[512,768]{1,0:T(8,128)(2,1)S(1)}, bf16[512,768]{1,0:T(8,128)(2,1)S(1)}, u32[]{:S(2)}, u32[]{:S(2)}) collective-permute-start(bf16[512,768]{1,0:T(8,128)(2,1)S(1)} %add_block.1.near.refs_0_), channel_id=1, source_target_pairs={{0,1},{1,0},{2,3},{3,2},{4,5},{5,4},{6,7},{7,6},{8,9},{9,8},{10,11... | collective-permute-start | bytes 2359304 | tf_op jit(solution)/shard_map/ppermute | solution.py:946
  272.4 4.3 %collective-permute-start.40 = (bf16[96,768]{1,0:T(8,128)(2,1)S(1)}, bf16[96,768]{1,0:T(8,128)(2,1)S(1)}, u32[]{:S(2)}, u32[]{:S(2)}) collective-permute-start(bf16[96,768]{1,0:T(8,128)(2,1)S(1)} %get-tuple-element.312), channel_id=1, source_target_pairs={{0,8},{8,0},{16,24},{24,16},{1,9},{9,1},{17,25},{25,17},{2,10},{10... | collective-permute-start | bytes 442376 | tf_op jit(solution)/shard_map/ppermute | solution.py:950
  273.6 11.5 %collective-permute-start.41 = (bf16[96,768]{1,0:T(8,128)(2,1)S(1)}, bf16[96,768]{1,0:T(8,128)(2,1)S(1)}, u32[]{:S(2)}, u32[]{:S(2)}) collective-permute-start(bf16[96,768]{1,0:T(8,128)(2,1)S(1)} %get-tuple-element.315), channel_id=1, source_target_pairs={{0,16},{8,24},{16,0},{24,8},{1,17},{9,25},{17,1},{25,9},{2,18},{10... | collective-permute-start | bytes 442376 | tf_op jit(solution)/shard_map/ppermute | solution.py:950
  273.6 11.5 %collective-permute-start.42 = (bf16[96,768]{1,0:T(8,128)(2,1)S(1)}, bf16[96,768]{1,0:T(8,128)(2,1)S(1)}, u32[]{:S(2)}, u32[]{:S(2)}) collective-permute-start(bf16[96,768]{1,0:T(8,128)(2,1)S(1)} %get-tuple-element.316), channel_id=1, source_target_pairs={{0,24},{8,16},{16,8},{24,0},{1,25},{9,17},{17,9},{25,1},{2,26},{10... | collective-permute-start | bytes 442376 | tf_op jit(solution)/shard_map/ppermute | solution.py:950
  276.7 14.0 %collective-permute-start.43 = (f32[16,768]{1,0:T(8,128)S(1)}, f32[16,768]{1,0:T(8,128)S(1)}, u32[]{:S(2)}, u32[]{:S(2)}) collective-permute-start(f32[16,768]{1,0:T(8,128)S(1)} %add.171), channel_id=1, source_target_pairs={{0,2},{1,3},{2,0},{3,1},{4,6},{5,7},{6,4},{7,5},{8,10},{9,11},{10,... | collective-permute-start | bytes 147464 | tf_op jit(solution)/shard_map/ppermute | solution.py:946
  292.2 4.6 %collective-permute-start.46 = (bf16[512,768]{1,0:T(8,128)(2,1)S(1)}, bf16[512,768]{1,0:T(8,128)(2,1)S(1)}, u32[]{:S(2)}, u32[]{:S(2)}) collective-permute-start(bf16[512,768]{1,0:T(8,128)(2,1)S(1)} %get-tuple-element.322), channel_id=1, source_target_pairs={{0,4},{4,0},{1,5},{5,1},{2,6},{6,2},{3,7},{7,3},{8,12},{12,8},{9,1... | collective-permute-start | bytes 2359304 | tf_op jit(solution)/shard_map/ppermute | solution.py:942
  295.0 10.8 %collective-permute-start.45 = (bf16[256,768]{1,0:T(8,128)(2,1)S(1)}, bf16[256,768]{1,0:T(8,128)(2,1)S(1)}, u32[]{:S(2)}, u32[]{:S(2)}) collective-permute-start(bf16[256,768]{1,0:T(8,128)(2,1)S(1)} %slice.86), channel_id=1, source_target_pairs={{0,1},{1,0},{2,3},{3,2},{4,5},{5,4},{6,7},{7,6},{8,9},{9,8},{10,11... | collective-permute-start | bytes 1179656 | tf_op jit(solution)/shard_map/ppermute | solution.py:946
  296.2 10.4 %collective-permute-start.44 = (bf16[256,768]{1,0:T(8,128)(2,1)S(1)}, bf16[256,768]{1,0:T(8,128)(2,1)S(1)}, u32[]{:S(2)}, u32[]{:S(2)}) collective-permute-start(bf16[256,768]{1,0:T(8,128)(2,1)S(1)} %slice.85), channel_id=1, source_target_pairs={{0,2},{1,3},{2,0},{3,1},{4,6},{5,7},{6,4},{7,5},{8,10},{9,11},{10,... | collective-permute-start | bytes 1179656 | tf_op jit(solution)/shard_map/ppermute | solution.py:946
  307.8 4.3 %collective-permute-start.47 = (bf16[512,768]{1,0:T(8,128)(2,1)}, bf16[512,768]{1,0:T(8,128)(2,1)S(1)}, u32[]{:S(2)}, u32[]{:S(2)}) collective-permute-start(bf16[512,768]{1,0:T(8,128)(2,1)} %maximum_select_fusion), channel_id=1, source_target_pairs={{0,4},{4,0},{1,5},{5,1},{2,6},{6,2},{3,7},{7,3},{8,12},{12,8},{9,1... | collective-permute-start | bytes 2359304 | tf_op jit(solution)/shard_map/ppermute | solution.py:942
  (32 other events, 156.2 us)
Sparse Core Ops, SparseCore 0:
  11.6 100.9 all-gather.1
  167.8 126.1 reduce-scatter.1
